TPU v7x, 128 devices: a whole 4x4x4 slice. The times are simulated.
128 devices in a mesh: gx: 16 (over y_lo, x, core), gy: 8 (over z, y_hi).
Axes of the slice: x: 4, y: 4 (y_hi: 2, y_lo: 2; y = y_hi * 2 + y_lo), z: 4, core: 2. Of those that a mesh axis runs over, the one named last changes fastest.
Arguments:
- previous: float32 [256, 256, 2048], P('gx', 'gy'), may hold values from -1.8 to 1.8
- source: float32 [256, 256, 2048], P('gx', 'gy'), may hold values from -5 to 5
- conductivity: float32 [256, 256, 2048], P('gx', 'gy'), may hold values from 0.24 to 8.1
Outputs:
- correction: float32 [256, 256, 2048], P('gx', 'gy')
All inputs are finite; a program needn't handle non-finite values.
Results may differ from a plain program's by a relative error of at most 0.000068.
Values sent between devices are 32-bit elements; how exact they have to be, the bound alone decides.
No kernel may reach another device: no remote copies, remote signals or barrier semaphores. Data moves between devices by JAX's collectives and lax.ppermute only.
A program may use at most 320 MiB of HBM per device.

v0:
```python
import functools
import jax
import jax.numpy as jnp
from jax import lax
from jax.experimental import pallas as pl
from jax.experimental.pallas import tpu as pltpu
from jax.sharding import PartitionSpec as P

F = 16
CSWEEPS = 32
REACTION = 0.2
DAMPING = 0.8
COARSE_FACTOR = 0.25
F32 = jnp.float32
BF16 = jnp.bfloat16
STRIP = 8

VM = pl.BlockSpec(memory_space=pltpu.VMEM)
SM = pl.BlockSpec(memory_space=pltpu.SMEM)
ANY = pl.BlockSpec(memory_space=pl.ANY)


def params(mib):
    return pltpu.CompilerParams(vmem_limit_bytes=mib * 1024 * 1024)


def cost(flops, nbytes):
    return pl.CostEstimate(flops=int(flops), bytes_accessed=int(nbytes), transcendentals=0)


def sds(*shape):
    return jax.ShapeDtypeStruct(shape, F32)


def zp(a):
    return pltpu.roll(a, a.shape[-1] - 1, a.ndim - 1)


def zm(a):
    return pltpu.roll(a, 1, a.ndim - 1)


def beside_rows(ref, x, r, rows, value):
    low, high = r * STRIP, (r + 1) * STRIP
    up = ref[x, low + 1 : high + 1, :] if high < rows else pltpu.roll(value, STRIP - 1, 0)
    down = ref[x, low - 1 : high - 1, :] if low > 0 else pltpu.roll(value, 1, 0)
    return up, down


def row_halves(r, rows, cols):
    sub = lax.broadcasted_iota(jnp.int32, (STRIP, cols), 0)
    up = jnp.where(sub == STRIP - 1, 0.0, 0.5).astype(F32) if (r + 1) * STRIP == rows else 0.5
    down = jnp.where(sub == 0, 0.0, 0.5).astype(F32) if r == 0 else 0.5
    return up, down


def couplings(k, x, planes, r, rows):
    k0 = k[x, r * STRIP : (r + 1) * STRIP, :]
    up, down = beside_rows(k, x, r, rows, k0)
    h_up, h_down = row_halves(r, rows, k0.shape[-1])
    h_next = jnp.where(x < planes - 1, 0.5, 0.0).astype(F32)
    h_prev = jnp.where(x > 0, 0.5, 0.0).astype(F32)
    xn, xp = jnp.minimum(x + 1, planes - 1), jnp.maximum(x - 1, 0)
    c_next = h_next * (k0 + k[xn, r * STRIP : (r + 1) * STRIP, :])
    c_prev = h_prev * (k0 + k[xp, r * STRIP : (r + 1) * STRIP, :])
    c_up = h_up * (k0 + up)
    c_down = h_down * (k0 + down)
    c_z = 0.5 * (k0 + zp(k0))
    return k0, xn, xp, c_next, c_prev, c_up, c_down, c_z


def inner_kernel(v, s, k, w_ref, f_ref, dpl, rpl, drow, rrow, sums):
    planes, rows, cols = v.shape
    sums[...] = jnp.zeros_like(sums)

    def plane(x, carry):
        for r in range(rows // STRIP):
            sl = slice(r * STRIP, (r + 1) * STRIP)
            k0, xn, xp, c_next, c_prev, c_up, c_down, c_z = couplings(k, x, planes, r, rows)
            v0 = v[x, sl, :]
            v_up, v_down = beside_rows(v, x, r, rows, v0)
            f_z = c_z * (v0 - zp(v0))
            diag = REACTION + c_next + c_prev + c_up + c_down + c_z + zm(c_z)
            res = (
                s[x, sl, :]
                - REACTION * v0
                - c_next * (v0 - v[xn, sl, :])
                - c_prev * (v0 - v[xp, sl, :])
                - c_up * (v0 - v_up)
                - c_down * (v0 - v_down)
                - f_z
                + zm(f_z)
            )
            w = DAMPING / diag
            w_ref[x, sl, :] = w
            f_ref[x, sl, :] = w * res
            half = r * STRIP // F
            sums[half * STRIP : (half + 1) * STRIP, :] += res
            sums[(2 + half) * STRIP : (3 + half) * STRIP, :] += k0
            if r == 0:
                drow[0, pl.ds(x, 1), :] = diag[0:1]
                rrow[0, pl.ds(x, 1), :] = res[0:1]
            if (r + 1) * STRIP == rows:
                drow[1, pl.ds(x, 1), :] = diag[STRIP - 1 :]
                rrow[1, pl.ds(x, 1), :] = res[STRIP - 1 :]

            @pl.when((x == 0) | (x == planes - 1))
            def _():
                side = jnp.where(x == 0, 0, 1)
                dpl[side, sl, :] = diag
                rpl[side, sl, :] = res

        return carry

    lax.fori_loop(0, planes, plane, 0)


def cross(gpl, grow, pl_ref, row_ref, sign):
    rows, planes = gpl.shape[1], grow.shape[1]
    pl_ref[...] = pl_ref[...] + sign * gpl[...]
    row_ref[...] = row_ref[...] + sign * grow[...]
    for a, x in ((0, 0), (1, planes - 1)):
        for b, y in ((0, 0), (1, rows - 1)):
            pl_ref[a, y : y + 1, :] = pl_ref[a, y : y + 1, :] + sign * grow[b, x : x + 1, :]
            row_ref[b, x : x + 1, :] = row_ref[b, x : x + 1, :] + sign * gpl[a, y : y + 1, :]


def split3(a):
    one = a.astype(BF16)
    rest = a - one.astype(F32)
    two = rest.astype(BF16)
    three = (rest - two.astype(F32)).astype(BF16)
    return jnp.concatenate([one, two, three], 0)


def joined3(a):
    n = a.shape[0] // 3
    return a[:n] + a[n : 2 * n] + a[2 * n :]


def edge_kernel(
    dpl, rpl, drow, rrow, pl_lo, pl_hi, rw_lo, rw_hi, xl, xh, yl, yh, sums,
    f_pl, f_row, w_pl, w_row, wc_pl, wc_row, payload,
    c_pl, c_row, q_pl, q_row,
):
    cols = dpl.shape[2]
    rows = dpl.shape[1]
    for side, mine, other in ((0, pl_lo, xl), (1, pl_hi, xh)):
        c_pl[side] = 0.5 * (mine[1] + other[1])
        q_pl[side] = c_pl[side] * (mine[0] - other[0])
    for side, mine, other in ((0, rw_lo, yl), (1, rw_hi, yh)):
        c_row[side] = 0.5 * (mine[1] + other[1])
        q_row[side] = c_row[side] * (mine[0] - other[0])
    w_pl[...] = dpl[...]
    w_row[...] = drow[...]
    cross(c_pl, c_row, w_pl, w_row, 1.0)
    f_pl[...] = rpl[...]
    f_row[...] = rrow[...]
    cross(q_pl, q_row, f_pl, f_row, -1.0)
    w_pl[...] = DAMPING / w_pl[...]
    w_row[...] = DAMPING / w_row[...]
    f_pl[...] = f_pl[...] * w_pl[...]
    f_row[...] = f_row[...] * w_row[...]
    wc_pl[...] = w_pl[...] * c_pl[...]
    wc_row[...] = w_row[...] * c_row[...]
    parts = []
    for half in range(rows // F):
        total = sums[half * STRIP : (half + 1) * STRIP, :]
        for side in range(2):
            for r in range(half * F // STRIP, (half + 1) * F // STRIP):
                total = total - q_pl[side, r * STRIP : (r + 1) * STRIP, :]
        if half == 0:
            for r in range(q_row.shape[1] // STRIP):
                total = total - q_row[0, r * STRIP : (r + 1) * STRIP, :]
        if half == rows // F - 1:
            for r in range(q_row.shape[1] // STRIP):
                total = total - q_row[1, r * STRIP : (r + 1) * STRIP, :]
        parts.append(total)
    parts.append(sums[2 * STRIP :, :])
    col = lax.broadcasted_iota(jnp.int32, (cols, cols // F), 0)
    cell = lax.broadcasted_iota(jnp.int32, (cols, cols // F), 1)
    gather = jnp.where(col // F == cell, 1.0, 0.0).astype(BF16)
    reduced = joined3(
        jnp.dot(split3(jnp.concatenate(parts, 0)), gather, preferred_element_type=F32)
    )
    means = [
        jnp.sum(reduced[i * STRIP : (i + 1) * STRIP], axis=0, keepdims=True) * (1.0 / F**3)
        for i in range(4)
    ]
    tile = jnp.concatenate(means + means, 0)
    for i in range(payload.shape[0] // STRIP):
        payload[i * STRIP : (i + 1) * STRIP, :] = tile


def put_edges(ref, e_pl, e_row):
    planes, rows, _ = ref.shape
    for x in range(planes):
        ref[x, 0:1, :] = e_row[0, x : x + 1, :]
        ref[x, rows - 1 : rows, :] = e_row[1, x : x + 1, :]
    ref[0] = e_pl[0]
    ref[planes - 1] = e_pl[1]


def neighbour_sum(k, u, x, planes, r, rows):
    sl = slice(r * STRIP, (r + 1) * STRIP)
    k0, xn, xp, c_next, c_prev, c_up, c_down, c_z = couplings(k, x, planes, r, rows)
    u0 = u[x, sl, :]
    u_up, u_down = beside_rows(u, x, r, rows, u0)
    total = (
        c_next * u[xn, sl, :]
        + c_prev * u[xp, sl, :]
        + c_up * u_up
        + c_down * u_down
        + c_z * zp(u0)
        + zm(c_z * u0)
    )
    return u0, total


def sweep_kernel(k, w, f, w_pl, w_row, f_pl, f_row, g_ref, g_pl, g_row):
    planes, rows, cols = k.shape
    put_edges(w, w_pl, w_row)
    put_edges(f, f_pl, f_row)

    def plane(x, carry):
        for r in range(rows // STRIP):
            sl = slice(r * STRIP, (r + 1) * STRIP)
            u0, total = neighbour_sum(k, f, x, planes, r, rows)
            new = (2.0 - DAMPING) * u0 + w[x, sl, :] * total
            g_ref[x, sl, :] = new
            if r == 0:
                g_row[0, pl.ds(x, 1), :] = new[0:1]
            if (r + 1) * STRIP == rows:
                g_row[1, pl.ds(x, 1), :] = new[STRIP - 1 :]
        return carry

    lax.fori_loop(0, planes, plane, 0)
    g_pl[0] = g_ref[0]
    g_pl[1] = g_ref[planes - 1]


def mid_kernel(g_pl, g_row, wc_pl, wc_row, xl, xh, yl, yh, o_pl, o_row, q_pl, q_row):
    for side, other in ((0, xl), (1, xh)):
        q_pl[side] = wc_pl[side] * other[...]
    for side, other in ((0, yl), (1, yh)):
        q_row[side] = wc_row[side] * other[...]
    o_pl[...] = g_pl[...]
    o_row[...] = g_row[...]
    cross(q_pl, q_row, o_pl, o_row, 1.0)


def last_kernel(k, w, f, g, interp, w_pl, w_row, f_pl, f_row, g_pl, g_row, out):
    planes, rows, cols = k.shape
    put_edges(w, w_pl, w_row)
    put_edges(f, f_pl, f_row)
    put_edges(g, g_pl, g_row)

    def plane(x, carry):
        offset = ((x % F).astype(F32) + 0.5) / F - 0.5
        weight = jnp.abs(offset)
        side = jnp.where(offset > 0, 2, 0)
        for r in range(rows // STRIP):
            sl = slice(r * STRIP, (r + 1) * STRIP)
            u0, total = neighbour_sum(k, g, x, planes, r, rows)
            coarse = (1.0 - weight) * interp[1, sl, :] + weight * interp[side, sl, :]
            new = f[x, sl, :] + (1.0 - DAMPING) * u0 + w[x, sl, :] * total
            out[x, sl, :] = new + coarse
        return carry

    lax.fori_loop(0, planes, plane, 0)


def finish_kernel(src, wc_pl, wc_row, xl, xh, yl, yh, out, b_pl, b_lo, b_hi, sems):
    planes, rows, _ = out.shape
    spots = (
        (out.at[0], b_pl.at[0]),
        (out.at[planes - 1], b_pl.at[1]),
        (out.at[1 : planes - 1, 0:STRIP, :], b_lo),
        (out.at[1 : planes - 1, rows - STRIP : rows, :], b_hi),
    )
    reads = [pltpu.make_async_copy(o, b, sems.at[i]) for i, (o, b) in enumerate(spots)]
    for c in reads:
        c.start()
    for c in reads:
        c.wait()
    for side, other in ((0, xl), (1, xh)):
        x = side * (planes - 1)
        b_pl[side] = b_pl[side] + wc_pl[side] * other[...]
        b_pl[side, 0:1, :] = b_pl[side, 0:1, :] + wc_row[0, x : x + 1, :] * yl[x : x + 1, :]
        b_pl[side, rows - 1 : rows, :] = (
            b_pl[side, rows - 1 : rows, :] + wc_row[1, x : x + 1, :] * yh[x : x + 1, :]
        )
    for x in range(1, planes - 1):
        b_lo[x - 1, 0:1, :] = b_lo[x - 1, 0:1, :] + wc_row[0, x : x + 1, :] * yl[x : x + 1, :]
        b_hi[x - 1, STRIP - 1 :, :] = (
            b_hi[x - 1, STRIP - 1 :, :] + wc_row[1, x : x + 1, :] * yh[x : x + 1, :]
        )
    writes = [pltpu.make_async_copy(b, o, sems.at[i]) for i, (o, b) in enumerate(spots)]
    for c in writes:
        c.start()
    for c in writes:
        c.wait()


def coarse_kernel(place, got, interp, coef, b_ref, u_ref, *, nx, ny, rows):
    nz = got.shape[1]
    per = 2 * 2

    def field(start):
        return [
            jnp.stack([got[pl.ds(p * ny * per + start + t, ny, stride=per), :] for p in range(nx)], 0)
            for t in range(2)
        ]

    resid, cond = field(0), field(2)

    def beside(a, t):
        mine = a[t]
        nxt = jnp.concatenate([mine[1:], mine[:1]], 0)
        prv = jnp.concatenate([mine[-1:], mine[:-1]], 0)
        up = a[1] if t == 0 else pltpu.roll(a[0], ny - 1, 1)
        down = a[0] if t == 1 else pltpu.roll(a[1], 1, 1)
        return nxt, prv, up, down, pltpu.roll(mine, 1, 2), pltpu.roll(mine, nz - 1, 2)

    for t in range(2):
        cs = [(0.5 * COARSE_FACTOR) * (cond[t] + other) for other in beside(cond, t)]
        diag = REACTION
        for c in cs:
            diag = diag + c
        inv = DAMPING / diag
        for i, c in enumerate(cs):
            coef[i, t] = inv * c
        b_ref[t] = inv * resid[t]
        u_ref[0, t] = b_ref[t]

    def sweep(src, dst):
        for p in range(nx):
            pn, pp = (p + 1) % nx, (p - 1) % nx
            u = [u_ref[src, t, p] for t in range(2)]
            for t in range(2):
                up = u[1] if t == 0 else pltpu.roll(u[0], ny - 1, 0)
                down = u[0] if t == 1 else pltpu.roll(u[1], 1, 0)
                a = b_ref[t, p] + (1.0 - DAMPING) * u[t]
                a = a + coef[0, t, p] * u_ref[src, t, pn]
                a = a + coef[1, t, p] * u_ref[src, t, pp]
                c = coef[2, t, p] * up + coef[3, t, p] * down
                c = c + coef[4, t, p] * pltpu.roll(u[t], 1, 1)
                c = c + coef[5, t, p] * pltpu.roll(u[t], nz - 1, 1)
                u_ref[dst, t, p] = a + c

    def pair(i, carry):
        sweep(0, 1)
        sweep(1, 0)
        return carry

    steps = CSWEEPS - 1
    lax.fori_loop(0, steps // 2, pair, 0)
    last = 0
    if steps % 2:
        sweep(0, 1)
        last = 1

    gx, gy = place[0], place[1]
    lines = []
    for d in (-1, 0, 1):
        p = lax.rem(gx + d + nx, nx)
        prev_s, next_s = lax.rem(gy + ny - 1, ny), lax.rem(gy + 1, ny)
        for t, s in ((1, prev_s), (0, gy), (1, gy), (0, next_s)):
            lines.append(u_ref[last, t, p, pl.ds(s, 1), :])
    lines = jnp.concatenate(lines + lines[:4], 0)
    cols = nz * F
    cell = lax.broadcasted_iota(jnp.int32, (nz, cols), 0)
    col = lax.broadcasted_iota(jnp.int32, (nz, cols), 1)
    base = col // F
    offset = ((col % F).astype(F32) + 0.5) / F - 0.5
    side = jnp.where(offset > 0, base + 1, base - 1)
    side = jnp.where(side < 0, side + nz, jnp.where(side >= nz, side - nz, side))
    weight = jnp.abs(offset)
    matrix = jnp.where(cell == base, 1.0 - weight, 0.0) + jnp.where(cell == side, weight, 0.0)
    wide = joined3(jnp.dot(split3(lines), matrix.astype(BF16), preferred_element_type=F32))
    sub = lax.broadcasted_iota(jnp.int32, (STRIP, cols), 0)
    for plane in range(3):
        for r in range(rows // STRIP):
            row = r * STRIP + sub
            off = ((row % F).astype(F32) + 0.5) / F - 0.5
            wt = jnp.abs(off)
            block = r * STRIP // F
            near = block + 1
            far = near + (1 if (r * STRIP) % F >= F // 2 else -1)
            a = wide[plane * 4 + near : plane * 4 + near + 1]
            c = wide[plane * 4 + far : plane * 4 + far + 1]
            interp[plane, r * STRIP : (r + 1) * STRIP, :] = (1.0 - wt) * a + wt * c


def swap(axis, low, high):
    count = lax.axis_size(axis)
    forward = [(i, (i + 1) % count) for i in range(count)]
    backward = [(i, (i - 1) % count) for i in range(count)]
    return lax.ppermute(high, axis, forward), lax.ppermute(low, axis, backward)


def per_device(nx, ny, v, s, k):
    planes, rows, cols = v.shape
    n = planes * rows * cols
    vm = pltpu.VMEM
    rw_lo = jnp.stack([v[:, 0], k[:, 0]])
    rw_hi = jnp.stack([v[:, rows - 1], k[:, rows - 1]])
    yl, yh = swap("gy", rw_lo, rw_hi)
    pl_lo = jnp.stack([v[0], k[0]])
    pl_hi = jnp.stack([v[planes - 1], k[planes - 1]])
    xl, xh = swap("gx", pl_lo, pl_hi)

    full, e_pl, e_row = sds(planes, rows, cols), sds(2, rows, cols), sds(2, planes, cols)
    w, f, dpl, rpl, drow, rrow, sums = pl.pallas_call(
        inner_kernel,
        out_shape=(full, full, e_pl, e_pl, e_row, e_row, sds(4 * STRIP, cols)),
        in_specs=[VM] * 3,
        out_specs=(VM,) * 7,
        compiler_params=params(40),
        cost_estimate=cost(50 * n, 20 * n),
        name="inner",
    )(v, s, k)

    devices = nx * ny
    f_pl, f_row, w_pl, w_row, wc_pl, wc_row, payload = pl.pallas_call(
        edge_kernel,
        out_shape=(e_pl, e_row, e_pl, e_row, e_pl, e_row, sds(devices * 4, cols // F)),
        in_specs=[VM] * 13,
        out_specs=(VM,) * 7,
        scratch_shapes=[vm(e.shape, F32) for e in (e_pl, e_row, e_pl, e_row)],
        compiler_params=params(32),
        cost_estimate=cost(10 * n // 8, n),
        name="edge",
    )(dpl, rpl, drow, rrow, pl_lo, pl_hi, rw_lo, rw_hi, xl, xh, yl, yh, sums)

    fyl, fyh = swap("gy", f_row[0], f_row[1])
    fxl, fxh = swap("gx", f_pl[0], f_pl[1])
    got = lax.all_to_all(payload, ("gx", "gy"), 0, 0, tiled=True)

    g, g_pl, g_row = pl.pallas_call(
        sweep_kernel,
        out_shape=(full, e_pl, e_row),
        in_specs=[VM] * 7,
        out_specs=(VM,) * 3,
        compiler_params=params(40),
        cost_estimate=cost(40 * n, 16 * n),
        name="sweep",
    )(k, w, f, w_pl, w_row, f_pl, f_row)

    h_pl, h_row = pl.pallas_call(
        mid_kernel,
        out_shape=(e_pl, e_row),
        in_specs=[VM] * 8,
        out_specs=(VM,) * 2,
        scratch_shapes=[vm(e_pl.shape, F32), vm(e_row.shape, F32)],
        compiler_params=params(24),
        cost_estimate=cost(n // 8, n // 2),
        name="mid",
    )(g_pl, g_row, wc_pl, wc_row, fxl, fxh, fyl, fyh)

    gyl, gyh = swap("gy", h_row[0], h_row[1])
    gxl, gxh = swap("gx", h_pl[0], h_pl[1])

    place = jnp.stack([lax.axis_index("gx"), lax.axis_index("gy")]).astype(jnp.int32)
    cells = (nx, ny, cols // F)
    interp = pl.pallas_call(
        functools.partial(coarse_kernel, nx=nx, ny=ny, rows=rows),
        out_shape=sds(3, rows, cols),
        in_specs=[SM, VM],
        out_specs=VM,
        scratch_shapes=[
            vm((6, 2) + cells, F32),
            vm((2,) + cells, F32),
            vm((2, 2) + cells, F32),
        ],
        compiler_params=params(24),
        cost_estimate=cost(20 * n, n),
        name="coarse",
    )(place, got)

    out = pl.pallas_call(
        last_kernel,
        out_shape=full,
        in_specs=[VM] * 11,
        out_specs=VM,
        compiler_params=params(44),
        cost_estimate=cost(40 * n, 20 * n),
        name="last",
    )(k, w, f, g, interp, w_pl, w_row, f_pl, f_row, h_pl, h_row)

    return pl.pallas_call(
        finish_kernel,
        out_shape=full,
        in_specs=[ANY] + [VM] * 6,
        out_specs=ANY,
        scratch_shapes=[
            vm((2, rows, cols), F32),
            vm((planes - 2, STRIP, cols), F32),
            vm((planes - 2, STRIP, cols), F32),
            pltpu.SemaphoreType.DMA((4,)),
        ],
        input_output_aliases={0: 0},
        compiler_params=params(24),
        cost_estimate=cost(n // 4, 6 * n),
        name="finish",
    )(out, wc_pl, wc_row, gxl, gxh, gyl, gyh)


def solution(mesh):
    placed = P("gx", "gy", None)
    body = functools.partial(per_device, mesh.shape["gx"], mesh.shape["gy"])
    return jax.shard_map(
        body, mesh=mesh, in_specs=(placed,) * 3, out_specs=placed, check_vma=False
    )
```

profile of v0, /device:TPU:0, one launch (start us, length us, event | category | flops | bytes accessed | tf_op | source)
XLA Modules:
  0.0 109.7 jit_solution(5062327922367154594)
XLA Ops:
  0.0 1.9 %fusion = (f32[16,1,2048]{2,1,0:T(1,128)S(1)}, f32[16,1,2048]{2,1,0:T(1,128)S(1)}) fusion(f32[16,32,2048]{2,1,0:T(8,128)} %v.1), kind=kLoop, calls=%fused_computation.17 | loop fusion | bytes 524288 | tf_op jit(solution)/shard_map/slice | solution.py:407
  1.9 1.7 %fusion.1 = (f32[16,1,2048]{2,1,0:T(1,128)S(1)}, f32[16,1,2048]{2,1,0:T(1,128)S(1)}) fusion(f32[16,32,2048]{2,1,0:T(8,128)} %k.5), kind=kLoop, calls=%fused_computation.18 | loop fusion | bytes 524288 | tf_op jit(solution)/shard_map/slice | solution.py:407
  3.7 6.8 %collective-permute-start.3 = (f32[2,16,2048]{2,1,0:T(8,128)S(1)}, f32[2,16,2048]{2,1,0:T(8,128)S(1)}, u32[]{:S(2)}, u32[]{:S(2)}) collective-permute-start(f32[2,16,2048]{2,1,0:T(8,128)S(1)} %pad_maximum_fusion.2.rw_lo), channel_id=1, source_target_pairs={{0,7},{1,0},{2,1},{3,2},{4,3},{5,4},{6,5},{7,6},{8,15},{9,8},{10,9... | collective-permute-start | bytes 786440 | tf_op jit(solution)/shard_map/ppermute | solution.py:399
  10.6 1.3 %fusion.2 = (f32[1,32,2048]{2,1,0:T(8,128)S(1)}, f32[1,32,2048]{2,1,0:T(8,128)S(1)}, f32[1,32,2048]{2,1,0:T(8,128)S(1)}, f32[1,32,2048]{2,1,0:T(8,128)S(1)}) fusion(f32[16,32,2048]{2,1,0:T(8,128)} %v.1, f32[16,32,2048]{2,1,0:T(8,128)} %k.5), kind=kLoop, calls=%fused_computation.19 | loop fusion | bytes 2097152 | tf_op jit(solution)/shard_map/slice | solution.py:410
  11.9 2.1 %collective-permute-start.1 = (f32[2,32,2048]{2,1,0:T(8,128)S(1)}, f32[2,32,2048]{2,1,0:T(8,128)S(1)}, u32[]{:S(2)}, u32[]{:S(2)}) collective-permute-start(f32[2,32,2048]{2,1,0:T(8,128)S(1)} %pad_maximum_fusion.pl_lo), channel_id=1, source_target_pairs={{0,120},{8,0},{16,8},{24,16},{32,24},{40,32},{48,40},{56,48},{64,5... | collective-permute-start | bytes 1572872 | tf_op jit(solution)/shard_map/ppermute | solution.py:399
  14.3 15.6 %inner.1 = (f32[16,32,2048]{2,1,0:T(8,128)S(1)}, f32[16,32,2048]{2,1,0:T(8,128)S(1)}, f32[2,32,2048]{2,1,0:T(8,128)S(1)}, f32[2,32,2048]{2,1,0:T(8,128)S(1)}, f3...) custom-call(f32[16,32,2048]{2,1,0:T(8,128)S(1)} %copy-done.4, f32[16,32,2048]{2,1,0:T(8,128)} %s.1, ...), custom_call_target="tpu_custom_call" | custom-call | flops 52428800 | bytes 20971520 | tf_op jit(solution)/shard_map/inner/pallas_call | solution.py:414
  29.9 2.0 %copy-done.2 = f32[16,32,2048]{2,1,0:T(8,128)} copy-done((f32[16,32,2048]{2,1,0:T(8,128)}, f32[16,32,2048]{2,1,0:T(8,128)S(1)}, u32[]{:S(2)}) %copy-start.2) | copy-done | bytes 4194328
  31.9 2.0 %copy-done.3 = f32[16,32,2048]{2,1,0:T(8,128)} copy-done((f32[16,32,2048]{2,1,0:T(8,128)}, f32[16,32,2048]{2,1,0:T(8,128)S(1)}, u32[]{:S(2)}) %copy-start.3) | copy-done | bytes 4194328
  33.9 1.8 %edge.1 = (f32[2,32,2048]{2,1,0:T(8,128)S(1)}, f32[2,16,2048]{2,1,0:T(8,128)S(1)}, f32[2,32,2048]{2,1,0:T(8,128)S(1)}, f32[2,16,2048]{2,1,0:T(8,128)S(1)}, f32[2...) custom-call(f32[2,32,2048]{2,1,0:T(8,128)S(1)} %get-tuple-element.26.dpl, ...), custom_call_target="tpu_custom_call" | custom-call | flops 1310720 | bytes 1048576 | tf_op jit(solution)/shard_map/edge/pallas_call | solution.py:425
  35.7 0.9 slice_bitcast_fusion.2
  36.6 3.8 %collective-permute-start.5 = (f32[32,2048]{1,0:T(8,128)}, f32[32,2048]{1,0:T(8,128)S(1)}, u32[]{:S(2)}, u32[]{:S(2)}) collective-permute-start(f32[32,2048]{1,0:T(8,128)} %get-tuple-element.53), channel_id=1, source_target_pairs={{0,120},{8,0},{16,8},{24,16},{32,24},{40,32},{48,40},{56,48},{64,5... | collective-permute-start | bytes 786440 | tf_op jit(solution)/shard_map/ppermute | solution.py:399
  40.4 0.7 slice_bitcast_fusion.6
  41.1 5.9 %collective-permute-start.7 = (f32[16,2048]{1,0:T(8,128)}, f32[16,2048]{1,0:T(8,128)S(1)}, u32[]{:S(2)}, u32[]{:S(2)}) collective-permute-start(f32[16,2048]{1,0:T(8,128)} %get-tuple-element.57), channel_id=1, source_target_pairs={{0,7},{1,0},{2,1},{3,2},{4,3},{5,4},{6,5},{7,6},{8,15},{9,8},{10,9... | collective-permute-start | bytes 393224 | tf_op jit(solution)/shard_map/ppermute | solution.py:399
  47.1 9.6 %all-to-all-start = ((f32[128,4,128]{2,1,0:T(4,128)}), f32[128,4,128]{2,1,0:T(4,128)S(1)}, u32[]{:S(2)}, u32[]{:S(2)}) async-start(f32[128,4,128]{2,1,0:T(4,128)} %bitcast.6), calls=%async_computation | async-start | bytes 524288 | tf_op jit(solution)/shard_map/all_to_all | solution.py:438
  56.7 2.2 %copy-done = f32[16,32,2048]{2,1,0:T(8,128)S(1)} copy-done((f32[16,32,2048]{2,1,0:T(8,128)S(1)}, f32[16,32,2048]{2,1,0:T(8,128)}, u32[]{:S(2)}) %copy-start) | copy-done | bytes 4194328
  58.8 9.3 %sweep.1 = (f32[16,32,2048]{2,1,0:T(8,128)S(1)}, f32[2,32,2048]{2,1,0:T(8,128)S(1)}, f32[2,16,2048]{2,1,0:T(8,128)S(1)}) custom-call(f32[16,32,2048]{2,1,0:T(8,128)S(1)} %copy-done, f32[16,32,2048]{2,1,0:T(8,128)} %copy-done.2, f32[16,32,2048]{2,1,0:T(8,128)} %copy-done.3, f32[2,32,2048]{2,1,0:T(8,128)S(1)} %get-tuple-element.31.w_pl, ...), custom_call_target="tpu_custom_call" | custom-call | flops 41943040 | bytes 16777216 | tf_op jit(solution)/shard_map/sweep/pallas_call | solution.py:440
  68.1 2.0 %copy-done.5 = f32[16,32,2048]{2,1,0:T(8,128)} copy-done((f32[16,32,2048]{2,1,0:T(8,128)}, f32[16,32,2048]{2,1,0:T(8,128)S(1)}, u32[]{:S(2)}) %copy-start.5) | copy-done | bytes 4194328
  70.1 0.7 copy-done.10
  70.8 0.7 copy-done.6
  71.5 0.7 copy-done.8
  72.2 0.9 copy-done.7
  73.2 0.9 copy-done.9
  74.1 0.9 copy-done.11
  75.0 0.2 mid.1
  75.3 0.9 slice_bitcast_fusion
  76.1 2.8 %collective-permute-start.9 = (f32[32,2048]{1,0:T(8,128)}, f32[32,2048]{1,0:T(8,128)}, u32[]{:S(2)}, u32[]{:S(2)}) collective-permute-start(f32[32,2048]{1,0:T(8,128)} %get-tuple-element.51), channel_id=1, source_target_pairs={{0,120},{8,0},{16,8},{24,16},{32,24},{40,32},{48,40},{56,48},{64,5... | collective-permute-start | bytes 786440 | tf_op jit(solution)/shard_map/ppermute | solution.py:399
  78.9 0.7 slice_bitcast_fusion.4
  79.7 5.7 %collective-permute-start.11 = (f32[16,2048]{1,0:T(8,128)}, f32[16,2048]{1,0:T(8,128)S(1)}, u32[]{:S(2)}, u32[]{:S(2)}) collective-permute-start(f32[16,2048]{1,0:T(8,128)} %get-tuple-element.55), channel_id=1, source_target_pairs={{0,7},{1,0},{2,1},{3,2},{4,3},{5,4},{6,5},{7,6},{8,15},{9,8},{10,9... | collective-permute-start | bytes 393224 | tf_op jit(solution)/shard_map/ppermute | solution.py:399
  85.4 4.6 %coarse.1.interp = f32[3,32,2048]{2,1,0:T(8,128)S(1)} custom-call(s32[2]{0:T(128)S(1)} %pad_add_fusion.place, f32[512,128]{1,0:T(8,128)S(1)} %bitcast.28), custom_call_target="tpu_custom_call" | custom-call | flops 20971520 | bytes 1048576 | tf_op jit(solution)/shard_map/coarse/pallas_call | solution.py:466
  90.1 2.2 %copy-done.1 = f32[16,32,2048]{2,1,0:T(8,128)S(1)} copy-done((f32[16,32,2048]{2,1,0:T(8,128)S(1)}, f32[16,32,2048]{2,1,0:T(8,128)}, u32[]{:S(2)}) %copy-start.1) | copy-done | bytes 4194328
  92.2 13.1 %last.1.src = f32[16,32,2048]{2,1,0:T(8,128)} custom-call(f32[16,32,2048]{2,1,0:T(8,128)S(1)} %copy-done.1, f32[16,32,2048]{2,1,0:T(8,128)} %copy-done.2, f32[16,32,2048]{2,1,0:T(8,128)} %copy-done.3, f32[16,32,2048]{2,1,0:T(8,128)} %copy-done.5, f32[3,32,2048]{2,1,0:T(8,128)S(1)} %coarse.1.interp, f32[2,32,2048]{2,1,0:T(8,128)S(1)} %get-tuple-element.31.w_pl, ...), custom_call_target="tpu_custom_call" | custom-call | flops 41943040 | bytes 20971520 | tf_op jit(solution)/shard_map/last/pallas_call | solution.py:481
  105.3 4.3 %finish.1 = f32[16,32,2048]{2,1,0:T(8,128)} custom-call(f32[16,32,2048]{2,1,0:T(8,128)} %last.1.src, f32[2,32,2048]{2,1,0:T(8,128)S(1)} %get-tuple-element.39.wc_pl, f32[2,16,2048]{2,1,0:T(8,128)S(1)} %get-tuple-element.40.wc_row, f32[32,2048]{1,0:T(8,128)} %collective-permute-done.8.xl, ...), custom_call_target="tpu_custom_call", output_to_operand_aliasing={{}: (0, {})} | custom-call | flops 262144 | bytes 6291456 | tf_op jit(solution)/shard_map/finish/pallas_call | solution.py:491
  (39 shorter events, 0.6 us)
Async XLA Ops:
  0.0 14.3 %copy-start.4 = (f32[16,32,2048]{2,1,0:T(8,128)S(1)}, f32[16,32,2048]{2,1,0:T(8,128)}, u32[]{:S(2)}) copy-start(f32[16,32,2048]{2,1,0:T(8,128)} %v.1) | copy-start | bytes 12582916
  3.7 30.1 %collective-permute-start.3 = (f32[2,16,2048]{2,1,0:T(8,128)S(1)}, f32[2,16,2048]{2,1,0:T(8,128)S(1)}, u32[]{:S(2)}, u32[]{:S(2)}) collective-permute-start(f32[2,16,2048]{2,1,0:T(8,128)S(1)} %pad_maximum_fusion.2.rw_lo), channel_id=1, source_target_pairs={{0,7},{1,0},{2,1},{3,2},{4,3},{5,4},{6,5},{7,6},{8,15},{9,8},{10,9... | collective-permute-start | bytes 786440 | tf_op jit(solution)/shard_map/ppermute | solution.py:399
  11.9 22.0 %collective-permute-start.1 = (f32[2,32,2048]{2,1,0:T(8,128)S(1)}, f32[2,32,2048]{2,1,0:T(8,128)S(1)}, u32[]{:S(2)}, u32[]{:S(2)}) collective-permute-start(f32[2,32,2048]{2,1,0:T(8,128)S(1)} %pad_maximum_fusion.pl_lo), channel_id=1, source_target_pairs={{0,120},{8,0},{16,8},{24,16},{32,24},{40,32},{48,40},{56,48},{64,5... | collective-permute-start | bytes 1572872 | tf_op jit(solution)/shard_map/ppermute | solution.py:399
  14.0 19.9 %collective-permute-start = (f32[2,32,2048]{2,1,0:T(8,128)S(1)}, f32[2,32,2048]{2,1,0:T(8,128)S(1)}, u32[]{:S(2)}, u32[]{:S(2)}) collective-permute-start(f32[2,32,2048]{2,1,0:T(8,128)S(1)} %pad_maximum_fusion.1.pl_hi), channel_id=1, source_target_pairs={{0,8},{8,16},{16,24},{24,32},{32,40},{40,48},{48,56},{56,64},{64,7... | collective-permute-start | bytes 1572872 | tf_op jit(solution)/shard_map/ppermute | solution.py:399
  14.2 19.7 %collective-permute-start.2 = (f32[2,16,2048]{2,1,0:T(8,128)S(1)}, f32[2,16,2048]{2,1,0:T(8,128)S(1)}, u32[]{:S(2)}, u32[]{:S(2)}) collective-permute-start(f32[2,16,2048]{2,1,0:T(8,128)S(1)} %pad_maximum_fusion.3.rw_hi), channel_id=1, source_target_pairs={{0,1},{1,2},{2,3},{3,4},{4,5},{5,6},{6,7},{7,0},{8,9},{9,10},{10,1... | collective-permute-start | bytes 786440 | tf_op jit(solution)/shard_map/ppermute | solution.py:399
  29.9 2.0 %copy-start.2 = (f32[16,32,2048]{2,1,0:T(8,128)}, f32[16,32,2048]{2,1,0:T(8,128)S(1)}, u32[]{:S(2)}) copy-start(f32[16,32,2048]{2,1,0:T(8,128)S(1)} %get-tuple-element.24.w) | copy-start | bytes 12582916
  31.9 2.0 %copy-start.3 = (f32[16,32,2048]{2,1,0:T(8,128)}, f32[16,32,2048]{2,1,0:T(8,128)S(1)}, u32[]{:S(2)}) copy-start(f32[16,32,2048]{2,1,0:T(8,128)S(1)} %get-tuple-element.25.f) | copy-start | bytes 12582916
  36.6 34.2 %collective-permute-start.5 = (f32[32,2048]{1,0:T(8,128)}, f32[32,2048]{1,0:T(8,128)S(1)}, u32[]{:S(2)}, u32[]{:S(2)}) collective-permute-start(f32[32,2048]{1,0:T(8,128)} %get-tuple-element.53), channel_id=1, source_target_pairs={{0,120},{8,0},{16,8},{24,16},{32,24},{40,32},{48,40},{56,48},{64,5... | collective-permute-start | bytes 786440 | tf_op jit(solution)/shard_map/ppermute | solution.py:399
  40.4 31.1 %collective-permute-start.4 = (f32[32,2048]{1,0:T(8,128)}, f32[32,2048]{1,0:T(8,128)S(1)}, u32[]{:S(2)}, u32[]{:S(2)}) collective-permute-start(f32[32,2048]{1,0:T(8,128)} %get-tuple-element.54), channel_id=1, source_target_pairs={{0,8},{8,16},{16,24},{24,32},{32,40},{40,48},{48,56},{56,64},{64,7... | collective-permute-start | bytes 786440 | tf_op jit(solution)/shard_map/ppermute | solution.py:399
  41.1 29.0 %collective-permute-start.7 = (f32[16,2048]{1,0:T(8,128)}, f32[16,2048]{1,0:T(8,128)S(1)}, u32[]{:S(2)}, u32[]{:S(2)}) collective-permute-start(f32[16,2048]{1,0:T(8,128)} %get-tuple-element.57), channel_id=1, source_target_pairs={{0,7},{1,0},{2,1},{3,2},{4,3},{5,4},{6,5},{7,6},{8,15},{9,8},{10,9... | collective-permute-start | bytes 393224 | tf_op jit(solution)/shard_map/ppermute | solution.py:399
  47.1 23.1 %collective-permute-start.6 = (f32[16,2048]{1,0:T(8,128)S(1)}, f32[16,2048]{1,0:T(8,128)S(1)}, u32[]{:S(2)}, u32[]{:S(2)}) collective-permute-start(f32[16,2048]{1,0:T(8,128)S(1)} %get-tuple-element.58), channel_id=1, source_target_pairs={{0,1},{1,2},{2,3},{3,4},{4,5},{5,6},{6,7},{7,0},{8,9},{9,10},{10,1... | collective-permute-start | bytes 393224 | tf_op jit(solution)/shard_map/ppermute | solution.py:399
  47.1 38.4 %all-to-all-start = ((f32[128,4,128]{2,1,0:T(4,128)}), f32[128,4,128]{2,1,0:T(4,128)S(1)}, u32[]{:S(2)}, u32[]{:S(2)}) async-start(f32[128,4,128]{2,1,0:T(4,128)} %bitcast.6), calls=%async_computation | async-start | bytes 524288 | tf_op jit(solution)/shard_map/all_to_all | solution.py:438
  56.7 2.2 %copy-start = (f32[16,32,2048]{2,1,0:T(8,128)S(1)}, f32[16,32,2048]{2,1,0:T(8,128)}, u32[]{:S(2)}) copy-start(f32[16,32,2048]{2,1,0:T(8,128)} %k.5) | copy-start | bytes 12582916
  68.1 2.0 %copy-start.5 = (f32[16,32,2048]{2,1,0:T(8,128)}, f32[16,32,2048]{2,1,0:T(8,128)S(1)}, u32[]{:S(2)}) copy-start(f32[16,32,2048]{2,1,0:T(8,128)S(1)} %get-tuple-element.35.g) | copy-start | bytes 12582916
  70.1 0.7 copy-start.10
  70.8 0.7 copy-start.6
  71.5 0.7 copy-start.8
  72.2 0.9 copy-start.7
  73.2 0.9 copy-start.9
  74.1 0.9 copy-start.11
  76.1 29.2 %collective-permute-start.9 = (f32[32,2048]{1,0:T(8,128)}, f32[32,2048]{1,0:T(8,128)}, u32[]{:S(2)}, u32[]{:S(2)}) collective-permute-start(f32[32,2048]{1,0:T(8,128)} %get-tuple-element.51), channel_id=1, source_target_pairs={{0,120},{8,0},{16,8},{24,16},{32,24},{40,32},{48,40},{56,48},{64,5... | collective-permute-start | bytes 786440 | tf_op jit(solution)/shard_map/ppermute | solution.py:399
  78.9 26.4 %collective-permute-start.8 = (f32[32,2048]{1,0:T(8,128)}, f32[32,2048]{1,0:T(8,128)}, u32[]{:S(2)}, u32[]{:S(2)}) collective-permute-start(f32[32,2048]{1,0:T(8,128)} %get-tuple-element.52), channel_id=1, source_target_pairs={{0,8},{8,16},{16,24},{24,32},{32,40},{40,48},{48,56},{56,64},{64,7... | collective-permute-start | bytes 786440 | tf_op jit(solution)/shard_map/ppermute | solution.py:399
  79.7 25.7 %collective-permute-start.11 = (f32[16,2048]{1,0:T(8,128)}, f32[16,2048]{1,0:T(8,128)S(1)}, u32[]{:S(2)}, u32[]{:S(2)}) collective-permute-start(f32[16,2048]{1,0:T(8,128)} %get-tuple-element.55), channel_id=1, source_target_pairs={{0,7},{1,0},{2,1},{3,2},{4,3},{5,4},{6,5},{7,6},{8,15},{9,8},{10,9... | collective-permute-start | bytes 393224 | tf_op jit(solution)/shard_map/ppermute | solution.py:399
  85.4 20.0 %collective-permute-start.10 = (f32[16,2048]{1,0:T(8,128)}, f32[16,2048]{1,0:T(8,128)}, u32[]{:S(2)}, u32[]{:S(2)}) collective-permute-start(f32[16,2048]{1,0:T(8,128)} %get-tuple-element.56), channel_id=1, source_target_pairs={{0,1},{1,2},{2,3},{3,4},{4,5},{5,6},{6,7},{7,0},{8,9},{9,10},{10,1... | collective-permute-start | bytes 393224 | tf_op jit(solution)/shard_map/ppermute | solution.py:399
  90.1 2.2 %copy-start.1 = (f32[16,32,2048]{2,1,0:T(8,128)S(1)}, f32[16,32,2048]{2,1,0:T(8,128)}, u32[]{:S(2)}) copy-start(f32[16,32,2048]{2,1,0:T(8,128)} %k.5) | copy-start | bytes 12582916
where the time goes:
time: 111 us; the launch traced here: 110 us
  Pallas kernels  48.9 us (44%)
  starting transfers between devices  36.9 us (33%)
  local copies, waits for them, and re-layouts  23.4 us (21%)
    ppermute x6, starting transfers between devices, swap(): lax.ppermute(low, axis, backward)  27.2 us
    pallas_call x1, Pallas kernels, per_device(): pl.pallas_call(inner_kernel, out_shape=(full, full, e_pl, e_pl, e_row, e_...  15.6 us
    unnamed x24, local copies, waits for them, and re-layouts  15.2 us
    pallas_call x1, Pallas kernels, per_device(): pl.pallas_call(last_kernel, out_shape=full, in_specs=[VM] * 11, out_specs...  13.1 us
    all_to_all x1, starting transfers between devices, per_device(): got = lax.all_to_all(payload, ('gx', 'gy'), 0, 0, tiled=True)  9.58 us
    pallas_call x1, Pallas kernels, per_device(): pl.pallas_call(sweep_kernel, out_shape=(full, e_pl, e_row), in_specs=[VM]...  9.28 us
    pallas_call x1, Pallas kernels, per_device(): pl.pallas_call(functools.partial(coarse_kernel, nx=nx, ny=ny, rows=rows),...  4.61 us
    pallas_call x1, Pallas kernels, per_device(): pl.pallas_call(finish_kernel, out_shape=full, in_specs=[ANY] + [VM] * 6,...  4.33 us
  transfers between devices with their start and end apart: 13, of which 0 were waited for; matrix products, arithmetic and copies ran while one was open for 3% of the time, Pallas kernels for 39%

commit v1 on v0

v1 whole, which is shorter than its diff:
```python
import functools
import jax
import jax.numpy as jnp
from jax import lax
from jax.experimental import pallas as pl
from jax.experimental.pallas import tpu as pltpu
from jax.sharding import PartitionSpec as P

F = 16
CSWEEPS = 32
REACTION = 0.2
DAMPING = 0.8
COARSE_FACTOR = 0.25
F32 = jnp.float32
BF16 = jnp.bfloat16
STRIP = 8

VM = pl.BlockSpec(memory_space=pltpu.VMEM)
SM = pl.BlockSpec(memory_space=pltpu.SMEM)
ANY = pl.BlockSpec(memory_space=pl.ANY)


def params(mib):
    return pltpu.CompilerParams(vmem_limit_bytes=mib * 1024 * 1024)


def cost(flops, nbytes):
    return pl.CostEstimate(flops=int(flops), bytes_accessed=int(nbytes), transcendentals=0)


def sds(*shape):
    return jax.ShapeDtypeStruct(shape, F32)


def zp(a):
    return pltpu.roll(a, a.shape[-1] - 1, a.ndim - 1)


def zm(a):
    return pltpu.roll(a, 1, a.ndim - 1)


def shifted_up(rolled, r):
    nxt = rolled[min(r + 1, len(rolled) - 1)]
    sub = lax.broadcasted_iota(jnp.int32, nxt.shape, 0)
    return jnp.where(sub == STRIP - 1, nxt, rolled[r])


def shifted_down(rolled, r):
    prv = rolled[r - 1]
    sub = lax.broadcasted_iota(jnp.int32, prv.shape, 0)
    return jnp.where(sub == 0, prv, rolled[r])


def strips(rows):
    return [slice(r * STRIP, (r + 1) * STRIP) for r in range(rows // STRIP)]


def ends_kernel(v, k, rw_lo, rw_hi, pl_lo, pl_hi, sems):
    planes, rows, _ = v.shape
    copies = []
    for i, a in enumerate((v, k)):
        for j, (src, dst) in enumerate(
            (
                (a.at[:, 0, :], rw_lo.at[i]),
                (a.at[:, rows - 1, :], rw_hi.at[i]),
                (a.at[0], pl_lo.at[i]),
                (a.at[planes - 1], pl_hi.at[i]),
            )
        ):
            copies.append(pltpu.make_async_copy(src, dst, sems.at[i, j]))
    for c in copies:
        c.start()
    for c in copies:
        c.wait()


def inner_kernel(
    v_hbm, s_hbm, k_hbm,
    w_ref, f_ref, cx, cy, cz, d_lo, d_hi, r_lo, r_hi, drow, rrow, sums,
    v, s, k, fx, sems,
):
    planes, rows, cols = v.shape
    sl = strips(rows)
    n = len(sl)

    def copy(i, x):
        src, dst = ((k_hbm, k), (v_hbm, v), (s_hbm, s))[i]
        return pltpu.make_async_copy(src.at[x], dst.at[x], sems.at[i, x])

    for x in range(planes):
        for i in range(3):
            copy(i, x).start()
    sums[...] = jnp.zeros_like(sums)
    fx[...] = jnp.zeros_like(fx)
    cx[0] = jnp.zeros_like(fx)
    copy(0, 0).wait()
    copy(1, 0).wait()

    def plane(x, carry):
        @pl.when(x < planes - 1)
        def _():
            copy(0, x + 1).wait()
            copy(1, x + 1).wait()

        copy(2, x).wait()
        xn = jnp.minimum(x + 1, planes - 1)
        h_next = jnp.where(x < planes - 1, 0.5, 0.0).astype(F32)
        k0 = [k[x, a, :] for a in sl]
        v0 = [v[x, a, :] for a in sl]
        k_up = [pltpu.roll(a, STRIP - 1, 0) for a in k0]
        v_up = [pltpu.roll(a, STRIP - 1, 0) for a in v0]
        c_y, f_y = [], []
        for r in range(n):
            c = 0.5 * (k0[r] + shifted_up(k_up, r))
            if r == n - 1:
                sub = lax.broadcasted_iota(jnp.int32, c.shape, 0)
                c = jnp.where(sub == STRIP - 1, 0.0, c)
            cy[x, sl[r], :] = c
            c_y.append(c)
            f_y.append(c * (v0[r] - shifted_up(v_up, r)))
        c_dn = [pltpu.roll(a, 1, 0) for a in c_y]
        f_dn = [pltpu.roll(a, 1, 0) for a in f_y]
        for r in range(n):
            a = sl[r]
            c_next = h_next * (k0[r] + k[xn, a, :])
            f_next = c_next * (v0[r] - v[xn, a, :])
            c_prev = cx[x, a, :]
            f_prev = fx[a, :]
            cx[x + 1, a, :] = c_next
            fx[a, :] = f_next
            c_z = 0.5 * (k0[r] + zp(k0[r]))
            f_z = c_z * (v0[r] - zp(v0[r]))
            cz[x, a, :] = c_z
            diag = ((REACTION + c_next) + (c_prev + c_y[r])) + (
                (shifted_down(c_dn, r) + c_z) + zm(c_z)
            )
            res = ((s[x, a, :] - REACTION * v0[r]) + (f_prev - f_next)) + (
                (shifted_down(f_dn, r) - f_y[r]) + (zm(f_z) - f_z)
            )
            w = DAMPING / diag
            w_ref[x, a, :] = w
            f_ref[x, a, :] = w * res
            half = r * STRIP // F
            sums[half * STRIP : (half + 1) * STRIP, :] += res
            sums[(2 + half) * STRIP : (3 + half) * STRIP, :] += k0[r]
            if r == 0:
                drow[0, pl.ds(x, 1), :] = diag[0:1]
                rrow[0, pl.ds(x, 1), :] = res[0:1]
            if r == n - 1:
                drow[1, pl.ds(x, 1), :] = diag[STRIP - 1 :]
                rrow[1, pl.ds(x, 1), :] = res[STRIP - 1 :]

            @pl.when(x == 0)
            def _():
                d_lo[a, :] = diag
                r_lo[a, :] = res

            @pl.when(x == planes - 1)
            def _():
                d_hi[a, :] = diag
                r_hi[a, :] = res

        return carry

    lax.fori_loop(0, planes, plane, 0)


def cross(q_pl, q_row, pls, rws, sign):
    rows, planes = q_pl.shape[1], q_row.shape[1]
    for a in range(2):
        pls[a][...] = pls[a][...] + sign * q_pl[a]
        rws[a][...] = rws[a][...] + sign * q_row[a]
    for a, x in ((0, 0), (1, planes - 1)):
        for b, y in ((0, 0), (1, rows - 1)):
            pls[a][y : y + 1, :] = pls[a][y : y + 1, :] + sign * q_row[b, x : x + 1, :]
            rws[b][x : x + 1, :] = rws[b][x : x + 1, :] + sign * q_pl[a, y : y + 1, :]


def split3(a):
    one = a.astype(BF16)
    rest = a - one.astype(F32)
    two = rest.astype(BF16)
    three = (rest - two.astype(F32)).astype(BF16)
    return jnp.concatenate([one, two, three], 0)


def joined3(a):
    n = a.shape[0] // 3
    return a[:n] + a[n : 2 * n] + a[2 * n :]


def edge_kernel(
    d_lo, d_hi, r_lo, r_hi, drow, rrow, pl_lo, pl_hi, rw_lo, rw_hi, xl, xh, yl, yh, sums,
    f_pl0, f_pl1, f_row0, f_row1, w_pl0, w_pl1, w_row0, w_row1, wc_pl, wc_row, payload,
    q_pl, q_row,
):
    rows, cols = d_lo.shape
    f_pl, f_row, w_pl, w_row = (f_pl0, f_pl1), (f_row0, f_row1), (w_pl0, w_pl1), (w_row0, w_row1)
    for side, mine, other in ((0, pl_lo, xl), (1, pl_hi, xh)):
        c = 0.5 * (mine[1] + other[1])
        wc_pl[side] = c
        q_pl[side] = c * (mine[0] - other[0])
    for side, mine, other in ((0, rw_lo, yl), (1, rw_hi, yh)):
        c = 0.5 * (mine[1] + other[1])
        wc_row[side] = c
        q_row[side] = c * (mine[0] - other[0])
    for side, d, r in ((0, d_lo, r_lo), (1, d_hi, r_hi)):
        w_pl[side][...] = d[...]
        f_pl[side][...] = r[...]
        w_row[side][...] = drow[side]
        f_row[side][...] = rrow[side]
    cross(wc_pl, wc_row, w_pl, w_row, 1.0)
    cross(q_pl, q_row, f_pl, f_row, -1.0)
    for w, f, wc in ((w_pl, f_pl, wc_pl), (w_row, f_row, wc_row)):
        for side in range(2):
            inv = DAMPING / w[side][...]
            w[side][...] = inv
            f[side][...] = f[side][...] * inv
            wc[side] = wc[side] * inv
    parts = []
    for half in range(rows // F):
        total = sums[half * STRIP : (half + 1) * STRIP, :]
        for side in range(2):
            for r in range(half * F // STRIP, (half + 1) * F // STRIP):
                total = total - q_pl[side, r * STRIP : (r + 1) * STRIP, :]
        if half == 0:
            for r in range(q_row.shape[1] // STRIP):
                total = total - q_row[0, r * STRIP : (r + 1) * STRIP, :]
        if half == rows // F - 1:
            for r in range(q_row.shape[1] // STRIP):
                total = total - q_row[1, r * STRIP : (r + 1) * STRIP, :]
        parts.append(total)
    parts.append(sums[2 * STRIP :, :])
    col = lax.broadcasted_iota(jnp.int32, (cols, cols // F), 0)
    cell = lax.broadcasted_iota(jnp.int32, (cols, cols // F), 1)
    gather = jnp.where(col // F == cell, 1.0, 0.0).astype(BF16)
    reduced = joined3(
        jnp.dot(split3(jnp.concatenate(parts, 0)), gather, preferred_element_type=F32)
    )
    means = [
        jnp.sum(reduced[i * STRIP : (i + 1) * STRIP], axis=0, keepdims=True) * (1.0 / F**3)
        for i in range(4)
    ]
    tile = jnp.concatenate(means + means, 0)
    for i in range(payload.shape[0] // STRIP):
        payload[i * STRIP : (i + 1) * STRIP, :] = tile


def put_edges(ref, e_pl0, e_pl1, e_row0, e_row1):
    planes, rows, _ = ref.shape
    for x in range(1, planes - 1):
        ref[x, 0:1, :] = e_row0[x : x + 1, :]
        ref[x, rows - 1 : rows, :] = e_row1[x : x + 1, :]
    ref[0] = e_pl0[...]
    ref[planes - 1] = e_pl1[...]


def neighbour_sums(x, u, cx, cy, cz):
    planes, rows, _ = u.shape
    sl = strips(rows)
    xn, xp = jnp.minimum(x + 1, planes - 1), jnp.maximum(x - 1, 0)
    u0 = [u[x, a, :] for a in sl]
    u_up = [pltpu.roll(a, STRIP - 1, 0) for a in u0]
    c_y = [cy[x, a, :] for a in sl]
    q_dn = [pltpu.roll(c * a, 1, 0) for c, a in zip(c_y, u0)]
    for r, a in enumerate(sl):
        c_z = cz[x, a, :]
        total = (
            (cx[x + 1, a, :] * u[xn, a, :] + cx[x, a, :] * u[xp, a, :])
            + (c_y[r] * shifted_up(u_up, r) + shifted_down(q_dn, r))
            + (c_z * zp(u0[r]) + zm(c_z * u0[r]))
        )
        yield r, a, u0[r], total


def sweep_kernel(
    w, f, cx, cy, cz, w_pl0, w_pl1, w_row0, w_row1, f_pl0, f_pl1, f_row0, f_row1,
    g_ref, g_pl, g_row,
):
    planes, rows, cols = w.shape
    put_edges(w, w_pl0, w_pl1, w_row0, w_row1)
    put_edges(f, f_pl0, f_pl1, f_row0, f_row1)

    def plane(x, carry):
        for r, a, u0, total in neighbour_sums(x, f, cx, cy, cz):
            new = (2.0 - DAMPING) * u0 + w[x, a, :] * total
            g_ref[x, a, :] = new
            if r == 0:
                g_row[0, pl.ds(x, 1), :] = new[0:1]
            if (r + 1) * STRIP == rows:
                g_row[1, pl.ds(x, 1), :] = new[STRIP - 1 :]
        return carry

    lax.fori_loop(0, planes, plane, 0)
    g_pl[0] = g_ref[0]
    g_pl[1] = g_ref[planes - 1]


def mid_kernel(
    g_pl, g_row, wc_pl, wc_row, xl, xh, yl, yh, o_pl0, o_pl1, o_row0, o_row1, q_pl, q_row
):
    for side, x, y in ((0, xl, yl), (1, xh, yh)):
        q_pl[side] = wc_pl[side] * x[...]
        q_row[side] = wc_row[side] * y[...]
    for side, p, r in ((0, o_pl0, o_row0), (1, o_pl1, o_row1)):
        p[...] = g_pl[side]
        r[...] = g_row[side]
    cross(q_pl, q_row, (o_pl0, o_pl1), (o_row0, o_row1), 1.0)


def last_kernel(
    w, f, cx, cy, cz, g, interp, w_pl0, w_pl1, w_row0, w_row1, f_pl0, f_pl1, f_row0, f_row1,
    g_pl0, g_pl1, g_row0, g_row1, out, b_pl, b_lo, b_hi, body, sems,
):
    planes, rows, cols = w.shape
    n = rows // STRIP
    put_edges(w, w_pl0, w_pl1, w_row0, w_row1)
    put_edges(f, f_pl0, f_pl1, f_row0, f_row1)
    put_edges(g, g_pl0, g_pl1, g_row0, g_row1)

    def copy(x):
        return pltpu.make_async_copy(
            body.at[x], out.at[x, STRIP : rows - STRIP, :], sems.at[x]
        )

    def plane(x, carry):
        offset = ((x % F).astype(F32) + 0.5) / F - 0.5
        weight = jnp.abs(offset)
        side = jnp.where(offset > 0, 2, 0)
        inside = (x > 0) & (x < planes - 1)
        slot = jnp.clip(x - 1, 0, planes - 3)
        end = jnp.where(x == 0, 0, 1)
        for r, a, u0, total in neighbour_sums(x, g, cx, cy, cz):
            coarse = (1.0 - weight) * interp[1, a, :] + weight * interp[side, a, :]
            new = (f[x, a, :] + (1.0 - DAMPING) * u0) + (w[x, a, :] * total + coarse)

            @pl.when(inside)
            def _():
                if r == 0:
                    b_lo[slot] = new
                elif r == n - 1:
                    b_hi[slot] = new
                else:
                    body[x, (r - 1) * STRIP : r * STRIP, :] = new

            @pl.when(jnp.logical_not(inside))
            def _():
                b_pl[end, a, :] = new

        @pl.when(inside)
        def _():
            copy(x).start()

        return carry

    lax.fori_loop(0, planes, plane, 0)
    for x in range(1, planes - 1):
        copy(x).wait()


def finish_kernel(
    src, b_pl, b_lo, b_hi, wc_pl, wc_row, xl, xh, yl, yh, out, s_pl, s_lo, s_hi, sems
):
    del src
    planes, rows, cols = out.shape
    spots = (
        (s_lo, out.at[1 : planes - 1, 0:STRIP, :]),
        (s_hi, out.at[1 : planes - 1, rows - STRIP : rows, :]),
        (s_pl.at[0], out.at[0]),
        (s_pl.at[1], out.at[planes - 1]),
    )
    copies = [pltpu.make_async_copy(a, b, sems.at[i]) for i, (a, b) in enumerate(spots)]
    sub = lax.broadcasted_iota(jnp.int32, (STRIP, cols), 0)
    for x in range(1, planes - 1):
        q = wc_row[0, x : x + 1, :] * yl[x : x + 1, :]
        s_lo[x - 1] = b_lo[x - 1] + jnp.where(sub == 0, q, 0.0)
    copies[0].start()
    for x in range(1, planes - 1):
        q = wc_row[1, x : x + 1, :] * yh[x : x + 1, :]
        s_hi[x - 1] = b_hi[x - 1] + jnp.where(sub == STRIP - 1, q, 0.0)
    copies[1].start()
    for side, other in ((0, xl), (1, xh)):
        x = side * (planes - 1)
        s_pl[side] = b_pl[side] + wc_pl[side] * other[...]
        for y, b, halo in ((0, 0, yl), (rows - 1, 1, yh)):
            s_pl[side, y : y + 1, :] = (
                s_pl[side, y : y + 1, :] + wc_row[b, x : x + 1, :] * halo[x : x + 1, :]
            )
        copies[2 + side].start()
    for c in copies:
        c.wait()


def coarse_kernel(place, got, interp, coef, b_ref, u_ref, *, nx, ny, rows):
    nz = got.shape[1]
    per = 2 * 2

    def field(start):
        return [
            jnp.stack([got[pl.ds(p * ny * per + start + t, ny, stride=per), :] for p in range(nx)], 0)
            for t in range(2)
        ]

    resid, cond = field(0), field(2)

    def beside(a, t):
        mine = a[t]
        nxt = jnp.concatenate([mine[1:], mine[:1]], 0)
        prv = jnp.concatenate([mine[-1:], mine[:-1]], 0)
        up = a[1] if t == 0 else pltpu.roll(a[0], ny - 1, 1)
        down = a[0] if t == 1 else pltpu.roll(a[1], 1, 1)
        return nxt, prv, up, down, pltpu.roll(mine, 1, 2), pltpu.roll(mine, nz - 1, 2)

    for t in range(2):
        cs = [(0.5 * COARSE_FACTOR) * (cond[t] + other) for other in beside(cond, t)]
        diag = REACTION
        for c in cs:
            diag = diag + c
        inv = DAMPING / diag
        for i, c in enumerate(cs):
            coef[i, t] = inv * c
        b_ref[t] = inv * resid[t]
        u_ref[0, t] = b_ref[t]

    def sweep(src, dst):
        for p in range(nx):
            pn, pp = (p + 1) % nx, (p - 1) % nx
            u = [u_ref[src, t, p] for t in range(2)]
            for t in range(2):
                up = u[1] if t == 0 else pltpu.roll(u[0], ny - 1, 0)
                down = u[0] if t == 1 else pltpu.roll(u[1], 1, 0)
                a = b_ref[t, p] + (1.0 - DAMPING) * u[t]
                a = a + coef[0, t, p] * u_ref[src, t, pn]
                a = a + coef[1, t, p] * u_ref[src, t, pp]
                c = coef[2, t, p] * up + coef[3, t, p] * down
                c = c + coef[4, t, p] * pltpu.roll(u[t], 1, 1)
                c = c + coef[5, t, p] * pltpu.roll(u[t], nz - 1, 1)
                u_ref[dst, t, p] = a + c

    def pair(i, carry):
        sweep(0, 1)
        sweep(1, 0)
        return carry

    steps = CSWEEPS - 1
    lax.fori_loop(0, steps // 2, pair, 0)
    last = 0
    if steps % 2:
        sweep(0, 1)
        last = 1

    gx, gy = place[0], place[1]
    lines = []
    for d in (-1, 0, 1):
        p = lax.rem(gx + d + nx, nx)
        prev_s, next_s = lax.rem(gy + ny - 1, ny), lax.rem(gy + 1, ny)
        for t, s in ((1, prev_s), (0, gy), (1, gy), (0, next_s)):
            lines.append(u_ref[last, t, p, pl.ds(s, 1), :])
    lines = jnp.concatenate(lines + lines[:4], 0)
    cols = nz * F
    cell = lax.broadcasted_iota(jnp.int32, (nz, cols), 0)
    col = lax.broadcasted_iota(jnp.int32, (nz, cols), 1)
    base = col // F
    offset = ((col % F).astype(F32) + 0.5) / F - 0.5
    side = jnp.where(offset > 0, base + 1, base - 1)
    side = jnp.where(side < 0, side + nz, jnp.where(side >= nz, side - nz, side))
    weight = jnp.abs(offset)
    matrix = jnp.where(cell == base, 1.0 - weight, 0.0) + jnp.where(cell == side, weight, 0.0)
    wide = joined3(jnp.dot(split3(lines), matrix.astype(BF16), preferred_element_type=F32))
    sub = lax.broadcasted_iota(jnp.int32, (STRIP, cols), 0)
    for plane in range(3):
        for r in range(rows // STRIP):
            row = r * STRIP + sub
            off = ((row % F).astype(F32) + 0.5) / F - 0.5
            wt = jnp.abs(off)
            block = r * STRIP // F
            near = block + 1
            far = near + (1 if (r * STRIP) % F >= F // 2 else -1)
            a = wide[plane * 4 + near : plane * 4 + near + 1]
            c = wide[plane * 4 + far : plane * 4 + far + 1]
            interp[plane, r * STRIP : (r + 1) * STRIP, :] = (1.0 - wt) * a + wt * c


def swap(axis, low, high):
    count = lax.axis_size(axis)
    forward = [(i, (i + 1) % count) for i in range(count)]
    backward = [(i, (i - 1) % count) for i in range(count)]
    return lax.ppermute(high, axis, forward), lax.ppermute(low, axis, backward)


def per_device(nx, ny, v, s, k):
    planes, rows, cols = v.shape
    n = planes * rows * cols
    vm = pltpu.VMEM
    dma = pltpu.SemaphoreType.DMA
    full, edge, line = sds(planes, rows, cols), sds(rows, cols), sds(planes, cols)
    edges, lines = sds(2, rows, cols), sds(2, planes, cols)

    rw_lo, rw_hi, pl_lo, pl_hi = pl.pallas_call(
        ends_kernel,
        out_shape=(lines, lines, edges, edges),
        in_specs=[ANY] * 2,
        out_specs=(VM,) * 4,
        scratch_shapes=[dma((2, 4))],
        compiler_params=params(4),
        cost_estimate=cost(0, n // 2),
        name="ends",
    )(v, k)
    yl, yh = swap("gy", rw_lo, rw_hi)
    xl, xh = swap("gx", pl_lo, pl_hi)

    w, f, cx, cy, cz, d_lo, d_hi, r_lo, r_hi, drow, rrow, sums = pl.pallas_call(
        inner_kernel,
        out_shape=(full, full, sds(planes + 1, rows, cols), full, full)
        + (edge,) * 4
        + (lines, lines, sds(4 * STRIP, cols)),
        in_specs=[ANY] * 3,
        out_specs=(VM,) * 12,
        scratch_shapes=[vm(full.shape, F32)] * 3 + [vm(edge.shape, F32), dma((3, planes))],
        compiler_params=params(18),
        cost_estimate=cost(50 * n, 32 * n),
        name="inner",
    )(v, s, k)

    devices = nx * ny
    out = pl.pallas_call(
        edge_kernel,
        out_shape=(edge, edge, line, line) * 2 + (edges, lines, sds(devices * 4, cols // F)),
        in_specs=[VM] * 15,
        out_specs=(VM,) * 11,
        scratch_shapes=[vm(edges.shape, F32), vm(lines.shape, F32)],
        compiler_params=params(6),
        cost_estimate=cost(10 * n // 8, n),
        name="edge",
    )(d_lo, d_hi, r_lo, r_hi, drow, rrow, pl_lo, pl_hi, rw_lo, rw_hi, xl, xh, yl, yh, sums)
    f_edges, w_edges, (wc_pl, wc_row, payload) = out[:4], out[4:8], out[8:]

    fyl, fyh = swap("gy", f_edges[2], f_edges[3])
    fxl, fxh = swap("gx", f_edges[0], f_edges[1])
    got = lax.all_to_all(payload, ("gx", "gy"), 0, 0, tiled=True)

    g, g_pl, g_row = pl.pallas_call(
        sweep_kernel,
        out_shape=(full, edges, lines),
        in_specs=[VM] * 13,
        out_specs=(VM,) * 3,
        compiler_params=params(4),
        cost_estimate=cost(40 * n, 16 * n),
        name="sweep",
    )(w, f, cx, cy, cz, *w_edges, *f_edges)

    g_edges = pl.pallas_call(
        mid_kernel,
        out_shape=(edge, edge, line, line),
        in_specs=[VM] * 8,
        out_specs=(VM,) * 4,
        scratch_shapes=[vm(edges.shape, F32), vm(lines.shape, F32)],
        compiler_params=params(4),
        cost_estimate=cost(n // 8, n // 2),
        name="mid",
    )(g_pl, g_row, wc_pl, wc_row, fxl, fxh, fyl, fyh)

    gyl, gyh = swap("gy", g_edges[2], g_edges[3])
    gxl, gxh = swap("gx", g_edges[0], g_edges[1])

    place = jnp.stack([lax.axis_index("gx"), lax.axis_index("gy")]).astype(jnp.int32)
    cells = (nx, ny, cols // F)
    interp = pl.pallas_call(
        functools.partial(coarse_kernel, nx=nx, ny=ny, rows=rows),
        out_shape=sds(3, rows, cols),
        in_specs=[SM, VM],
        out_specs=VM,
        scratch_shapes=[
            vm((6, 2) + cells, F32),
            vm((2,) + cells, F32),
            vm((2, 2) + cells, F32),
        ],
        compiler_params=params(8),
        cost_estimate=cost(20 * n, n),
        name="coarse",
    )(place, got)

    b_side = sds(planes - 2, STRIP, cols)
    out, b_pl, b_lo, b_hi = pl.pallas_call(
        last_kernel,
        out_shape=(full, edges, b_side, b_side),
        in_specs=[VM] * 19,
        out_specs=(ANY, VM, VM, VM),
        scratch_shapes=[vm((planes, rows - 2 * STRIP, cols), F32), dma((planes,))],
        compiler_params=params(8),
        cost_estimate=cost(40 * n, 20 * n),
        name="last",
    )(w, f, cx, cy, cz, g, interp, *w_edges, *f_edges, *g_edges)

    return pl.pallas_call(
        finish_kernel,
        out_shape=full,
        in_specs=[ANY] + [VM] * 9,
        out_specs=ANY,
        scratch_shapes=[
            vm(edges.shape, F32), vm(b_side.shape, F32), vm(b_side.shape, F32), dma((4,)),
        ],
        input_output_aliases={0: 0},
        compiler_params=params(6),
        cost_estimate=cost(n // 4, 3 * n),
        name="finish",
    )(out, b_pl, b_lo, b_hi, wc_pl, wc_row, gxl, gxh, gyl, gyh)


def solution(mesh):
    placed = P("gx", "gy", None)
    body = functools.partial(per_device, mesh.shape["gx"], mesh.shape["gy"])
    return jax.shard_map(
        body, mesh=mesh, in_specs=(placed,) * 3, out_specs=placed, check_vma=False
    )
```

time: 111 us -> 124 us (1.12)
  local copies, waits for them, and re-layouts: 23.4 us -> 47.6 us
  Pallas kernels: 48.9 us -> 37.5 us
    unnamed x24 -> x56, local copies, waits for them, and re-layouts: 15.2 us -> 47.6 us
    pallas_call x6 -> x7, Pallas kernels: 44.3 us -> 32.9 us  [the longest x1 14.5 us: per_device(): pl.pallas_call(inner_kernel, out_shape=(full, full, sds(planes + 1, rows,...]
    slice x3 -> x0, local copies, waits for them, and re-layouts: 4.89 us -> none  [the longest x2 3.61 us: per_device(): rw_hi = jnp.stack([v[:, rows - 1], k[:, rows - 1]])]
    squeeze x4 -> x0, local copies, waits for them, and re-layouts: 3.12 us -> none  [the longest x1 0.86 us: per_device(): fxl, fxh = swap('gx', f_pl[0], f_pl[1])]
  transfers between devices with their start and end apart: 13 -> 13, of which waited for: 0 -> 0; matrix products, arithmetic and copies ran while one was open for 3% -> 0% of each run, Pallas kernels for 39% -> 27%
where the time goes in v1:
time: 124 us; the launch traced here: 122 us
  local copies, waits for them, and re-layouts  47.6 us (38%)
  Pallas kernels  37.5 us (30%)
  starting transfers between devices  36.8 us (30%)
    unnamed x56, local copies, waits for them, and re-layouts  47.6 us
    ppermute x6, starting transfers between devices, swap(): lax.ppermute(low, axis, backward)  27.2 us
    pallas_call x1, Pallas kernels, per_device(): pl.pallas_call(inner_kernel, out_shape=(full, full, sds(planes + 1, rows,...  14.5 us
    all_to_all x1, starting transfers between devices, per_device(): got = lax.all_to_all(payload, ('gx', 'gy'), 0, 0, tiled=True)  9.58 us
    pallas_call x1, Pallas kernels, per_device(): pl.pallas_call(last_kernel, out_shape=(full, edges, b_side, b_side), in_s...  8.4 us
    pallas_call x1, Pallas kernels, per_device(): pl.pallas_call(functools.partial(coarse_kernel, nx=nx, ny=ny, rows=rows),...  4.61 us
    pallas_call x1, Pallas kernels, per_device(): pl.pallas_call(sweep_kernel, out_shape=(full, edges, lines), in_specs=[VM...  4.17 us
    pallas_call x1, Pallas kernels, per_device(): pl.pallas_call(finish_kernel, out_shape=full, in_specs=[ANY] + [VM] * 9,...  2.62 us
  transfers between devices with their start and end apart: 13, of which 0 were waited for; matrix products, arithmetic and copies ran while one was open for 0% of the time, Pallas kernels for 27%

profile of v1, /device:TPU:0, one launch (start us, length us, event | category | flops | bytes accessed | tf_op | source)
XLA Modules:
  0.0 122.2 jit_solution(14841918893225443952)
XLA Ops:
  0.0 2.2 %copy-done.3 = f32[16,32,2048]{2,1,0:T(8,128)S(1)} copy-done((f32[16,32,2048]{2,1,0:T(8,128)S(1)}, f32[16,32,2048]{2,1,0:T(8,128)}, u32[]{:S(2)}) %copy-start.3) | copy-done | bytes 4194328
  2.2 2.2 %copy-done.5 = f32[16,32,2048]{2,1,0:T(8,128)S(1)} copy-done((f32[16,32,2048]{2,1,0:T(8,128)S(1)}, f32[16,32,2048]{2,1,0:T(8,128)}, u32[]{:S(2)}) %copy-start.5) | copy-done | bytes 4194328
  4.9 3.4 %collective-permute-start.1 = (f32[2,32,2048]{2,1,0:T(8,128)S(1)}, f32[2,32,2048]{2,1,0:T(8,128)S(1)}, u32[]{:S(2)}, u32[]{:S(2)}) collective-permute-start(f32[2,32,2048]{2,1,0:T(8,128)S(1)} %get-tuple-element.54.pl_lo), channel_id=1, source_target_pairs={{0,120},{8,0},{16,8},{24,16},{32,24},{40,32},{48,40},{56,48},{64,5... | collective-permute-start | bytes 1572872 | tf_op jit(solution)/shard_map/ppermute | solution.py:489
  8.3 6.4 %collective-permute-start.3 = (f32[2,16,2048]{2,1,0:T(8,128)S(1)}, f32[2,16,2048]{2,1,0:T(8,128)S(1)}, u32[]{:S(2)}, u32[]{:S(2)}) collective-permute-start(f32[2,16,2048]{2,1,0:T(8,128)S(1)} %get-tuple-element.56.rw_lo), channel_id=1, source_target_pairs={{0,7},{1,0},{2,1},{3,2},{4,3},{5,4},{6,5},{7,6},{8,15},{9,8},{10,9... | collective-permute-start | bytes 786440 | tf_op jit(solution)/shard_map/ppermute | solution.py:489
  14.7 2.2 %copy-done.19 = f32[16,32,2048]{2,1,0:T(8,128)S(1)} copy-done((f32[16,32,2048]{2,1,0:T(8,128)S(1)}, f32[16,32,2048]{2,1,0:T(8,128)}, u32[]{:S(2)}) %copy-start.19) | copy-done | bytes 4194328
  16.9 14.5 %inner.1 = (f32[16,32,2048]{2,1,0:T(8,128)S(1)}, f32[16,32,2048]{2,1,0:T(8,128)S(1)}, f32[17,32,2048]{2,1,0:T(8,128)S(1)}, f32[16,32,2048]{2,1,0:T(8,128)S(1)}, ...) custom-call(f32[16,32,2048]{2,1,0:T(8,128)S(1)} %copy-done.4, ...), custom_call_target="tpu_custom_call" | custom-call | flops 52428800 | bytes 33554432 | tf_op jit(solution)/shard_map/inner/pallas_call | solution.py:513
  31.4 2.1 %copy-done = f32[17,32,2048]{2,1,0:T(8,128)} copy-done((f32[17,32,2048]{2,1,0:T(8,128)}, f32[17,32,2048]{2,1,0:T(8,128)S(1)}, u32[]{:S(2)}) %copy-start) | copy-done | bytes 4456472
  33.5 2.0 %copy-done.7 = f32[16,32,2048]{2,1,0:T(8,128)} copy-done((f32[16,32,2048]{2,1,0:T(8,128)}, f32[16,32,2048]{2,1,0:T(8,128)S(1)}, u32[]{:S(2)}) %copy-start.7) | copy-done | bytes 4194328
  35.5 2.0 %copy-done.10 = f32[16,32,2048]{2,1,0:T(8,128)} copy-done((f32[16,32,2048]{2,1,0:T(8,128)}, f32[16,32,2048]{2,1,0:T(8,128)S(1)}, u32[]{:S(2)}) %copy-start.10) | copy-done | bytes 4194328
  37.5 2.1 %copy-done.13 = f32[16,32,2048]{2,1,0:T(8,128)} copy-done((f32[16,32,2048]{2,1,0:T(8,128)}, f32[16,32,2048]{2,1,0:T(8,128)S(1)}, u32[]{:S(2)}) %copy-start.13) | copy-done | bytes 4194328
  39.6 1.9 %copy-done.16 = f32[16,32,2048]{2,1,0:T(8,128)} copy-done((f32[16,32,2048]{2,1,0:T(8,128)}, f32[16,32,2048]{2,1,0:T(8,128)S(1)}, u32[]{:S(2)}) %copy-start.16) | copy-done | bytes 4194328
  43.3 3.0 %collective-permute-start.5 = (f32[32,2048]{1,0:T(8,128)S(1)}, f32[32,2048]{1,0:T(8,128)S(1)}, u32[]{:S(2)}, u32[]{:S(2)}) collective-permute-start(f32[32,2048]{1,0:T(8,128)S(1)} %get-tuple-element.63.f_pl0), channel_id=1, source_target_pairs={{0,120},{8,0},{16,8},{24,16},{32,24},{40,32},{48,40},{56,48},{64,5... | collective-permute-start | bytes 786440 | tf_op jit(solution)/shard_map/ppermute | solution.py:489
  46.3 6.0 %collective-permute-start.7 = (f32[16,2048]{1,0:T(8,128)S(1)}, f32[16,2048]{1,0:T(8,128)S(1)}, u32[]{:S(2)}, u32[]{:S(2)}) collective-permute-start(f32[16,2048]{1,0:T(8,128)S(1)} %get-tuple-element.65.f_row0), channel_id=1, source_target_pairs={{0,7},{1,0},{2,1},{3,2},{4,3},{5,4},{6,5},{7,6},{8,15},{9,8},{10,9... | collective-permute-start | bytes 393224 | tf_op jit(solution)/shard_map/ppermute | solution.py:489
  52.2 9.6 %all-to-all-start = ((f32[128,4,128]{2,1,0:T(4,128)}), f32[128,4,128]{2,1,0:T(4,128)S(1)}, u32[]{:S(2)}, u32[]{:S(2)}) async-start(f32[128,4,128]{2,1,0:T(4,128)} %bitcast.2), calls=%async_computation | async-start | bytes 524288 | tf_op jit(solution)/shard_map/all_to_all | solution.py:541
  61.8 2.3 %copy-done.1 = f32[17,32,2048]{2,1,0:T(8,128)S(1)} copy-done((f32[17,32,2048]{2,1,0:T(8,128)S(1)}, f32[17,32,2048]{2,1,0:T(8,128)}, u32[]{:S(2)}) %copy-start.1) | copy-done | bytes 4456472
  64.1 2.2 %copy-done.8 = f32[16,32,2048]{2,1,0:T(8,128)S(1)} copy-done((f32[16,32,2048]{2,1,0:T(8,128)S(1)}, f32[16,32,2048]{2,1,0:T(8,128)}, u32[]{:S(2)}) %copy-start.8) | copy-done | bytes 4194328
  66.3 2.2 %copy-done.11 = f32[16,32,2048]{2,1,0:T(8,128)S(1)} copy-done((f32[16,32,2048]{2,1,0:T(8,128)S(1)}, f32[16,32,2048]{2,1,0:T(8,128)}, u32[]{:S(2)}) %copy-start.11) | copy-done | bytes 4194328
  68.5 2.2 %copy-done.14 = f32[16,32,2048]{2,1,0:T(8,128)S(1)} copy-done((f32[16,32,2048]{2,1,0:T(8,128)S(1)}, f32[16,32,2048]{2,1,0:T(8,128)}, u32[]{:S(2)}) %copy-start.14) | copy-done | bytes 4194328
  70.6 2.2 %copy-done.17 = f32[16,32,2048]{2,1,0:T(8,128)S(1)} copy-done((f32[16,32,2048]{2,1,0:T(8,128)S(1)}, f32[16,32,2048]{2,1,0:T(8,128)}, u32[]{:S(2)}) %copy-start.17) | copy-done | bytes 4194328
  72.8 4.2 %sweep.1 = (f32[16,32,2048]{2,1,0:T(8,128)S(1)}, f32[2,32,2048]{2,1,0:T(8,128)S(1)}, f32[2,16,2048]{2,1,0:T(8,128)S(1)}) custom-call(f32[16,32,2048]{2,1,0:T(8,128)S(1)} %copy-done.8, f32[16,32,2048]{2,1,0:T(8,128)S(1)} %copy-done.11, f32[17,32,2048]{2,1,0:T(8,128)S(1)} %copy-done.1, f32[16,32,2048]{2,1,0:T(8,128)S(1)} %copy-done.14, ...), custom_call_target="tpu_custom_call" | custom-call | flops 41943040 | bytes 16777216 | tf_op jit(solution)/shard_map/sweep/pallas_call | solution.py:543
  77.0 2.0 %copy-done.20 = f32[16,32,2048]{2,1,0:T(8,128)} copy-done((f32[16,32,2048]{2,1,0:T(8,128)}, f32[16,32,2048]{2,1,0:T(8,128)S(1)}, u32[]{:S(2)}) %copy-start.20) | copy-done | bytes 4194328
  84.7 2.8 %collective-permute-start.9 = (f32[32,2048]{1,0:T(8,128)S(1)}, f32[32,2048]{1,0:T(8,128)S(1)}, u32[]{:S(2)}, u32[]{:S(2)}) collective-permute-start(f32[32,2048]{1,0:T(8,128)S(1)} %get-tuple-element.73.g_pl0), channel_id=1, source_target_pairs={{0,120},{8,0},{16,8},{24,16},{32,24},{40,32},{48,40},{56,48},{64,5... | collective-permute-start | bytes 786440 | tf_op jit(solution)/shard_map/ppermute | solution.py:489
  87.5 5.7 %collective-permute-start.11 = (f32[16,2048]{1,0:T(8,128)}, f32[16,2048]{1,0:T(8,128)}, u32[]{:S(2)}, u32[]{:S(2)}) collective-permute-start(f32[16,2048]{1,0:T(8,128)} %get-tuple-element.75.g_row0), channel_id=1, source_target_pairs={{0,7},{1,0},{2,1},{3,2},{4,3},{5,4},{6,5},{7,6},{8,15},{9,8},{10,9... | collective-permute-start | bytes 393224 | tf_op jit(solution)/shard_map/ppermute | solution.py:489
  93.3 4.6 %coarse.1.interp = f32[3,32,2048]{2,1,0:T(8,128)S(1)} custom-call(s32[2]{0:T(128)S(1)} %pad_add_fusion.place, f32[512,128]{1,0:T(8,128)S(1)} %bitcast.4), custom_call_target="tpu_custom_call" | custom-call | flops 20971520 | bytes 1048576 | tf_op jit(solution)/shard_map/coarse/pallas_call | solution.py:569
  97.9 2.3 %copy-done.2 = f32[17,32,2048]{2,1,0:T(8,128)S(1)} copy-done((f32[17,32,2048]{2,1,0:T(8,128)S(1)}, f32[17,32,2048]{2,1,0:T(8,128)}, u32[]{:S(2)}) %copy-start.2) | copy-done | bytes 4456472
  100.1 2.2 %copy-done.9 = f32[16,32,2048]{2,1,0:T(8,128)S(1)} copy-done((f32[16,32,2048]{2,1,0:T(8,128)S(1)}, f32[16,32,2048]{2,1,0:T(8,128)}, u32[]{:S(2)}) %copy-start.9) | copy-done | bytes 4194328
  102.3 2.2 %copy-done.12 = f32[16,32,2048]{2,1,0:T(8,128)S(1)} copy-done((f32[16,32,2048]{2,1,0:T(8,128)S(1)}, f32[16,32,2048]{2,1,0:T(8,128)}, u32[]{:S(2)}) %copy-start.12) | copy-done | bytes 4194328
  104.5 2.2 %copy-done.15 = f32[16,32,2048]{2,1,0:T(8,128)S(1)} copy-done((f32[16,32,2048]{2,1,0:T(8,128)S(1)}, f32[16,32,2048]{2,1,0:T(8,128)}, u32[]{:S(2)}) %copy-start.15) | copy-done | bytes 4194328
  106.7 2.2 %copy-done.18 = f32[16,32,2048]{2,1,0:T(8,128)S(1)} copy-done((f32[16,32,2048]{2,1,0:T(8,128)S(1)}, f32[16,32,2048]{2,1,0:T(8,128)}, u32[]{:S(2)}) %copy-start.18) | copy-done | bytes 4194328
  108.9 2.2 %copy-done.21 = f32[16,32,2048]{2,1,0:T(8,128)S(1)} copy-done((f32[16,32,2048]{2,1,0:T(8,128)S(1)}, f32[16,32,2048]{2,1,0:T(8,128)}, u32[]{:S(2)}) %copy-start.21) | copy-done | bytes 4194328
  111.1 8.4 %last.1 = (f32[16,32,2048]{2,1,0:T(8,128)}, f32[2,32,2048]{2,1,0:T(8,128)S(1)}, f32[14,8,2048]{2,1,0:T(8,128)S(1)}, f32[14,8,2048]{2,1,0:T(8,128)S(1)}) custom-call(f32[16,32,2048]{2,1,0:T(8,128)S(1)} %copy-done.9, f32[16,32,2048]{2,1,0:T(8,128)S(1)} %copy-done.12, f32[17,32,2048]{2,1,0:T(8,128)S(1)} %copy-done.2, f32[16,32,2048]{2,1,0:T(8,128)S(1)} %copy-done.15, ...), custom_call_target="tpu_custom_call" | custom-call | flops 41943040 | bytes 20971520 | tf_op jit(solution)/shard_map/last/pallas_call | solution.py:585
  119.5 2.6 %finish.1 = f32[16,32,2048]{2,1,0:T(8,128)} custom-call(f32[16,32,2048]{2,1,0:T(8,128)} %get-tuple-element.77.src, f32[2,32,2048]{2,1,0:T(8,128)S(1)} %get-tuple-element.78.b_pl, f32[14,8,2048]{2,1,0:T(8,128)S(1)} %get-tuple-element.79.b_lo, f32[14,8,2048]{2,1,0:T(8,128)S(1)} %get-tuple-element.80.b_hi, ...), custom_call_target="tpu_custom_call", output_to_operand_aliasing={{}: (0, {})} | custom-call | flops 262144 | bytes 3145728 | tf_op jit(solution)/shard_map/finish/pallas_call | solution.py:596
  (59 shorter events, 8.1 us)
Async XLA Ops:
  0.0 2.2 %copy-start.3 = (f32[16,32,2048]{2,1,0:T(8,128)S(1)}, f32[16,32,2048]{2,1,0:T(8,128)}, u32[]{:S(2)}) copy-start(f32[16,32,2048]{2,1,0:T(8,128)} %v.1) | copy-start | bytes 12582916
  2.2 2.2 %copy-start.5 = (f32[16,32,2048]{2,1,0:T(8,128)S(1)}, f32[16,32,2048]{2,1,0:T(8,128)}, u32[]{:S(2)}) copy-start(f32[16,32,2048]{2,1,0:T(8,128)} %k.1) | copy-start | bytes 12582916
  4.4 10.3 %copy-start.4 = (f32[16,32,2048]{2,1,0:T(8,128)S(1)}, f32[16,32,2048]{2,1,0:T(8,128)}, u32[]{:S(2)}) copy-start(f32[16,32,2048]{2,1,0:T(8,128)} %v.1) | copy-start | bytes 12582916
  4.4 10.3 %copy-start.6 = (f32[16,32,2048]{2,1,0:T(8,128)S(1)}, f32[16,32,2048]{2,1,0:T(8,128)}, u32[]{:S(2)}) copy-start(f32[16,32,2048]{2,1,0:T(8,128)} %k.1) | copy-start | bytes 12582916
  4.9 36.6 %collective-permute-start.1 = (f32[2,32,2048]{2,1,0:T(8,128)S(1)}, f32[2,32,2048]{2,1,0:T(8,128)S(1)}, u32[]{:S(2)}, u32[]{:S(2)}) collective-permute-start(f32[2,32,2048]{2,1,0:T(8,128)S(1)} %get-tuple-element.54.pl_lo), channel_id=1, source_target_pairs={{0,120},{8,0},{16,8},{24,16},{32,24},{40,32},{48,40},{56,48},{64,5... | collective-permute-start | bytes 1572872 | tf_op jit(solution)/shard_map/ppermute | solution.py:489
  8.3 33.2 %collective-permute-start = (f32[2,32,2048]{2,1,0:T(8,128)S(1)}, f32[2,32,2048]{2,1,0:T(8,128)S(1)}, u32[]{:S(2)}, u32[]{:S(2)}) collective-permute-start(f32[2,32,2048]{2,1,0:T(8,128)S(1)} %get-tuple-element.55.pl_hi), channel_id=1, source_target_pairs={{0,8},{8,16},{16,24},{24,32},{32,40},{40,48},{48,56},{56,64},{64,7... | collective-permute-start | bytes 1572872 | tf_op jit(solution)/shard_map/ppermute | solution.py:489
  8.3 33.2 %collective-permute-start.3 = (f32[2,16,2048]{2,1,0:T(8,128)S(1)}, f32[2,16,2048]{2,1,0:T(8,128)S(1)}, u32[]{:S(2)}, u32[]{:S(2)}) collective-permute-start(f32[2,16,2048]{2,1,0:T(8,128)S(1)} %get-tuple-element.56.rw_lo), channel_id=1, source_target_pairs={{0,7},{1,0},{2,1},{3,2},{4,3},{5,4},{6,5},{7,6},{8,15},{9,8},{10,9... | collective-permute-start | bytes 786440 | tf_op jit(solution)/shard_map/ppermute | solution.py:489
  14.7 26.9 %collective-permute-start.2 = (f32[2,16,2048]{2,1,0:T(8,128)S(1)}, f32[2,16,2048]{2,1,0:T(8,128)S(1)}, u32[]{:S(2)}, u32[]{:S(2)}) collective-permute-start(f32[2,16,2048]{2,1,0:T(8,128)S(1)} %get-tuple-element.57.rw_hi), channel_id=1, source_target_pairs={{0,1},{1,2},{2,3},{3,4},{4,5},{5,6},{6,7},{7,0},{8,9},{9,10},{10,1... | collective-permute-start | bytes 786440 | tf_op jit(solution)/shard_map/ppermute | solution.py:489
  14.7 2.2 %copy-start.19 = (f32[16,32,2048]{2,1,0:T(8,128)S(1)}, f32[16,32,2048]{2,1,0:T(8,128)}, u32[]{:S(2)}) copy-start(f32[16,32,2048]{2,1,0:T(8,128)} %s_hbm.1) | copy-start | bytes 12582916
  31.4 2.1 %copy-start = (f32[17,32,2048]{2,1,0:T(8,128)}, f32[17,32,2048]{2,1,0:T(8,128)S(1)}, u32[]{:S(2)}) copy-start(f32[17,32,2048]{2,1,0:T(8,128)S(1)} %get-tuple-element.45.cx) | copy-start | bytes 13369348
  33.5 2.0 %copy-start.7 = (f32[16,32,2048]{2,1,0:T(8,128)}, f32[16,32,2048]{2,1,0:T(8,128)S(1)}, u32[]{:S(2)}) copy-start(f32[16,32,2048]{2,1,0:T(8,128)S(1)} %get-tuple-element.43.w) | copy-start | bytes 12582916
  37.5 2.1 %copy-start.13 = (f32[16,32,2048]{2,1,0:T(8,128)}, f32[16,32,2048]{2,1,0:T(8,128)S(1)}, u32[]{:S(2)}) copy-start(f32[16,32,2048]{2,1,0:T(8,128)S(1)} %get-tuple-element.46.cy) | copy-start | bytes 12582916
  43.3 37.0 %collective-permute-start.5 = (f32[32,2048]{1,0:T(8,128)S(1)}, f32[32,2048]{1,0:T(8,128)S(1)}, u32[]{:S(2)}, u32[]{:S(2)}) collective-permute-start(f32[32,2048]{1,0:T(8,128)S(1)} %get-tuple-element.63.f_pl0), channel_id=1, source_target_pairs={{0,120},{8,0},{16,8},{24,16},{32,24},{40,32},{48,40},{56,48},{64,5... | collective-permute-start | bytes 786440 | tf_op jit(solution)/shard_map/ppermute | solution.py:489
  46.3 34.1 %collective-permute-start.4 = (f32[32,2048]{1,0:T(8,128)S(1)}, f32[32,2048]{1,0:T(8,128)S(1)}, u32[]{:S(2)}, u32[]{:S(2)}) collective-permute-start(f32[32,2048]{1,0:T(8,128)S(1)} %get-tuple-element.64.f_pl1), channel_id=1, source_target_pairs={{0,8},{8,16},{16,24},{24,32},{32,40},{40,48},{48,56},{56,64},{64,7... | collective-permute-start | bytes 786440 | tf_op jit(solution)/shard_map/ppermute | solution.py:489
  46.3 32.8 %collective-permute-start.7 = (f32[16,2048]{1,0:T(8,128)S(1)}, f32[16,2048]{1,0:T(8,128)S(1)}, u32[]{:S(2)}, u32[]{:S(2)}) collective-permute-start(f32[16,2048]{1,0:T(8,128)S(1)} %get-tuple-element.65.f_row0), channel_id=1, source_target_pairs={{0,7},{1,0},{2,1},{3,2},{4,3},{5,4},{6,5},{7,6},{8,15},{9,8},{10,9... | collective-permute-start | bytes 393224 | tf_op jit(solution)/shard_map/ppermute | solution.py:489
  52.2 27.5 %collective-permute-start.6 = (f32[16,2048]{1,0:T(8,128)S(1)}, f32[16,2048]{1,0:T(8,128)S(1)}, u32[]{:S(2)}, u32[]{:S(2)}) collective-permute-start(f32[16,2048]{1,0:T(8,128)S(1)} %get-tuple-element.66.f_row1), channel_id=1, source_target_pairs={{0,1},{1,2},{2,3},{3,4},{4,5},{5,6},{6,7},{7,0},{8,9},{9,10},{10,1... | collective-permute-start | bytes 393224 | tf_op jit(solution)/shard_map/ppermute | solution.py:489
  52.2 41.0 %all-to-all-start = ((f32[128,4,128]{2,1,0:T(4,128)}), f32[128,4,128]{2,1,0:T(4,128)S(1)}, u32[]{:S(2)}, u32[]{:S(2)}) async-start(f32[128,4,128]{2,1,0:T(4,128)} %bitcast.2), calls=%async_computation | async-start | bytes 524288 | tf_op jit(solution)/shard_map/all_to_all | solution.py:541
  61.8 2.3 %copy-start.1 = (f32[17,32,2048]{2,1,0:T(8,128)S(1)}, f32[17,32,2048]{2,1,0:T(8,128)}, u32[]{:S(2)}) copy-start(f32[17,32,2048]{2,1,0:T(8,128)} %copy-done) | copy-start | bytes 13369348
  64.1 2.2 %copy-start.8 = (f32[16,32,2048]{2,1,0:T(8,128)S(1)}, f32[16,32,2048]{2,1,0:T(8,128)}, u32[]{:S(2)}) copy-start(f32[16,32,2048]{2,1,0:T(8,128)} %copy-done.7) | copy-start | bytes 12582916
  66.3 2.2 %copy-start.11 = (f32[16,32,2048]{2,1,0:T(8,128)S(1)}, f32[16,32,2048]{2,1,0:T(8,128)}, u32[]{:S(2)}) copy-start(f32[16,32,2048]{2,1,0:T(8,128)} %copy-done.10) | copy-start | bytes 12582916
  68.5 2.2 %copy-start.14 = (f32[16,32,2048]{2,1,0:T(8,128)S(1)}, f32[16,32,2048]{2,1,0:T(8,128)}, u32[]{:S(2)}) copy-start(f32[16,32,2048]{2,1,0:T(8,128)} %copy-done.13) | copy-start | bytes 12582916
  70.6 2.2 %copy-start.17 = (f32[16,32,2048]{2,1,0:T(8,128)S(1)}, f32[16,32,2048]{2,1,0:T(8,128)}, u32[]{:S(2)}) copy-start(f32[16,32,2048]{2,1,0:T(8,128)} %copy-done.16) | copy-start | bytes 12582916
  84.7 34.9 %collective-permute-start.9 = (f32[32,2048]{1,0:T(8,128)S(1)}, f32[32,2048]{1,0:T(8,128)S(1)}, u32[]{:S(2)}, u32[]{:S(2)}) collective-permute-start(f32[32,2048]{1,0:T(8,128)S(1)} %get-tuple-element.73.g_pl0), channel_id=1, source_target_pairs={{0,120},{8,0},{16,8},{24,16},{32,24},{40,32},{48,40},{56,48},{64,5... | collective-permute-start | bytes 786440 | tf_op jit(solution)/shard_map/ppermute | solution.py:489
  87.5 32.0 %collective-permute-start.8 = (f32[32,2048]{1,0:T(8,128)S(1)}, f32[32,2048]{1,0:T(8,128)}, u32[]{:S(2)}, u32[]{:S(2)}) collective-permute-start(f32[32,2048]{1,0:T(8,128)S(1)} %get-tuple-element.74.g_pl1), channel_id=1, source_target_pairs={{0,8},{8,16},{16,24},{24,32},{32,40},{40,48},{48,56},{56,64},{64,7... | collective-permute-start | bytes 786440 | tf_op jit(solution)/shard_map/ppermute | solution.py:489
  87.5 32.0 %collective-permute-start.11 = (f32[16,2048]{1,0:T(8,128)}, f32[16,2048]{1,0:T(8,128)}, u32[]{:S(2)}, u32[]{:S(2)}) collective-permute-start(f32[16,2048]{1,0:T(8,128)} %get-tuple-element.75.g_row0), channel_id=1, source_target_pairs={{0,7},{1,0},{2,1},{3,2},{4,3},{5,4},{6,5},{7,6},{8,15},{9,8},{10,9... | collective-permute-start | bytes 393224 | tf_op jit(solution)/shard_map/ppermute | solution.py:489
  93.2 26.3 %collective-permute-start.10 = (f32[16,2048]{1,0:T(8,128)S(1)}, f32[16,2048]{1,0:T(8,128)}, u32[]{:S(2)}, u32[]{:S(2)}) collective-permute-start(f32[16,2048]{1,0:T(8,128)S(1)} %get-tuple-element.76.g_row1), channel_id=1, source_target_pairs={{0,1},{1,2},{2,3},{3,4},{4,5},{5,6},{6,7},{7,0},{8,9},{9,10},{10,1... | collective-permute-start | bytes 393224 | tf_op jit(solution)/shard_map/ppermute | solution.py:489
  97.9 2.3 %copy-start.2 = (f32[17,32,2048]{2,1,0:T(8,128)S(1)}, f32[17,32,2048]{2,1,0:T(8,128)}, u32[]{:S(2)}) copy-start(f32[17,32,2048]{2,1,0:T(8,128)} %copy-done) | copy-start | bytes 13369348
  100.1 2.2 %copy-start.9 = (f32[16,32,2048]{2,1,0:T(8,128)S(1)}, f32[16,32,2048]{2,1,0:T(8,128)}, u32[]{:S(2)}) copy-start(f32[16,32,2048]{2,1,0:T(8,128)} %copy-done.7) | copy-start | bytes 12582916
  102.3 2.2 %copy-start.12 = (f32[16,32,2048]{2,1,0:T(8,128)S(1)}, f32[16,32,2048]{2,1,0:T(8,128)}, u32[]{:S(2)}) copy-start(f32[16,32,2048]{2,1,0:T(8,128)} %copy-done.10) | copy-start | bytes 12582916
  104.5 2.2 %copy-start.15 = (f32[16,32,2048]{2,1,0:T(8,128)S(1)}, f32[16,32,2048]{2,1,0:T(8,128)}, u32[]{:S(2)}) copy-start(f32[16,32,2048]{2,1,0:T(8,128)} %copy-done.13) | copy-start | bytes 12582916
  106.7 2.2 %copy-start.18 = (f32[16,32,2048]{2,1,0:T(8,128)S(1)}, f32[16,32,2048]{2,1,0:T(8,128)}, u32[]{:S(2)}) copy-start(f32[16,32,2048]{2,1,0:T(8,128)} %copy-done.16) | copy-start | bytes 12582916
  108.9 2.2 %copy-start.21 = (f32[16,32,2048]{2,1,0:T(8,128)S(1)}, f32[16,32,2048]{2,1,0:T(8,128)}, u32[]{:S(2)}) copy-start(f32[16,32,2048]{2,1,0:T(8,128)} %copy-done.20) | copy-start | bytes 12582916
  (9 other events, 10.7 us)

commit v2 on v1

--- a/solution.py
+++ b/solution.py
@@ -16,8 +16,8 @@
 STRIP = 8
 
 VM = pl.BlockSpec(memory_space=pltpu.VMEM)
-SM = pl.BlockSpec(memory_space=pltpu.SMEM)
 ANY = pl.BlockSpec(memory_space=pl.ANY)
+HBM = pl.BlockSpec(memory_space=pltpu.HBM)
 
 
 def params(mib):
@@ -50,6 +50,14 @@
     prv = rolled[r - 1]
     sub = lax.broadcasted_iota(jnp.int32, prv.shape, 0)
     return jnp.where(sub == 0, prv, rolled[r])
+
+
+def up_coupling(k0, k_up, r):
+    c = 0.5 * (k0[r] + shifted_up(k_up, r))
+    if r == len(k0) - 1:
+        sub = lax.broadcasted_iota(jnp.int32, c.shape, 0)
+        c = jnp.where(sub == STRIP - 1, 0.0, c)
+    return c
 
 
 def strips(rows):
@@ -77,8 +85,8 @@
 
 def inner_kernel(
     v_hbm, s_hbm, k_hbm,
-    w_ref, f_ref, cx, cy, cz, d_lo, d_hi, r_lo, r_hi, drow, rrow, sums,
-    v, s, k, fx, sems,
+    w_hbm, f_hbm, d_lo, d_hi, r_lo, r_hi, drow, rrow, sums,
+    v, s, k, w_ref, f_ref, cx, fx, sems, out_sems,
 ):
     planes, rows, cols = v.shape
     sl = strips(rows)
@@ -87,13 +95,17 @@
     def copy(i, x):
         src, dst = ((k_hbm, k), (v_hbm, v), (s_hbm, s))[i]
         return pltpu.make_async_copy(src.at[x], dst.at[x], sems.at[i, x])
+
+    def out_copy(i, x):
+        src, dst = ((w_ref, w_hbm), (f_ref, f_hbm))[i]
+        return pltpu.make_async_copy(src.at[x], dst.at[x], out_sems.at[i, x])
 
     for x in range(planes):
         for i in range(3):
             copy(i, x).start()
     sums[...] = jnp.zeros_like(sums)
     fx[...] = jnp.zeros_like(fx)
-    cx[0] = jnp.zeros_like(fx)
+    cx[...] = jnp.zeros_like(cx)
     copy(0, 0).wait()
     copy(1, 0).wait()
 
@@ -112,11 +124,7 @@
         v_up = [pltpu.roll(a, STRIP - 1, 0) for a in v0]
         c_y, f_y = [], []
         for r in range(n):
-            c = 0.5 * (k0[r] + shifted_up(k_up, r))
-            if r == n - 1:
-                sub = lax.broadcasted_iota(jnp.int32, c.shape, 0)
-                c = jnp.where(sub == STRIP - 1, 0.0, c)
-            cy[x, sl[r], :] = c
+            c = up_coupling(k0, k_up, r)
             c_y.append(c)
             f_y.append(c * (v0[r] - shifted_up(v_up, r)))
         c_dn = [pltpu.roll(a, 1, 0) for a in c_y]
@@ -125,13 +133,12 @@
             a = sl[r]
             c_next = h_next * (k0[r] + k[xn, a, :])
             f_next = c_next * (v0[r] - v[xn, a, :])
-            c_prev = cx[x, a, :]
+            c_prev = cx[a, :]
             f_prev = fx[a, :]
-            cx[x + 1, a, :] = c_next
+            cx[a, :] = c_next
             fx[a, :] = f_next
             c_z = 0.5 * (k0[r] + zp(k0[r]))
             f_z = c_z * (v0[r] - zp(v0[r]))
-            cz[x, a, :] = c_z
             diag = ((REACTION + c_next) + (c_prev + c_y[r])) + (
                 (shifted_down(c_dn, r) + c_z) + zm(c_z)
             )
@@ -161,9 +168,14 @@
                 d_hi[a, :] = diag
                 r_hi[a, :] = res
 
+        out_copy(0, x).start()
+        out_copy(1, x).start()
         return carry
 
     lax.fori_loop(0, planes, plane, 0)
+    for x in range(planes):
+        for i in range(2):
+            out_copy(i, x).wait()
 
 
 def cross(q_pl, q_row, pls, rws, sign):
@@ -247,13 +259,18 @@
         payload[i * STRIP : (i + 1) * STRIP, :] = tile
 
 
-def put_edges(ref, e_pl0, e_pl1, e_row0, e_row1):
+def put_edges(ref, x, e_pl0, e_pl1, e_row0, e_row1):
     planes, rows, _ = ref.shape
-    for x in range(1, planes - 1):
-        ref[x, 0:1, :] = e_row0[x : x + 1, :]
-        ref[x, rows - 1 : rows, :] = e_row1[x : x + 1, :]
-    ref[0] = e_pl0[...]
-    ref[planes - 1] = e_pl1[...]
+    ref[x, 0:1, :] = e_row0[pl.ds(x, 1), :]
+    ref[x, rows - 1 : rows, :] = e_row1[pl.ds(x, 1), :]
+
+    @pl.when(x == 0)
+    def _():
+        ref[x] = e_pl0[...]
+
+    @pl.when(x == planes - 1)
+    def _():
+        ref[x] = e_pl1[...]
 
 
 def neighbour_sums(x, u, cx, cy, cz):
@@ -275,14 +292,45 @@
 
 
 def sweep_kernel(
-    w, f, cx, cy, cz, w_pl0, w_pl1, w_row0, w_row1, f_pl0, f_pl1, f_row0, f_row1,
-    g_ref, g_pl, g_row,
+    k_hbm, w_hbm, f_hbm, w_pl0, w_pl1, w_row0, w_row1, f_pl0, f_pl1, f_row0, f_row1,
+    w, f, cx_hbm, cy, cz, g_ref, g_pl, g_row, k, cx, sems, out_sems,
 ):
     planes, rows, cols = w.shape
-    put_edges(w, w_pl0, w_pl1, w_row0, w_row1)
-    put_edges(f, f_pl0, f_pl1, f_row0, f_row1)
+    sl = strips(rows)
+
+    def out_copy(x):
+        return pltpu.make_async_copy(cx.at[x], cx_hbm.at[x], out_sems.at[x])
+
+    def copy(i, x):
+        src, dst = ((k_hbm, k), (f_hbm, f), (w_hbm, w))[i]
+        return pltpu.make_async_copy(src.at[x], dst.at[x], sems.at[i, x])
+
+    def arrive(x):
+        for i in range(3):
+            copy(i, x).wait()
+        put_edges(f, x, f_pl0, f_pl1, f_row0, f_row1)
+        put_edges(w, x, w_pl0, w_pl1, w_row0, w_row1)
+
+    for x in range(planes):
+        for i in range(3):
+            copy(i, x).start()
+    cx[0] = jnp.zeros_like(k[0])
+    out_copy(0).start()
+    arrive(0)
 
     def plane(x, carry):
+        @pl.when(x < planes - 1)
+        def _():
+            arrive(x + 1)
+
+        xn = jnp.minimum(x + 1, planes - 1)
+        h_next = jnp.where(x < planes - 1, 0.5, 0.0).astype(F32)
+        k0 = [k[x, a, :] for a in sl]
+        k_up = [pltpu.roll(a, STRIP - 1, 0) for a in k0]
+        for r, a in enumerate(sl):
+            cx[x + 1, a, :] = h_next * (k0[r] + k[xn, a, :])
+            cy[x, a, :] = up_coupling(k0, k_up, r)
+            cz[x, a, :] = 0.5 * (k0[r] + zp(k0[r]))
         for r, a, u0, total in neighbour_sums(x, f, cx, cy, cz):
             new = (2.0 - DAMPING) * u0 + w[x, a, :] * total
             g_ref[x, a, :] = new
@@ -290,11 +338,14 @@
                 g_row[0, pl.ds(x, 1), :] = new[0:1]
             if (r + 1) * STRIP == rows:
                 g_row[1, pl.ds(x, 1), :] = new[STRIP - 1 :]
+        out_copy(x + 1).start()
         return carry
 
     lax.fori_loop(0, planes, plane, 0)
     g_pl[0] = g_ref[0]
     g_pl[1] = g_ref[planes - 1]
+    for x in range(planes + 1):
+        out_copy(x).wait()
 
 
 def mid_kernel(
@@ -310,21 +361,40 @@
 
 
 def last_kernel(
-    w, f, cx, cy, cz, g, interp, w_pl0, w_pl1, w_row0, w_row1, f_pl0, f_pl1, f_row0, f_row1,
-    g_pl0, g_pl1, g_row0, g_row1, out, b_pl, b_lo, b_hi, body, sems,
+    w, f, cx_hbm, cy, cz, g_any, interp, g_pl0, g_pl1, g_row0, g_row1,
+    out, b_pl, b_lo, b_hi, g, cx, body, in_sems, cx_sems, sems,
 ):
     planes, rows, cols = w.shape
     n = rows // STRIP
-    put_edges(w, w_pl0, w_pl1, w_row0, w_row1)
-    put_edges(f, f_pl0, f_pl1, f_row0, f_row1)
-    put_edges(g, g_pl0, g_pl1, g_row0, g_row1)
+
+    def in_copy(x):
+        return pltpu.make_async_copy(g_any.at[x], g.at[x], in_sems.at[x])
 
     def copy(x):
         return pltpu.make_async_copy(
             body.at[x], out.at[x, STRIP : rows - STRIP, :], sems.at[x]
         )
 
+    def cx_copy(x):
+        return pltpu.make_async_copy(cx_hbm.at[x], cx.at[x], cx_sems.at[x])
+
+    def arrive(x):
+        cx_copy(x + 1).wait()
+        in_copy(x).wait()
+        put_edges(g, x, g_pl0, g_pl1, g_row0, g_row1)
+
+    cx_copy(0).start()
+    for x in range(planes):
+        in_copy(x).start()
+        cx_copy(x + 1).start()
+    cx_copy(0).wait()
+    arrive(0)
+
     def plane(x, carry):
+        @pl.when(x < planes - 1)
+        def _():
+            arrive(x + 1)
+
         offset = ((x % F).astype(F32) + 0.5) / F - 0.5
         weight = jnp.abs(offset)
         side = jnp.where(offset > 0, 2, 0)
@@ -392,7 +462,7 @@
         c.wait()
 
 
-def coarse_kernel(place, got, interp, coef, b_ref, u_ref, *, nx, ny, rows):
+def coarse_kernel(got, interp, coef, b_ref, u_ref, *, nx, ny, rows):
     nz = got.shape[1]
     per = 2 * 2
 
@@ -450,7 +520,7 @@
         sweep(0, 1)
         last = 1
 
-    gx, gy = place[0], place[1]
+    gx, gy = lax.axis_index("gx"), lax.axis_index("gy")
     lines = []
     for d in (-1, 0, 1):
         p = lax.rem(gx + d + nx, nx)
@@ -500,26 +570,26 @@
     rw_lo, rw_hi, pl_lo, pl_hi = pl.pallas_call(
         ends_kernel,
         out_shape=(lines, lines, edges, edges),
-        in_specs=[ANY] * 2,
+        in_specs=[HBM] * 2,
         out_specs=(VM,) * 4,
         scratch_shapes=[dma((2, 4))],
-        compiler_params=params(4),
+        compiler_params=params(58),
         cost_estimate=cost(0, n // 2),
         name="ends",
     )(v, k)
     yl, yh = swap("gy", rw_lo, rw_hi)
     xl, xh = swap("gx", pl_lo, pl_hi)
 
-    w, f, cx, cy, cz, d_lo, d_hi, r_lo, r_hi, drow, rrow, sums = pl.pallas_call(
+    w, f, d_lo, d_hi, r_lo, r_hi, drow, rrow, sums = pl.pallas_call(
         inner_kernel,
-        out_shape=(full, full, sds(planes + 1, rows, cols), full, full)
-        + (edge,) * 4
-        + (lines, lines, sds(4 * STRIP, cols)),
-        in_specs=[ANY] * 3,
-        out_specs=(VM,) * 12,
-        scratch_shapes=[vm(full.shape, F32)] * 3 + [vm(edge.shape, F32), dma((3, planes))],
-        compiler_params=params(18),
-        cost_estimate=cost(50 * n, 32 * n),
+        out_shape=(full, full) + (edge,) * 4 + (lines, lines, sds(4 * STRIP, cols)),
+        in_specs=[HBM] * 3,
+        out_specs=(HBM,) * 2 + (VM,) * 7,
+        scratch_shapes=[vm(full.shape, F32)] * 5
+        + [vm(edge.shape, F32)] * 2
+        + [dma((3, planes)), dma((2, planes))],
+        compiler_params=params(52),
+        cost_estimate=cost(50 * n, 20 * n),
         name="inner",
     )(v, s, k)
 
@@ -540,15 +610,23 @@
     fxl, fxh = swap("gx", f_edges[0], f_edges[1])
     got = lax.all_to_all(payload, ("gx", "gy"), 0, 0, tiled=True)
 
-    g, g_pl, g_row = pl.pallas_call(
+    got, w, f, k = lax.optimization_barrier((got, w, f, k))
+
+    w, f, cx, cy, cz, g, g_pl, g_row = pl.pallas_call(
         sweep_kernel,
-        out_shape=(full, edges, lines),
-        in_specs=[VM] * 13,
-        out_specs=(VM,) * 3,
-        compiler_params=params(4),
-        cost_estimate=cost(40 * n, 16 * n),
+        out_shape=(full, full, sds(planes + 1, rows, cols), full, full, full, edges, lines),
+        in_specs=[HBM] * 3 + [VM] * 8,
+        out_specs=(VM, VM, HBM) + (VM,) * 5,
+        scratch_shapes=[
+            vm(full.shape, F32),
+            vm((planes + 1, rows, cols), F32),
+            dma((3, planes)),
+            dma((planes + 1,)),
+        ],
+        compiler_params=params(31),
+        cost_estimate=cost(40 * n, 12 * n),
         name="sweep",
-    )(w, f, cx, cy, cz, *w_edges, *f_edges)
+    )(k, w, f, *w_edges, *f_edges)
 
     g_edges = pl.pallas_call(
         mid_kernel,
@@ -564,12 +642,11 @@
     gyl, gyh = swap("gy", g_edges[2], g_edges[3])
     gxl, gxh = swap("gx", g_edges[0], g_edges[1])
 
-    place = jnp.stack([lax.axis_index("gx"), lax.axis_index("gy")]).astype(jnp.int32)
     cells = (nx, ny, cols // F)
     interp = pl.pallas_call(
         functools.partial(coarse_kernel, nx=nx, ny=ny, rows=rows),
         out_shape=sds(3, rows, cols),
-        in_specs=[SM, VM],
+        in_specs=[VM],
         out_specs=VM,
         scratch_shapes=[
             vm((6, 2) + cells, F32),
@@ -579,25 +656,32 @@
         compiler_params=params(8),
         cost_estimate=cost(20 * n, n),
         name="coarse",
-    )(place, got)
+    )(got)
 
     b_side = sds(planes - 2, STRIP, cols)
     out, b_pl, b_lo, b_hi = pl.pallas_call(
         last_kernel,
         out_shape=(full, edges, b_side, b_side),
-        in_specs=[VM] * 19,
-        out_specs=(ANY, VM, VM, VM),
-        scratch_shapes=[vm((planes, rows - 2 * STRIP, cols), F32), dma((planes,))],
-        compiler_params=params(8),
+        in_specs=[VM] * 2 + [HBM] + [VM] * 2 + [ANY] + [VM] * 5,
+        out_specs=(HBM, VM, VM, VM),
+        scratch_shapes=[
+            vm(full.shape, F32),
+            vm((planes + 1, rows, cols), F32),
+            vm((planes, rows - 2 * STRIP, cols), F32),
+            dma((planes,)),
+            dma((planes + 1,)),
+            dma((planes,)),
+        ],
+        compiler_params=params(30),
         cost_estimate=cost(40 * n, 20 * n),
         name="last",
-    )(w, f, cx, cy, cz, g, interp, *w_edges, *f_edges, *g_edges)
+    )(w, f, cx, cy, cz, g, interp, *g_edges)
 
     return pl.pallas_call(
         finish_kernel,
         out_shape=full,
-        in_specs=[ANY] + [VM] * 9,
-        out_specs=ANY,
+        in_specs=[HBM] + [VM] * 9,
+        out_specs=HBM,
         scratch_shapes=[
             vm(edges.shape, F32), vm(b_side.shape, F32), vm(b_side.shape, F32), dma((4,)),
         ],

time: 124 us -> 82.8 us (0.67); the launches traced: 122 us -> 82.6 us
  local copies, waits for them, and re-layouts: 47.6 us -> 0.01 us
  Pallas kernels: 37.5 us -> 43.5 us
  waiting for transfers between devices: 0.03 us -> 1.43 us
    unnamed x56 -> x8, local copies, waits for them, and re-layouts: 47.6 us -> 0.01 us
    ppermute x6, starting transfers between devices: 0.02 us -> 7.34 us  [swap(): lax.ppermute(high, axis, forward)]
    ppermute x6, starting transfers between devices: 27.2 us -> 22.5 us  [swap(): lax.ppermute(low, axis, backward)]
    pallas_call x3, Pallas kernels: 21.3 us -> 25.8 us  [the longest x1 15.9 us: per_device(): pl.pallas_call(inner_kernel, out_shape=(full, full) + (edge,) * 4 + (line...]
    pallas_call x1, Pallas kernels: 0.52 us -> 2.69 us  [per_device(): pl.pallas_call(ends_kernel, out_shape=(lines, lines, edges, edges), in_sp...]
    all_to_all x1, starting transfers between devices: 9.58 us -> 7.59 us  [per_device(): got = lax.all_to_all(payload, ('gx', 'gy'), 0, 0, tiled=True)]
    all_to_all x1, waiting for transfers between devices: 0.01 us -> 1.4 us  [per_device(): got = lax.all_to_all(payload, ('gx', 'gy'), 0, 0, tiled=True)]
  transfers between devices with their start and end apart: 13 -> 13, of which waited for: 0 -> 1; matrix products, arithmetic and copies ran while one was open for 0% -> 0% of each run, Pallas kernels for 27% -> 45%
where the time goes in v2:
time: 82.8 us; the launch traced here: 82.6 us
  Pallas kernels  43.5 us (53%)
  starting transfers between devices  37.4 us (45%)
  waiting for transfers between devices  1.43 us (2%)
    ppermute x6, starting transfers between devices, swap(): lax.ppermute(low, axis, backward)  22.5 us
    pallas_call x1, Pallas kernels, per_device(): pl.pallas_call(inner_kernel, out_shape=(full, full) + (edge,) * 4 + (line...  15.9 us
    pallas_call x1, Pallas kernels, per_device(): pl.pallas_call(last_kernel, out_shape=(full, edges, b_side, b_side), in_s...  9 us
    pallas_call x1, Pallas kernels, per_device(): pl.pallas_call(sweep_kernel, out_shape=(full, full, sds(planes + 1, rows,...  8.29 us
    all_to_all x1, starting transfers between devices, per_device(): got = lax.all_to_all(payload, ('gx', 'gy'), 0, 0, tiled=True)  7.59 us
    ppermute x6, starting transfers between devices, swap(): lax.ppermute(high, axis, forward)  7.34 us
    pallas_call x1, Pallas kernels, per_device(): pl.pallas_call(functools.partial(coarse_kernel, nx=nx, ny=ny, rows=rows),...  4.07 us
    pallas_call x1, Pallas kernels, per_device(): pl.pallas_call(ends_kernel, out_shape=(lines, lines, edges, edges), in_sp...  2.69 us
  transfers between devices with their start and end apart: 13, of which 1 were waited for; matrix products, arithmetic and copies ran while one was open for 0% of the time, Pallas kernels for 45%

profile of v2, /device:TPU:0, one launch (start us, length us, event | category | flops | bytes accessed | tf_op | source)
XLA Modules:
  0.0 82.6 jit_solution(6304677065201827272)
XLA Ops:
  0.0 2.7 %ends.1 = (f32[2,16,2048]{2,1,0:T(8,128)}, f32[2,16,2048]{2,1,0:T(8,128)}, f32[2,32,2048]{2,1,0:T(8,128)}, f32[2,32,2048]{2,1,0:T(8,128)}) custom-call(f32[16,32,2048]{2,1,0:T(8,128)} %v.1, f32[16,32,2048]{2,1,0:T(8,128)} %k_hbm.2), custom_call_target="tpu_custom_call" | custom-call | bytes 524288 | tf_op jit(solution)/shard_map/ends/pallas_call | solution.py:570
  2.7 0.1 collective-permute-start
  2.8 3.8 %collective-permute-start.1 = (f32[2,32,2048]{2,1,0:T(8,128)}, f32[2,32,2048]{2,1,0:T(8,128)S(1)}, u32[]{:S(2)}, u32[]{:S(2)}) collective-permute-start(f32[2,32,2048]{2,1,0:T(8,128)} %get-tuple-element.55.pl_lo), channel_id=1, source_target_pairs={{0,120},{8,0},{16,8},{24,16},{32,24},{40,32},{48,40},{56,48},{64,5... | collective-permute-start | bytes 1572872 | tf_op jit(solution)/shard_map/ppermute | solution.py:559
  6.6 3.3 %collective-permute-start.2 = (f32[2,16,2048]{2,1,0:T(8,128)}, f32[2,16,2048]{2,1,0:T(8,128)S(1)}, u32[]{:S(2)}, u32[]{:S(2)}) collective-permute-start(f32[2,16,2048]{2,1,0:T(8,128)} %get-tuple-element.58.rw_hi), channel_id=1, source_target_pairs={{0,1},{1,2},{2,3},{3,4},{4,5},{5,6},{6,7},{7,0},{8,9},{9,10},{10,1... | collective-permute-start | bytes 786440 | tf_op jit(solution)/shard_map/ppermute | solution.py:559
  9.9 3.6 %collective-permute-start.3 = (f32[2,16,2048]{2,1,0:T(8,128)}, f32[2,16,2048]{2,1,0:T(8,128)S(1)}, u32[]{:S(2)}, u32[]{:S(2)}) collective-permute-start(f32[2,16,2048]{2,1,0:T(8,128)} %get-tuple-element.57.rw_lo), channel_id=1, source_target_pairs={{0,7},{1,0},{2,1},{3,2},{4,3},{5,4},{6,5},{7,6},{8,15},{9,8},{10,9... | collective-permute-start | bytes 786440 | tf_op jit(solution)/shard_map/ppermute | solution.py:559
  13.5 15.9 %inner.1 = (f32[16,32,2048]{2,1,0:T(8,128)}, f32[16,32,2048]{2,1,0:T(8,128)}, f32[32,2048]{1,0:T(8,128)S(1)}, f32[32,2048]{1,0:T(8,128)S(1)}, f32[32,2048]{1,0:T...) custom-call(f32[16,32,2048]{2,1,0:T(8,128)} %v.1, ...), custom_call_target="tpu_custom_call" | custom-call | flops 52428800 | bytes 20971520 | tf_op jit(solution)/shard_map/inner/pallas_call | solution.py:583
  29.4 0.0 collective-permute-done.2.yl
  29.4 0.0 collective-permute-done.3.yh
  29.4 0.0 collective-permute-done.xl
  29.4 0.0 collective-permute-done.1.xh
  29.5 1.8 %edge.1 = (f32[32,2048]{1,0:T(8,128)S(1)}, f32[32,2048]{1,0:T(8,128)S(1)}, f32[16,2048]{1,0:T(8,128)S(1)}, f32[16,2048]{1,0:T(8,128)S(1)}, f32[32,2048]{1,0:T(8,...) custom-call(f32[32,2048]{1,0:T(8,128)S(1)} %get-tuple-element.49.d_l, ...), custom_call_target="tpu_custom_call" | custom-call | flops 1310720 | bytes 1048576 | tf_op jit(solution)/shard_map/edge/pallas_call | solution.py:597
  31.2 7.6 %all-to-all-start = ((f32[128,4,128]{2,1,0:T(4,128)}), f32[128,4,128]{2,1,0:T(4,128)S(1)}, u32[]{:S(2)}, u32[]{:S(2)}) async-start(f32[128,4,128]{2,1,0:T(4,128)} %bitcast), calls=%async_computation | async-start | bytes 524288 | tf_op jit(solution)/shard_map/all_to_all | solution.py:611
  38.8 0.1 collective-permute-start.4
  38.9 3.8 %collective-permute-start.5 = (f32[32,2048]{1,0:T(8,128)S(1)}, f32[32,2048]{1,0:T(8,128)S(1)}, u32[]{:S(2)}, u32[]{:S(2)}) collective-permute-start(f32[32,2048]{1,0:T(8,128)S(1)} %get-tuple-element.70.f_pl0), channel_id=1, source_target_pairs={{0,120},{8,0},{16,8},{24,16},{32,24},{40,32},{48,40},{56,48},{64,5... | collective-permute-start | bytes 786440 | tf_op jit(solution)/shard_map/ppermute | solution.py:559
  42.7 2.5 %collective-permute-start.6 = (f32[16,2048]{1,0:T(8,128)S(1)}, f32[16,2048]{1,0:T(8,128)S(1)}, u32[]{:S(2)}, u32[]{:S(2)}) collective-permute-start(f32[16,2048]{1,0:T(8,128)S(1)} %get-tuple-element.73.f_row1), channel_id=1, source_target_pairs={{0,1},{1,2},{2,3},{3,4},{4,5},{5,6},{6,7},{7,0},{8,9},{9,10},{10,1... | collective-permute-start | bytes 393224 | tf_op jit(solution)/shard_map/ppermute | solution.py:559
  45.2 3.2 %collective-permute-start.7 = (f32[16,2048]{1,0:T(8,128)S(1)}, f32[16,2048]{1,0:T(8,128)S(1)}, u32[]{:S(2)}, u32[]{:S(2)}) collective-permute-start(f32[16,2048]{1,0:T(8,128)S(1)} %get-tuple-element.72.f_row0), channel_id=1, source_target_pairs={{0,7},{1,0},{2,1},{3,2},{4,3},{5,4},{6,5},{7,6},{8,15},{9,8},{10,9... | collective-permute-start | bytes 393224 | tf_op jit(solution)/shard_map/ppermute | solution.py:559
  48.4 1.4 %all-to-all-done = f32[128,4,128]{2,1,0:T(4,128)S(1)} async-done(((f32[128,4,128]{2,1,0:T(4,128)}), f32[128,4,128]{2,1,0:T(4,128)S(1)}, u32[]{:S(2)}, u32[]{:S(2)}) %all-to-all-start) | async-done | bytes 262176 | tf_op jit(solution)/shard_map/all_to_all | solution.py:611
  49.8 8.3 %sweep.1 = (f32[16,32,2048]{2,1,0:T(8,128)S(1)}, f32[16,32,2048]{2,1,0:T(8,128)S(1)}, f32[17,32,2048]{2,1,0:T(8,128)}, f32[16,32,2048]{2,1,0:T(8,128)S(1)}, f32[...) custom-call(f32[16,32,2048]{2,1,0:T(8,128)} %k_hbm.2, ...), custom_call_target="tpu_custom_call" | custom-call | flops 41943040 | bytes 12582912 | tf_op jit(solution)/shard_map/sweep/pallas_call | solution.py:615
  58.1 0.0 collective-permute-done.6.yl
  58.1 0.0 collective-permute-done.4.xl
  58.1 0.0 collective-permute-done.5.xh
  58.1 0.2 mid.1
  58.3 0.1 collective-permute-start.8
  58.4 3.8 %collective-permute-start.9 = (f32[32,2048]{1,0:T(8,128)S(1)}, f32[32,2048]{1,0:T(8,128)S(1)}, u32[]{:S(2)}, u32[]{:S(2)}) collective-permute-start(f32[32,2048]{1,0:T(8,128)S(1)} %get-tuple-element.85.g_pl0), channel_id=1, source_target_pairs={{0,120},{8,0},{16,8},{24,16},{32,24},{40,32},{48,40},{56,48},{64,5... | collective-permute-start | bytes 786440 | tf_op jit(solution)/shard_map/ppermute | solution.py:559
  62.3 1.4 %collective-permute-start.10 = (f32[16,2048]{1,0:T(8,128)S(1)}, f32[16,2048]{1,0:T(8,128)S(1)}, u32[]{:S(2)}, u32[]{:S(2)}) collective-permute-start(f32[16,2048]{1,0:T(8,128)S(1)} %get-tuple-element.88.g_row1), channel_id=1, source_target_pairs={{0,1},{1,2},{2,3},{3,4},{4,5},{5,6},{6,7},{7,0},{8,9},{9,10},{10,1... | collective-permute-start | bytes 393224 | tf_op jit(solution)/shard_map/ppermute | solution.py:559
  63.6 4.3 %collective-permute-start.11 = (f32[16,2048]{1,0:T(8,128)S(1)}, f32[16,2048]{1,0:T(8,128)S(1)}, u32[]{:S(2)}, u32[]{:S(2)}) collective-permute-start(f32[16,2048]{1,0:T(8,128)S(1)} %get-tuple-element.87.g_row0), channel_id=1, source_target_pairs={{0,7},{1,0},{2,1},{3,2},{4,3},{5,4},{6,5},{7,6},{8,15},{9,8},{10,9... | collective-permute-start | bytes 393224 | tf_op jit(solution)/shard_map/ppermute | solution.py:559
  67.9 4.1 %coarse.1.interp = f32[3,32,2048]{2,1,0:T(8,128)S(1)} custom-call(f32[512,128]{1,0:T(8,128)S(1)} %bitcast.2), custom_call_target="tpu_custom_call" | custom-call | flops 20971520 | bytes 1048576 | tf_op jit(solution)/shard_map/coarse/pallas_call | solution.py:646
  72.0 9.0 %last.1 = (f32[16,32,2048]{2,1,0:T(8,128)}, f32[2,32,2048]{2,1,0:T(8,128)S(1)}, f32[14,8,2048]{2,1,0:T(8,128)S(1)}, f32[14,8,2048]{2,1,0:T(8,128)S(1)}) custom-call(f32[16,32,2048]{2,1,0:T(8,128)S(1)} %get-tuple-element.74.w, f32[16,32,2048]{2,1,0:T(8,128)S(1)} %get-tuple-element.75.f, f32[17,32,2048]{2,1,0:T(8,128)} %get-tuple-element.76.cx_hbm, ...), custom_call_target="tpu_custom_call" | custom-call | flops 41943040 | bytes 20971520 | tf_op jit(solution)/shard_map/last/pallas_call | solution.py:662
  81.0 0.0 collective-permute-done.10.yl
  81.0 0.0 collective-permute-done.8.xl
  81.0 0.0 collective-permute-done.9.xh
  81.0 1.6 %finish.1 = f32[16,32,2048]{2,1,0:T(8,128)} custom-call(f32[16,32,2048]{2,1,0:T(8,128)} %get-tuple-element.89.src, f32[2,32,2048]{2,1,0:T(8,128)S(1)} %get-tuple-element.90.b_pl, f32[14,8,2048]{2,1,0:T(8,128)S(1)} %get-tuple-element.91.b_lo, f32[14,8,2048]{2,1,0:T(8,128)S(1)} %get-tuple-element.92.b_hi, ...), custom_call_target="tpu_custom_call", output_to_operand_aliasing={{}: (0, {})} | custom-call | flops 262144 | bytes 3145728 | tf_op jit(solution)/shard_map/finish/pallas_call | solution.py:680
  (10 shorter events, 0.0 us)
Async XLA Ops:
  2.7 26.7 %collective-permute-start = (f32[2,32,2048]{2,1,0:T(8,128)}, f32[2,32,2048]{2,1,0:T(8,128)S(1)}, u32[]{:S(2)}, u32[]{:S(2)}) collective-permute-start(f32[2,32,2048]{2,1,0:T(8,128)} %get-tuple-element.56.pl_hi), channel_id=1, source_target_pairs={{0,8},{8,16},{16,24},{24,32},{32,40},{40,48},{48,56},{56,64},{64,7... | collective-permute-start | bytes 1572872 | tf_op jit(solution)/shard_map/ppermute | solution.py:559
  2.8 26.6 %collective-permute-start.1 = (f32[2,32,2048]{2,1,0:T(8,128)}, f32[2,32,2048]{2,1,0:T(8,128)S(1)}, u32[]{:S(2)}, u32[]{:S(2)}) collective-permute-start(f32[2,32,2048]{2,1,0:T(8,128)} %get-tuple-element.55.pl_lo), channel_id=1, source_target_pairs={{0,120},{8,0},{16,8},{24,16},{32,24},{40,32},{48,40},{56,48},{64,5... | collective-permute-start | bytes 1572872 | tf_op jit(solution)/shard_map/ppermute | solution.py:559
  6.6 22.8 %collective-permute-start.2 = (f32[2,16,2048]{2,1,0:T(8,128)}, f32[2,16,2048]{2,1,0:T(8,128)S(1)}, u32[]{:S(2)}, u32[]{:S(2)}) collective-permute-start(f32[2,16,2048]{2,1,0:T(8,128)} %get-tuple-element.58.rw_hi), channel_id=1, source_target_pairs={{0,1},{1,2},{2,3},{3,4},{4,5},{5,6},{6,7},{7,0},{8,9},{9,10},{10,1... | collective-permute-start | bytes 786440 | tf_op jit(solution)/shard_map/ppermute | solution.py:559
  9.9 19.5 %copy-start = (f32[2,32,2048]{2,1,0:T(8,128)S(1)}, f32[2,32,2048]{2,1,0:T(8,128)}, u32[]{:S(2)}) copy-start(f32[2,32,2048]{2,1,0:T(8,128)} %get-tuple-element.55.pl_lo) | copy-start | bytes 1572868
  9.9 19.5 %copy-start.1 = (f32[2,32,2048]{2,1,0:T(8,128)S(1)}, f32[2,32,2048]{2,1,0:T(8,128)}, u32[]{:S(2)}) copy-start(f32[2,32,2048]{2,1,0:T(8,128)} %get-tuple-element.56.pl_hi) | copy-start | bytes 1572868
  9.9 19.6 %copy-start.2 = (f32[2,16,2048]{2,1,0:T(8,128)S(1)}, f32[2,16,2048]{2,1,0:T(8,128)}, u32[]{:S(2)}) copy-start(f32[2,16,2048]{2,1,0:T(8,128)} %get-tuple-element.57.rw_lo) | copy-start | bytes 786436
  9.9 19.6 %copy-start.3 = (f32[2,16,2048]{2,1,0:T(8,128)S(1)}, f32[2,16,2048]{2,1,0:T(8,128)}, u32[]{:S(2)}) copy-start(f32[2,16,2048]{2,1,0:T(8,128)} %get-tuple-element.58.rw_hi) | copy-start | bytes 786436
  9.9 19.5 %collective-permute-start.3 = (f32[2,16,2048]{2,1,0:T(8,128)}, f32[2,16,2048]{2,1,0:T(8,128)S(1)}, u32[]{:S(2)}, u32[]{:S(2)}) collective-permute-start(f32[2,16,2048]{2,1,0:T(8,128)} %get-tuple-element.57.rw_lo), channel_id=1, source_target_pairs={{0,7},{1,0},{2,1},{3,2},{4,3},{5,4},{6,5},{7,6},{8,15},{9,8},{10,9... | collective-permute-start | bytes 786440 | tf_op jit(solution)/shard_map/ppermute | solution.py:559
  31.2 18.6 %all-to-all-start = ((f32[128,4,128]{2,1,0:T(4,128)}), f32[128,4,128]{2,1,0:T(4,128)S(1)}, u32[]{:S(2)}, u32[]{:S(2)}) async-start(f32[128,4,128]{2,1,0:T(4,128)} %bitcast), calls=%async_computation | async-start | bytes 524288 | tf_op jit(solution)/shard_map/all_to_all | solution.py:611
  38.8 19.3 %collective-permute-start.4 = (f32[32,2048]{1,0:T(8,128)S(1)}, f32[32,2048]{1,0:T(8,128)S(1)}, u32[]{:S(2)}, u32[]{:S(2)}) collective-permute-start(f32[32,2048]{1,0:T(8,128)S(1)} %get-tuple-element.71.f_pl1), channel_id=1, source_target_pairs={{0,8},{8,16},{16,24},{24,32},{32,40},{40,48},{48,56},{56,64},{64,7... | collective-permute-start | bytes 786440 | tf_op jit(solution)/shard_map/ppermute | solution.py:559
  38.9 19.2 %collective-permute-start.5 = (f32[32,2048]{1,0:T(8,128)S(1)}, f32[32,2048]{1,0:T(8,128)S(1)}, u32[]{:S(2)}, u32[]{:S(2)}) collective-permute-start(f32[32,2048]{1,0:T(8,128)S(1)} %get-tuple-element.70.f_pl0), channel_id=1, source_target_pairs={{0,120},{8,0},{16,8},{24,16},{32,24},{40,32},{48,40},{56,48},{64,5... | collective-permute-start | bytes 786440 | tf_op jit(solution)/shard_map/ppermute | solution.py:559
  42.7 15.3 %collective-permute-start.6 = (f32[16,2048]{1,0:T(8,128)S(1)}, f32[16,2048]{1,0:T(8,128)S(1)}, u32[]{:S(2)}, u32[]{:S(2)}) collective-permute-start(f32[16,2048]{1,0:T(8,128)S(1)} %get-tuple-element.73.f_row1), channel_id=1, source_target_pairs={{0,1},{1,2},{2,3},{3,4},{4,5},{5,6},{6,7},{7,0},{8,9},{9,10},{10,1... | collective-permute-start | bytes 393224 | tf_op jit(solution)/shard_map/ppermute | solution.py:559
  45.2 12.9 %collective-permute-start.7 = (f32[16,2048]{1,0:T(8,128)S(1)}, f32[16,2048]{1,0:T(8,128)S(1)}, u32[]{:S(2)}, u32[]{:S(2)}) collective-permute-start(f32[16,2048]{1,0:T(8,128)S(1)} %get-tuple-element.72.f_row0), channel_id=1, source_target_pairs={{0,7},{1,0},{2,1},{3,2},{4,3},{5,4},{6,5},{7,6},{8,15},{9,8},{10,9... | collective-permute-start | bytes 393224 | tf_op jit(solution)/shard_map/ppermute | solution.py:559
  58.3 22.7 %collective-permute-start.8 = (f32[32,2048]{1,0:T(8,128)S(1)}, f32[32,2048]{1,0:T(8,128)S(1)}, u32[]{:S(2)}, u32[]{:S(2)}) collective-permute-start(f32[32,2048]{1,0:T(8,128)S(1)} %get-tuple-element.86.g_pl1), channel_id=1, source_target_pairs={{0,8},{8,16},{16,24},{24,32},{32,40},{40,48},{48,56},{56,64},{64,7... | collective-permute-start | bytes 786440 | tf_op jit(solution)/shard_map/ppermute | solution.py:559
  58.4 22.6 %collective-permute-start.9 = (f32[32,2048]{1,0:T(8,128)S(1)}, f32[32,2048]{1,0:T(8,128)S(1)}, u32[]{:S(2)}, u32[]{:S(2)}) collective-permute-start(f32[32,2048]{1,0:T(8,128)S(1)} %get-tuple-element.85.g_pl0), channel_id=1, source_target_pairs={{0,120},{8,0},{16,8},{24,16},{32,24},{40,32},{48,40},{56,48},{64,5... | collective-permute-start | bytes 786440 | tf_op jit(solution)/shard_map/ppermute | solution.py:559
  62.3 18.7 %collective-permute-start.10 = (f32[16,2048]{1,0:T(8,128)S(1)}, f32[16,2048]{1,0:T(8,128)S(1)}, u32[]{:S(2)}, u32[]{:S(2)}) collective-permute-start(f32[16,2048]{1,0:T(8,128)S(1)} %get-tuple-element.88.g_row1), channel_id=1, source_target_pairs={{0,1},{1,2},{2,3},{3,4},{4,5},{5,6},{6,7},{7,0},{8,9},{9,10},{10,1... | collective-permute-start | bytes 393224 | tf_op jit(solution)/shard_map/ppermute | solution.py:559
  63.6 17.4 %collective-permute-start.11 = (f32[16,2048]{1,0:T(8,128)S(1)}, f32[16,2048]{1,0:T(8,128)S(1)}, u32[]{:S(2)}, u32[]{:S(2)}) collective-permute-start(f32[16,2048]{1,0:T(8,128)S(1)} %get-tuple-element.87.g_row0), channel_id=1, source_target_pairs={{0,7},{1,0},{2,1},{3,2},{4,3},{5,4},{6,5},{7,6},{8,15},{9,8},{10,9... | collective-permute-start | bytes 393224 | tf_op jit(solution)/shard_map/ppermute | solution.py:559

commit v3 on v2

--- a/solution.py
+++ b/solution.py
@@ -14,6 +14,7 @@
 F32 = jnp.float32
 BF16 = jnp.bfloat16
 STRIP = 8
+LANES = 128
 
 VM = pl.BlockSpec(memory_space=pltpu.VMEM)
 ANY = pl.BlockSpec(memory_space=pl.ANY)
@@ -32,32 +33,30 @@
     return jax.ShapeDtypeStruct(shape, F32)
 
 
-def zp(a):
-    return pltpu.roll(a, a.shape[-1] - 1, a.ndim - 1)
-
-
-def zm(a):
-    return pltpu.roll(a, 1, a.ndim - 1)
-
-
-def shifted_up(rolled, r):
-    nxt = rolled[min(r + 1, len(rolled) - 1)]
-    sub = lax.broadcasted_iota(jnp.int32, nxt.shape, 0)
-    return jnp.where(sub == STRIP - 1, nxt, rolled[r])
-
-
-def shifted_down(rolled, r):
-    prv = rolled[r - 1]
-    sub = lax.broadcasted_iota(jnp.int32, prv.shape, 0)
-    return jnp.where(sub == 0, prv, rolled[r])
-
-
-def up_coupling(k0, k_up, r):
-    c = 0.5 * (k0[r] + shifted_up(k_up, r))
-    if r == len(k0) - 1:
-        sub = lax.broadcasted_iota(jnp.int32, c.shape, 0)
-        c = jnp.where(sub == STRIP - 1, 0.0, c)
-    return c
+def left(a):
+    return pltpu.roll(a, LANES - 1, 1)
+
+
+def right(a):
+    return pltpu.roll(a, 1, 1)
+
+
+def upward(a):
+    return pltpu.roll(a, STRIP - 1, 0)
+
+
+def downward(a):
+    return pltpu.roll(a, 1, 0)
+
+
+def masks():
+    lane = lax.broadcasted_iota(jnp.int32, (STRIP, LANES), 1)
+    sub = lax.broadcasted_iota(jnp.int32, (STRIP, LANES), 0)
+    return lane == 0, lane == LANES - 1, sub == 0, sub == STRIP - 1
+
+
+def tiles(cols):
+    return [slice(j * LANES, (j + 1) * LANES) for j in range(cols // LANES)]
 
 
 def strips(rows):
@@ -86,7 +85,7 @@
 def inner_kernel(
     v_hbm, s_hbm, k_hbm,
     w_hbm, f_hbm, d_lo, d_hi, r_lo, r_hi, drow, rrow, sums,
-    v, s, k, w_ref, f_ref, cx, fx, sems, out_sems,
+    v, s, k, w_ref, f_ref, cx, fx, ends, sems, out_sems,
 ):
     planes, rows, cols = v.shape
     sl = strips(rows)
@@ -108,71 +107,95 @@
     cx[...] = jnp.zeros_like(cx)
     copy(0, 0).wait()
     copy(1, 0).wait()
-
-    def plane(x, carry):
-        @pl.when(x < planes - 1)
-        def _():
+    tl = tiles(cols)
+    m = len(tl)
+    lane0, lane1, sub0, sub1 = masks()
+
+    def plane(x, first=False, last=False):
+        xn = x if last else x + 1
+        if not last:
             copy(0, x + 1).wait()
             copy(1, x + 1).wait()
-
         copy(2, x).wait()
-        xn = jnp.minimum(x + 1, planes - 1)
-        h_next = jnp.where(x < planes - 1, 0.5, 0.0).astype(F32)
-        k0 = [k[x, a, :] for a in sl]
-        v0 = [v[x, a, :] for a in sl]
-        k_up = [pltpu.roll(a, STRIP - 1, 0) for a in k0]
-        v_up = [pltpu.roll(a, STRIP - 1, 0) for a in v0]
-        c_y, f_y = [], []
-        for r in range(n):
-            c = up_coupling(k0, k_up, r)
-            c_y.append(c)
-            f_y.append(c * (v0[r] - shifted_up(v_up, r)))
-        c_dn = [pltpu.roll(a, 1, 0) for a in c_y]
-        f_dn = [pltpu.roll(a, 1, 0) for a in f_y]
-        for r in range(n):
-            a = sl[r]
-            c_next = h_next * (k0[r] + k[xn, a, :])
-            f_next = c_next * (v0[r] - v[xn, a, :])
-            c_prev = cx[a, :]
-            f_prev = fx[a, :]
-            cx[a, :] = c_next
-            fx[a, :] = f_next
-            c_z = 0.5 * (k0[r] + zp(k0[r]))
-            f_z = c_z * (v0[r] - zp(v0[r]))
-            diag = ((REACTION + c_next) + (c_prev + c_y[r])) + (
-                (shifted_down(c_dn, r) + c_z) + zm(c_z)
-            )
-            res = ((s[x, a, :] - REACTION * v0[r]) + (f_prev - f_next)) + (
-                (shifted_down(f_dn, r) - f_y[r]) + (zm(f_z) - f_z)
-            )
-            w = DAMPING / diag
-            w_ref[x, a, :] = w
-            f_ref[x, a, :] = w * res
-            half = r * STRIP // F
-            sums[half * STRIP : (half + 1) * STRIP, :] += res
-            sums[(2 + half) * STRIP : (3 + half) * STRIP, :] += k0[r]
-            if r == 0:
-                drow[0, pl.ds(x, 1), :] = diag[0:1]
-                rrow[0, pl.ds(x, 1), :] = res[0:1]
-            if r == n - 1:
-                drow[1, pl.ds(x, 1), :] = diag[STRIP - 1 :]
-                rrow[1, pl.ds(x, 1), :] = res[STRIP - 1 :]
-
-            @pl.when(x == 0)
-            def _():
-                d_lo[a, :] = diag
-                r_lo[a, :] = res
-
-            @pl.when(x == planes - 1)
-            def _():
-                d_hi[a, :] = diag
-                r_hi[a, :] = res
-
+        rk = [left(k[x, a, tl[0]]) for a in sl]
+        rv = [left(v[x, a, tl[0]]) for a in sl]
+        pc, pf = [], []
+        for r, a in enumerate(sl):
+            k0, v0 = k[x, a, tl[-1]], v[x, a, tl[-1]]
+            c = 0.5 * (k0 + jnp.where(lane1, rk[r], left(k0)))
+            pc.append(right(c))
+            pf.append(right(c * (v0 - jnp.where(lane1, rv[r], left(v0)))))
+        for j in range(m):
+            t, tn = tl[j], tl[(j + 1) % m]
+            ks = [k[x, a, t] for a in sl]
+            vs = [v[x, a, t] for a in sl]
+            ku = [upward(a) for a in ks]
+            vu = [upward(a) for a in vs]
+            dc = df = 0.0
+            res_sum = k_sum = None
+            for r, a in enumerate(sl):
+                k0, v0 = ks[r], vs[r]
+                nk, nv = left(k[x, a, tn]), left(v[x, a, tn])
+                c_z = 0.5 * (k0 + jnp.where(lane1, nk, rk[r]))
+                f_z = c_z * (v0 - jnp.where(lane1, nv, rv[r]))
+                rk[r], rv[r] = nk, nv
+                mc, mf = right(c_z), right(f_z)
+                diag = c_z + jnp.where(lane0, pc[r], mc)
+                res = jnp.where(lane0, pf[r], mf) - f_z
+                pc[r], pf[r] = mc, mf
+                if r < n - 1:
+                    c_y = 0.5 * (k0 + jnp.where(sub1, ku[r + 1], ku[r]))
+                    f_y = c_y * (v0 - jnp.where(sub1, vu[r + 1], vu[r]))
+                else:
+                    c_y = jnp.where(sub1, 0.0, 0.5 * (k0 + ku[r]))
+                    f_y = c_y * (v0 - vu[r])
+                nc, nf = downward(c_y), downward(f_y)
+                diag = diag + (c_y + jnp.where(sub0, dc, nc))
+                res = res + (jnp.where(sub0, df, nf) - f_y)
+                dc, df = nc, nf
+                if not first:
+                    diag = diag + cx[a, t]
+                    res = res + fx[a, t]
+                if not last:
+                    c_x = 0.5 * (k0 + k[xn, a, t])
+                    f_x = c_x * (v0 - v[xn, a, t])
+                    cx[a, t] = c_x
+                    fx[a, t] = f_x
+                    diag = diag + c_x
+                    res = res - f_x
+                diag = diag + REACTION
+                res = res + (s[x, a, t] - REACTION * v0)
+                w = DAMPING / diag
+                w_ref[x, a, t] = w
+                f_ref[x, a, t] = w * res
+                half = r * STRIP // F
+                res_sum = res if r * STRIP % F == 0 else res_sum + res
+                k_sum = k0 if r * STRIP % F == 0 else k_sum + k0
+                if (r + 1) * STRIP % F == 0:
+                    sums[half * STRIP : (half + 1) * STRIP, t] += res_sum
+                    sums[(2 + half) * STRIP : (3 + half) * STRIP, t] += k_sum
+                if r in (0, n - 1):
+                    ends[min(r, 1), 0, :, t] = diag
+                    ends[min(r, 1), 1, :, t] = res
+                if first:
+                    d_lo[a, t] = diag
+                    r_lo[a, t] = res
+                if last:
+                    d_hi[a, t] = diag
+                    r_hi[a, t] = res
+        for b, y in ((0, 0), (1, STRIP - 1)):
+            drow[b, pl.ds(x, 1), :] = ends[b, 0, y : y + 1, :]
+            rrow[b, pl.ds(x, 1), :] = ends[b, 1, y : y + 1, :]
         out_copy(0, x).start()
         out_copy(1, x).start()
+
+    def body(x, carry):
+        plane(x)
         return carry
 
-    lax.fori_loop(0, planes, plane, 0)
+    plane(0, first=True)
+    lax.fori_loop(1, planes - 1, body, 0)
+    plane(planes - 1, last=True)
     for x in range(planes):
         for i in range(2):
             out_copy(i, x).wait()
@@ -273,22 +296,34 @@
         ref[x] = e_pl1[...]
 
 
-def neighbour_sums(x, u, cx, cy, cz):
-    planes, rows, _ = u.shape
-    sl = strips(rows)
+def tile_sums(x, u, coupling, side_coupling):
+    planes, rows, cols = u.shape
+    sl, tl = strips(rows), tiles(cols)
+    m = len(tl)
+    lane0, lane1, sub0, sub1 = masks()
     xn, xp = jnp.minimum(x + 1, planes - 1), jnp.maximum(x - 1, 0)
-    u0 = [u[x, a, :] for a in sl]
-    u_up = [pltpu.roll(a, STRIP - 1, 0) for a in u0]
-    c_y = [cy[x, a, :] for a in sl]
-    q_dn = [pltpu.roll(c * a, 1, 0) for c, a in zip(c_y, u0)]
-    for r, a in enumerate(sl):
-        c_z = cz[x, a, :]
-        total = (
-            (cx[x + 1, a, :] * u[xn, a, :] + cx[x, a, :] * u[xp, a, :])
-            + (c_y[r] * shifted_up(u_up, r) + shifted_down(q_dn, r))
-            + (c_z * zp(u0[r]) + zm(c_z * u0[r]))
-        )
-        yield r, a, u0[r], total
+    ru = [left(u[x, a, tl[0]]) for a in sl]
+    pm = [right(side_coupling(r) * u[x, a, tl[-1]]) for r, a in enumerate(sl)]
+    for j in range(m):
+        t, tn = tl[j], tl[(j + 1) % m]
+        us = [u[x, a, t] for a in sl]
+        uu = [upward(a) for a in us]
+        dn = 0.0
+        for r, a in enumerate(sl):
+            c_next, c_prev, c_up, c_z = coupling(r, a, j, t, tn)
+            u0 = us[r]
+            nu = left(u[x, a, tn])
+            total = c_next * u[xn, a, t] + c_prev * u[xp, a, t]
+            total = total + c_z * jnp.where(lane1, nu, ru[r])
+            ru[r] = nu
+            mu = right(c_z * u0)
+            total = total + jnp.where(lane0, pm[r], mu)
+            pm[r] = mu
+            above = jnp.where(sub1, uu[r + 1], uu[r]) if r + 1 < len(sl) else uu[r]
+            nd = downward(c_up * u0)
+            total = total + (c_up * above + jnp.where(sub0, dn, nd))
+            dn = nd
+            yield r, a, t, u0, total
 
 
 def sweep_kernel(
@@ -296,7 +331,7 @@
     w, f, cx_hbm, cy, cz, g_ref, g_pl, g_row, k, cx, sems, out_sems,
 ):
     planes, rows, cols = w.shape
-    sl = strips(rows)
+    sl, tl = strips(rows), tiles(cols)
 
     def out_copy(x):
         return pltpu.make_async_copy(cx.at[x], cx_hbm.at[x], out_sems.at[x])
@@ -325,19 +360,34 @@
 
         xn = jnp.minimum(x + 1, planes - 1)
         h_next = jnp.where(x < planes - 1, 0.5, 0.0).astype(F32)
-        k0 = [k[x, a, :] for a in sl]
-        k_up = [pltpu.roll(a, STRIP - 1, 0) for a in k0]
-        for r, a in enumerate(sl):
-            cx[x + 1, a, :] = h_next * (k0[r] + k[xn, a, :])
-            cy[x, a, :] = up_coupling(k0, k_up, r)
-            cz[x, a, :] = 0.5 * (k0[r] + zp(k0[r]))
-        for r, a, u0, total in neighbour_sums(x, f, cx, cy, cz):
-            new = (2.0 - DAMPING) * u0 + w[x, a, :] * total
-            g_ref[x, a, :] = new
-            if r == 0:
-                g_row[0, pl.ds(x, 1), :] = new[0:1]
-            if (r + 1) * STRIP == rows:
-                g_row[1, pl.ds(x, 1), :] = new[STRIP - 1 :]
+        rk = [left(k[x, a, tl[0]]) for a in sl]
+        lane0, lane1, sub0, sub1 = masks()
+
+        def side_coupling(r):
+            k0 = k[x, sl[r], tl[-1]]
+            return 0.5 * (k0 + jnp.where(lane1, rk[r], left(k0)))
+
+        def coupling(r, a, j, t, tn):
+            k0 = k[x, a, t]
+            up = upward(k0)
+            if r + 1 < len(sl):
+                c_up = 0.5 * (k0 + jnp.where(sub1, upward(k[x, sl[r + 1], t]), up))
+            else:
+                c_up = jnp.where(sub1, 0.0, 0.5 * (k0 + up))
+            nk = left(k[x, a, tn])
+            c_z = 0.5 * (k0 + jnp.where(lane1, nk, rk[r]))
+            rk[r] = nk
+            c_next = h_next * (k0 + k[xn, a, t])
+            cx[x + 1, a, t] = c_next
+            cy[x, a, t] = c_up
+            cz[x, a, t] = c_z
+            return c_next, cx[x, a, t], c_up, c_z
+
+        for r, a, t, u0, total in tile_sums(x, f, coupling, side_coupling):
+            new = (2.0 - DAMPING) * u0 + w[x, a, t] * total
+            g_ref[x, a, t] = new
+        g_row[0, pl.ds(x, 1), :] = g_ref[x, 0:1, :]
+        g_row[1, pl.ds(x, 1), :] = g_ref[x, rows - 1 : rows, :]
         out_copy(x + 1).start()
         return carry
 
@@ -362,17 +412,16 @@
 
 def last_kernel(
     w, f, cx_hbm, cy, cz, g_any, interp, g_pl0, g_pl1, g_row0, g_row1,
-    out, b_pl, b_lo, b_hi, g, cx, body, in_sems, cx_sems, sems,
+    out, body, g, cx, in_sems, cx_sems, sems,
 ):
     planes, rows, cols = w.shape
-    n = rows // STRIP
 
     def in_copy(x):
         return pltpu.make_async_copy(g_any.at[x], g.at[x], in_sems.at[x])
 
     def copy(x):
         return pltpu.make_async_copy(
-            body.at[x], out.at[x, STRIP : rows - STRIP, :], sems.at[x]
+            body.at[x, STRIP : rows - STRIP, :], out.at[x, STRIP : rows - STRIP, :], sems.at[x]
         )
 
     def cx_copy(x):
@@ -398,27 +447,19 @@
         offset = ((x % F).astype(F32) + 0.5) / F - 0.5
         weight = jnp.abs(offset)
         side = jnp.where(offset > 0, 2, 0)
-        inside = (x > 0) & (x < planes - 1)
-        slot = jnp.clip(x - 1, 0, planes - 3)
-        end = jnp.where(x == 0, 0, 1)
-        for r, a, u0, total in neighbour_sums(x, g, cx, cy, cz):
-            coarse = (1.0 - weight) * interp[1, a, :] + weight * interp[side, a, :]
-            new = (f[x, a, :] + (1.0 - DAMPING) * u0) + (w[x, a, :] * total + coarse)
-
-            @pl.when(inside)
-            def _():
-                if r == 0:
-                    b_lo[slot] = new
-                elif r == n - 1:
-                    b_hi[slot] = new
-                else:
-                    body[x, (r - 1) * STRIP : r * STRIP, :] = new
-
-            @pl.when(jnp.logical_not(inside))
-            def _():
-                b_pl[end, a, :] = new
-
-        @pl.when(inside)
+
+        def coupling(r, a, j, t, tn):
+            return cx[x + 1, a, t], cx[x, a, t], cy[x, a, t], cz[x, a, t]
+
+        def side_coupling(r):
+            return cz[x, strips(rows)[r], tiles(cols)[-1]]
+
+        for r, a, t, u0, total in tile_sums(x, g, coupling, side_coupling):
+            coarse = (1.0 - weight) * interp[1, a, t] + weight * interp[side, a, t]
+            new = f[x, a, t] + (1.0 - DAMPING) * u0 + coarse
+            body[x, a, t] = new + w[x, a, t] * total
+
+        @pl.when((x > 0) & (x < planes - 1))
         def _():
             copy(x).start()
 
@@ -430,7 +471,7 @@
 
 
 def finish_kernel(
-    src, b_pl, b_lo, b_hi, wc_pl, wc_row, xl, xh, yl, yh, out, s_pl, s_lo, s_hi, sems
+    src, body, wc_pl, wc_row, xl, xh, yl, yh, out, s_pl, s_lo, s_hi, sems
 ):
     del src
     planes, rows, cols = out.shape
@@ -444,15 +485,15 @@
     sub = lax.broadcasted_iota(jnp.int32, (STRIP, cols), 0)
     for x in range(1, planes - 1):
         q = wc_row[0, x : x + 1, :] * yl[x : x + 1, :]
-        s_lo[x - 1] = b_lo[x - 1] + jnp.where(sub == 0, q, 0.0)
+        s_lo[x - 1] = body[x, :STRIP, :] + jnp.where(sub == 0, q, 0.0)
     copies[0].start()
     for x in range(1, planes - 1):
         q = wc_row[1, x : x + 1, :] * yh[x : x + 1, :]
-        s_hi[x - 1] = b_hi[x - 1] + jnp.where(sub == STRIP - 1, q, 0.0)
+        s_hi[x - 1] = body[x, rows - STRIP :, :] + jnp.where(sub == STRIP - 1, q, 0.0)
     copies[1].start()
     for side, other in ((0, xl), (1, xh)):
         x = side * (planes - 1)
-        s_pl[side] = b_pl[side] + wc_pl[side] * other[...]
+        s_pl[side] = body[x] + wc_pl[side] * other[...]
         for y, b, halo in ((0, 0, yl), (rows - 1, 1, yh)):
             s_pl[side, y : y + 1, :] = (
                 s_pl[side, y : y + 1, :] + wc_row[b, x : x + 1, :] * halo[x : x + 1, :]
@@ -587,6 +628,7 @@
         out_specs=(HBM,) * 2 + (VM,) * 7,
         scratch_shapes=[vm(full.shape, F32)] * 5
         + [vm(edge.shape, F32)] * 2
+        + [vm((2, 2, STRIP, cols), F32)]
         + [dma((3, planes)), dma((2, planes))],
         compiler_params=params(52),
         cost_estimate=cost(50 * n, 20 * n),
@@ -623,7 +665,7 @@
             dma((3, planes)),
             dma((planes + 1,)),
         ],
-        compiler_params=params(31),
+        compiler_params=params(30),
         cost_estimate=cost(40 * n, 12 * n),
         name="sweep",
     )(k, w, f, *w_edges, *f_edges)
@@ -659,37 +701,35 @@
     )(got)
 
     b_side = sds(planes - 2, STRIP, cols)
-    out, b_pl, b_lo, b_hi = pl.pallas_call(
+    out, body = pl.pallas_call(
         last_kernel,
-        out_shape=(full, edges, b_side, b_side),
+        out_shape=(full, full),
         in_specs=[VM] * 2 + [HBM] + [VM] * 2 + [ANY] + [VM] * 5,
-        out_specs=(HBM, VM, VM, VM),
+        out_specs=(HBM, VM),
         scratch_shapes=[
             vm(full.shape, F32),
             vm((planes + 1, rows, cols), F32),
-            vm((planes, rows - 2 * STRIP, cols), F32),
             dma((planes,)),
             dma((planes + 1,)),
             dma((planes,)),
         ],
-        compiler_params=params(30),
+        compiler_params=params(27),
         cost_estimate=cost(40 * n, 20 * n),
         name="last",
     )(w, f, cx, cy, cz, g, interp, *g_edges)
 
+    b_side = (planes - 2, STRIP, cols)
     return pl.pallas_call(
         finish_kernel,
         out_shape=full,
-        in_specs=[HBM] + [VM] * 9,
+        in_specs=[HBM] + [VM] * 7,
         out_specs=HBM,
-        scratch_shapes=[
-            vm(edges.shape, F32), vm(b_side.shape, F32), vm(b_side.shape, F32), dma((4,)),
-        ],
+        scratch_shapes=[vm(edges.shape, F32), vm(b_side, F32), vm(b_side, F32), dma((4,))],
         input_output_aliases={0: 0},
         compiler_params=params(6),
         cost_estimate=cost(n // 4, 3 * n),
         name="finish",
-    )(out, b_pl, b_lo, b_hi, wc_pl, wc_row, gxl, gxh, gyl, gyh)
+    )(out, body, wc_pl, wc_row, gxl, gxh, gyl, gyh)
 
 
 def solution(mesh):

time: 82.8 us -> 121 us (1.46)
  Pallas kernels: 43.5 us -> 83.1 us
  starting transfers between devices: 37.4 us -> 35.7 us
    pallas_call x1, Pallas kernels: 15.9 us -> 45.1 us  [per_device(): pl.pallas_call(inner_kernel, out_shape=(full, full) + (edge,) * 4 + (line...]
    pallas_call x1, Pallas kernels: 8.29 us -> 20.6 us  [per_device(): pl.pallas_call(sweep_kernel, out_shape=(full, full, sds(planes + 1, rows,...]
    pallas_call x2, Pallas kernels: 10.6 us -> 8.72 us  [the longest x1 7.14 us: per_device(): pl.pallas_call(last_kernel, out_shape=(full, full), in_specs=[VM] * 2 + [...]
    all_to_all x1, starting transfers between devices: 7.59 us -> 5.8 us  [per_device(): got = lax.all_to_all(payload, ('gx', 'gy'), 0, 0, tiled=True)]
  transfers between devices with their start and end apart: 13 -> 13, of which waited for: 1 -> 1; matrix products, arithmetic and copies ran while one was open for 0% -> 0% of each run, Pallas kernels for 45% -> 64%
where the time goes in v3:
time: 121 us; the launch traced here: 120 us
  Pallas kernels  83.1 us (69%)
  starting transfers between devices  35.7 us (30%)
  waiting for transfers between devices  1.43 us (1%)
    pallas_call x1, Pallas kernels, per_device(): pl.pallas_call(inner_kernel, out_shape=(full, full) + (edge,) * 4 + (line...  45.1 us
    ppermute x6, starting transfers between devices, swap(): lax.ppermute(low, axis, backward)  22.5 us
    pallas_call x1, Pallas kernels, per_device(): pl.pallas_call(sweep_kernel, out_shape=(full, full, sds(planes + 1, rows,...  20.6 us
    ppermute x6, starting transfers between devices, swap(): lax.ppermute(high, axis, forward)  7.34 us
    pallas_call x1, Pallas kernels, per_device(): pl.pallas_call(last_kernel, out_shape=(full, full), in_specs=[VM] * 2 + [...  7.14 us
    all_to_all x1, starting transfers between devices, per_device(): got = lax.all_to_all(payload, ('gx', 'gy'), 0, 0, tiled=True)  5.8 us
    pallas_call x1, Pallas kernels, per_device(): pl.pallas_call(functools.partial(coarse_kernel, nx=nx, ny=ny, rows=rows),...  4.07 us
    pallas_call x1, Pallas kernels, per_device(): pl.pallas_call(ends_kernel, out_shape=(lines, lines, edges, edges), in_sp...  2.69 us
  transfers between devices with their start and end apart: 13, of which 1 were waited for; matrix products, arithmetic and copies ran while one was open for 0% of the time, Pallas kernels for 64%

profile of v3, /device:TPU:0, one launch (start us, length us, event | category | flops | bytes accessed | tf_op | source)
XLA Modules:
  0.0 120.4 jit_solution(7632291771557850413)
XLA Ops:
  0.0 2.7 %ends.1 = (f32[2,16,2048]{2,1,0:T(8,128)}, f32[2,16,2048]{2,1,0:T(8,128)}, f32[2,32,2048]{2,1,0:T(8,128)}, f32[2,32,2048]{2,1,0:T(8,128)}) custom-call(f32[16,32,2048]{2,1,0:T(8,128)} %v.1, f32[16,32,2048]{2,1,0:T(8,128)} %k_hbm.2), custom_call_target="tpu_custom_call" | custom-call | bytes 524288 | tf_op jit(solution)/shard_map/ends/pallas_call | solution.py:611
  2.7 0.1 collective-permute-start
  2.8 3.8 %collective-permute-start.1 = (f32[2,32,2048]{2,1,0:T(8,128)}, f32[2,32,2048]{2,1,0:T(8,128)S(1)}, u32[]{:S(2)}, u32[]{:S(2)}) collective-permute-start(f32[2,32,2048]{2,1,0:T(8,128)} %get-tuple-element.53.pl_lo), channel_id=1, source_target_pairs={{0,120},{8,0},{16,8},{24,16},{32,24},{40,32},{48,40},{56,48},{64,5... | collective-permute-start | bytes 1572872 | tf_op jit(solution)/shard_map/ppermute | solution.py:600
  6.6 3.3 %collective-permute-start.2 = (f32[2,16,2048]{2,1,0:T(8,128)}, f32[2,16,2048]{2,1,0:T(8,128)S(1)}, u32[]{:S(2)}, u32[]{:S(2)}) collective-permute-start(f32[2,16,2048]{2,1,0:T(8,128)} %get-tuple-element.56.rw_hi), channel_id=1, source_target_pairs={{0,1},{1,2},{2,3},{3,4},{4,5},{5,6},{6,7},{7,0},{8,9},{9,10},{10,1... | collective-permute-start | bytes 786440 | tf_op jit(solution)/shard_map/ppermute | solution.py:600
  9.9 3.6 %collective-permute-start.3 = (f32[2,16,2048]{2,1,0:T(8,128)}, f32[2,16,2048]{2,1,0:T(8,128)S(1)}, u32[]{:S(2)}, u32[]{:S(2)}) collective-permute-start(f32[2,16,2048]{2,1,0:T(8,128)} %get-tuple-element.55.rw_lo), channel_id=1, source_target_pairs={{0,7},{1,0},{2,1},{3,2},{4,3},{5,4},{6,5},{7,6},{8,15},{9,8},{10,9... | collective-permute-start | bytes 786440 | tf_op jit(solution)/shard_map/ppermute | solution.py:600
  13.5 45.1 %inner.1 = (f32[16,32,2048]{2,1,0:T(8,128)}, f32[16,32,2048]{2,1,0:T(8,128)}, f32[32,2048]{1,0:T(8,128)S(1)}, f32[32,2048]{1,0:T(8,128)S(1)}, f32[32,2048]{1,0:T...) custom-call(f32[16,32,2048]{2,1,0:T(8,128)} %v.1, ...), custom_call_target="tpu_custom_call" | custom-call | flops 52428800 | bytes 20971520 | tf_op jit(solution)/shard_map/inner/pallas_call | solution.py:624
  58.6 0.0 collective-permute-done.2.yl
  58.6 0.0 collective-permute-done.3.yh
  58.6 0.0 collective-permute-done.xl
  58.6 0.0 collective-permute-done.1.xh
  58.6 1.8 %edge.1 = (f32[32,2048]{1,0:T(8,128)S(1)}, f32[32,2048]{1,0:T(8,128)S(1)}, f32[16,2048]{1,0:T(8,128)S(1)}, f32[16,2048]{1,0:T(8,128)S(1)}, f32[32,2048]{1,0:T(8,...) custom-call(f32[32,2048]{1,0:T(8,128)S(1)} %get-tuple-element.47.d_l, ...), custom_call_target="tpu_custom_call" | custom-call | flops 1310720 | bytes 1048576 | tf_op jit(solution)/shard_map/edge/pallas_call | solution.py:639
  60.4 5.8 %all-to-all-start = ((f32[128,4,128]{2,1,0:T(4,128)}), f32[128,4,128]{2,1,0:T(4,128)S(1)}, u32[]{:S(2)}, u32[]{:S(2)}) async-start(f32[128,4,128]{2,1,0:T(4,128)} %bitcast), calls=%async_computation | async-start | bytes 524288 | tf_op jit(solution)/shard_map/all_to_all | solution.py:653
  66.2 0.1 collective-permute-start.4
  66.3 3.8 %collective-permute-start.5 = (f32[32,2048]{1,0:T(8,128)S(1)}, f32[32,2048]{1,0:T(8,128)S(1)}, u32[]{:S(2)}, u32[]{:S(2)}) collective-permute-start(f32[32,2048]{1,0:T(8,128)S(1)} %get-tuple-element.68.f_pl0), channel_id=1, source_target_pairs={{0,120},{8,0},{16,8},{24,16},{32,24},{40,32},{48,40},{56,48},{64,5... | collective-permute-start | bytes 786440 | tf_op jit(solution)/shard_map/ppermute | solution.py:600
  70.1 2.5 %collective-permute-start.6 = (f32[16,2048]{1,0:T(8,128)S(1)}, f32[16,2048]{1,0:T(8,128)S(1)}, u32[]{:S(2)}, u32[]{:S(2)}) collective-permute-start(f32[16,2048]{1,0:T(8,128)S(1)} %get-tuple-element.71.f_row1), channel_id=1, source_target_pairs={{0,1},{1,2},{2,3},{3,4},{4,5},{5,6},{6,7},{7,0},{8,9},{9,10},{10,1... | collective-permute-start | bytes 393224 | tf_op jit(solution)/shard_map/ppermute | solution.py:600
  72.6 3.2 %collective-permute-start.7 = (f32[16,2048]{1,0:T(8,128)S(1)}, f32[16,2048]{1,0:T(8,128)S(1)}, u32[]{:S(2)}, u32[]{:S(2)}) collective-permute-start(f32[16,2048]{1,0:T(8,128)S(1)} %get-tuple-element.70.f_row0), channel_id=1, source_target_pairs={{0,7},{1,0},{2,1},{3,2},{4,3},{5,4},{6,5},{7,6},{8,15},{9,8},{10,9... | collective-permute-start | bytes 393224 | tf_op jit(solution)/shard_map/ppermute | solution.py:600
  75.8 1.4 %all-to-all-done = f32[128,4,128]{2,1,0:T(4,128)S(1)} async-done(((f32[128,4,128]{2,1,0:T(4,128)}), f32[128,4,128]{2,1,0:T(4,128)S(1)}, u32[]{:S(2)}, u32[]{:S(2)}) %all-to-all-start) | async-done | bytes 262176 | tf_op jit(solution)/shard_map/all_to_all | solution.py:653
  77.2 20.6 %sweep.1 = (f32[16,32,2048]{2,1,0:T(8,128)S(1)}, f32[16,32,2048]{2,1,0:T(8,128)S(1)}, f32[17,32,2048]{2,1,0:T(8,128)}, f32[16,32,2048]{2,1,0:T(8,128)S(1)}, f32[...) custom-call(f32[16,32,2048]{2,1,0:T(8,128)} %k_hbm.2, ...), custom_call_target="tpu_custom_call" | custom-call | flops 41943040 | bytes 12582912 | tf_op jit(solution)/shard_map/sweep/pallas_call | solution.py:657
  97.8 0.0 collective-permute-done.6.yl
  97.8 0.0 collective-permute-done.7.yh
  97.8 0.0 collective-permute-done.4.xl
  97.8 0.0 collective-permute-done.5.xh
  97.8 0.2 mid.1
  98.0 0.1 collective-permute-start.8
  98.1 3.8 %collective-permute-start.9 = (f32[32,2048]{1,0:T(8,128)S(1)}, f32[32,2048]{1,0:T(8,128)S(1)}, u32[]{:S(2)}, u32[]{:S(2)}) collective-permute-start(f32[32,2048]{1,0:T(8,128)S(1)} %get-tuple-element.83.g_pl0), channel_id=1, source_target_pairs={{0,120},{8,0},{16,8},{24,16},{32,24},{40,32},{48,40},{56,48},{64,5... | collective-permute-start | bytes 786440 | tf_op jit(solution)/shard_map/ppermute | solution.py:600
  102.0 1.4 %collective-permute-start.10 = (f32[16,2048]{1,0:T(8,128)S(1)}, f32[16,2048]{1,0:T(8,128)S(1)}, u32[]{:S(2)}, u32[]{:S(2)}) collective-permute-start(f32[16,2048]{1,0:T(8,128)S(1)} %get-tuple-element.86.g_row1), channel_id=1, source_target_pairs={{0,1},{1,2},{2,3},{3,4},{4,5},{5,6},{6,7},{7,0},{8,9},{9,10},{10,1... | collective-permute-start | bytes 393224 | tf_op jit(solution)/shard_map/ppermute | solution.py:600
  103.3 4.3 %collective-permute-start.11 = (f32[16,2048]{1,0:T(8,128)S(1)}, f32[16,2048]{1,0:T(8,128)S(1)}, u32[]{:S(2)}, u32[]{:S(2)}) collective-permute-start(f32[16,2048]{1,0:T(8,128)S(1)} %get-tuple-element.85.g_row0), channel_id=1, source_target_pairs={{0,7},{1,0},{2,1},{3,2},{4,3},{5,4},{6,5},{7,6},{8,15},{9,8},{10,9... | collective-permute-start | bytes 393224 | tf_op jit(solution)/shard_map/ppermute | solution.py:600
  107.6 4.1 %coarse.1.interp = f32[3,32,2048]{2,1,0:T(8,128)S(1)} custom-call(f32[512,128]{1,0:T(8,128)S(1)} %bitcast.2), custom_call_target="tpu_custom_call" | custom-call | flops 20971520 | bytes 1048576 | tf_op jit(solution)/shard_map/coarse/pallas_call | solution.py:688
  111.7 7.1 %last.1 = (f32[16,32,2048]{2,1,0:T(8,128)}, f32[16,32,2048]{2,1,0:T(8,128)S(1)}) custom-call(f32[16,32,2048]{2,1,0:T(8,128)S(1)} %get-tuple-element.72.w, f32[16,32,2048]{2,1,0:T(8,128)S(1)} %get-tuple-element.73.f, f32[17,32,2048]{2,1,0:T(8,128)} %get-tuple-element.74.cx_hbm, f32[16,32,2048]{2,1,0:T(8,128)S(1)} %get-tuple-element.75.cy, ...), custom_call_target="tpu_custom_call" | custom-call | flops 41943040 | bytes 20971520 | tf_op jit(solution)/shard_map/last/pallas_call | solution.py:704
  118.8 0.0 collective-permute-done.11.yh
  118.8 0.0 collective-permute-done.8.xl
  118.9 1.6 %finish.1 = f32[16,32,2048]{2,1,0:T(8,128)} custom-call(f32[16,32,2048]{2,1,0:T(8,128)} %get-tuple-element.87.src, f32[16,32,2048]{2,1,0:T(8,128)S(1)} %get-tuple-element.88.body, f32[2,32,2048]{2,1,0:T(8,128)S(1)} %get-tuple-element.81.wc_pl, f32[2,16,2048]{2,1,0:T(8,128)S(1)} %get-tuple-element.82.wc_row, ...), custom_call_target="tpu_custom_call", output_to_operand_aliasing={{}: (0, {})} | custom-call | flops 262144 | bytes 3145728 | tf_op jit(solution)/shard_map/finish/pallas_call | solution.py:722
  (10 shorter events, 0.0 us)
Async XLA Ops:
  2.7 55.9 %collective-permute-start = (f32[2,32,2048]{2,1,0:T(8,128)}, f32[2,32,2048]{2,1,0:T(8,128)S(1)}, u32[]{:S(2)}, u32[]{:S(2)}) collective-permute-start(f32[2,32,2048]{2,1,0:T(8,128)} %get-tuple-element.54.pl_hi), channel_id=1, source_target_pairs={{0,8},{8,16},{16,24},{24,32},{32,40},{40,48},{48,56},{56,64},{64,7... | collective-permute-start | bytes 1572872 | tf_op jit(solution)/shard_map/ppermute | solution.py:600
  2.8 55.8 %collective-permute-start.1 = (f32[2,32,2048]{2,1,0:T(8,128)}, f32[2,32,2048]{2,1,0:T(8,128)S(1)}, u32[]{:S(2)}, u32[]{:S(2)}) collective-permute-start(f32[2,32,2048]{2,1,0:T(8,128)} %get-tuple-element.53.pl_lo), channel_id=1, source_target_pairs={{0,120},{8,0},{16,8},{24,16},{32,24},{40,32},{48,40},{56,48},{64,5... | collective-permute-start | bytes 1572872 | tf_op jit(solution)/shard_map/ppermute | solution.py:600
  6.6 51.9 %collective-permute-start.2 = (f32[2,16,2048]{2,1,0:T(8,128)}, f32[2,16,2048]{2,1,0:T(8,128)S(1)}, u32[]{:S(2)}, u32[]{:S(2)}) collective-permute-start(f32[2,16,2048]{2,1,0:T(8,128)} %get-tuple-element.56.rw_hi), channel_id=1, source_target_pairs={{0,1},{1,2},{2,3},{3,4},{4,5},{5,6},{6,7},{7,0},{8,9},{9,10},{10,1... | collective-permute-start | bytes 786440 | tf_op jit(solution)/shard_map/ppermute | solution.py:600
  9.9 48.7 %copy-start = (f32[2,32,2048]{2,1,0:T(8,128)S(1)}, f32[2,32,2048]{2,1,0:T(8,128)}, u32[]{:S(2)}) copy-start(f32[2,32,2048]{2,1,0:T(8,128)} %get-tuple-element.53.pl_lo) | copy-start | bytes 1572868
  9.9 48.7 %copy-start.1 = (f32[2,32,2048]{2,1,0:T(8,128)S(1)}, f32[2,32,2048]{2,1,0:T(8,128)}, u32[]{:S(2)}) copy-start(f32[2,32,2048]{2,1,0:T(8,128)} %get-tuple-element.54.pl_hi) | copy-start | bytes 1572868
  9.9 48.7 %copy-start.2 = (f32[2,16,2048]{2,1,0:T(8,128)S(1)}, f32[2,16,2048]{2,1,0:T(8,128)}, u32[]{:S(2)}) copy-start(f32[2,16,2048]{2,1,0:T(8,128)} %get-tuple-element.55.rw_lo) | copy-start | bytes 786436
  9.9 48.7 %copy-start.3 = (f32[2,16,2048]{2,1,0:T(8,128)S(1)}, f32[2,16,2048]{2,1,0:T(8,128)}, u32[]{:S(2)}) copy-start(f32[2,16,2048]{2,1,0:T(8,128)} %get-tuple-element.56.rw_hi) | copy-start | bytes 786436
  9.9 48.7 %collective-permute-start.3 = (f32[2,16,2048]{2,1,0:T(8,128)}, f32[2,16,2048]{2,1,0:T(8,128)S(1)}, u32[]{:S(2)}, u32[]{:S(2)}) collective-permute-start(f32[2,16,2048]{2,1,0:T(8,128)} %get-tuple-element.55.rw_lo), channel_id=1, source_target_pairs={{0,7},{1,0},{2,1},{3,2},{4,3},{5,4},{6,5},{7,6},{8,15},{9,8},{10,9... | collective-permute-start | bytes 786440 | tf_op jit(solution)/shard_map/ppermute | solution.py:600
  60.4 16.8 %all-to-all-start = ((f32[128,4,128]{2,1,0:T(4,128)}), f32[128,4,128]{2,1,0:T(4,128)S(1)}, u32[]{:S(2)}, u32[]{:S(2)}) async-start(f32[128,4,128]{2,1,0:T(4,128)} %bitcast), calls=%async_computation | async-start | bytes 524288 | tf_op jit(solution)/shard_map/all_to_all | solution.py:653
  66.2 31.6 %collective-permute-start.4 = (f32[32,2048]{1,0:T(8,128)S(1)}, f32[32,2048]{1,0:T(8,128)S(1)}, u32[]{:S(2)}, u32[]{:S(2)}) collective-permute-start(f32[32,2048]{1,0:T(8,128)S(1)} %get-tuple-element.69.f_pl1), channel_id=1, source_target_pairs={{0,8},{8,16},{16,24},{24,32},{32,40},{40,48},{48,56},{56,64},{64,7... | collective-permute-start | bytes 786440 | tf_op jit(solution)/shard_map/ppermute | solution.py:600
  66.3 31.5 %collective-permute-start.5 = (f32[32,2048]{1,0:T(8,128)S(1)}, f32[32,2048]{1,0:T(8,128)S(1)}, u32[]{:S(2)}, u32[]{:S(2)}) collective-permute-start(f32[32,2048]{1,0:T(8,128)S(1)} %get-tuple-element.68.f_pl0), channel_id=1, source_target_pairs={{0,120},{8,0},{16,8},{24,16},{32,24},{40,32},{48,40},{56,48},{64,5... | collective-permute-start | bytes 786440 | tf_op jit(solution)/shard_map/ppermute | solution.py:600
  70.1 27.7 %collective-permute-start.6 = (f32[16,2048]{1,0:T(8,128)S(1)}, f32[16,2048]{1,0:T(8,128)S(1)}, u32[]{:S(2)}, u32[]{:S(2)}) collective-permute-start(f32[16,2048]{1,0:T(8,128)S(1)} %get-tuple-element.71.f_row1), channel_id=1, source_target_pairs={{0,1},{1,2},{2,3},{3,4},{4,5},{5,6},{6,7},{7,0},{8,9},{9,10},{10,1... | collective-permute-start | bytes 393224 | tf_op jit(solution)/shard_map/ppermute | solution.py:600
  72.6 25.2 %collective-permute-start.7 = (f32[16,2048]{1,0:T(8,128)S(1)}, f32[16,2048]{1,0:T(8,128)S(1)}, u32[]{:S(2)}, u32[]{:S(2)}) collective-permute-start(f32[16,2048]{1,0:T(8,128)S(1)} %get-tuple-element.70.f_row0), channel_id=1, source_target_pairs={{0,7},{1,0},{2,1},{3,2},{4,3},{5,4},{6,5},{7,6},{8,15},{9,8},{10,9... | collective-permute-start | bytes 393224 | tf_op jit(solution)/shard_map/ppermute | solution.py:600
  98.0 20.8 %collective-permute-start.8 = (f32[32,2048]{1,0:T(8,128)S(1)}, f32[32,2048]{1,0:T(8,128)S(1)}, u32[]{:S(2)}, u32[]{:S(2)}) collective-permute-start(f32[32,2048]{1,0:T(8,128)S(1)} %get-tuple-element.84.g_pl1), channel_id=1, source_target_pairs={{0,8},{8,16},{16,24},{24,32},{32,40},{40,48},{48,56},{56,64},{64,7... | collective-permute-start | bytes 786440 | tf_op jit(solution)/shard_map/ppermute | solution.py:600
  98.1 20.7 %collective-permute-start.9 = (f32[32,2048]{1,0:T(8,128)S(1)}, f32[32,2048]{1,0:T(8,128)S(1)}, u32[]{:S(2)}, u32[]{:S(2)}) collective-permute-start(f32[32,2048]{1,0:T(8,128)S(1)} %get-tuple-element.83.g_pl0), channel_id=1, source_target_pairs={{0,120},{8,0},{16,8},{24,16},{32,24},{40,32},{48,40},{56,48},{64,5... | collective-permute-start | bytes 786440 | tf_op jit(solution)/shard_map/ppermute | solution.py:600
  102.0 16.9 %collective-permute-start.10 = (f32[16,2048]{1,0:T(8,128)S(1)}, f32[16,2048]{1,0:T(8,128)S(1)}, u32[]{:S(2)}, u32[]{:S(2)}) collective-permute-start(f32[16,2048]{1,0:T(8,128)S(1)} %get-tuple-element.86.g_row1), channel_id=1, source_target_pairs={{0,1},{1,2},{2,3},{3,4},{4,5},{5,6},{6,7},{7,0},{8,9},{9,10},{10,1... | collective-permute-start | bytes 393224 | tf_op jit(solution)/shard_map/ppermute | solution.py:600
  103.3 15.5 %collective-permute-start.11 = (f32[16,2048]{1,0:T(8,128)S(1)}, f32[16,2048]{1,0:T(8,128)S(1)}, u32[]{:S(2)}, u32[]{:S(2)}) collective-permute-start(f32[16,2048]{1,0:T(8,128)S(1)} %get-tuple-element.85.g_row0), channel_id=1, source_target_pairs={{0,7},{1,0},{2,1},{3,2},{4,3},{5,4},{6,5},{7,6},{8,15},{9,8},{10,9... | collective-permute-start | bytes 393224 | tf_op jit(solution)/shard_map/ppermute | solution.py:600

commit v4 on v3

v4 whole, which is shorter than its diff:
```python
import functools
import jax
import jax.numpy as jnp
from jax import lax
from jax.experimental import pallas as pl
from jax.experimental.pallas import tpu as pltpu
from jax.sharding import PartitionSpec as P

F = 16
CSWEEPS = 32
REACTION = 0.2
DAMPING = 0.8
COARSE_FACTOR = 0.25
F32 = jnp.float32
BF16 = jnp.bfloat16
STRIP = 8
LANES = 512

VM = pl.BlockSpec(memory_space=pltpu.VMEM)
ANY = pl.BlockSpec(memory_space=pl.ANY)
HBM = pl.BlockSpec(memory_space=pltpu.HBM)


def params(mib):
    return pltpu.CompilerParams(vmem_limit_bytes=mib * 1024 * 1024)


def cost(flops, nbytes):
    return pl.CostEstimate(flops=int(flops), bytes_accessed=int(nbytes), transcendentals=0)


def sds(*shape):
    return jax.ShapeDtypeStruct(shape, F32)


def left(a):
    return pltpu.roll(a, a.shape[1] - 1, 1)


def right(a):
    return pltpu.roll(a, 1, 1)


def upward(a):
    return pltpu.roll(a, STRIP - 1, 0)


def downward(a):
    return pltpu.roll(a, 1, 0)


def strips(rows):
    return [slice(r * STRIP, (r + 1) * STRIP) for r in range(rows // STRIP)]


def edge_spots(axis, count):
    odd = lax.rem(lax.axis_index(axis), 2)
    return (1 - odd) * (count - 1), odd * (count - 1)


def low_high(axis):
    odd = lax.rem(lax.axis_index(axis), 2)
    return 1 - odd, odd


def ends_kernel(v, k, rw_a, rw_b, pl_a, pl_b, sems):
    planes, rows, _ = v.shape
    xs, ys = edge_spots("gx", planes), edge_spots("gy", rows)
    copies = []
    for i, a in enumerate((v, k)):
        for j, (src, dst) in enumerate(
            (
                (a.at[:, ys[0], :], rw_a.at[i]),
                (a.at[:, ys[1], :], rw_b.at[i]),
                (a.at[xs[0]], pl_a.at[i]),
                (a.at[xs[1]], pl_b.at[i]),
            )
        ):
            copies.append(pltpu.make_async_copy(src, dst, sems.at[i, j]))
    for c in copies:
        c.start()
    for c in copies:
        c.wait()


def inner_kernel(
    v_hbm, s_hbm, k_hbm,
    w_hbm, f_hbm, w_pl, f_pl, w_row, f_row, sums,
    v, s, k, w_ref, f_ref, cx, fx, sems, out_sems,
):
    planes, rows, cols = v.shape
    sl = strips(rows)
    n = len(sl)
    low, high = low_high("gy")

    def copy(i, x):
        src, dst = ((k_hbm, k), (v_hbm, v), (s_hbm, s))[i]
        return pltpu.make_async_copy(src.at[x], dst.at[x], sems.at[i, x])

    def out_copy(i, x):
        src, dst = ((w_ref, w_hbm), (f_ref, f_hbm))[i]
        return pltpu.make_async_copy(src.at[x], dst.at[x], out_sems.at[i, x])

    for x in range(planes):
        for i in range(3):
            copy(i, x).start()
    sums[...] = jnp.zeros_like(sums)
    fx[...] = jnp.zeros_like(fx)
    cx[...] = jnp.zeros_like(cx)
    copy(0, 0).wait()
    copy(1, 0).wait()
    sub = lax.broadcasted_iota(jnp.int32, (STRIP, cols), 0)
    sub0, sub1 = sub == 0, sub == STRIP - 1

    def plane(x, carry):
        @pl.when(x < planes - 1)
        def _():
            copy(0, x + 1).wait()
            copy(1, x + 1).wait()

        copy(2, x).wait()
        xn = jnp.minimum(x + 1, planes - 1)
        h_next = jnp.where(x < planes - 1, 0.5, 0.0).astype(F32)
        dc = df = 0.0
        k0, v0 = k[x, sl[0], :], v[x, sl[0], :]
        ku, vu = upward(k0), upward(v0)
        res_sum = k_sum = None
        for r, a in enumerate(sl):
            c_z = 0.5 * (k0 + left(k0))
            f_z = c_z * (v0 - left(v0))
            diag = c_z + right(c_z)
            res = right(f_z) - f_z
            if r + 1 < n:
                k1, v1 = k[x, sl[r + 1], :], v[x, sl[r + 1], :]
                ku1, vu1 = upward(k1), upward(v1)
                c_y = 0.5 * (k0 + jnp.where(sub1, ku1, ku))
                f_y = c_y * (v0 - jnp.where(sub1, vu1, vu))
            else:
                c_y = jnp.where(sub1, 0.0, 0.5 * (k0 + ku))
                f_y = c_y * (v0 - vu)
            nc, nf = downward(c_y), downward(f_y)
            diag = diag + (c_y + jnp.where(sub0, dc, nc))
            res = res + (jnp.where(sub0, df, nf) - f_y)
            dc, df = nc, nf
            c_x = h_next * (k0 + k[xn, a, :])
            f_x = c_x * (v0 - v[xn, a, :])
            diag = diag + ((cx[a, :] + c_x) + REACTION)
            res = res + ((fx[a, :] - f_x) + (s[x, a, :] - REACTION * v0))
            cx[a, :] = c_x
            fx[a, :] = f_x
            w = DAMPING / diag
            w_ref[x, a, :] = w
            f_ref[x, a, :] = w * res
            half = r * STRIP // F
            res_sum = res if r * STRIP % F == 0 else res_sum + res
            k_sum = k0 if r * STRIP % F == 0 else k_sum + k0
            if (r + 1) * STRIP % F == 0:
                sums[half * STRIP : (half + 1) * STRIP, :] += res_sum
                sums[(2 + half) * STRIP : (3 + half) * STRIP, :] += k_sum
            if r + 1 < n:
                k0, v0, ku, vu = k1, v1, ku1, vu1
        out_copy(0, x).start()
        out_copy(1, x).start()
        for place, y in ((low, 0), (high, rows - 1)):
            w_row[place, pl.ds(x, 1), :] = w_ref[x, y : y + 1, :]
            f_row[place, pl.ds(x, 1), :] = f_ref[x, y : y + 1, :]
        return carry

    lax.fori_loop(0, planes, plane, 0)
    for side, x in enumerate(edge_spots("gx", planes)):
        w_pl[side] = w_ref[x]
        f_pl[side] = f_ref[x]
    for x in range(planes):
        for i in range(2):
            out_copy(i, x).wait()


def cross(q_pl, q_row, pls, rws, sign):
    rows, planes = q_pl.shape[1], q_row.shape[1]
    for a in range(2):
        pls[a][...] = pls[a][...] + sign * q_pl[a]
        rws[a][...] = rws[a][...] + sign * q_row[a]
    for a, x in enumerate(edge_spots("gx", planes)):
        for b, y in enumerate(edge_spots("gy", rows)):
            px, py = pl.ds(x, 1), pl.ds(y, 1)
            pls[a][py, :] = pls[a][py, :] + sign * q_row[b, px, :]
            rws[b][px, :] = rws[b][px, :] + sign * q_pl[a, py, :]


def split3(a):
    one = a.astype(BF16)
    rest = a - one.astype(F32)
    two = rest.astype(BF16)
    three = (rest - two.astype(F32)).astype(BF16)
    return jnp.concatenate([one, two, three], 0)


def joined3(a):
    n = a.shape[0] // 3
    return a[:n] + a[n : 2 * n] + a[2 * n :]


def edge_kernel(
    wi_pl, fi_pl, wi_row, fi_row, pl_a, pl_b, rw_a, rw_b, xa, xb, ya, yb, sums,
    f_pl0, f_pl1, f_row0, f_row1, w_pl0, w_pl1, w_row0, w_row1, wc_pl, wc_row, payload,
    q_pl, q_row,
):
    rows, cols = f_pl0.shape
    f_pl, f_row, w_pl, w_row = (f_pl0, f_pl1), (f_row0, f_row1), (w_pl0, w_pl1), (w_row0, w_row1)
    for side, mine, other in ((0, pl_a, xa), (1, pl_b, xb)):
        c = 0.5 * (mine[1] + other[1])
        wc_pl[side] = c
        q_pl[side] = c * (mine[0] - other[0])
    for side, mine, other in ((0, rw_a, ya), (1, rw_b, yb)):
        c = 0.5 * (mine[1] + other[1])
        wc_row[side] = c
        q_row[side] = c * (mine[0] - other[0])
    for w, f, wi, fi in ((w_pl, f_pl, wi_pl, fi_pl), (w_row, f_row, wi_row, fi_row)):
        for side in range(2):
            diag = DAMPING / wi[side]
            w[side][...] = diag
            f[side][...] = fi[side] * (diag * (1.0 / DAMPING))
    cross(wc_pl, wc_row, w_pl, w_row, 1.0)
    cross(q_pl, q_row, f_pl, f_row, -1.0)
    for w, f, wc in ((w_pl, f_pl, wc_pl), (w_row, f_row, wc_row)):
        for side in range(2):
            inv = DAMPING / w[side][...]
            w[side][...] = inv
            f[side][...] = f[side][...] * inv
            wc[side] = wc[side] * inv
    low, high = low_high("gy")
    parts = []
    for half in range(rows // F):
        total = sums[half * STRIP : (half + 1) * STRIP, :]
        for side in range(2):
            for r in range(half * F // STRIP, (half + 1) * F // STRIP):
                total = total - q_pl[side, r * STRIP : (r + 1) * STRIP, :]
        if half == 0:
            for r in range(q_row.shape[1] // STRIP):
                total = total - q_row[low, r * STRIP : (r + 1) * STRIP, :]
        if half == rows // F - 1:
            for r in range(q_row.shape[1] // STRIP):
                total = total - q_row[high, r * STRIP : (r + 1) * STRIP, :]
        parts.append(total)
    parts.append(sums[2 * STRIP :, :])
    col = lax.broadcasted_iota(jnp.int32, (cols, cols // F), 0)
    cell = lax.broadcasted_iota(jnp.int32, (cols, cols // F), 1)
    gather = jnp.where(col // F == cell, 1.0, 0.0).astype(BF16)
    reduced = joined3(
        jnp.dot(split3(jnp.concatenate(parts, 0)), gather, preferred_element_type=F32)
    )
    means = [
        jnp.sum(reduced[i * STRIP : (i + 1) * STRIP], axis=0, keepdims=True) * (1.0 / F**3)
        for i in range(4)
    ]
    tile = jnp.concatenate(means + means, 0)
    for i in range(payload.shape[0] // STRIP):
        payload[i * STRIP : (i + 1) * STRIP, :] = tile


def put_edges(ref, x, e_pl0, e_pl1, e_row0, e_row1):
    planes, rows, _ = ref.shape
    for y, line in zip(edge_spots("gy", rows), (e_row0, e_row1)):
        ref[x, pl.ds(y, 1), :] = line[pl.ds(x, 1), :]
    for spot, plane in zip(edge_spots("gx", planes), (e_pl0, e_pl1)):

        @pl.when(x == spot)
        def _():
            ref[x] = plane[...]


def shifted_up(rolled, r):
    nxt = rolled[min(r + 1, len(rolled) - 1)]
    sub = lax.broadcasted_iota(jnp.int32, nxt.shape, 0)
    return jnp.where(sub == STRIP - 1, nxt, rolled[r])


def shifted_down(rolled, r):
    prv = rolled[r - 1]
    sub = lax.broadcasted_iota(jnp.int32, prv.shape, 0)
    return jnp.where(sub == 0, prv, rolled[r])


def up_coupling(k0, k_up, r):
    c = 0.5 * (k0[r] + shifted_up(k_up, r))
    if r == len(k0) - 1:
        sub = lax.broadcasted_iota(jnp.int32, c.shape, 0)
        c = jnp.where(sub == STRIP - 1, 0.0, c)
    return c


def neighbour_sums(x, u, cx, cy, cz):
    planes, rows, _ = u.shape
    sl = strips(rows)
    xn, xp = jnp.minimum(x + 1, planes - 1), jnp.maximum(x - 1, 0)
    u0 = [u[x, a, :] for a in sl]
    u_up = [pltpu.roll(a, STRIP - 1, 0) for a in u0]
    c_y = [cy[x, a, :] for a in sl]
    q_dn = [pltpu.roll(c * a, 1, 0) for c, a in zip(c_y, u0)]
    for r, a in enumerate(sl):
        c_z = cz[x, a, :]
        total = (
            (cx[x + 1, a, :] * u[xn, a, :] + cx[x, a, :] * u[xp, a, :])
            + (c_y[r] * shifted_up(u_up, r) + shifted_down(q_dn, r))
            + (c_z * left(u0[r]) + right(c_z * u0[r]))
        )
        yield r, a, u0[r], total


def sweep_kernel(
    k_hbm, w_hbm, f_hbm, w_pl0, w_pl1, w_row0, w_row1, f_pl0, f_pl1, f_row0, f_row1,
    w, f, cx_hbm, cy, cz, g_ref, g_pl, g_row, k, cx, sems, out_sems,
):
    planes, rows, cols = w.shape
    sl = strips(rows)
    low, high = low_high("gy")

    def out_copy(x):
        return pltpu.make_async_copy(cx.at[x], cx_hbm.at[x], out_sems.at[x])

    def copy(i, x):
        src, dst = ((k_hbm, k), (f_hbm, f), (w_hbm, w))[i]
        return pltpu.make_async_copy(src.at[x], dst.at[x], sems.at[i, x])

    def arrive(x):
        for i in range(3):
            copy(i, x).wait()
        put_edges(f, x, f_pl0, f_pl1, f_row0, f_row1)
        put_edges(w, x, w_pl0, w_pl1, w_row0, w_row1)

    for x in range(planes):
        for i in range(3):
            copy(i, x).start()
    cx[0] = jnp.zeros_like(k[0])
    out_copy(0).start()
    arrive(0)

    def plane(x, carry):
        @pl.when(x < planes - 1)
        def _():
            arrive(x + 1)

        xn = jnp.minimum(x + 1, planes - 1)
        h_next = jnp.where(x < planes - 1, 0.5, 0.0).astype(F32)
        k0 = [k[x, a, :] for a in sl]
        k_up = [pltpu.roll(a, STRIP - 1, 0) for a in k0]
        for r, a in enumerate(sl):
            cx[x + 1, a, :] = h_next * (k0[r] + k[xn, a, :])
            cy[x, a, :] = up_coupling(k0, k_up, r)
            cz[x, a, :] = 0.5 * (k0[r] + left(k0[r]))
        for r, a, u0, total in neighbour_sums(x, f, cx, cy, cz):
            new = (2.0 - DAMPING) * u0 + w[x, a, :] * total
            g_ref[x, a, :] = new
            if r == 0:
                g_row[low, pl.ds(x, 1), :] = new[0:1]
            if (r + 1) * STRIP == rows:
                g_row[high, pl.ds(x, 1), :] = new[STRIP - 1 :]
        out_copy(x + 1).start()
        return carry

    lax.fori_loop(0, planes, plane, 0)
    for side, x in enumerate(edge_spots("gx", planes)):
        g_pl[side] = g_ref[x]
    for x in range(planes + 1):
        out_copy(x).wait()


def mid_kernel(
    g_pl, g_row, wc_pl, wc_row, xa, xb, ya, yb, o_pl0, o_pl1, o_row0, o_row1, q_pl, q_row
):
    for side, x, y in ((0, xa, ya), (1, xb, yb)):
        q_pl[side] = wc_pl[side] * x[...]
        q_row[side] = wc_row[side] * y[...]
    for side, p, r in ((0, o_pl0, o_row0), (1, o_pl1, o_row1)):
        p[...] = g_pl[side]
        r[...] = g_row[side]
    cross(q_pl, q_row, (o_pl0, o_pl1), (o_row0, o_row1), 1.0)


def tile_sums(x, u, cx, cy, cz):
    planes, rows, cols = u.shape
    sl = strips(rows)
    tl = [slice(j, j + LANES) for j in range(0, cols, LANES)]
    lane = lax.broadcasted_iota(jnp.int32, (STRIP, LANES), 1)
    sub = lax.broadcasted_iota(jnp.int32, (STRIP, LANES), 0)
    xn, xp = jnp.minimum(x + 1, planes - 1), jnp.maximum(x - 1, 0)
    ru = [left(u[x, a, tl[0]]) for a in sl]
    pm = [right(cz[x, a, tl[-1]] * u[x, a, tl[-1]]) for a in sl]
    for j, t in enumerate(tl):
        us = [u[x, a, t] for a in sl]
        uu = [upward(a) for a in us]
        dn = 0.0
        for r, a in enumerate(sl):
            u0, c_y, c_z = us[r], cy[x, a, t], cz[x, a, t]
            nu = left(u[x, a, tl[(j + 1) % len(tl)]])
            total = cx[x + 1, a, t] * u[xn, a, t] + cx[x, a, t] * u[xp, a, t]
            total = total + c_z * jnp.where(lane == LANES - 1, nu, ru[r])
            mu = right(c_z * u0)
            total = total + jnp.where(lane == 0, pm[r], mu)
            ru[r], pm[r] = nu, mu
            above = jnp.where(sub == STRIP - 1, uu[r + 1], uu[r]) if r + 1 < len(sl) else uu[r]
            nd = downward(c_y * u0)
            total = total + (c_y * above + jnp.where(sub == 0, dn, nd))
            dn = nd
            yield a, t, u0, total


def last_kernel(
    w, f, cx_hbm, cy, cz, g_any, interp, g_pl0, g_pl1, g_row0, g_row1,
    out, body, g, cx, in_sems, cx_sems, sems,
):
    planes, rows, cols = w.shape

    def in_copy(x):
        return pltpu.make_async_copy(g_any.at[x], g.at[x], in_sems.at[x])

    def copy(x):
        return pltpu.make_async_copy(
            body.at[x, STRIP : rows - STRIP, :], out.at[x, STRIP : rows - STRIP, :], sems.at[x]
        )

    def cx_copy(x):
        return pltpu.make_async_copy(cx_hbm.at[x], cx.at[x], cx_sems.at[x])

    def arrive(x):
        cx_copy(x + 1).wait()
        in_copy(x).wait()
        put_edges(g, x, g_pl0, g_pl1, g_row0, g_row1)

    cx_copy(0).start()
    for x in range(planes):
        in_copy(x).start()
        cx_copy(x + 1).start()
    cx_copy(0).wait()
    arrive(0)

    def plane(x, carry):
        @pl.when(x < planes - 1)
        def _():
            arrive(x + 1)

        offset = ((x % F).astype(F32) + 0.5) / F - 0.5
        weight = jnp.abs(offset)
        side = jnp.where(offset > 0, 2, 0)
        for a, t, u0, total in tile_sums(x, g, cx, cy, cz):
            coarse = (1.0 - weight) * interp[1, a, t] + weight * interp[side, a, t]
            new = f[x, a, t] + (1.0 - DAMPING) * u0 + coarse
            body[x, a, t] = new + w[x, a, t] * total

        @pl.when((x > 0) & (x < planes - 1))
        def _():
            copy(x).start()

        return carry

    lax.fori_loop(0, planes, plane, 0)
    for x in range(1, planes - 1):
        copy(x).wait()


def finish_kernel(
    src, body, wc_pl, wc_row, xa, xb, ya, yb, out, s_pl, s_lo, s_hi, q_row, sems
):
    del src
    planes, rows, cols = out.shape
    xs, ys = edge_spots("gx", planes), edge_spots("gy", rows)
    low, high = low_high("gy")
    spots = (
        (s_lo, out.at[1 : planes - 1, 0:STRIP, :]),
        (s_hi, out.at[1 : planes - 1, rows - STRIP : rows, :]),
        (s_pl.at[0], out.at[xs[0]]),
        (s_pl.at[1], out.at[xs[1]]),
    )
    copies = [pltpu.make_async_copy(a, b, sems.at[i]) for i, (a, b) in enumerate(spots)]
    sub = lax.broadcasted_iota(jnp.int32, (STRIP, cols), 0)
    q_row[0] = wc_row[0] * ya[...]
    q_row[1] = wc_row[1] * yb[...]
    for x in range(1, planes - 1):
        q = q_row[low, x : x + 1, :]
        s_lo[x - 1] = body[x, :STRIP, :] + jnp.where(sub == 0, q, 0.0)
    copies[0].start()
    for x in range(1, planes - 1):
        q = q_row[high, x : x + 1, :]
        s_hi[x - 1] = body[x, rows - STRIP :, :] + jnp.where(sub == STRIP - 1, q, 0.0)
    copies[1].start()
    for side, other in ((0, xa), (1, xb)):
        x = xs[side]
        s_pl[side] = body[x] + wc_pl[side] * other[...]
        for b, y in enumerate(ys):
            py = pl.ds(y, 1)
            s_pl[side, py, :] = s_pl[side, py, :] + q_row[b, pl.ds(x, 1), :]
        copies[2 + side].start()
    for c in copies:
        c.wait()


def coarse_kernel(got, interp, coef, b_ref, u_ref, *, nx, ny, rows):
    nz = got.shape[1]
    per = 2 * 2

    def field(start):
        return [
            jnp.stack([got[pl.ds(p * ny * per + start + t, ny, stride=per), :] for p in range(nx)], 0)
            for t in range(2)
        ]

    resid, cond = field(0), field(2)

    def beside(a, t):
        mine = a[t]
        nxt = jnp.concatenate([mine[1:], mine[:1]], 0)
        prv = jnp.concatenate([mine[-1:], mine[:-1]], 0)
        up = a[1] if t == 0 else pltpu.roll(a[0], ny - 1, 1)
        down = a[0] if t == 1 else pltpu.roll(a[1], 1, 1)
        return nxt, prv, up, down, pltpu.roll(mine, 1, 2), pltpu.roll(mine, nz - 1, 2)

    for t in range(2):
        cs = [(0.5 * COARSE_FACTOR) * (cond[t] + other) for other in beside(cond, t)]
        diag = REACTION
        for c in cs:
            diag = diag + c
        inv = DAMPING / diag
        for i, c in enumerate(cs):
            coef[i, t] = inv * c
        b_ref[t] = inv * resid[t]
        u_ref[0, t] = b_ref[t]

    def sweep(src, dst):
        for p in range(nx):
            pn, pp = (p + 1) % nx, (p - 1) % nx
            u = [u_ref[src, t, p] for t in range(2)]
            for t in range(2):
                up = u[1] if t == 0 else pltpu.roll(u[0], ny - 1, 0)
                down = u[0] if t == 1 else pltpu.roll(u[1], 1, 0)
                a = b_ref[t, p] + (1.0 - DAMPING) * u[t]
                a = a + coef[0, t, p] * u_ref[src, t, pn]
                a = a + coef[1, t, p] * u_ref[src, t, pp]
                c = coef[2, t, p] * up + coef[3, t, p] * down
                c = c + coef[4, t, p] * pltpu.roll(u[t], 1, 1)
                c = c + coef[5, t, p] * pltpu.roll(u[t], nz - 1, 1)
                u_ref[dst, t, p] = a + c

    def pair(i, carry):
        sweep(0, 1)
        sweep(1, 0)
        return carry

    steps = CSWEEPS - 1
    lax.fori_loop(0, steps // 2, pair, 0)
    last = 0
    if steps % 2:
        sweep(0, 1)
        last = 1

    gx, gy = lax.axis_index("gx"), lax.axis_index("gy")
    lines = []
    for d in (-1, 0, 1):
        p = lax.rem(gx + d + nx, nx)
        prev_s, next_s = lax.rem(gy + ny - 1, ny), lax.rem(gy + 1, ny)
        for t, s in ((1, prev_s), (0, gy), (1, gy), (0, next_s)):
            lines.append(u_ref[last, t, p, pl.ds(s, 1), :])
    lines = jnp.concatenate(lines + lines[:4], 0)
    cols = nz * F
    cell = lax.broadcasted_iota(jnp.int32, (nz, cols), 0)
    col = lax.broadcasted_iota(jnp.int32, (nz, cols), 1)
    base = col // F
    offset = ((col % F).astype(F32) + 0.5) / F - 0.5
    side = jnp.where(offset > 0, base + 1, base - 1)
    side = jnp.where(side < 0, side + nz, jnp.where(side >= nz, side - nz, side))
    weight = jnp.abs(offset)
    matrix = jnp.where(cell == base, 1.0 - weight, 0.0) + jnp.where(cell == side, weight, 0.0)
    wide = joined3(jnp.dot(split3(lines), matrix.astype(BF16), preferred_element_type=F32))
    sub = lax.broadcasted_iota(jnp.int32, (STRIP, cols), 0)
    for plane in range(3):
        for r in range(rows // STRIP):
            row = r * STRIP + sub
            off = ((row % F).astype(F32) + 0.5) / F - 0.5
            wt = jnp.abs(off)
            block = r * STRIP // F
            near = block + 1
            far = near + (1 if (r * STRIP) % F >= F // 2 else -1)
            a = wide[plane * 4 + near : plane * 4 + near + 1]
            c = wide[plane * 4 + far : plane * 4 + far + 1]
            interp[plane, r * STRIP : (r + 1) * STRIP, :] = (1.0 - wt) * a + wt * c


def swap(axis, first, second):
    count = lax.axis_size(axis)
    pairs = [(i, i ^ 1) for i in range(count)]
    others = [(i, (i + 1 if i % 2 else i - 1) % count) for i in range(count)]
    return lax.ppermute(first, axis, pairs), lax.ppermute(second, axis, others)


def per_device(nx, ny, v, s, k):
    planes, rows, cols = v.shape
    n = planes * rows * cols
    vm = pltpu.VMEM
    dma = pltpu.SemaphoreType.DMA
    full, edge, line = sds(planes, rows, cols), sds(rows, cols), sds(planes, cols)
    edges, lines = sds(2, rows, cols), sds(2, planes, cols)

    rw_a, rw_b, pl_a, pl_b = pl.pallas_call(
        ends_kernel,
        out_shape=(lines, lines, edges, edges),
        in_specs=[HBM] * 2,
        out_specs=(VM,) * 4,
        scratch_shapes=[dma((2, 4))],
        compiler_params=params(58),
        cost_estimate=cost(0, n // 2),
        name="ends",
    )(v, k)
    ya, yb = swap("gy", rw_a, rw_b)
    xa, xb = swap("gx", pl_a, pl_b)

    w, f, wi_pl, fi_pl, wi_row, fi_row, sums = pl.pallas_call(
        inner_kernel,
        out_shape=(full, full, edges, edges, lines, lines, sds(4 * STRIP, cols)),
        in_specs=[HBM] * 3,
        out_specs=(HBM,) * 2 + (VM,) * 5,
        scratch_shapes=[vm(full.shape, F32)] * 5
        + [vm(edge.shape, F32)] * 2
        + [dma((3, planes)), dma((2, planes))],
        compiler_params=params(52),
        cost_estimate=cost(50 * n, 20 * n),
        name="inner",
    )(v, s, k)

    devices = nx * ny
    out = pl.pallas_call(
        edge_kernel,
        out_shape=(edge, edge, line, line) * 2 + (edges, lines, sds(devices * 4, cols // F)),
        in_specs=[VM] * 13,
        out_specs=(VM,) * 11,
        scratch_shapes=[vm(edges.shape, F32), vm(lines.shape, F32)],
        compiler_params=params(6),
        cost_estimate=cost(10 * n // 8, n),
        name="edge",
    )(wi_pl, fi_pl, wi_row, fi_row, pl_a, pl_b, rw_a, rw_b, xa, xb, ya, yb, sums)
    f_edges, w_edges, (wc_pl, wc_row, payload) = out[:4], out[4:8], out[8:]

    fya, fyb = swap("gy", f_edges[2], f_edges[3])
    fxa, fxb = swap("gx", f_edges[0], f_edges[1])
    got = lax.all_to_all(payload, ("gx", "gy"), 0, 0, tiled=True)

    got, w, f, k = lax.optimization_barrier((got, w, f, k))

    w, f, cx, cy, cz, g, g_pl, g_row = pl.pallas_call(
        sweep_kernel,
        out_shape=(full, full, sds(planes + 1, rows, cols), full, full, full, edges, lines),
        in_specs=[HBM] * 3 + [VM] * 8,
        out_specs=(VM, VM, HBM) + (VM,) * 5,
        scratch_shapes=[
            vm(full.shape, F32),
            vm((planes + 1, rows, cols), F32),
            dma((3, planes)),
            dma((planes + 1,)),
        ],
        compiler_params=params(30),
        cost_estimate=cost(40 * n, 12 * n),
        name="sweep",
    )(k, w, f, *w_edges, *f_edges)

    g_edges = pl.pallas_call(
        mid_kernel,
        out_shape=(edge, edge, line, line),
        in_specs=[VM] * 8,
        out_specs=(VM,) * 4,
        scratch_shapes=[vm(edges.shape, F32), vm(lines.shape, F32)],
        compiler_params=params(4),
        cost_estimate=cost(n // 8, n // 2),
        name="mid",
    )(g_pl, g_row, wc_pl, wc_row, fxa, fxb, fya, fyb)

    gya, gyb = swap("gy", g_edges[2], g_edges[3])
    gxa, gxb = swap("gx", g_edges[0], g_edges[1])

    cells = (nx, ny, cols // F)
    interp = pl.pallas_call(
        functools.partial(coarse_kernel, nx=nx, ny=ny, rows=rows),
        out_shape=sds(3, rows, cols),
        in_specs=[VM],
        out_specs=VM,
        scratch_shapes=[
            vm((6, 2) + cells, F32),
            vm((2,) + cells, F32),
            vm((2, 2) + cells, F32),
        ],
        compiler_params=params(8),
        cost_estimate=cost(20 * n, n),
        name="coarse",
    )(got)

    b_side = sds(planes - 2, STRIP, cols)
    out, body = pl.pallas_call(
        last_kernel,
        out_shape=(full, full),
        in_specs=[VM] * 2 + [HBM] + [VM] * 2 + [ANY] + [VM] * 5,
        out_specs=(HBM, VM),
        scratch_shapes=[
            vm(full.shape, F32),
            vm((planes + 1, rows, cols), F32),
            dma((planes,)),
            dma((planes + 1,)),
            dma((planes,)),
        ],
        compiler_params=params(27),
        cost_estimate=cost(40 * n, 20 * n),
        name="last",
    )(w, f, cx, cy, cz, g, interp, *g_edges)

    b_side = (planes - 2, STRIP, cols)
    return pl.pallas_call(
        finish_kernel,
        out_shape=full,
        in_specs=[HBM] + [VM] * 7,
        out_specs=HBM,
        scratch_shapes=[
            vm(edges.shape, F32), vm(b_side, F32), vm(b_side, F32), vm(lines.shape, F32), dma((4,)),
        ],
        input_output_aliases={0: 0},
        compiler_params=params(6),
        cost_estimate=cost(n // 4, 3 * n),
        name="finish",
    )(out, body, wc_pl, wc_row, gxa, gxb, gya, gyb)


def solution(mesh):
    placed = P("gx", "gy", None)
    body = functools.partial(per_device, mesh.shape["gx"], mesh.shape["gy"])
    return jax.shard_map(
        body, mesh=mesh, in_specs=(placed,) * 3, out_specs=placed, check_vma=False
    )
```

time: 121 us -> 75.7 us (0.63)
  Pallas kernels: 83.1 us -> 37.3 us
  waiting for transfers between devices: 1.43 us -> 4.83 us
  starting transfers between devices: 35.7 us -> 33.2 us
    pallas_call x1, Pallas kernels: 45.1 us -> 11.8 us  [per_device(): pl.pallas_call(inner_kernel, out_shape=(full, full, edges, edges, lines,...]
    pallas_call x1, Pallas kernels: 20.6 us -> 8.34 us  [per_device(): pl.pallas_call(sweep_kernel, out_shape=(full, full, sds(planes + 1, rows,...]
    ppermute x12, starting transfers between devices: 29.9 us -> 25.3 us  [the longest x6 17.2 us: swap(): lax.ppermute(second, axis, others)]
    ppermute x12, waiting for transfers between devices: 0.03 us -> 3.55 us  [the longest x6 3.53 us: swap(): lax.ppermute(second, axis, others)]
    all_to_all x1, starting transfers between devices: 5.8 us -> 7.92 us  [per_device(): got = lax.all_to_all(payload, ('gx', 'gy'), 0, 0, tiled=True)]
  transfers between devices with their start and end apart: 13 -> 13, of which waited for: 1 -> 2; matrix products, arithmetic and copies ran while one was open for 0% -> 0% of each run, Pallas kernels for 64% -> 41%
where the time goes in v4:
time: 75.7 us; the launch traced here: 75.5 us
  Pallas kernels  37.3 us (49%)
  starting transfers between devices  33.2 us (44%)
  waiting for transfers between devices  4.83 us (6%)
    ppermute x6, starting transfers between devices, swap(): lax.ppermute(second, axis, others)  17.2 us
    pallas_call x1, Pallas kernels, per_device(): pl.pallas_call(inner_kernel, out_shape=(full, full, edges, edges, lines,...  11.8 us
    pallas_call x1, Pallas kernels, per_device(): pl.pallas_call(sweep_kernel, out_shape=(full, full, sds(planes + 1, rows,...  8.34 us
    ppermute x6, starting transfers between devices, swap(): lax.ppermute(first, axis, pairs)  8.12 us
    all_to_all x1, starting transfers between devices, per_device(): got = lax.all_to_all(payload, ('gx', 'gy'), 0, 0, tiled=True)  7.92 us
    pallas_call x1, Pallas kernels, per_device(): pl.pallas_call(last_kernel, out_shape=(full, full), in_specs=[VM] * 2 + [...  6.71 us
    pallas_call x1, Pallas kernels, per_device(): pl.pallas_call(functools.partial(coarse_kernel, nx=nx, ny=ny, rows=rows),...  4.07 us
    ppermute x6, waiting for transfers between devices, swap(): lax.ppermute(second, axis, others)  3.53 us
  transfers between devices with their start and end apart: 13, of which 2 were waited for; matrix products, arithmetic and copies ran while one was open for 0% of the time, Pallas kernels for 41%

profile of v4, /device:TPU:0, one launch (start us, length us, event | category | flops | bytes accessed | tf_op | source)
XLA Modules:
  0.0 75.5 jit_solution(11021429215332479963)
XLA Ops:
  0.0 2.7 %ends.1 = (f32[2,16,2048]{2,1,0:T(8,128)}, f32[2,16,2048]{2,1,0:T(8,128)}, f32[2,32,2048]{2,1,0:T(8,128)}, f32[2,32,2048]{2,1,0:T(8,128)}) custom-call(f32[16,32,2048]{2,1,0:T(8,128)} %v.1, f32[16,32,2048]{2,1,0:T(8,128)} %k_hbm.2), custom_call_target="tpu_custom_call" | custom-call | bytes 524288 | tf_op jit(solution)/shard_map/ends/pallas_call | solution.py:602
  2.7 0.1 collective-permute-start
  2.8 4.0 %collective-permute-start.1 = (f32[2,32,2048]{2,1,0:T(8,128)}, f32[2,32,2048]{2,1,0:T(8,128)S(1)}, u32[]{:S(2)}, u32[]{:S(2)}) collective-permute-start(f32[2,32,2048]{2,1,0:T(8,128)} %get-tuple-element.50.pl_b), channel_id=1, source_target_pairs={{0,120},{8,16},{16,8},{24,32},{32,24},{40,48},{48,40},{56,64},{64,... | collective-permute-start | bytes 1572872 | tf_op jit(solution)/shard_map/ppermute | solution.py:591
  6.7 2.9 %collective-permute-start.2 = (f32[2,16,2048]{2,1,0:T(8,128)}, f32[2,16,2048]{2,1,0:T(8,128)S(1)}, u32[]{:S(2)}, u32[]{:S(2)}) collective-permute-start(f32[2,16,2048]{2,1,0:T(8,128)} %get-tuple-element.51.rw_a), channel_id=1, source_target_pairs={{0,1},{1,0},{2,3},{3,2},{4,5},{5,4},{6,7},{7,6},{8,9},{9,8},{10,11... | collective-permute-start | bytes 786440 | tf_op jit(solution)/shard_map/ppermute | solution.py:591
  9.7 4.2 %collective-permute-start.3 = (f32[2,16,2048]{2,1,0:T(8,128)}, f32[2,16,2048]{2,1,0:T(8,128)S(1)}, u32[]{:S(2)}, u32[]{:S(2)}) collective-permute-start(f32[2,16,2048]{2,1,0:T(8,128)} %get-tuple-element.52.rw_b), channel_id=1, source_target_pairs={{0,7},{1,2},{2,1},{3,4},{4,3},{5,6},{6,5},{7,0},{8,15},{9,10},{10,... | collective-permute-start | bytes 786440 | tf_op jit(solution)/shard_map/ppermute | solution.py:591
  13.8 11.8 %inner.1 = (f32[16,32,2048]{2,1,0:T(8,128)}, f32[16,32,2048]{2,1,0:T(8,128)}, f32[2,32,2048]{2,1,0:T(8,128)S(1)}, f32[2,32,2048]{2,1,0:T(8,128)S(1)}, f32[2,16,2...) custom-call(f32[16,32,2048]{2,1,0:T(8,128)} %v.1, f32[16,32,2048]{2,1,0:T(8,128)} %s_hbm.1, ...), custom_call_target="tpu_custom_call" | custom-call | flops 52428800 | bytes 20971520 | tf_op jit(solution)/shard_map/inner/pallas_call | solution.py:615
  25.7 0.0 collective-permute-done.2.ya
  25.7 3.5 %collective-permute-done.3.yb = f32[2,16,2048]{2,1,0:T(8,128)S(1)} collective-permute-done((f32[2,16,2048]{2,1,0:T(8,128)}, f32[2,16,2048]{2,1,0:T(8,128)S(1)}, u32[]{:S(2)}, u32[]{:S(2)}) %collective-permute-start.3) | collective-permute-done | bytes 262176 | tf_op jit(solution)/shard_map/ppermute | solution.py:591
  29.2 0.0 collective-permute-done.xa
  29.2 0.0 collective-permute-done.1.xb
  29.2 1.9 %edge.1 = (f32[32,2048]{1,0:T(8,128)S(1)}, f32[32,2048]{1,0:T(8,128)S(1)}, f32[16,2048]{1,0:T(8,128)S(1)}, f32[16,2048]{1,0:T(8,128)S(1)}, f32[32,2048]{1,0:T(8,...) custom-call(f32[2,32,2048]{2,1,0:T(8,128)S(1)} %get-tuple-element.45, ...), custom_call_target="tpu_custom_call" | custom-call | flops 1310720 | bytes 1048576 | tf_op jit(solution)/shard_map/edge/pallas_call | solution.py:629
  31.1 7.9 %all-to-all-start = ((f32[128,4,128]{2,1,0:T(4,128)}), f32[128,4,128]{2,1,0:T(4,128)S(1)}, u32[]{:S(2)}, u32[]{:S(2)}) async-start(f32[128,4,128]{2,1,0:T(4,128)} %bitcast), calls=%async_computation | async-start | bytes 524288 | tf_op jit(solution)/shard_map/all_to_all | solution.py:643
  39.0 0.1 collective-permute-start.4
  39.1 3.2 %collective-permute-start.5 = (f32[32,2048]{1,0:T(8,128)S(1)}, f32[32,2048]{1,0:T(8,128)S(1)}, u32[]{:S(2)}, u32[]{:S(2)}) collective-permute-start(f32[32,2048]{1,0:T(8,128)S(1)} %get-tuple-element.65.f_pl1), channel_id=1, source_target_pairs={{0,120},{8,16},{16,8},{24,32},{32,24},{40,48},{48,40},{56,64},{64,... | collective-permute-start | bytes 786440 | tf_op jit(solution)/shard_map/ppermute | solution.py:591
  42.3 2.8 %collective-permute-start.6 = (f32[16,2048]{1,0:T(8,128)S(1)}, f32[16,2048]{1,0:T(8,128)S(1)}, u32[]{:S(2)}, u32[]{:S(2)}) collective-permute-start(f32[16,2048]{1,0:T(8,128)S(1)} %get-tuple-element.66.f_row0), channel_id=1, source_target_pairs={{0,1},{1,0},{2,3},{3,2},{4,5},{5,4},{6,7},{7,6},{8,9},{9,8},{10,11... | collective-permute-start | bytes 393224 | tf_op jit(solution)/shard_map/ppermute | solution.py:591
  45.1 3.6 %collective-permute-start.7 = (f32[16,2048]{1,0:T(8,128)S(1)}, f32[16,2048]{1,0:T(8,128)S(1)}, u32[]{:S(2)}, u32[]{:S(2)}) collective-permute-start(f32[16,2048]{1,0:T(8,128)S(1)} %get-tuple-element.67.f_row1), channel_id=1, source_target_pairs={{0,7},{1,2},{2,1},{3,4},{4,3},{5,6},{6,5},{7,0},{8,15},{9,10},{10,... | collective-permute-start | bytes 393224 | tf_op jit(solution)/shard_map/ppermute | solution.py:591
  48.7 1.3 %all-to-all-done = f32[128,4,128]{2,1,0:T(4,128)S(1)} async-done(((f32[128,4,128]{2,1,0:T(4,128)}), f32[128,4,128]{2,1,0:T(4,128)S(1)}, u32[]{:S(2)}, u32[]{:S(2)}) %all-to-all-start) | async-done | bytes 262176 | tf_op jit(solution)/shard_map/all_to_all | solution.py:643
  50.0 8.3 %sweep.1 = (f32[16,32,2048]{2,1,0:T(8,128)S(1)}, f32[16,32,2048]{2,1,0:T(8,128)S(1)}, f32[17,32,2048]{2,1,0:T(8,128)}, f32[16,32,2048]{2,1,0:T(8,128)S(1)}, f32[...) custom-call(f32[16,32,2048]{2,1,0:T(8,128)} %k_hbm.2, ...), custom_call_target="tpu_custom_call" | custom-call | flops 41943040 | bytes 12582912 | tf_op jit(solution)/shard_map/sweep/pallas_call | solution.py:647
  58.3 0.0 collective-permute-done.6.ya
  58.3 0.0 collective-permute-done.7.yb
  58.3 0.0 collective-permute-done.4.xa
  58.4 0.0 collective-permute-done.5.xb
  58.4 0.2 mid.1
  58.6 0.1 collective-permute-start.8
  58.7 1.0 %collective-permute-start.9 = (f32[32,2048]{1,0:T(8,128)S(1)}, f32[32,2048]{1,0:T(8,128)S(1)}, u32[]{:S(2)}, u32[]{:S(2)}) collective-permute-start(f32[32,2048]{1,0:T(8,128)S(1)} %get-tuple-element.80.g_pl1), channel_id=1, source_target_pairs={{0,120},{8,16},{16,8},{24,32},{32,24},{40,48},{48,40},{56,64},{64,... | collective-permute-start | bytes 786440 | tf_op jit(solution)/shard_map/ppermute | solution.py:591
  59.7 2.2 %collective-permute-start.10 = (f32[16,2048]{1,0:T(8,128)S(1)}, f32[16,2048]{1,0:T(8,128)S(1)}, u32[]{:S(2)}, u32[]{:S(2)}) collective-permute-start(f32[16,2048]{1,0:T(8,128)S(1)} %get-tuple-element.81.g_row0), channel_id=1, source_target_pairs={{0,1},{1,0},{2,3},{3,2},{4,5},{5,4},{6,7},{7,6},{8,9},{9,8},{10,11... | collective-permute-start | bytes 393224 | tf_op jit(solution)/shard_map/ppermute | solution.py:591
  61.9 1.2 %collective-permute-start.11 = (f32[16,2048]{1,0:T(8,128)S(1)}, f32[16,2048]{1,0:T(8,128)S(1)}, u32[]{:S(2)}, u32[]{:S(2)}) collective-permute-start(f32[16,2048]{1,0:T(8,128)S(1)} %get-tuple-element.82.g_row1), channel_id=1, source_target_pairs={{0,7},{1,2},{2,1},{3,4},{4,3},{5,6},{6,5},{7,0},{8,15},{9,10},{10,... | collective-permute-start | bytes 393224 | tf_op jit(solution)/shard_map/ppermute | solution.py:591
  63.1 4.1 %coarse.1.interp = f32[3,32,2048]{2,1,0:T(8,128)S(1)} custom-call(f32[512,128]{1,0:T(8,128)S(1)} %bitcast.2), custom_call_target="tpu_custom_call" | custom-call | flops 20971520 | bytes 1048576 | tf_op jit(solution)/shard_map/coarse/pallas_call | solution.py:678
  67.2 6.7 %last.1 = (f32[16,32,2048]{2,1,0:T(8,128)}, f32[16,32,2048]{2,1,0:T(8,128)S(1)}) custom-call(f32[16,32,2048]{2,1,0:T(8,128)S(1)} %get-tuple-element.68.w, f32[16,32,2048]{2,1,0:T(8,128)S(1)} %get-tuple-element.69.f, f32[17,32,2048]{2,1,0:T(8,128)} %get-tuple-element.70.cx_hbm, f32[16,32,2048]{2,1,0:T(8,128)S(1)} %get-tuple-element.71.cy, ...), custom_call_target="tpu_custom_call" | custom-call | flops 41943040 | bytes 20971520 | tf_op jit(solution)/shard_map/last/pallas_call | solution.py:694
  73.9 0.0 collective-permute-done.10.ya
  73.9 0.0 collective-permute-done.9.xb
  73.9 1.6 %finish.1 = f32[16,32,2048]{2,1,0:T(8,128)} custom-call(f32[16,32,2048]{2,1,0:T(8,128)} %get-tuple-element.83.src, f32[16,32,2048]{2,1,0:T(8,128)S(1)} %get-tuple-element.84.body, f32[2,32,2048]{2,1,0:T(8,128)S(1)} %get-tuple-element.77.wc_pl, f32[2,16,2048]{2,1,0:T(8,128)S(1)} %get-tuple-element.78.wc_row, ...), custom_call_target="tpu_custom_call", output_to_operand_aliasing={{}: (0, {})} | custom-call | flops 262144 | bytes 3145728 | tf_op jit(solution)/shard_map/finish/pallas_call | solution.py:712
  (10 shorter events, 0.0 us)
Async XLA Ops:
  2.7 26.5 %collective-permute-start = (f32[2,32,2048]{2,1,0:T(8,128)}, f32[2,32,2048]{2,1,0:T(8,128)S(1)}, u32[]{:S(2)}, u32[]{:S(2)}) collective-permute-start(f32[2,32,2048]{2,1,0:T(8,128)} %get-tuple-element.49.pl_a), channel_id=1, source_target_pairs={{0,8},{8,0},{16,24},{24,16},{32,40},{40,32},{48,56},{56,48},{64,72... | collective-permute-start | bytes 1572872 | tf_op jit(solution)/shard_map/ppermute | solution.py:591
  2.8 26.4 %collective-permute-start.1 = (f32[2,32,2048]{2,1,0:T(8,128)}, f32[2,32,2048]{2,1,0:T(8,128)S(1)}, u32[]{:S(2)}, u32[]{:S(2)}) collective-permute-start(f32[2,32,2048]{2,1,0:T(8,128)} %get-tuple-element.50.pl_b), channel_id=1, source_target_pairs={{0,120},{8,16},{16,8},{24,32},{32,24},{40,48},{48,40},{56,64},{64,... | collective-permute-start | bytes 1572872 | tf_op jit(solution)/shard_map/ppermute | solution.py:591
  6.7 18.9 %collective-permute-start.2 = (f32[2,16,2048]{2,1,0:T(8,128)}, f32[2,16,2048]{2,1,0:T(8,128)S(1)}, u32[]{:S(2)}, u32[]{:S(2)}) collective-permute-start(f32[2,16,2048]{2,1,0:T(8,128)} %get-tuple-element.51.rw_a), channel_id=1, source_target_pairs={{0,1},{1,0},{2,3},{3,2},{4,5},{5,4},{6,7},{7,6},{8,9},{9,8},{10,11... | collective-permute-start | bytes 786440 | tf_op jit(solution)/shard_map/ppermute | solution.py:591
  9.6 19.6 %copy-start = (f32[2,32,2048]{2,1,0:T(8,128)S(1)}, f32[2,32,2048]{2,1,0:T(8,128)}, u32[]{:S(2)}) copy-start(f32[2,32,2048]{2,1,0:T(8,128)} %get-tuple-element.49.pl_a) | copy-start | bytes 1572868
  9.6 19.6 %copy-start.1 = (f32[2,32,2048]{2,1,0:T(8,128)S(1)}, f32[2,32,2048]{2,1,0:T(8,128)}, u32[]{:S(2)}) copy-start(f32[2,32,2048]{2,1,0:T(8,128)} %get-tuple-element.50.pl_b) | copy-start | bytes 1572868
  9.6 19.6 %copy-start.2 = (f32[2,16,2048]{2,1,0:T(8,128)S(1)}, f32[2,16,2048]{2,1,0:T(8,128)}, u32[]{:S(2)}) copy-start(f32[2,16,2048]{2,1,0:T(8,128)} %get-tuple-element.51.rw_a) | copy-start | bytes 786436
  9.6 19.6 %copy-start.3 = (f32[2,16,2048]{2,1,0:T(8,128)S(1)}, f32[2,16,2048]{2,1,0:T(8,128)}, u32[]{:S(2)}) copy-start(f32[2,16,2048]{2,1,0:T(8,128)} %get-tuple-element.52.rw_b) | copy-start | bytes 786436
  9.7 19.5 %collective-permute-start.3 = (f32[2,16,2048]{2,1,0:T(8,128)}, f32[2,16,2048]{2,1,0:T(8,128)S(1)}, u32[]{:S(2)}, u32[]{:S(2)}) collective-permute-start(f32[2,16,2048]{2,1,0:T(8,128)} %get-tuple-element.52.rw_b), channel_id=1, source_target_pairs={{0,7},{1,2},{2,1},{3,4},{4,3},{5,6},{6,5},{7,0},{8,15},{9,10},{10,... | collective-permute-start | bytes 786440 | tf_op jit(solution)/shard_map/ppermute | solution.py:591
  31.1 18.9 %all-to-all-start = ((f32[128,4,128]{2,1,0:T(4,128)}), f32[128,4,128]{2,1,0:T(4,128)S(1)}, u32[]{:S(2)}, u32[]{:S(2)}) async-start(f32[128,4,128]{2,1,0:T(4,128)} %bitcast), calls=%async_computation | async-start | bytes 524288 | tf_op jit(solution)/shard_map/all_to_all | solution.py:643
  39.0 19.3 %collective-permute-start.4 = (f32[32,2048]{1,0:T(8,128)S(1)}, f32[32,2048]{1,0:T(8,128)S(1)}, u32[]{:S(2)}, u32[]{:S(2)}) collective-permute-start(f32[32,2048]{1,0:T(8,128)S(1)} %get-tuple-element.64.f_pl0), channel_id=1, source_target_pairs={{0,8},{8,0},{16,24},{24,16},{32,40},{40,32},{48,56},{56,48},{64,72... | collective-permute-start | bytes 786440 | tf_op jit(solution)/shard_map/ppermute | solution.py:591
  39.1 19.3 %collective-permute-start.5 = (f32[32,2048]{1,0:T(8,128)S(1)}, f32[32,2048]{1,0:T(8,128)S(1)}, u32[]{:S(2)}, u32[]{:S(2)}) collective-permute-start(f32[32,2048]{1,0:T(8,128)S(1)} %get-tuple-element.65.f_pl1), channel_id=1, source_target_pairs={{0,120},{8,16},{16,8},{24,32},{32,24},{40,48},{48,40},{56,64},{64,... | collective-permute-start | bytes 786440 | tf_op jit(solution)/shard_map/ppermute | solution.py:591
  42.3 16.0 %collective-permute-start.6 = (f32[16,2048]{1,0:T(8,128)S(1)}, f32[16,2048]{1,0:T(8,128)S(1)}, u32[]{:S(2)}, u32[]{:S(2)}) collective-permute-start(f32[16,2048]{1,0:T(8,128)S(1)} %get-tuple-element.66.f_row0), channel_id=1, source_target_pairs={{0,1},{1,0},{2,3},{3,2},{4,5},{5,4},{6,7},{7,6},{8,9},{9,8},{10,11... | collective-permute-start | bytes 393224 | tf_op jit(solution)/shard_map/ppermute | solution.py:591
  45.1 13.3 %collective-permute-start.7 = (f32[16,2048]{1,0:T(8,128)S(1)}, f32[16,2048]{1,0:T(8,128)S(1)}, u32[]{:S(2)}, u32[]{:S(2)}) collective-permute-start(f32[16,2048]{1,0:T(8,128)S(1)} %get-tuple-element.67.f_row1), channel_id=1, source_target_pairs={{0,7},{1,2},{2,1},{3,4},{4,3},{5,6},{6,5},{7,0},{8,15},{9,10},{10,... | collective-permute-start | bytes 393224 | tf_op jit(solution)/shard_map/ppermute | solution.py:591
  58.6 15.3 %collective-permute-start.8 = (f32[32,2048]{1,0:T(8,128)S(1)}, f32[32,2048]{1,0:T(8,128)S(1)}, u32[]{:S(2)}, u32[]{:S(2)}) collective-permute-start(f32[32,2048]{1,0:T(8,128)S(1)} %get-tuple-element.79.g_pl0), channel_id=1, source_target_pairs={{0,8},{8,0},{16,24},{24,16},{32,40},{40,32},{48,56},{56,48},{64,72... | collective-permute-start | bytes 786440 | tf_op jit(solution)/shard_map/ppermute | solution.py:591
  58.7 15.2 %collective-permute-start.9 = (f32[32,2048]{1,0:T(8,128)S(1)}, f32[32,2048]{1,0:T(8,128)S(1)}, u32[]{:S(2)}, u32[]{:S(2)}) collective-permute-start(f32[32,2048]{1,0:T(8,128)S(1)} %get-tuple-element.80.g_pl1), channel_id=1, source_target_pairs={{0,120},{8,16},{16,8},{24,32},{32,24},{40,48},{48,40},{56,64},{64,... | collective-permute-start | bytes 786440 | tf_op jit(solution)/shard_map/ppermute | solution.py:591
  59.7 14.2 %collective-permute-start.10 = (f32[16,2048]{1,0:T(8,128)S(1)}, f32[16,2048]{1,0:T(8,128)S(1)}, u32[]{:S(2)}, u32[]{:S(2)}) collective-permute-start(f32[16,2048]{1,0:T(8,128)S(1)} %get-tuple-element.81.g_row0), channel_id=1, source_target_pairs={{0,1},{1,0},{2,3},{3,2},{4,5},{5,4},{6,7},{7,6},{8,9},{9,8},{10,11... | collective-permute-start | bytes 393224 | tf_op jit(solution)/shard_map/ppermute | solution.py:591
  61.9 12.0 %collective-permute-start.11 = (f32[16,2048]{1,0:T(8,128)S(1)}, f32[16,2048]{1,0:T(8,128)S(1)}, u32[]{:S(2)}, u32[]{:S(2)}) collective-permute-start(f32[16,2048]{1,0:T(8,128)S(1)} %get-tuple-element.82.g_row1), channel_id=1, source_target_pairs={{0,7},{1,2},{2,1},{3,4},{4,3},{5,6},{6,5},{7,0},{8,15},{9,10},{10,... | collective-permute-start | bytes 393224 | tf_op jit(solution)/shard_map/ppermute | solution.py:591

commit v5 on v4

--- a/solution.py
+++ b/solution.py
@@ -269,54 +269,15 @@
             ref[x] = plane[...]
 
 
-def shifted_up(rolled, r):
-    nxt = rolled[min(r + 1, len(rolled) - 1)]
-    sub = lax.broadcasted_iota(jnp.int32, nxt.shape, 0)
-    return jnp.where(sub == STRIP - 1, nxt, rolled[r])
-
-
-def shifted_down(rolled, r):
-    prv = rolled[r - 1]
-    sub = lax.broadcasted_iota(jnp.int32, prv.shape, 0)
-    return jnp.where(sub == 0, prv, rolled[r])
-
-
-def up_coupling(k0, k_up, r):
-    c = 0.5 * (k0[r] + shifted_up(k_up, r))
-    if r == len(k0) - 1:
-        sub = lax.broadcasted_iota(jnp.int32, c.shape, 0)
-        c = jnp.where(sub == STRIP - 1, 0.0, c)
-    return c
-
-
-def neighbour_sums(x, u, cx, cy, cz):
-    planes, rows, _ = u.shape
-    sl = strips(rows)
-    xn, xp = jnp.minimum(x + 1, planes - 1), jnp.maximum(x - 1, 0)
-    u0 = [u[x, a, :] for a in sl]
-    u_up = [pltpu.roll(a, STRIP - 1, 0) for a in u0]
-    c_y = [cy[x, a, :] for a in sl]
-    q_dn = [pltpu.roll(c * a, 1, 0) for c, a in zip(c_y, u0)]
-    for r, a in enumerate(sl):
-        c_z = cz[x, a, :]
-        total = (
-            (cx[x + 1, a, :] * u[xn, a, :] + cx[x, a, :] * u[xp, a, :])
-            + (c_y[r] * shifted_up(u_up, r) + shifted_down(q_dn, r))
-            + (c_z * left(u0[r]) + right(c_z * u0[r]))
-        )
-        yield r, a, u0[r], total
-
-
 def sweep_kernel(
     k_hbm, w_hbm, f_hbm, w_pl0, w_pl1, w_row0, w_row1, f_pl0, f_pl1, f_row0, f_row1,
-    w, f, cx_hbm, cy, cz, g_ref, g_pl, g_row, k, cx, sems, out_sems,
+    w, f, k, cy, cz, g_ref, g_pl, g_row, cx, sems,
 ):
     planes, rows, cols = w.shape
     sl = strips(rows)
     low, high = low_high("gy")
-
-    def out_copy(x):
-        return pltpu.make_async_copy(cx.at[x], cx_hbm.at[x], out_sems.at[x])
+    sub = lax.broadcasted_iota(jnp.int32, (STRIP, cols), 0)
+    sub0, sub1 = sub == 0, sub == STRIP - 1
 
     def copy(i, x):
         src, dst = ((k_hbm, k), (f_hbm, f), (w_hbm, w))[i]
@@ -331,8 +292,7 @@
     for x in range(planes):
         for i in range(3):
             copy(i, x).start()
-    cx[0] = jnp.zeros_like(k[0])
-    out_copy(0).start()
+    cx[...] = jnp.zeros_like(cx)
     arrive(0)
 
     def plane(x, carry):
@@ -342,27 +302,39 @@
 
         xn = jnp.minimum(x + 1, planes - 1)
         h_next = jnp.where(x < planes - 1, 0.5, 0.0).astype(F32)
-        k0 = [k[x, a, :] for a in sl]
-        k_up = [pltpu.roll(a, STRIP - 1, 0) for a in k0]
+        xp = jnp.maximum(x - 1, 0)
+        dn = 0.0
+        k0, u0 = k[x, sl[0], :], f[x, sl[0], :]
+        ku, uu = upward(k0), upward(u0)
         for r, a in enumerate(sl):
-            cx[x + 1, a, :] = h_next * (k0[r] + k[xn, a, :])
-            cy[x, a, :] = up_coupling(k0, k_up, r)
-            cz[x, a, :] = 0.5 * (k0[r] + left(k0[r]))
-        for r, a, u0, total in neighbour_sums(x, f, cx, cy, cz):
-            new = (2.0 - DAMPING) * u0 + w[x, a, :] * total
-            g_ref[x, a, :] = new
-            if r == 0:
-                g_row[low, pl.ds(x, 1), :] = new[0:1]
-            if (r + 1) * STRIP == rows:
-                g_row[high, pl.ds(x, 1), :] = new[STRIP - 1 :]
-        out_copy(x + 1).start()
+            c_z = 0.5 * (k0 + left(k0))
+            total = c_z * left(u0) + right(c_z * u0)
+            if r + 1 < len(sl):
+                k1, u1 = k[x, sl[r + 1], :], f[x, sl[r + 1], :]
+                ku1, uu1 = upward(k1), upward(u1)
+                c_y = 0.5 * (k0 + jnp.where(sub1, ku1, ku))
+                above = jnp.where(sub1, uu1, uu)
+            else:
+                c_y = jnp.where(sub1, 0.0, 0.5 * (k0 + ku))
+                above = uu
+            nd = downward(c_y * u0)
+            total = total + (c_y * above + jnp.where(sub0, dn, nd))
+            dn = nd
+            c_x = h_next * (k0 + k[xn, a, :])
+            total = total + (c_x * f[xn, a, :] + cx[a, :] * f[xp, a, :])
+            cx[a, :] = c_x
+            cy[x, a, :] = c_y
+            cz[x, a, :] = c_z
+            g_ref[x, a, :] = (2.0 - DAMPING) * u0 + w[x, a, :] * total
+            if r + 1 < len(sl):
+                k0, u0, ku, uu = k1, u1, ku1, uu1
+        for place, y in ((low, 0), (high, rows - 1)):
+            g_row[place, pl.ds(x, 1), :] = g_ref[x, y : y + 1, :]
         return carry
 
     lax.fori_loop(0, planes, plane, 0)
     for side, x in enumerate(edge_spots("gx", planes)):
         g_pl[side] = g_ref[x]
-    for x in range(planes + 1):
-        out_copy(x).wait()
 
 
 def mid_kernel(
@@ -377,13 +349,14 @@
     cross(q_pl, q_row, (o_pl0, o_pl1), (o_row0, o_row1), 1.0)
 
 
-def tile_sums(x, u, cx, cy, cz):
+def tile_sums(x, u, k, cx, cy, cz):
     planes, rows, cols = u.shape
     sl = strips(rows)
     tl = [slice(j, j + LANES) for j in range(0, cols, LANES)]
     lane = lax.broadcasted_iota(jnp.int32, (STRIP, LANES), 1)
     sub = lax.broadcasted_iota(jnp.int32, (STRIP, LANES), 0)
     xn, xp = jnp.minimum(x + 1, planes - 1), jnp.maximum(x - 1, 0)
+    h_next = jnp.where(x < planes - 1, 0.5, 0.0).astype(F32)
     ru = [left(u[x, a, tl[0]]) for a in sl]
     pm = [right(cz[x, a, tl[-1]] * u[x, a, tl[-1]]) for a in sl]
     for j, t in enumerate(tl):
@@ -393,7 +366,9 @@
         for r, a in enumerate(sl):
             u0, c_y, c_z = us[r], cy[x, a, t], cz[x, a, t]
             nu = left(u[x, a, tl[(j + 1) % len(tl)]])
-            total = cx[x + 1, a, t] * u[xn, a, t] + cx[x, a, t] * u[xp, a, t]
+            c_x = h_next * (k[x, a, t] + k[xn, a, t])
+            total = c_x * u[xn, a, t] + cx[a, t] * u[xp, a, t]
+            cx[a, t] = c_x
             total = total + c_z * jnp.where(lane == LANES - 1, nu, ru[r])
             mu = right(c_z * u0)
             total = total + jnp.where(lane == 0, pm[r], mu)
@@ -406,32 +381,21 @@
 
 
 def last_kernel(
-    w, f, cx_hbm, cy, cz, g_any, interp, g_pl0, g_pl1, g_row0, g_row1,
-    out, body, g, cx, in_sems, cx_sems, sems,
+    w, f, k, cy, cz, g_in, interp, g_pl0, g_pl1, g_row0, g_row1,
+    out, body, g, cx, sems,
 ):
     planes, rows, cols = w.shape
-
-    def in_copy(x):
-        return pltpu.make_async_copy(g_any.at[x], g.at[x], in_sems.at[x])
 
     def copy(x):
         return pltpu.make_async_copy(
             body.at[x, STRIP : rows - STRIP, :], out.at[x, STRIP : rows - STRIP, :], sems.at[x]
         )
 
-    def cx_copy(x):
-        return pltpu.make_async_copy(cx_hbm.at[x], cx.at[x], cx_sems.at[x])
-
     def arrive(x):
-        cx_copy(x + 1).wait()
-        in_copy(x).wait()
+        g[x] = g_in[x]
         put_edges(g, x, g_pl0, g_pl1, g_row0, g_row1)
 
-    cx_copy(0).start()
-    for x in range(planes):
-        in_copy(x).start()
-        cx_copy(x + 1).start()
-    cx_copy(0).wait()
+    cx[...] = jnp.zeros_like(cx)
     arrive(0)
 
     def plane(x, carry):
@@ -442,7 +406,7 @@
         offset = ((x % F).astype(F32) + 0.5) / F - 0.5
         weight = jnp.abs(offset)
         side = jnp.where(offset > 0, 2, 0)
-        for a, t, u0, total in tile_sums(x, g, cx, cy, cz):
+        for a, t, u0, total in tile_sums(x, g, k, cx, cy, cz):
             coarse = (1.0 - weight) * interp[1, a, t] + weight * interp[side, a, t]
             new = f[x, a, t] + (1.0 - DAMPING) * u0 + coarse
             body[x, a, t] = new + w[x, a, t] * total
@@ -644,18 +608,13 @@
 
     got, w, f, k = lax.optimization_barrier((got, w, f, k))
 
-    w, f, cx, cy, cz, g, g_pl, g_row = pl.pallas_call(
+    w, f, k, cy, cz, g, g_pl, g_row = pl.pallas_call(
         sweep_kernel,
-        out_shape=(full, full, sds(planes + 1, rows, cols), full, full, full, edges, lines),
+        out_shape=(full,) * 6 + (edges, lines),
         in_specs=[HBM] * 3 + [VM] * 8,
-        out_specs=(VM, VM, HBM) + (VM,) * 5,
-        scratch_shapes=[
-            vm(full.shape, F32),
-            vm((planes + 1, rows, cols), F32),
-            dma((3, planes)),
-            dma((planes + 1,)),
-        ],
-        compiler_params=params(30),
+        out_specs=(VM,) * 8,
+        scratch_shapes=[vm(edge.shape, F32), dma((3, planes))],
+        compiler_params=params(33),
         cost_estimate=cost(40 * n, 12 * n),
         name="sweep",
     )(k, w, f, *w_edges, *f_edges)
@@ -694,19 +653,13 @@
     out, body = pl.pallas_call(
         last_kernel,
         out_shape=(full, full),
-        in_specs=[VM] * 2 + [HBM] + [VM] * 2 + [ANY] + [VM] * 5,
+        in_specs=[VM] * 11,
         out_specs=(HBM, VM),
-        scratch_shapes=[
-            vm(full.shape, F32),
-            vm((planes + 1, rows, cols), F32),
-            dma((planes,)),
-            dma((planes + 1,)),
-            dma((planes,)),
-        ],
-        compiler_params=params(27),
+        scratch_shapes=[vm(full.shape, F32), vm(edge.shape, F32), dma((planes,))],
+        compiler_params=params(31),
         cost_estimate=cost(40 * n, 20 * n),
         name="last",
-    )(w, f, cx, cy, cz, g, interp, *g_edges)
+    )(w, f, k, cy, cz, g, interp, *g_edges)
 
     b_side = (planes - 2, STRIP, cols)
     return pl.pallas_call(

time: 75.7 us -> 81.6 us (1.078)
  Pallas kernels: 37.3 us -> 43.2 us
    pallas_call x2, Pallas kernels: 15 us -> 20.9 us  [the longest x1 11.7 us: per_device(): pl.pallas_call(sweep_kernel, out_shape=(full,) * 6 + (edges, lines), in_s...]
  transfers between devices with their start and end apart: 13 -> 13, of which waited for: 2 -> 2; matrix products, arithmetic and copies ran while one was open for 0% -> 0% of each run, Pallas kernels for 41% -> 45%
where the time goes in v5:
time: 81.6 us; the launch traced here: 81.4 us
  Pallas kernels  43.2 us (53%)
  starting transfers between devices  33.2 us (41%)
  waiting for transfers between devices  4.83 us (6%)
    ppermute x6, starting transfers between devices, swap(): lax.ppermute(second, axis, others)  17.2 us
    pallas_call x1, Pallas kernels, per_device(): pl.pallas_call(inner_kernel, out_shape=(full, full, edges, edges, lines,...  11.8 us
    pallas_call x1, Pallas kernels, per_device(): pl.pallas_call(sweep_kernel, out_shape=(full,) * 6 + (edges, lines), in_s...  11.7 us
    pallas_call x1, Pallas kernels, per_device(): pl.pallas_call(last_kernel, out_shape=(full, full), in_specs=[VM] * 11, o...  9.26 us
    ppermute x6, starting transfers between devices, swap(): lax.ppermute(first, axis, pairs)  8.12 us
    all_to_all x1, starting transfers between devices, per_device(): got = lax.all_to_all(payload, ('gx', 'gy'), 0, 0, tiled=True)  7.92 us
    pallas_call x1, Pallas kernels, per_device(): pl.pallas_call(functools.partial(coarse_kernel, nx=nx, ny=ny, rows=rows),...  4.07 us
    ppermute x6, waiting for transfers between devices, swap(): lax.ppermute(second, axis, others)  3.54 us
  transfers between devices with their start and end apart: 13, of which 2 were waited for; matrix products, arithmetic and copies ran while one was open for 0% of the time, Pallas kernels for 45%

profile of v5, /device:TPU:0, one launch (start us, length us, event | category | flops | bytes accessed | tf_op | source)
XLA Modules:
  0.0 81.4 jit_solution(4897678461083866879)
XLA Ops:
  0.0 2.7 %ends.1 = (f32[2,16,2048]{2,1,0:T(8,128)}, f32[2,16,2048]{2,1,0:T(8,128)}, f32[2,32,2048]{2,1,0:T(8,128)}, f32[2,32,2048]{2,1,0:T(8,128)}) custom-call(f32[16,32,2048]{2,1,0:T(8,128)} %v.1, f32[16,32,2048]{2,1,0:T(8,128)} %k_hbm.2), custom_call_target="tpu_custom_call" | custom-call | bytes 524288 | tf_op jit(solution)/shard_map/ends/pallas_call | solution.py:566
  2.7 0.1 collective-permute-start
  2.8 4.0 %collective-permute-start.1 = (f32[2,32,2048]{2,1,0:T(8,128)}, f32[2,32,2048]{2,1,0:T(8,128)S(1)}, u32[]{:S(2)}, u32[]{:S(2)}) collective-permute-start(f32[2,32,2048]{2,1,0:T(8,128)} %get-tuple-element.50.pl_b), channel_id=1, source_target_pairs={{0,120},{8,16},{16,8},{24,32},{32,24},{40,48},{48,40},{56,64},{64,... | collective-permute-start | bytes 1572872 | tf_op jit(solution)/shard_map/ppermute | solution.py:555
  6.8 2.9 %collective-permute-start.2 = (f32[2,16,2048]{2,1,0:T(8,128)}, f32[2,16,2048]{2,1,0:T(8,128)S(1)}, u32[]{:S(2)}, u32[]{:S(2)}) collective-permute-start(f32[2,16,2048]{2,1,0:T(8,128)} %get-tuple-element.51.rw_a), channel_id=1, source_target_pairs={{0,1},{1,0},{2,3},{3,2},{4,5},{5,4},{6,7},{7,6},{8,9},{9,8},{10,11... | collective-permute-start | bytes 786440 | tf_op jit(solution)/shard_map/ppermute | solution.py:555
  9.7 4.2 %collective-permute-start.3 = (f32[2,16,2048]{2,1,0:T(8,128)}, f32[2,16,2048]{2,1,0:T(8,128)S(1)}, u32[]{:S(2)}, u32[]{:S(2)}) collective-permute-start(f32[2,16,2048]{2,1,0:T(8,128)} %get-tuple-element.52.rw_b), channel_id=1, source_target_pairs={{0,7},{1,2},{2,1},{3,4},{4,3},{5,6},{6,5},{7,0},{8,15},{9,10},{10,... | collective-permute-start | bytes 786440 | tf_op jit(solution)/shard_map/ppermute | solution.py:555
  13.9 11.8 %inner.1 = (f32[16,32,2048]{2,1,0:T(8,128)}, f32[16,32,2048]{2,1,0:T(8,128)}, f32[2,32,2048]{2,1,0:T(8,128)S(1)}, f32[2,32,2048]{2,1,0:T(8,128)S(1)}, f32[2,16,2...) custom-call(f32[16,32,2048]{2,1,0:T(8,128)} %v.1, f32[16,32,2048]{2,1,0:T(8,128)} %s_hbm.1, ...), custom_call_target="tpu_custom_call" | custom-call | flops 52428800 | bytes 20971520 | tf_op jit(solution)/shard_map/inner/pallas_call | solution.py:579
  25.7 0.0 collective-permute-done.2.ya
  25.7 3.5 %collective-permute-done.3.yb = f32[2,16,2048]{2,1,0:T(8,128)S(1)} collective-permute-done((f32[2,16,2048]{2,1,0:T(8,128)}, f32[2,16,2048]{2,1,0:T(8,128)S(1)}, u32[]{:S(2)}, u32[]{:S(2)}) %collective-permute-start.3) | collective-permute-done | bytes 262176 | tf_op jit(solution)/shard_map/ppermute | solution.py:555
  29.2 0.0 collective-permute-done.xa
  29.2 0.0 collective-permute-done.1.xb
  29.2 1.9 %edge.1 = (f32[32,2048]{1,0:T(8,128)S(1)}, f32[32,2048]{1,0:T(8,128)S(1)}, f32[16,2048]{1,0:T(8,128)S(1)}, f32[16,2048]{1,0:T(8,128)S(1)}, f32[32,2048]{1,0:T(8,...) custom-call(f32[2,32,2048]{2,1,0:T(8,128)S(1)} %get-tuple-element.45, ...), custom_call_target="tpu_custom_call" | custom-call | flops 1310720 | bytes 1048576 | tf_op jit(solution)/shard_map/edge/pallas_call | solution.py:593
  31.1 7.9 %all-to-all-start = ((f32[128,4,128]{2,1,0:T(4,128)}), f32[128,4,128]{2,1,0:T(4,128)S(1)}, u32[]{:S(2)}, u32[]{:S(2)}) async-start(f32[128,4,128]{2,1,0:T(4,128)} %bitcast), calls=%async_computation | async-start | bytes 524288 | tf_op jit(solution)/shard_map/all_to_all | solution.py:607
  39.0 0.1 collective-permute-start.4
  39.1 3.2 %collective-permute-start.5 = (f32[32,2048]{1,0:T(8,128)S(1)}, f32[32,2048]{1,0:T(8,128)S(1)}, u32[]{:S(2)}, u32[]{:S(2)}) collective-permute-start(f32[32,2048]{1,0:T(8,128)S(1)} %get-tuple-element.65.f_pl1), channel_id=1, source_target_pairs={{0,120},{8,16},{16,8},{24,32},{32,24},{40,48},{48,40},{56,64},{64,... | collective-permute-start | bytes 786440 | tf_op jit(solution)/shard_map/ppermute | solution.py:555
  42.3 2.8 %collective-permute-start.6 = (f32[16,2048]{1,0:T(8,128)S(1)}, f32[16,2048]{1,0:T(8,128)S(1)}, u32[]{:S(2)}, u32[]{:S(2)}) collective-permute-start(f32[16,2048]{1,0:T(8,128)S(1)} %get-tuple-element.66.f_row0), channel_id=1, source_target_pairs={{0,1},{1,0},{2,3},{3,2},{4,5},{5,4},{6,7},{7,6},{8,9},{9,8},{10,11... | collective-permute-start | bytes 393224 | tf_op jit(solution)/shard_map/ppermute | solution.py:555
  45.1 3.6 %collective-permute-start.7 = (f32[16,2048]{1,0:T(8,128)S(1)}, f32[16,2048]{1,0:T(8,128)S(1)}, u32[]{:S(2)}, u32[]{:S(2)}) collective-permute-start(f32[16,2048]{1,0:T(8,128)S(1)} %get-tuple-element.67.f_row1), channel_id=1, source_target_pairs={{0,7},{1,2},{2,1},{3,4},{4,3},{5,6},{6,5},{7,0},{8,15},{9,10},{10,... | collective-permute-start | bytes 393224 | tf_op jit(solution)/shard_map/ppermute | solution.py:555
  48.7 1.3 %all-to-all-done = f32[128,4,128]{2,1,0:T(4,128)S(1)} async-done(((f32[128,4,128]{2,1,0:T(4,128)}), f32[128,4,128]{2,1,0:T(4,128)S(1)}, u32[]{:S(2)}, u32[]{:S(2)}) %all-to-all-start) | async-done | bytes 262176 | tf_op jit(solution)/shard_map/all_to_all | solution.py:607
  50.0 11.7 %sweep.1 = (f32[16,32,2048]{2,1,0:T(8,128)S(1)}, f32[16,32,2048]{2,1,0:T(8,128)S(1)}, f32[16,32,2048]{2,1,0:T(8,128)S(1)}, f32[16,32,2048]{2,1,0:T(8,128)S(1)}, ...) custom-call(f32[16,32,2048]{2,1,0:T(8,128)} %k_hbm.2, ...), custom_call_target="tpu_custom_call" | custom-call | flops 41943040 | bytes 12582912 | tf_op jit(solution)/shard_map/sweep/pallas_call | solution.py:611
  61.7 0.0 collective-permute-done.6.ya
  61.7 0.0 collective-permute-done.4.xa
  61.7 0.0 collective-permute-done.5.xb
  61.7 0.2 mid.1
  61.9 0.1 collective-permute-start.8
  62.0 1.0 %collective-permute-start.9 = (f32[32,2048]{1,0:T(8,128)S(1)}, f32[32,2048]{1,0:T(8,128)S(1)}, u32[]{:S(2)}, u32[]{:S(2)}) collective-permute-start(f32[32,2048]{1,0:T(8,128)S(1)} %get-tuple-element.80.g_pl1), channel_id=1, source_target_pairs={{0,120},{8,16},{16,8},{24,32},{32,24},{40,48},{48,40},{56,64},{64,... | collective-permute-start | bytes 786440 | tf_op jit(solution)/shard_map/ppermute | solution.py:555
  63.1 2.2 %collective-permute-start.10 = (f32[16,2048]{1,0:T(8,128)S(1)}, f32[16,2048]{1,0:T(8,128)S(1)}, u32[]{:S(2)}, u32[]{:S(2)}) collective-permute-start(f32[16,2048]{1,0:T(8,128)S(1)} %get-tuple-element.81.g_row0), channel_id=1, source_target_pairs={{0,1},{1,0},{2,3},{3,2},{4,5},{5,4},{6,7},{7,6},{8,9},{9,8},{10,11... | collective-permute-start | bytes 393224 | tf_op jit(solution)/shard_map/ppermute | solution.py:555
  65.3 1.2 %collective-permute-start.11 = (f32[16,2048]{1,0:T(8,128)S(1)}, f32[16,2048]{1,0:T(8,128)S(1)}, u32[]{:S(2)}, u32[]{:S(2)}) collective-permute-start(f32[16,2048]{1,0:T(8,128)S(1)} %get-tuple-element.82.g_row1), channel_id=1, source_target_pairs={{0,7},{1,2},{2,1},{3,4},{4,3},{5,6},{6,5},{7,0},{8,15},{9,10},{10,... | collective-permute-start | bytes 393224 | tf_op jit(solution)/shard_map/ppermute | solution.py:555
  66.5 4.1 %coarse.1.interp = f32[3,32,2048]{2,1,0:T(8,128)S(1)} custom-call(f32[512,128]{1,0:T(8,128)S(1)} %bitcast.2), custom_call_target="tpu_custom_call" | custom-call | flops 20971520 | bytes 1048576 | tf_op jit(solution)/shard_map/coarse/pallas_call | solution.py:637
  70.5 9.3 %last.1 = (f32[16,32,2048]{2,1,0:T(8,128)}, f32[16,32,2048]{2,1,0:T(8,128)S(1)}) custom-call(f32[16,32,2048]{2,1,0:T(8,128)S(1)} %get-tuple-element.68.w, f32[16,32,2048]{2,1,0:T(8,128)S(1)} %get-tuple-element.69.f, f32[16,32,2048]{2,1,0:T(8,128)S(1)} %get-tuple-element.70.k, f32[16,32,2048]{2,1,0:T(8,128)S(1)} %get-tuple-element.71.cy, ...), custom_call_target="tpu_custom_call" | custom-call | flops 41943040 | bytes 20971520 | tf_op jit(solution)/shard_map/last/pallas_call | solution.py:653
  79.8 0.0 collective-permute-done.10.ya
  79.8 0.0 collective-permute-done.11.yb
  79.8 0.0 collective-permute-done.9.xb
  79.8 1.6 %finish.1 = f32[16,32,2048]{2,1,0:T(8,128)} custom-call(f32[16,32,2048]{2,1,0:T(8,128)} %get-tuple-element.83.src, f32[16,32,2048]{2,1,0:T(8,128)S(1)} %get-tuple-element.84.body, f32[2,32,2048]{2,1,0:T(8,128)S(1)} %get-tuple-element.77.wc_pl, f32[2,16,2048]{2,1,0:T(8,128)S(1)} %get-tuple-element.78.wc_row, ...), custom_call_target="tpu_custom_call", output_to_operand_aliasing={{}: (0, {})} | custom-call | flops 262144 | bytes 3145728 | tf_op jit(solution)/shard_map/finish/pallas_call | solution.py:665
  (10 shorter events, 0.0 us)
Async XLA Ops:
  2.7 26.5 %collective-permute-start = (f32[2,32,2048]{2,1,0:T(8,128)}, f32[2,32,2048]{2,1,0:T(8,128)S(1)}, u32[]{:S(2)}, u32[]{:S(2)}) collective-permute-start(f32[2,32,2048]{2,1,0:T(8,128)} %get-tuple-element.49.pl_a), channel_id=1, source_target_pairs={{0,8},{8,0},{16,24},{24,16},{32,40},{40,32},{48,56},{56,48},{64,72... | collective-permute-start | bytes 1572872 | tf_op jit(solution)/shard_map/ppermute | solution.py:555
  2.8 26.4 %collective-permute-start.1 = (f32[2,32,2048]{2,1,0:T(8,128)}, f32[2,32,2048]{2,1,0:T(8,128)S(1)}, u32[]{:S(2)}, u32[]{:S(2)}) collective-permute-start(f32[2,32,2048]{2,1,0:T(8,128)} %get-tuple-element.50.pl_b), channel_id=1, source_target_pairs={{0,120},{8,16},{16,8},{24,32},{32,24},{40,48},{48,40},{56,64},{64,... | collective-permute-start | bytes 1572872 | tf_op jit(solution)/shard_map/ppermute | solution.py:555
  6.8 18.9 %collective-permute-start.2 = (f32[2,16,2048]{2,1,0:T(8,128)}, f32[2,16,2048]{2,1,0:T(8,128)S(1)}, u32[]{:S(2)}, u32[]{:S(2)}) collective-permute-start(f32[2,16,2048]{2,1,0:T(8,128)} %get-tuple-element.51.rw_a), channel_id=1, source_target_pairs={{0,1},{1,0},{2,3},{3,2},{4,5},{5,4},{6,7},{7,6},{8,9},{9,8},{10,11... | collective-permute-start | bytes 786440 | tf_op jit(solution)/shard_map/ppermute | solution.py:555
  9.7 19.6 %copy-start = (f32[2,32,2048]{2,1,0:T(8,128)S(1)}, f32[2,32,2048]{2,1,0:T(8,128)}, u32[]{:S(2)}) copy-start(f32[2,32,2048]{2,1,0:T(8,128)} %get-tuple-element.49.pl_a) | copy-start | bytes 1572868
  9.7 19.6 %copy-start.1 = (f32[2,32,2048]{2,1,0:T(8,128)S(1)}, f32[2,32,2048]{2,1,0:T(8,128)}, u32[]{:S(2)}) copy-start(f32[2,32,2048]{2,1,0:T(8,128)} %get-tuple-element.50.pl_b) | copy-start | bytes 1572868
  9.7 19.6 %copy-start.2 = (f32[2,16,2048]{2,1,0:T(8,128)S(1)}, f32[2,16,2048]{2,1,0:T(8,128)}, u32[]{:S(2)}) copy-start(f32[2,16,2048]{2,1,0:T(8,128)} %get-tuple-element.51.rw_a) | copy-start | bytes 786436
  9.7 19.6 %copy-start.3 = (f32[2,16,2048]{2,1,0:T(8,128)S(1)}, f32[2,16,2048]{2,1,0:T(8,128)}, u32[]{:S(2)}) copy-start(f32[2,16,2048]{2,1,0:T(8,128)} %get-tuple-element.52.rw_b) | copy-start | bytes 786436
  9.7 19.5 %collective-permute-start.3 = (f32[2,16,2048]{2,1,0:T(8,128)}, f32[2,16,2048]{2,1,0:T(8,128)S(1)}, u32[]{:S(2)}, u32[]{:S(2)}) collective-permute-start(f32[2,16,2048]{2,1,0:T(8,128)} %get-tuple-element.52.rw_b), channel_id=1, source_target_pairs={{0,7},{1,2},{2,1},{3,4},{4,3},{5,6},{6,5},{7,0},{8,15},{9,10},{10,... | collective-permute-start | bytes 786440 | tf_op jit(solution)/shard_map/ppermute | solution.py:555
  31.1 18.9 %all-to-all-start = ((f32[128,4,128]{2,1,0:T(4,128)}), f32[128,4,128]{2,1,0:T(4,128)S(1)}, u32[]{:S(2)}, u32[]{:S(2)}) async-start(f32[128,4,128]{2,1,0:T(4,128)} %bitcast), calls=%async_computation | async-start | bytes 524288 | tf_op jit(solution)/shard_map/all_to_all | solution.py:607
  39.0 22.7 %collective-permute-start.4 = (f32[32,2048]{1,0:T(8,128)S(1)}, f32[32,2048]{1,0:T(8,128)S(1)}, u32[]{:S(2)}, u32[]{:S(2)}) collective-permute-start(f32[32,2048]{1,0:T(8,128)S(1)} %get-tuple-element.64.f_pl0), channel_id=1, source_target_pairs={{0,8},{8,0},{16,24},{24,16},{32,40},{40,32},{48,56},{56,48},{64,72... | collective-permute-start | bytes 786440 | tf_op jit(solution)/shard_map/ppermute | solution.py:555
  39.1 22.6 %collective-permute-start.5 = (f32[32,2048]{1,0:T(8,128)S(1)}, f32[32,2048]{1,0:T(8,128)S(1)}, u32[]{:S(2)}, u32[]{:S(2)}) collective-permute-start(f32[32,2048]{1,0:T(8,128)S(1)} %get-tuple-element.65.f_pl1), channel_id=1, source_target_pairs={{0,120},{8,16},{16,8},{24,32},{32,24},{40,48},{48,40},{56,64},{64,... | collective-permute-start | bytes 786440 | tf_op jit(solution)/shard_map/ppermute | solution.py:555
  42.3 19.4 %collective-permute-start.6 = (f32[16,2048]{1,0:T(8,128)S(1)}, f32[16,2048]{1,0:T(8,128)S(1)}, u32[]{:S(2)}, u32[]{:S(2)}) collective-permute-start(f32[16,2048]{1,0:T(8,128)S(1)} %get-tuple-element.66.f_row0), channel_id=1, source_target_pairs={{0,1},{1,0},{2,3},{3,2},{4,5},{5,4},{6,7},{7,6},{8,9},{9,8},{10,11... | collective-permute-start | bytes 393224 | tf_op jit(solution)/shard_map/ppermute | solution.py:555
  45.1 16.6 %collective-permute-start.7 = (f32[16,2048]{1,0:T(8,128)S(1)}, f32[16,2048]{1,0:T(8,128)S(1)}, u32[]{:S(2)}, u32[]{:S(2)}) collective-permute-start(f32[16,2048]{1,0:T(8,128)S(1)} %get-tuple-element.67.f_row1), channel_id=1, source_target_pairs={{0,7},{1,2},{2,1},{3,4},{4,3},{5,6},{6,5},{7,0},{8,15},{9,10},{10,... | collective-permute-start | bytes 393224 | tf_op jit(solution)/shard_map/ppermute | solution.py:555
  61.9 17.9 %collective-permute-start.8 = (f32[32,2048]{1,0:T(8,128)S(1)}, f32[32,2048]{1,0:T(8,128)S(1)}, u32[]{:S(2)}, u32[]{:S(2)}) collective-permute-start(f32[32,2048]{1,0:T(8,128)S(1)} %get-tuple-element.79.g_pl0), channel_id=1, source_target_pairs={{0,8},{8,0},{16,24},{24,16},{32,40},{40,32},{48,56},{56,48},{64,72... | collective-permute-start | bytes 786440 | tf_op jit(solution)/shard_map/ppermute | solution.py:555
  62.0 17.8 %collective-permute-start.9 = (f32[32,2048]{1,0:T(8,128)S(1)}, f32[32,2048]{1,0:T(8,128)S(1)}, u32[]{:S(2)}, u32[]{:S(2)}) collective-permute-start(f32[32,2048]{1,0:T(8,128)S(1)} %get-tuple-element.80.g_pl1), channel_id=1, source_target_pairs={{0,120},{8,16},{16,8},{24,32},{32,24},{40,48},{48,40},{56,64},{64,... | collective-permute-start | bytes 786440 | tf_op jit(solution)/shard_map/ppermute | solution.py:555
  63.1 16.7 %collective-permute-start.10 = (f32[16,2048]{1,0:T(8,128)S(1)}, f32[16,2048]{1,0:T(8,128)S(1)}, u32[]{:S(2)}, u32[]{:S(2)}) collective-permute-start(f32[16,2048]{1,0:T(8,128)S(1)} %get-tuple-element.81.g_row0), channel_id=1, source_target_pairs={{0,1},{1,0},{2,3},{3,2},{4,5},{5,4},{6,7},{7,6},{8,9},{9,8},{10,11... | collective-permute-start | bytes 393224 | tf_op jit(solution)/shard_map/ppermute | solution.py:555
  65.3 14.6 %collective-permute-start.11 = (f32[16,2048]{1,0:T(8,128)S(1)}, f32[16,2048]{1,0:T(8,128)S(1)}, u32[]{:S(2)}, u32[]{:S(2)}) collective-permute-start(f32[16,2048]{1,0:T(8,128)S(1)} %get-tuple-element.82.g_row1), channel_id=1, source_target_pairs={{0,7},{1,2},{2,1},{3,4},{4,3},{5,6},{6,5},{7,0},{8,15},{9,10},{10,... | collective-permute-start | bytes 393224 | tf_op jit(solution)/shard_map/ppermute | solution.py:555

commit v6 on v5

--- a/solution.py
+++ b/solution.py
@@ -63,30 +63,34 @@
     return 1 - odd, odd
 
 
-def ends_kernel(v, k, rw_a, rw_b, pl_a, pl_b, sems):
-    planes, rows, _ = v.shape
-    xs, ys = edge_spots("gx", planes), edge_spots("gy", rows)
-    copies = []
-    for i, a in enumerate((v, k)):
-        for j, (src, dst) in enumerate(
-            (
-                (a.at[:, ys[0], :], rw_a.at[i]),
-                (a.at[:, ys[1], :], rw_b.at[i]),
-                (a.at[xs[0]], pl_a.at[i]),
-                (a.at[xs[1]], pl_b.at[i]),
-            )
-        ):
-            copies.append(pltpu.make_async_copy(src, dst, sems.at[i, j]))
+def planes_kernel(v, k, pl_a, pl_b, sems):
+    copies = [
+        pltpu.make_async_copy(src.at[x], dst.at[i], sems.at[i, j])
+        for i, src in enumerate((v, k))
+        for j, (x, dst) in enumerate(zip(edge_spots("gx", v.shape[0]), (pl_a, pl_b)))
+    ]
     for c in copies:
         c.start()
     for c in copies:
         c.wait()
 
 
+def rows_kernel(v, k, rw_a, rw_b, sems):
+    copies = [
+        pltpu.make_async_copy(src.at[:, y, :], dst.at[i], sems.at[i, j])
+        for i, src in enumerate((v, k))
+        for j, (y, dst) in enumerate(zip(edge_spots("gy", v.shape[1]), (rw_a, rw_b)))
+    ]
+    for c in copies:
+        c.start()
+    for c in copies:
+        c.wait()
+
+
 def inner_kernel(
     v_hbm, s_hbm, k_hbm,
     w_hbm, f_hbm, w_pl, f_pl, w_row, f_row, sums,
-    v, s, k, w_ref, f_ref, cx, fx, sems, out_sems,
+    v, s, k, w_ref, f_ref, sems, out_sems,
 ):
     planes, rows, cols = v.shape
     sl = strips(rows)
@@ -105,8 +109,6 @@
         for i in range(3):
             copy(i, x).start()
     sums[...] = jnp.zeros_like(sums)
-    fx[...] = jnp.zeros_like(fx)
-    cx[...] = jnp.zeros_like(cx)
     copy(0, 0).wait()
     copy(1, 0).wait()
     sub = lax.broadcasted_iota(jnp.int32, (STRIP, cols), 0)
@@ -119,7 +121,8 @@
             copy(1, x + 1).wait()
 
         copy(2, x).wait()
-        xn = jnp.minimum(x + 1, planes - 1)
+        xn, xp = jnp.minimum(x + 1, planes - 1), jnp.maximum(x - 1, 0)
+        h_prev = jnp.where(x > 0, 0.5, 0.0).astype(F32)
         h_next = jnp.where(x < planes - 1, 0.5, 0.0).astype(F32)
         dc = df = 0.0
         k0, v0 = k[x, sl[0], :], v[x, sl[0], :]
@@ -144,10 +147,10 @@
             dc, df = nc, nf
             c_x = h_next * (k0 + k[xn, a, :])
             f_x = c_x * (v0 - v[xn, a, :])
-            diag = diag + ((cx[a, :] + c_x) + REACTION)
-            res = res + ((fx[a, :] - f_x) + (s[x, a, :] - REACTION * v0))
-            cx[a, :] = c_x
-            fx[a, :] = f_x
+            c_p = h_prev * (k0 + k[xp, a, :])
+            f_p = c_p * (v[xp, a, :] - v0)
+            diag = diag + ((c_p + c_x) + REACTION)
+            res = res + ((f_p - f_x) + (s[x, a, :] - REACTION * v0))
             w = DAMPING / diag
             w_ref[x, a, :] = w
             f_ref[x, a, :] = w * res
@@ -271,7 +274,7 @@
 
 def sweep_kernel(
     k_hbm, w_hbm, f_hbm, w_pl0, w_pl1, w_row0, w_row1, f_pl0, f_pl1, f_row0, f_row1,
-    w, f, k, cy, cz, g_ref, g_pl, g_row, cx, sems,
+    w, f, k, cy, cz, g_ref, g_pl, g_row, sems,
 ):
     planes, rows, cols = w.shape
     sl = strips(rows)
@@ -292,7 +295,6 @@
     for x in range(planes):
         for i in range(3):
             copy(i, x).start()
-    cx[...] = jnp.zeros_like(cx)
     arrive(0)
 
     def plane(x, carry):
@@ -302,6 +304,7 @@
 
         xn = jnp.minimum(x + 1, planes - 1)
         h_next = jnp.where(x < planes - 1, 0.5, 0.0).astype(F32)
+        h_prev = jnp.where(x > 0, 0.5, 0.0).astype(F32)
         xp = jnp.maximum(x - 1, 0)
         dn = 0.0
         k0, u0 = k[x, sl[0], :], f[x, sl[0], :]
@@ -321,8 +324,8 @@
             total = total + (c_y * above + jnp.where(sub0, dn, nd))
             dn = nd
             c_x = h_next * (k0 + k[xn, a, :])
-            total = total + (c_x * f[xn, a, :] + cx[a, :] * f[xp, a, :])
-            cx[a, :] = c_x
+            c_p = h_prev * (k0 + k[xp, a, :])
+            total = total + (c_x * f[xn, a, :] + c_p * f[xp, a, :])
             cy[x, a, :] = c_y
             cz[x, a, :] = c_z
             g_ref[x, a, :] = (2.0 - DAMPING) * u0 + w[x, a, :] * total
@@ -349,7 +352,7 @@
     cross(q_pl, q_row, (o_pl0, o_pl1), (o_row0, o_row1), 1.0)
 
 
-def tile_sums(x, u, k, cx, cy, cz):
+def tile_sums(x, u, k, cy, cz):
     planes, rows, cols = u.shape
     sl = strips(rows)
     tl = [slice(j, j + LANES) for j in range(0, cols, LANES)]
@@ -357,6 +360,7 @@
     sub = lax.broadcasted_iota(jnp.int32, (STRIP, LANES), 0)
     xn, xp = jnp.minimum(x + 1, planes - 1), jnp.maximum(x - 1, 0)
     h_next = jnp.where(x < planes - 1, 0.5, 0.0).astype(F32)
+    h_prev = jnp.where(x > 0, 0.5, 0.0).astype(F32)
     ru = [left(u[x, a, tl[0]]) for a in sl]
     pm = [right(cz[x, a, tl[-1]] * u[x, a, tl[-1]]) for a in sl]
     for j, t in enumerate(tl):
@@ -367,8 +371,8 @@
             u0, c_y, c_z = us[r], cy[x, a, t], cz[x, a, t]
             nu = left(u[x, a, tl[(j + 1) % len(tl)]])
             c_x = h_next * (k[x, a, t] + k[xn, a, t])
-            total = c_x * u[xn, a, t] + cx[a, t] * u[xp, a, t]
-            cx[a, t] = c_x
+            c_p = h_prev * (k[x, a, t] + k[xp, a, t])
+            total = c_x * u[xn, a, t] + c_p * u[xp, a, t]
             total = total + c_z * jnp.where(lane == LANES - 1, nu, ru[r])
             mu = right(c_z * u0)
             total = total + jnp.where(lane == 0, pm[r], mu)
@@ -382,7 +386,7 @@
 
 def last_kernel(
     w, f, k, cy, cz, g_in, interp, g_pl0, g_pl1, g_row0, g_row1,
-    out, body, g, cx, sems,
+    out, body, g, sems,
 ):
     planes, rows, cols = w.shape
 
@@ -395,7 +399,6 @@
         g[x] = g_in[x]
         put_edges(g, x, g_pl0, g_pl1, g_row0, g_row1)
 
-    cx[...] = jnp.zeros_like(cx)
     arrive(0)
 
     def plane(x, carry):
@@ -406,7 +409,7 @@
         offset = ((x % F).astype(F32) + 0.5) / F - 0.5
         weight = jnp.abs(offset)
         side = jnp.where(offset > 0, 2, 0)
-        for a, t, u0, total in tile_sums(x, g, k, cx, cy, cz):
+        for a, t, u0, total in tile_sums(x, g, k, cy, cz):
             coarse = (1.0 - weight) * interp[1, a, t] + weight * interp[side, a, t]
             new = f[x, a, t] + (1.0 - DAMPING) * u0 + coarse
             body[x, a, t] = new + w[x, a, t] * total
@@ -563,18 +566,28 @@
     full, edge, line = sds(planes, rows, cols), sds(rows, cols), sds(planes, cols)
     edges, lines = sds(2, rows, cols), sds(2, planes, cols)
 
-    rw_a, rw_b, pl_a, pl_b = pl.pallas_call(
-        ends_kernel,
-        out_shape=(lines, lines, edges, edges),
+    pl_a, pl_b = pl.pallas_call(
+        planes_kernel,
+        out_shape=(edges, edges),
         in_specs=[HBM] * 2,
-        out_specs=(VM,) * 4,
-        scratch_shapes=[dma((2, 4))],
+        out_specs=(VM,) * 2,
+        scratch_shapes=[dma((2, 2))],
         compiler_params=params(58),
-        cost_estimate=cost(0, n // 2),
-        name="ends",
+        cost_estimate=cost(0, n // 4),
+        name="planes",
+    )(v, k)
+    xa, xb = swap("gx", pl_a, pl_b)
+    rw_a, rw_b = pl.pallas_call(
+        rows_kernel,
+        out_shape=(lines, lines),
+        in_specs=[HBM] * 2,
+        out_specs=(VM,) * 2,
+        scratch_shapes=[dma((2, 2))],
+        compiler_params=params(58),
+        cost_estimate=cost(0, n // 4),
+        name="rows",
     )(v, k)
     ya, yb = swap("gy", rw_a, rw_b)
-    xa, xb = swap("gx", pl_a, pl_b)
 
     w, f, wi_pl, fi_pl, wi_row, fi_row, sums = pl.pallas_call(
         inner_kernel,
@@ -582,7 +595,6 @@
         in_specs=[HBM] * 3,
         out_specs=(HBM,) * 2 + (VM,) * 5,
         scratch_shapes=[vm(full.shape, F32)] * 5
-        + [vm(edge.shape, F32)] * 2
         + [dma((3, planes)), dma((2, planes))],
         compiler_params=params(52),
         cost_estimate=cost(50 * n, 20 * n),
@@ -613,8 +625,8 @@
         out_shape=(full,) * 6 + (edges, lines),
         in_specs=[HBM] * 3 + [VM] * 8,
         out_specs=(VM,) * 8,
-        scratch_shapes=[vm(edge.shape, F32), dma((3, planes))],
-        compiler_params=params(33),
+        scratch_shapes=[dma((3, planes))],
+        compiler_params=params(26),
         cost_estimate=cost(40 * n, 12 * n),
         name="sweep",
     )(k, w, f, *w_edges, *f_edges)
@@ -655,8 +667,8 @@
         out_shape=(full, full),
         in_specs=[VM] * 11,
         out_specs=(HBM, VM),
-        scratch_shapes=[vm(full.shape, F32), vm(edge.shape, F32), dma((planes,))],
-        compiler_params=params(31),
+        scratch_shapes=[vm(full.shape, F32), dma((planes,))],
+        compiler_params=params(22),
         cost_estimate=cost(40 * n, 20 * n),
         name="last",
     )(w, f, k, cy, cz, g, interp, *g_edges)

time: 81.6 us -> 74.8 us (0.917)
  Pallas kernels: 43.2 us -> 38.3 us
  starting transfers between devices: 33.2 us -> 31.6 us
    pallas_call x1, Pallas kernels: 9.26 us -> 5.97 us  [per_device(): pl.pallas_call(last_kernel, out_shape=(full, full), in_specs=[VM] * 11, o...]
    pallas_call x1, Pallas kernels: 11.7 us -> 8.4 us  [per_device(): pl.pallas_call(sweep_kernel, out_shape=(full,) * 6 + (edges, lines), in_s...]
    all_to_all x1, starting transfers between devices: 7.92 us -> 6.25 us  [per_device(): got = lax.all_to_all(payload, ('gx', 'gy'), 0, 0, tiled=True)]
    pallas_call x1 -> x2, Pallas kernels: 2.7 us -> 4.24 us  [the longest x1 2.23 us: per_device(): pl.pallas_call(planes_kernel, out_shape=(edges, edges), in_specs=[HBM] *...]
  transfers between devices with their start and end apart: 13 -> 13, of which waited for: 2 -> 2; matrix products, arithmetic and copies ran while one was open for 0% -> 0% of each run, Pallas kernels for 45% -> 43%
where the time goes in v6:
time: 74.8 us; the launch traced here: 74.6 us
  Pallas kernels  38.3 us (51%)
  starting transfers between devices  31.6 us (42%)
  waiting for transfers between devices  4.42 us (6%)
    ppermute x6, starting transfers between devices, swap(): lax.ppermute(second, axis, others)  17.2 us
    pallas_call x1, Pallas kernels, per_device(): pl.pallas_call(inner_kernel, out_shape=(full, full, edges, edges, lines,...  12 us
    pallas_call x1, Pallas kernels, per_device(): pl.pallas_call(sweep_kernel, out_shape=(full,) * 6 + (edges, lines), in_s...  8.4 us
    ppermute x6, starting transfers between devices, swap(): lax.ppermute(first, axis, pairs)  8.2 us
    all_to_all x1, starting transfers between devices, per_device(): got = lax.all_to_all(payload, ('gx', 'gy'), 0, 0, tiled=True)  6.25 us
    pallas_call x1, Pallas kernels, per_device(): pl.pallas_call(last_kernel, out_shape=(full, full), in_specs=[VM] * 11, o...  5.97 us
    pallas_call x1, Pallas kernels, per_device(): pl.pallas_call(functools.partial(coarse_kernel, nx=nx, ny=ny, rows=rows),...  4.07 us
    ppermute x6, waiting for transfers between devices, swap(): lax.ppermute(second, axis, others)  3.12 us
  transfers between devices with their start and end apart: 13, of which 2 were waited for; matrix products, arithmetic and copies ran while one was open for 0% of the time, Pallas kernels for 43%

profile of v6, /device:TPU:0, one launch (start us, length us, event | category | flops | bytes accessed | tf_op | source)
XLA Modules:
  0.0 74.6 jit_solution(14085037854572936144)
XLA Ops:
  0.0 2.2 %planes.1 = (f32[2,32,2048]{2,1,0:T(8,128)}, f32[2,32,2048]{2,1,0:T(8,128)}) custom-call(f32[16,32,2048]{2,1,0:T(8,128)} %v.3, f32[16,32,2048]{2,1,0:T(8,128)} %k_hbm.2), custom_call_target="tpu_custom_call" | custom-call | bytes 262144 | tf_op jit(solution)/shard_map/planes/pallas_call | solution.py:569
  2.2 0.1 collective-permute-start
  2.3 4.0 %collective-permute-start.1 = (f32[2,32,2048]{2,1,0:T(8,128)}, f32[2,32,2048]{2,1,0:T(8,128)S(1)}, u32[]{:S(2)}, u32[]{:S(2)}) collective-permute-start(f32[2,32,2048]{2,1,0:T(8,128)} %get-tuple-element.50.pl_b), channel_id=1, source_target_pairs={{0,120},{8,16},{16,8},{24,32},{32,24},{40,48},{48,40},{56,64},{64,... | collective-permute-start | bytes 1572872 | tf_op jit(solution)/shard_map/ppermute | solution.py:558
  6.3 2.0 %rows.1 = (f32[2,16,2048]{2,1,0:T(8,128)}, f32[2,16,2048]{2,1,0:T(8,128)}) custom-call(f32[16,32,2048]{2,1,0:T(8,128)} %v.3, f32[16,32,2048]{2,1,0:T(8,128)} %k_hbm.2), custom_call_target="tpu_custom_call" | custom-call | bytes 262144 | tf_op jit(solution)/shard_map/rows/pallas_call | solution.py:580
  8.3 3.0 %collective-permute-start.2 = (f32[2,16,2048]{2,1,0:T(8,128)}, f32[2,16,2048]{2,1,0:T(8,128)S(1)}, u32[]{:S(2)}, u32[]{:S(2)}) collective-permute-start(f32[2,16,2048]{2,1,0:T(8,128)} %get-tuple-element.51.rw_a), channel_id=1, source_target_pairs={{0,1},{1,0},{2,3},{3,2},{4,5},{5,4},{6,7},{7,6},{8,9},{9,8},{10,11... | collective-permute-start | bytes 786440 | tf_op jit(solution)/shard_map/ppermute | solution.py:558
  11.3 4.2 %collective-permute-start.3 = (f32[2,16,2048]{2,1,0:T(8,128)}, f32[2,16,2048]{2,1,0:T(8,128)S(1)}, u32[]{:S(2)}, u32[]{:S(2)}) collective-permute-start(f32[2,16,2048]{2,1,0:T(8,128)} %get-tuple-element.52.rw_b), channel_id=1, source_target_pairs={{0,7},{1,2},{2,1},{3,4},{4,3},{5,6},{6,5},{7,0},{8,15},{9,10},{10,... | collective-permute-start | bytes 786440 | tf_op jit(solution)/shard_map/ppermute | solution.py:558
  15.5 12.0 %inner.1 = (f32[16,32,2048]{2,1,0:T(8,128)}, f32[16,32,2048]{2,1,0:T(8,128)}, f32[2,32,2048]{2,1,0:T(8,128)S(1)}, f32[2,32,2048]{2,1,0:T(8,128)S(1)}, f32[2,16,2...) custom-call(f32[16,32,2048]{2,1,0:T(8,128)} %v.3, f32[16,32,2048]{2,1,0:T(8,128)} %s_hbm.1, ...), custom_call_target="tpu_custom_call" | custom-call | flops 52428800 | bytes 20971520 | tf_op jit(solution)/shard_map/inner/pallas_call | solution.py:592
  27.5 0.0 collective-permute-done.2.ya
  27.5 3.1 %collective-permute-done.3.yb = f32[2,16,2048]{2,1,0:T(8,128)S(1)} collective-permute-done((f32[2,16,2048]{2,1,0:T(8,128)}, f32[2,16,2048]{2,1,0:T(8,128)S(1)}, u32[]{:S(2)}, u32[]{:S(2)}) %collective-permute-start.3) | collective-permute-done | bytes 262176 | tf_op jit(solution)/shard_map/ppermute | solution.py:558
  30.6 0.0 collective-permute-done.xa
  30.6 0.0 collective-permute-done.1.xb
  30.6 1.9 %edge.1 = (f32[32,2048]{1,0:T(8,128)S(1)}, f32[32,2048]{1,0:T(8,128)S(1)}, f32[16,2048]{1,0:T(8,128)S(1)}, f32[16,2048]{1,0:T(8,128)S(1)}, f32[32,2048]{1,0:T(8,...) custom-call(f32[2,32,2048]{2,1,0:T(8,128)S(1)} %get-tuple-element.45, ...), custom_call_target="tpu_custom_call" | custom-call | flops 1310720 | bytes 1048576 | tf_op jit(solution)/shard_map/edge/pallas_call | solution.py:605
  32.5 6.2 %all-to-all-start = ((f32[128,4,128]{2,1,0:T(4,128)}), f32[128,4,128]{2,1,0:T(4,128)S(1)}, u32[]{:S(2)}, u32[]{:S(2)}) async-start(f32[128,4,128]{2,1,0:T(4,128)} %bitcast), calls=%async_computation | async-start | bytes 524288 | tf_op jit(solution)/shard_map/all_to_all | solution.py:619
  38.8 0.1 collective-permute-start.4
  38.9 3.2 %collective-permute-start.5 = (f32[32,2048]{1,0:T(8,128)S(1)}, f32[32,2048]{1,0:T(8,128)S(1)}, u32[]{:S(2)}, u32[]{:S(2)}) collective-permute-start(f32[32,2048]{1,0:T(8,128)S(1)} %get-tuple-element.65.f_pl1), channel_id=1, source_target_pairs={{0,120},{8,16},{16,8},{24,32},{32,24},{40,48},{48,40},{56,64},{64,... | collective-permute-start | bytes 786440 | tf_op jit(solution)/shard_map/ppermute | solution.py:558
  42.0 2.8 %collective-permute-start.6 = (f32[16,2048]{1,0:T(8,128)S(1)}, f32[16,2048]{1,0:T(8,128)S(1)}, u32[]{:S(2)}, u32[]{:S(2)}) collective-permute-start(f32[16,2048]{1,0:T(8,128)S(1)} %get-tuple-element.66.f_row0), channel_id=1, source_target_pairs={{0,1},{1,0},{2,3},{3,2},{4,5},{5,4},{6,7},{7,6},{8,9},{9,8},{10,11... | collective-permute-start | bytes 393224 | tf_op jit(solution)/shard_map/ppermute | solution.py:558
  44.8 3.6 %collective-permute-start.7 = (f32[16,2048]{1,0:T(8,128)S(1)}, f32[16,2048]{1,0:T(8,128)S(1)}, u32[]{:S(2)}, u32[]{:S(2)}) collective-permute-start(f32[16,2048]{1,0:T(8,128)S(1)} %get-tuple-element.67.f_row1), channel_id=1, source_target_pairs={{0,7},{1,2},{2,1},{3,4},{4,3},{5,6},{6,5},{7,0},{8,15},{9,10},{10,... | collective-permute-start | bytes 393224 | tf_op jit(solution)/shard_map/ppermute | solution.py:558
  48.4 1.3 %all-to-all-done = f32[128,4,128]{2,1,0:T(4,128)S(1)} async-done(((f32[128,4,128]{2,1,0:T(4,128)}), f32[128,4,128]{2,1,0:T(4,128)S(1)}, u32[]{:S(2)}, u32[]{:S(2)}) %all-to-all-start) | async-done | bytes 262176 | tf_op jit(solution)/shard_map/all_to_all | solution.py:619
  49.7 8.4 %sweep.1 = (f32[16,32,2048]{2,1,0:T(8,128)S(1)}, f32[16,32,2048]{2,1,0:T(8,128)S(1)}, f32[16,32,2048]{2,1,0:T(8,128)S(1)}, f32[16,32,2048]{2,1,0:T(8,128)S(1)}, ...) custom-call(f32[16,32,2048]{2,1,0:T(8,128)} %k_hbm.2, ...), custom_call_target="tpu_custom_call" | custom-call | flops 41943040 | bytes 12582912 | tf_op jit(solution)/shard_map/sweep/pallas_call | solution.py:623
  58.1 0.0 collective-permute-done.6.ya
  58.1 0.0 collective-permute-done.7.yb
  58.2 0.0 collective-permute-done.4.xa
  58.2 0.2 mid.1
  58.4 0.1 collective-permute-start.8
  58.5 1.0 %collective-permute-start.9 = (f32[32,2048]{1,0:T(8,128)S(1)}, f32[32,2048]{1,0:T(8,128)S(1)}, u32[]{:S(2)}, u32[]{:S(2)}) collective-permute-start(f32[32,2048]{1,0:T(8,128)S(1)} %get-tuple-element.80.g_pl1), channel_id=1, source_target_pairs={{0,120},{8,16},{16,8},{24,32},{32,24},{40,48},{48,40},{56,64},{64,... | collective-permute-start | bytes 786440 | tf_op jit(solution)/shard_map/ppermute | solution.py:558
  59.5 2.2 %collective-permute-start.10 = (f32[16,2048]{1,0:T(8,128)S(1)}, f32[16,2048]{1,0:T(8,128)S(1)}, u32[]{:S(2)}, u32[]{:S(2)}) collective-permute-start(f32[16,2048]{1,0:T(8,128)S(1)} %get-tuple-element.81.g_row0), channel_id=1, source_target_pairs={{0,1},{1,0},{2,3},{3,2},{4,5},{5,4},{6,7},{7,6},{8,9},{9,8},{10,11... | collective-permute-start | bytes 393224 | tf_op jit(solution)/shard_map/ppermute | solution.py:558
  61.7 1.2 %collective-permute-start.11 = (f32[16,2048]{1,0:T(8,128)S(1)}, f32[16,2048]{1,0:T(8,128)S(1)}, u32[]{:S(2)}, u32[]{:S(2)}) collective-permute-start(f32[16,2048]{1,0:T(8,128)S(1)} %get-tuple-element.82.g_row1), channel_id=1, source_target_pairs={{0,7},{1,2},{2,1},{3,4},{4,3},{5,6},{6,5},{7,0},{8,15},{9,10},{10,... | collective-permute-start | bytes 393224 | tf_op jit(solution)/shard_map/ppermute | solution.py:558
  62.9 4.1 %coarse.1.interp = f32[3,32,2048]{2,1,0:T(8,128)S(1)} custom-call(f32[512,128]{1,0:T(8,128)S(1)} %bitcast.2), custom_call_target="tpu_custom_call" | custom-call | flops 20971520 | bytes 1048576 | tf_op jit(solution)/shard_map/coarse/pallas_call | solution.py:649
  67.0 6.0 %last.1 = (f32[16,32,2048]{2,1,0:T(8,128)}, f32[16,32,2048]{2,1,0:T(8,128)S(1)}) custom-call(f32[16,32,2048]{2,1,0:T(8,128)S(1)} %get-tuple-element.68.w, f32[16,32,2048]{2,1,0:T(8,128)S(1)} %get-tuple-element.69.f, f32[16,32,2048]{2,1,0:T(8,128)S(1)} %get-tuple-element.70.k, f32[16,32,2048]{2,1,0:T(8,128)S(1)} %get-tuple-element.71.cy, ...), custom_call_target="tpu_custom_call" | custom-call | flops 41943040 | bytes 20971520 | tf_op jit(solution)/shard_map/last/pallas_call | solution.py:665
  73.0 0.0 collective-permute-done.11.yb
  73.0 0.0 collective-permute-done.8.xa
  73.0 1.6 %finish.1 = f32[16,32,2048]{2,1,0:T(8,128)} custom-call(f32[16,32,2048]{2,1,0:T(8,128)} %get-tuple-element.83.src, f32[16,32,2048]{2,1,0:T(8,128)S(1)} %get-tuple-element.84.body, f32[2,32,2048]{2,1,0:T(8,128)S(1)} %get-tuple-element.77.wc_pl, f32[2,16,2048]{2,1,0:T(8,128)S(1)} %get-tuple-element.78.wc_row, ...), custom_call_target="tpu_custom_call", output_to_operand_aliasing={{}: (0, {})} | custom-call | flops 262144 | bytes 3145728 | tf_op jit(solution)/shard_map/finish/pallas_call | solution.py:677
  (11 shorter events, 0.0 us)
Async XLA Ops:
  2.2 28.3 %collective-permute-start = (f32[2,32,2048]{2,1,0:T(8,128)}, f32[2,32,2048]{2,1,0:T(8,128)S(1)}, u32[]{:S(2)}, u32[]{:S(2)}) collective-permute-start(f32[2,32,2048]{2,1,0:T(8,128)} %get-tuple-element.49.pl_a), channel_id=1, source_target_pairs={{0,8},{8,0},{16,24},{24,16},{32,40},{40,32},{48,56},{56,48},{64,72... | collective-permute-start | bytes 1572872 | tf_op jit(solution)/shard_map/ppermute | solution.py:558
  2.3 28.3 %collective-permute-start.1 = (f32[2,32,2048]{2,1,0:T(8,128)}, f32[2,32,2048]{2,1,0:T(8,128)S(1)}, u32[]{:S(2)}, u32[]{:S(2)}) collective-permute-start(f32[2,32,2048]{2,1,0:T(8,128)} %get-tuple-element.50.pl_b), channel_id=1, source_target_pairs={{0,120},{8,16},{16,8},{24,32},{32,24},{40,48},{48,40},{56,64},{64,... | collective-permute-start | bytes 1572872 | tf_op jit(solution)/shard_map/ppermute | solution.py:558
  8.3 19.2 %collective-permute-start.2 = (f32[2,16,2048]{2,1,0:T(8,128)}, f32[2,16,2048]{2,1,0:T(8,128)S(1)}, u32[]{:S(2)}, u32[]{:S(2)}) collective-permute-start(f32[2,16,2048]{2,1,0:T(8,128)} %get-tuple-element.51.rw_a), channel_id=1, source_target_pairs={{0,1},{1,0},{2,3},{3,2},{4,5},{5,4},{6,7},{7,6},{8,9},{9,8},{10,11... | collective-permute-start | bytes 786440 | tf_op jit(solution)/shard_map/ppermute | solution.py:558
  11.3 19.3 %copy-start = (f32[2,32,2048]{2,1,0:T(8,128)S(1)}, f32[2,32,2048]{2,1,0:T(8,128)}, u32[]{:S(2)}) copy-start(f32[2,32,2048]{2,1,0:T(8,128)} %get-tuple-element.49.pl_a) | copy-start | bytes 1572868
  11.3 19.3 %copy-start.1 = (f32[2,32,2048]{2,1,0:T(8,128)S(1)}, f32[2,32,2048]{2,1,0:T(8,128)}, u32[]{:S(2)}) copy-start(f32[2,32,2048]{2,1,0:T(8,128)} %get-tuple-element.50.pl_b) | copy-start | bytes 1572868
  11.3 19.3 %copy-start.2 = (f32[2,16,2048]{2,1,0:T(8,128)S(1)}, f32[2,16,2048]{2,1,0:T(8,128)}, u32[]{:S(2)}) copy-start(f32[2,16,2048]{2,1,0:T(8,128)} %get-tuple-element.51.rw_a) | copy-start | bytes 786436
  11.3 19.3 %copy-start.3 = (f32[2,16,2048]{2,1,0:T(8,128)S(1)}, f32[2,16,2048]{2,1,0:T(8,128)}, u32[]{:S(2)}) copy-start(f32[2,16,2048]{2,1,0:T(8,128)} %get-tuple-element.52.rw_b) | copy-start | bytes 786436
  11.3 19.3 %collective-permute-start.3 = (f32[2,16,2048]{2,1,0:T(8,128)}, f32[2,16,2048]{2,1,0:T(8,128)S(1)}, u32[]{:S(2)}, u32[]{:S(2)}) collective-permute-start(f32[2,16,2048]{2,1,0:T(8,128)} %get-tuple-element.52.rw_b), channel_id=1, source_target_pairs={{0,7},{1,2},{2,1},{3,4},{4,3},{5,6},{6,5},{7,0},{8,15},{9,10},{10,... | collective-permute-start | bytes 786440 | tf_op jit(solution)/shard_map/ppermute | solution.py:558
  32.5 17.2 %all-to-all-start = ((f32[128,4,128]{2,1,0:T(4,128)}), f32[128,4,128]{2,1,0:T(4,128)S(1)}, u32[]{:S(2)}, u32[]{:S(2)}) async-start(f32[128,4,128]{2,1,0:T(4,128)} %bitcast), calls=%async_computation | async-start | bytes 524288 | tf_op jit(solution)/shard_map/all_to_all | solution.py:619
  38.8 19.4 %collective-permute-start.4 = (f32[32,2048]{1,0:T(8,128)S(1)}, f32[32,2048]{1,0:T(8,128)S(1)}, u32[]{:S(2)}, u32[]{:S(2)}) collective-permute-start(f32[32,2048]{1,0:T(8,128)S(1)} %get-tuple-element.64.f_pl0), channel_id=1, source_target_pairs={{0,8},{8,0},{16,24},{24,16},{32,40},{40,32},{48,56},{56,48},{64,72... | collective-permute-start | bytes 786440 | tf_op jit(solution)/shard_map/ppermute | solution.py:558
  38.9 19.3 %collective-permute-start.5 = (f32[32,2048]{1,0:T(8,128)S(1)}, f32[32,2048]{1,0:T(8,128)S(1)}, u32[]{:S(2)}, u32[]{:S(2)}) collective-permute-start(f32[32,2048]{1,0:T(8,128)S(1)} %get-tuple-element.65.f_pl1), channel_id=1, source_target_pairs={{0,120},{8,16},{16,8},{24,32},{32,24},{40,48},{48,40},{56,64},{64,... | collective-permute-start | bytes 786440 | tf_op jit(solution)/shard_map/ppermute | solution.py:558
  42.0 16.1 %collective-permute-start.6 = (f32[16,2048]{1,0:T(8,128)S(1)}, f32[16,2048]{1,0:T(8,128)S(1)}, u32[]{:S(2)}, u32[]{:S(2)}) collective-permute-start(f32[16,2048]{1,0:T(8,128)S(1)} %get-tuple-element.66.f_row0), channel_id=1, source_target_pairs={{0,1},{1,0},{2,3},{3,2},{4,5},{5,4},{6,7},{7,6},{8,9},{9,8},{10,11... | collective-permute-start | bytes 393224 | tf_op jit(solution)/shard_map/ppermute | solution.py:558
  44.8 13.3 %collective-permute-start.7 = (f32[16,2048]{1,0:T(8,128)S(1)}, f32[16,2048]{1,0:T(8,128)S(1)}, u32[]{:S(2)}, u32[]{:S(2)}) collective-permute-start(f32[16,2048]{1,0:T(8,128)S(1)} %get-tuple-element.67.f_row1), channel_id=1, source_target_pairs={{0,7},{1,2},{2,1},{3,4},{4,3},{5,6},{6,5},{7,0},{8,15},{9,10},{10,... | collective-permute-start | bytes 393224 | tf_op jit(solution)/shard_map/ppermute | solution.py:558
  58.4 14.6 %collective-permute-start.8 = (f32[32,2048]{1,0:T(8,128)S(1)}, f32[32,2048]{1,0:T(8,128)S(1)}, u32[]{:S(2)}, u32[]{:S(2)}) collective-permute-start(f32[32,2048]{1,0:T(8,128)S(1)} %get-tuple-element.79.g_pl0), channel_id=1, source_target_pairs={{0,8},{8,0},{16,24},{24,16},{32,40},{40,32},{48,56},{56,48},{64,72... | collective-permute-start | bytes 786440 | tf_op jit(solution)/shard_map/ppermute | solution.py:558
  58.5 14.5 %collective-permute-start.9 = (f32[32,2048]{1,0:T(8,128)S(1)}, f32[32,2048]{1,0:T(8,128)S(1)}, u32[]{:S(2)}, u32[]{:S(2)}) collective-permute-start(f32[32,2048]{1,0:T(8,128)S(1)} %get-tuple-element.80.g_pl1), channel_id=1, source_target_pairs={{0,120},{8,16},{16,8},{24,32},{32,24},{40,48},{48,40},{56,64},{64,... | collective-permute-start | bytes 786440 | tf_op jit(solution)/shard_map/ppermute | solution.py:558
  59.5 13.4 %collective-permute-start.10 = (f32[16,2048]{1,0:T(8,128)S(1)}, f32[16,2048]{1,0:T(8,128)S(1)}, u32[]{:S(2)}, u32[]{:S(2)}) collective-permute-start(f32[16,2048]{1,0:T(8,128)S(1)} %get-tuple-element.81.g_row0), channel_id=1, source_target_pairs={{0,1},{1,0},{2,3},{3,2},{4,5},{5,4},{6,7},{7,6},{8,9},{9,8},{10,11... | collective-permute-start | bytes 393224 | tf_op jit(solution)/shard_map/ppermute | solution.py:558
  61.7 11.3 %collective-permute-start.11 = (f32[16,2048]{1,0:T(8,128)S(1)}, f32[16,2048]{1,0:T(8,128)S(1)}, u32[]{:S(2)}, u32[]{:S(2)}) collective-permute-start(f32[16,2048]{1,0:T(8,128)S(1)} %get-tuple-element.82.g_row1), channel_id=1, source_target_pairs={{0,7},{1,2},{2,1},{3,4},{4,3},{5,6},{6,5},{7,0},{8,15},{9,10},{10,... | collective-permute-start | bytes 393224 | tf_op jit(solution)/shard_map/ppermute | solution.py:558

commit v7 on v6

--- a/solution.py
+++ b/solution.py
@@ -473,39 +473,51 @@
 
     resid, cond = field(0), field(2)
 
-    def beside(a, t):
-        mine = a[t]
-        nxt = jnp.concatenate([mine[1:], mine[:1]], 0)
-        prv = jnp.concatenate([mine[-1:], mine[:-1]], 0)
-        up = a[1] if t == 0 else pltpu.roll(a[0], ny - 1, 1)
-        down = a[0] if t == 1 else pltpu.roll(a[1], 1, 1)
-        return nxt, prv, up, down, pltpu.roll(mine, 1, 2), pltpu.roll(mine, nz - 1, 2)
-
+    half = 0.5 * COARSE_FACTOR
+
+    def up(a):
+        return pltpu.roll(a, ny - 1, a.ndim - 2)
+
+    def down(a):
+        return pltpu.roll(a, 1, a.ndim - 2)
+
+    def after(a):
+        return pltpu.roll(a, nz - 1, a.ndim - 1)
+
+    def before(a):
+        return pltpu.roll(a, 1, a.ndim - 1)
+
+    inside = half * (cond[0] + cond[1])
+    across = half * (cond[1] + up(cond[0]))
+    coef[2, 0], coef[2, 1] = inside, across
     for t in range(2):
-        cs = [(0.5 * COARSE_FACTOR) * (cond[t] + other) for other in beside(cond, t)]
-        diag = REACTION
-        for c in cs:
-            diag = diag + c
+        c_x = half * (cond[t] + jnp.concatenate([cond[t][1:], cond[t][:1]], 0))
+        c_z = half * (cond[t] + after(cond[t]))
+        diag = REACTION + (c_x + jnp.concatenate([c_x[-1:], c_x[:-1]], 0))
+        diag = diag + (c_z + before(c_z)) + (inside + (across if t else down(across)))
         inv = DAMPING / diag
-        for i, c in enumerate(cs):
-            coef[i, t] = inv * c
+        coef[0, t], coef[1, t], coef[3, t] = c_x, c_z, inv
         b_ref[t] = inv * resid[t]
         u_ref[0, t] = b_ref[t]
 
     def sweep(src, dst):
+        prv, cur = [[u_ref[src, t, p] for t in range(2)] for p in (nx - 1, 0)]
+        c_prv = [coef[0, t, nx - 1] for t in range(2)]
         for p in range(nx):
-            pn, pp = (p + 1) % nx, (p - 1) % nx
-            u = [u_ref[src, t, p] for t in range(2)]
+            nxt = [u_ref[src, t, (p + 1) % nx] for t in range(2)]
+            c_x = [coef[0, t, p] for t in range(2)]
+            c_in, c_ac = coef[2, 0, p], coef[2, 1, p]
+            rows_part = (
+                c_in * cur[1] + down(c_ac * cur[1]),
+                c_in * cur[0] + c_ac * up(cur[0]),
+            )
             for t in range(2):
-                up = u[1] if t == 0 else pltpu.roll(u[0], ny - 1, 0)
-                down = u[0] if t == 1 else pltpu.roll(u[1], 1, 0)
-                a = b_ref[t, p] + (1.0 - DAMPING) * u[t]
-                a = a + coef[0, t, p] * u_ref[src, t, pn]
-                a = a + coef[1, t, p] * u_ref[src, t, pp]
-                c = coef[2, t, p] * up + coef[3, t, p] * down
-                c = c + coef[4, t, p] * pltpu.roll(u[t], 1, 1)
-                c = c + coef[5, t, p] * pltpu.roll(u[t], nz - 1, 1)
-                u_ref[dst, t, p] = a + c
+                c_z = coef[1, t, p]
+                total = (c_x[t] * nxt[t] + c_prv[t] * prv[t]) + rows_part[t]
+                total = total + (c_z * after(cur[t]) + before(c_z * cur[t]))
+                new = (b_ref[t, p] + (1.0 - DAMPING) * cur[t]) + coef[3, t, p] * total
+                u_ref[dst, t, p] = new
+            prv, cur, c_prv = cur, nxt, c_x
 
     def pair(i, carry):
         sweep(0, 1)
@@ -572,7 +584,7 @@
         in_specs=[HBM] * 2,
         out_specs=(VM,) * 2,
         scratch_shapes=[dma((2, 2))],
-        compiler_params=params(58),
+        compiler_params=params(50),
         cost_estimate=cost(0, n // 4),
         name="planes",
     )(v, k)
@@ -583,7 +595,7 @@
         in_specs=[HBM] * 2,
         out_specs=(VM,) * 2,
         scratch_shapes=[dma((2, 2))],
-        compiler_params=params(58),
+        compiler_params=params(50),
         cost_estimate=cost(0, n // 4),
         name="rows",
     )(v, k)
@@ -652,7 +664,7 @@
         in_specs=[VM],
         out_specs=VM,
         scratch_shapes=[
-            vm((6, 2) + cells, F32),
+            vm((4, 2) + cells, F32),
             vm((2,) + cells, F32),
             vm((2, 2) + cells, F32),
         ],

time: 74.8 us -> 73.5 us (0.983)
  Pallas kernels: 38.3 us -> 36.5 us
    pallas_call x1, Pallas kernels: 2.23 us -> 1.22 us  [per_device(): pl.pallas_call(planes_kernel, out_shape=(edges, edges), in_specs=[HBM] *...]
    pallas_call x1, Pallas kernels: 2.01 us -> 1.21 us  [per_device(): pl.pallas_call(rows_kernel, out_shape=(lines, lines), in_specs=[HBM] * 2,...]
where the time goes in v7:
time: 73.5 us; the launch traced here: 73.3 us
  Pallas kernels  36.5 us (50%)
  starting transfers between devices  32.1 us (44%)
  waiting for transfers between devices  4.55 us (6%)
    ppermute x6, starting transfers between devices, swap(): lax.ppermute(second, axis, others)  17.1 us
    pallas_call x1, Pallas kernels, per_device(): pl.pallas_call(inner_kernel, out_shape=(full, full, edges, edges, lines,...  12 us
    pallas_call x1, Pallas kernels, per_device(): pl.pallas_call(sweep_kernel, out_shape=(full,) * 6 + (edges, lines), in_s...  8.4 us
    ppermute x6, starting transfers between devices, swap(): lax.ppermute(first, axis, pairs)  8.2 us
    all_to_all x1, starting transfers between devices, per_device(): got = lax.all_to_all(payload, ('gx', 'gy'), 0, 0, tiled=True)  6.79 us
    pallas_call x1, Pallas kernels, per_device(): pl.pallas_call(last_kernel, out_shape=(full, full), in_specs=[VM] * 11, o...  5.97 us
    pallas_call x1, Pallas kernels, per_device(): pl.pallas_call(functools.partial(coarse_kernel, nx=nx, ny=ny, rows=rows),...  4.09 us
    ppermute x6, waiting for transfers between devices, swap(): lax.ppermute(second, axis, others)  3.26 us
  transfers between devices with their start and end apart: 13, of which 2 were waited for; matrix products, arithmetic and copies ran while one was open for 0% of the time, Pallas kernels for 43%

profile of v7, /device:TPU:0, one launch (start us, length us, event | category | flops | bytes accessed | tf_op | source)
XLA Modules:
  0.0 73.3 jit_solution(8859393149997724035)
XLA Ops:
  0.0 1.2 %planes.1 = (f32[2,32,2048]{2,1,0:T(8,128)S(1)}, f32[2,32,2048]{2,1,0:T(8,128)S(1)}) custom-call(f32[16,32,2048]{2,1,0:T(8,128)} %v.3, f32[16,32,2048]{2,1,0:T(8,128)} %k_hbm.2), custom_call_target="tpu_custom_call" | custom-call | bytes 262144 | tf_op jit(solution)/shard_map/planes/pallas_call | solution.py:581
  1.2 0.1 collective-permute-start
  1.3 4.0 %collective-permute-start.1 = (f32[2,32,2048]{2,1,0:T(8,128)S(1)}, f32[2,32,2048]{2,1,0:T(8,128)S(1)}, u32[]{:S(2)}, u32[]{:S(2)}) collective-permute-start(f32[2,32,2048]{2,1,0:T(8,128)S(1)} %get-tuple-element.50.pl_b), channel_id=1, source_target_pairs={{0,120},{8,16},{16,8},{24,32},{32,24},{40,48},{48,40},{56,64},{64,... | collective-permute-start | bytes 1572872 | tf_op jit(solution)/shard_map/ppermute | solution.py:570
  5.3 1.2 %rows.1 = (f32[2,16,2048]{2,1,0:T(8,128)S(1)}, f32[2,16,2048]{2,1,0:T(8,128)S(1)}) custom-call(f32[16,32,2048]{2,1,0:T(8,128)} %v.3, f32[16,32,2048]{2,1,0:T(8,128)} %k_hbm.2), custom_call_target="tpu_custom_call" | custom-call | bytes 262144 | tf_op jit(solution)/shard_map/rows/pallas_call | solution.py:592
  6.5 3.0 %collective-permute-start.2 = (f32[2,16,2048]{2,1,0:T(8,128)S(1)}, f32[2,16,2048]{2,1,0:T(8,128)S(1)}, u32[]{:S(2)}, u32[]{:S(2)}) collective-permute-start(f32[2,16,2048]{2,1,0:T(8,128)S(1)} %get-tuple-element.51.rw_a), channel_id=1, source_target_pairs={{0,1},{1,0},{2,3},{3,2},{4,5},{5,4},{6,7},{7,6},{8,9},{9,8},{10,11... | collective-permute-start | bytes 786440 | tf_op jit(solution)/shard_map/ppermute | solution.py:570
  9.5 4.1 %collective-permute-start.3 = (f32[2,16,2048]{2,1,0:T(8,128)S(1)}, f32[2,16,2048]{2,1,0:T(8,128)S(1)}, u32[]{:S(2)}, u32[]{:S(2)}) collective-permute-start(f32[2,16,2048]{2,1,0:T(8,128)S(1)} %get-tuple-element.52.rw_b), channel_id=1, source_target_pairs={{0,7},{1,2},{2,1},{3,4},{4,3},{5,6},{6,5},{7,0},{8,15},{9,10},{10,... | collective-permute-start | bytes 786440 | tf_op jit(solution)/shard_map/ppermute | solution.py:570
  13.6 12.0 %inner.1 = (f32[16,32,2048]{2,1,0:T(8,128)}, f32[16,32,2048]{2,1,0:T(8,128)}, f32[2,32,2048]{2,1,0:T(8,128)S(1)}, f32[2,32,2048]{2,1,0:T(8,128)S(1)}, f32[2,16,2...) custom-call(f32[16,32,2048]{2,1,0:T(8,128)} %v.3, f32[16,32,2048]{2,1,0:T(8,128)} %s_hbm.1, ...), custom_call_target="tpu_custom_call" | custom-call | flops 52428800 | bytes 20971520 | tf_op jit(solution)/shard_map/inner/pallas_call | solution.py:604
  25.6 0.0 collective-permute-done.2.ya
  25.6 3.2 %collective-permute-done.3.yb = f32[2,16,2048]{2,1,0:T(8,128)S(1)} collective-permute-done((f32[2,16,2048]{2,1,0:T(8,128)S(1)}, f32[2,16,2048]{2,1,0:T(8,128)S(1)}, u32[]{:S(2)}, u32[]{:S(2)}) %collective-permute-start.3) | collective-permute-done | bytes 262176 | tf_op jit(solution)/shard_map/ppermute | solution.py:570
  28.8 0.0 collective-permute-done.xa
  28.8 0.0 collective-permute-done.1.xb
  28.8 1.9 %edge.1 = (f32[32,2048]{1,0:T(8,128)S(1)}, f32[32,2048]{1,0:T(8,128)S(1)}, f32[16,2048]{1,0:T(8,128)S(1)}, f32[16,2048]{1,0:T(8,128)S(1)}, f32[32,2048]{1,0:T(8,...) custom-call(f32[2,32,2048]{2,1,0:T(8,128)S(1)} %get-tuple-element.45, ...), custom_call_target="tpu_custom_call" | custom-call | flops 1310720 | bytes 1048576 | tf_op jit(solution)/shard_map/edge/pallas_call | solution.py:617
  30.7 6.8 %all-to-all-start = ((f32[128,4,128]{2,1,0:T(4,128)}), f32[128,4,128]{2,1,0:T(4,128)S(1)}, u32[]{:S(2)}, u32[]{:S(2)}) async-start(f32[128,4,128]{2,1,0:T(4,128)} %bitcast), calls=%async_computation | async-start | bytes 524288 | tf_op jit(solution)/shard_map/all_to_all | solution.py:631
  37.5 0.1 collective-permute-start.4
  37.6 3.2 %collective-permute-start.5 = (f32[32,2048]{1,0:T(8,128)S(1)}, f32[32,2048]{1,0:T(8,128)S(1)}, u32[]{:S(2)}, u32[]{:S(2)}) collective-permute-start(f32[32,2048]{1,0:T(8,128)S(1)} %get-tuple-element.65.f_pl1), channel_id=1, source_target_pairs={{0,120},{8,16},{16,8},{24,32},{32,24},{40,48},{48,40},{56,64},{64,... | collective-permute-start | bytes 786440 | tf_op jit(solution)/shard_map/ppermute | solution.py:570
  40.8 2.8 %collective-permute-start.6 = (f32[16,2048]{1,0:T(8,128)S(1)}, f32[16,2048]{1,0:T(8,128)S(1)}, u32[]{:S(2)}, u32[]{:S(2)}) collective-permute-start(f32[16,2048]{1,0:T(8,128)S(1)} %get-tuple-element.66.f_row0), channel_id=1, source_target_pairs={{0,1},{1,0},{2,3},{3,2},{4,5},{5,4},{6,7},{7,6},{8,9},{9,8},{10,11... | collective-permute-start | bytes 393224 | tf_op jit(solution)/shard_map/ppermute | solution.py:570
  43.5 3.6 %collective-permute-start.7 = (f32[16,2048]{1,0:T(8,128)S(1)}, f32[16,2048]{1,0:T(8,128)S(1)}, u32[]{:S(2)}, u32[]{:S(2)}) collective-permute-start(f32[16,2048]{1,0:T(8,128)S(1)} %get-tuple-element.67.f_row1), channel_id=1, source_target_pairs={{0,7},{1,2},{2,1},{3,4},{4,3},{5,6},{6,5},{7,0},{8,15},{9,10},{10,... | collective-permute-start | bytes 393224 | tf_op jit(solution)/shard_map/ppermute | solution.py:570
  47.2 1.3 %all-to-all-done = f32[128,4,128]{2,1,0:T(4,128)S(1)} async-done(((f32[128,4,128]{2,1,0:T(4,128)}), f32[128,4,128]{2,1,0:T(4,128)S(1)}, u32[]{:S(2)}, u32[]{:S(2)}) %all-to-all-start) | async-done | bytes 262176 | tf_op jit(solution)/shard_map/all_to_all | solution.py:631
  48.5 8.4 %sweep.1 = (f32[16,32,2048]{2,1,0:T(8,128)S(1)}, f32[16,32,2048]{2,1,0:T(8,128)S(1)}, f32[16,32,2048]{2,1,0:T(8,128)S(1)}, f32[16,32,2048]{2,1,0:T(8,128)S(1)}, ...) custom-call(f32[16,32,2048]{2,1,0:T(8,128)} %k_hbm.2, ...), custom_call_target="tpu_custom_call" | custom-call | flops 41943040 | bytes 12582912 | tf_op jit(solution)/shard_map/sweep/pallas_call | solution.py:635
  56.9 0.0 collective-permute-done.6.ya
  56.9 0.0 collective-permute-done.7.yb
  56.9 0.0 collective-permute-done.4.xa
  56.9 0.2 mid.1
  57.1 0.1 collective-permute-start.8
  57.2 1.0 %collective-permute-start.9 = (f32[32,2048]{1,0:T(8,128)S(1)}, f32[32,2048]{1,0:T(8,128)S(1)}, u32[]{:S(2)}, u32[]{:S(2)}) collective-permute-start(f32[32,2048]{1,0:T(8,128)S(1)} %get-tuple-element.80.g_pl1), channel_id=1, source_target_pairs={{0,120},{8,16},{16,8},{24,32},{32,24},{40,48},{48,40},{56,64},{64,... | collective-permute-start | bytes 786440 | tf_op jit(solution)/shard_map/ppermute | solution.py:570
  58.2 2.2 %collective-permute-start.10 = (f32[16,2048]{1,0:T(8,128)S(1)}, f32[16,2048]{1,0:T(8,128)S(1)}, u32[]{:S(2)}, u32[]{:S(2)}) collective-permute-start(f32[16,2048]{1,0:T(8,128)S(1)} %get-tuple-element.81.g_row0), channel_id=1, source_target_pairs={{0,1},{1,0},{2,3},{3,2},{4,5},{5,4},{6,7},{7,6},{8,9},{9,8},{10,11... | collective-permute-start | bytes 393224 | tf_op jit(solution)/shard_map/ppermute | solution.py:570
  60.4 1.2 %collective-permute-start.11 = (f32[16,2048]{1,0:T(8,128)S(1)}, f32[16,2048]{1,0:T(8,128)S(1)}, u32[]{:S(2)}, u32[]{:S(2)}) collective-permute-start(f32[16,2048]{1,0:T(8,128)S(1)} %get-tuple-element.82.g_row1), channel_id=1, source_target_pairs={{0,7},{1,2},{2,1},{3,4},{4,3},{5,6},{6,5},{7,0},{8,15},{9,10},{10,... | collective-permute-start | bytes 393224 | tf_op jit(solution)/shard_map/ppermute | solution.py:570
  61.6 4.1 %coarse.1.interp = f32[3,32,2048]{2,1,0:T(8,128)S(1)} custom-call(f32[512,128]{1,0:T(8,128)S(1)} %bitcast.2), custom_call_target="tpu_custom_call" | custom-call | flops 20971520 | bytes 1048576 | tf_op jit(solution)/shard_map/coarse/pallas_call | solution.py:661
  65.7 6.0 %last.1 = (f32[16,32,2048]{2,1,0:T(8,128)}, f32[16,32,2048]{2,1,0:T(8,128)S(1)}) custom-call(f32[16,32,2048]{2,1,0:T(8,128)S(1)} %get-tuple-element.68.w, f32[16,32,2048]{2,1,0:T(8,128)S(1)} %get-tuple-element.69.f, f32[16,32,2048]{2,1,0:T(8,128)S(1)} %get-tuple-element.70.k, f32[16,32,2048]{2,1,0:T(8,128)S(1)} %get-tuple-element.71.cy, ...), custom_call_target="tpu_custom_call" | custom-call | flops 41943040 | bytes 20971520 | tf_op jit(solution)/shard_map/last/pallas_call | solution.py:677
  71.7 0.0 collective-permute-done.11.yb
  71.7 0.0 collective-permute-done.8.xa
  71.7 1.6 %finish.1 = f32[16,32,2048]{2,1,0:T(8,128)} custom-call(f32[16,32,2048]{2,1,0:T(8,128)} %get-tuple-element.83.src, f32[16,32,2048]{2,1,0:T(8,128)S(1)} %get-tuple-element.84.body, f32[2,32,2048]{2,1,0:T(8,128)S(1)} %get-tuple-element.77.wc_pl, f32[2,16,2048]{2,1,0:T(8,128)S(1)} %get-tuple-element.78.wc_row, ...), custom_call_target="tpu_custom_call", output_to_operand_aliasing={{}: (0, {})} | custom-call | flops 262144 | bytes 3145728 | tf_op jit(solution)/shard_map/finish/pallas_call | solution.py:689
  (3 shorter events, 0.0 us)
Async XLA Ops:
  1.2 27.6 %collective-permute-start = (f32[2,32,2048]{2,1,0:T(8,128)S(1)}, f32[2,32,2048]{2,1,0:T(8,128)S(1)}, u32[]{:S(2)}, u32[]{:S(2)}) collective-permute-start(f32[2,32,2048]{2,1,0:T(8,128)S(1)} %get-tuple-element.49.pl_a), channel_id=1, source_target_pairs={{0,8},{8,0},{16,24},{24,16},{32,40},{40,32},{48,56},{56,48},{64,72... | collective-permute-start | bytes 1572872 | tf_op jit(solution)/shard_map/ppermute | solution.py:570
  1.3 27.5 %collective-permute-start.1 = (f32[2,32,2048]{2,1,0:T(8,128)S(1)}, f32[2,32,2048]{2,1,0:T(8,128)S(1)}, u32[]{:S(2)}, u32[]{:S(2)}) collective-permute-start(f32[2,32,2048]{2,1,0:T(8,128)S(1)} %get-tuple-element.50.pl_b), channel_id=1, source_target_pairs={{0,120},{8,16},{16,8},{24,32},{32,24},{40,48},{48,40},{56,64},{64,... | collective-permute-start | bytes 1572872 | tf_op jit(solution)/shard_map/ppermute | solution.py:570
  6.5 19.1 %collective-permute-start.2 = (f32[2,16,2048]{2,1,0:T(8,128)S(1)}, f32[2,16,2048]{2,1,0:T(8,128)S(1)}, u32[]{:S(2)}, u32[]{:S(2)}) collective-permute-start(f32[2,16,2048]{2,1,0:T(8,128)S(1)} %get-tuple-element.51.rw_a), channel_id=1, source_target_pairs={{0,1},{1,0},{2,3},{3,2},{4,5},{5,4},{6,7},{7,6},{8,9},{9,8},{10,11... | collective-permute-start | bytes 786440 | tf_op jit(solution)/shard_map/ppermute | solution.py:570
  9.5 19.3 %collective-permute-start.3 = (f32[2,16,2048]{2,1,0:T(8,128)S(1)}, f32[2,16,2048]{2,1,0:T(8,128)S(1)}, u32[]{:S(2)}, u32[]{:S(2)}) collective-permute-start(f32[2,16,2048]{2,1,0:T(8,128)S(1)} %get-tuple-element.52.rw_b), channel_id=1, source_target_pairs={{0,7},{1,2},{2,1},{3,4},{4,3},{5,6},{6,5},{7,0},{8,15},{9,10},{10,... | collective-permute-start | bytes 786440 | tf_op jit(solution)/shard_map/ppermute | solution.py:570
  30.7 17.8 %all-to-all-start = ((f32[128,4,128]{2,1,0:T(4,128)}), f32[128,4,128]{2,1,0:T(4,128)S(1)}, u32[]{:S(2)}, u32[]{:S(2)}) async-start(f32[128,4,128]{2,1,0:T(4,128)} %bitcast), calls=%async_computation | async-start | bytes 524288 | tf_op jit(solution)/shard_map/all_to_all | solution.py:631
  37.5 19.4 %collective-permute-start.4 = (f32[32,2048]{1,0:T(8,128)S(1)}, f32[32,2048]{1,0:T(8,128)S(1)}, u32[]{:S(2)}, u32[]{:S(2)}) collective-permute-start(f32[32,2048]{1,0:T(8,128)S(1)} %get-tuple-element.64.f_pl0), channel_id=1, source_target_pairs={{0,8},{8,0},{16,24},{24,16},{32,40},{40,32},{48,56},{56,48},{64,72... | collective-permute-start | bytes 786440 | tf_op jit(solution)/shard_map/ppermute | solution.py:570
  37.6 19.3 %collective-permute-start.5 = (f32[32,2048]{1,0:T(8,128)S(1)}, f32[32,2048]{1,0:T(8,128)S(1)}, u32[]{:S(2)}, u32[]{:S(2)}) collective-permute-start(f32[32,2048]{1,0:T(8,128)S(1)} %get-tuple-element.65.f_pl1), channel_id=1, source_target_pairs={{0,120},{8,16},{16,8},{24,32},{32,24},{40,48},{48,40},{56,64},{64,... | collective-permute-start | bytes 786440 | tf_op jit(solution)/shard_map/ppermute | solution.py:570
  40.8 16.1 %collective-permute-start.6 = (f32[16,2048]{1,0:T(8,128)S(1)}, f32[16,2048]{1,0:T(8,128)S(1)}, u32[]{:S(2)}, u32[]{:S(2)}) collective-permute-start(f32[16,2048]{1,0:T(8,128)S(1)} %get-tuple-element.66.f_row0), channel_id=1, source_target_pairs={{0,1},{1,0},{2,3},{3,2},{4,5},{5,4},{6,7},{7,6},{8,9},{9,8},{10,11... | collective-permute-start | bytes 393224 | tf_op jit(solution)/shard_map/ppermute | solution.py:570
  43.5 13.3 %collective-permute-start.7 = (f32[16,2048]{1,0:T(8,128)S(1)}, f32[16,2048]{1,0:T(8,128)S(1)}, u32[]{:S(2)}, u32[]{:S(2)}) collective-permute-start(f32[16,2048]{1,0:T(8,128)S(1)} %get-tuple-element.67.f_row1), channel_id=1, source_target_pairs={{0,7},{1,2},{2,1},{3,4},{4,3},{5,6},{6,5},{7,0},{8,15},{9,10},{10,... | collective-permute-start | bytes 393224 | tf_op jit(solution)/shard_map/ppermute | solution.py:570
  57.1 14.6 %collective-permute-start.8 = (f32[32,2048]{1,0:T(8,128)S(1)}, f32[32,2048]{1,0:T(8,128)S(1)}, u32[]{:S(2)}, u32[]{:S(2)}) collective-permute-start(f32[32,2048]{1,0:T(8,128)S(1)} %get-tuple-element.79.g_pl0), channel_id=1, source_target_pairs={{0,8},{8,0},{16,24},{24,16},{32,40},{40,32},{48,56},{56,48},{64,72... | collective-permute-start | bytes 786440 | tf_op jit(solution)/shard_map/ppermute | solution.py:570
  57.2 14.5 %collective-permute-start.9 = (f32[32,2048]{1,0:T(8,128)S(1)}, f32[32,2048]{1,0:T(8,128)S(1)}, u32[]{:S(2)}, u32[]{:S(2)}) collective-permute-start(f32[32,2048]{1,0:T(8,128)S(1)} %get-tuple-element.80.g_pl1), channel_id=1, source_target_pairs={{0,120},{8,16},{16,8},{24,32},{32,24},{40,48},{48,40},{56,64},{64,... | collective-permute-start | bytes 786440 | tf_op jit(solution)/shard_map/ppermute | solution.py:570
  58.2 13.5 %collective-permute-start.10 = (f32[16,2048]{1,0:T(8,128)S(1)}, f32[16,2048]{1,0:T(8,128)S(1)}, u32[]{:S(2)}, u32[]{:S(2)}) collective-permute-start(f32[16,2048]{1,0:T(8,128)S(1)} %get-tuple-element.81.g_row0), channel_id=1, source_target_pairs={{0,1},{1,0},{2,3},{3,2},{4,5},{5,4},{6,7},{7,6},{8,9},{9,8},{10,11... | collective-permute-start | bytes 393224 | tf_op jit(solution)/shard_map/ppermute | solution.py:570
  60.4 11.3 %collective-permute-start.11 = (f32[16,2048]{1,0:T(8,128)S(1)}, f32[16,2048]{1,0:T(8,128)S(1)}, u32[]{:S(2)}, u32[]{:S(2)}) collective-permute-start(f32[16,2048]{1,0:T(8,128)S(1)} %get-tuple-element.82.g_row1), channel_id=1, source_target_pairs={{0,7},{1,2},{2,1},{3,4},{4,3},{5,6},{6,5},{7,0},{8,15},{9,10},{10,... | collective-permute-start | bytes 393224 | tf_op jit(solution)/shard_map/ppermute | solution.py:570

commit v8 on v6

--- a/solution.py
+++ b/solution.py
@@ -34,19 +34,19 @@
 
 
 def left(a):
-    return pltpu.roll(a, a.shape[1] - 1, 1)
+    return pltpu.roll(a, a.shape[-1] - 1, a.ndim - 1)
 
 
 def right(a):
-    return pltpu.roll(a, 1, 1)
+    return pltpu.roll(a, 1, a.ndim - 1)
 
 
 def upward(a):
-    return pltpu.roll(a, STRIP - 1, 0)
+    return pltpu.roll(a, a.shape[-2] - 1, a.ndim - 2)
 
 
 def downward(a):
-    return pltpu.roll(a, 1, 0)
+    return pltpu.roll(a, 1, a.ndim - 2)
 
 
 def strips(rows):
@@ -272,9 +272,93 @@
             ref[x] = plane[...]
 
 
+def coarse_start(got, coef, b_ref, u_ref):
+    nx, ny, nz = u_ref.shape[2:]
+    per = 2 * 2
+
+    def field(start):
+        return [
+            jnp.stack([got[pl.ds(p * ny * per + start + t, ny, stride=per), :] for p in range(nx)], 0)
+            for t in range(2)
+        ]
+
+    resid, cond = field(0), field(2)
+
+    half = 0.5 * COARSE_FACTOR
+
+    inside = half * (cond[0] + cond[1])
+    across = half * (cond[1] + upward(cond[0]))
+    coef[2, 0], coef[2, 1] = inside, across
+    for t in range(2):
+        c_x = half * (cond[t] + jnp.concatenate([cond[t][1:], cond[t][:1]], 0))
+        c_z = half * (cond[t] + left(cond[t]))
+        diag = REACTION + (c_x + jnp.concatenate([c_x[-1:], c_x[:-1]], 0))
+        diag = diag + (c_z + right(c_z)) + (inside + (across if t else downward(across)))
+        inv = DAMPING / diag
+        coef[0, t], coef[1, t], coef[3, t] = c_x, c_z, inv
+        b_ref[t] = inv * resid[t]
+        u_ref[0, t] = jnp.zeros_like(inv)
+
+
+def coarse_sweep(src, dst, coef, b_ref, u_ref):
+    nx = u_ref.shape[2]
+    prv, cur = [[u_ref[src, t, p] for t in range(2)] for p in (nx - 1, 0)]
+    c_prv = [coef[0, t, nx - 1] for t in range(2)]
+    for p in range(nx):
+        nxt = [u_ref[src, t, (p + 1) % nx] for t in range(2)]
+        c_x = [coef[0, t, p] for t in range(2)]
+        c_in, c_ac = coef[2, 0, p], coef[2, 1, p]
+        rows_part = (
+            c_in * cur[1] + downward(c_ac * cur[1]),
+            c_in * cur[0] + c_ac * upward(cur[0]),
+        )
+        for t in range(2):
+            c_z = coef[1, t, p]
+            total = (c_x[t] * nxt[t] + c_prv[t] * prv[t]) + rows_part[t]
+            total = total + (c_z * left(cur[t]) + right(c_z * cur[t]))
+            new = (b_ref[t, p] + (1.0 - DAMPING) * cur[t]) + coef[3, t, p] * total
+            u_ref[dst, t, p] = new
+        prv, cur, c_prv = cur, nxt, c_x
+
+
+def coarse_finish(u_ref, interp):
+    nx, ny, nz = u_ref.shape[2:]
+    rows = interp.shape[1]
+    gx, gy = lax.axis_index("gx"), lax.axis_index("gy")
+    lines = []
+    for d in (-1, 0, 1):
+        p = lax.rem(gx + d + nx, nx)
+        prev_s, next_s = lax.rem(gy + ny - 1, ny), lax.rem(gy + 1, ny)
+        for t, s in ((1, prev_s), (0, gy), (1, gy), (0, next_s)):
+            lines.append(u_ref[0, t, p, pl.ds(s, 1), :])
+    lines = jnp.concatenate(lines + lines[:4], 0)
+    cols = nz * F
+    cell = lax.broadcasted_iota(jnp.int32, (nz, cols), 0)
+    col = lax.broadcasted_iota(jnp.int32, (nz, cols), 1)
+    base = col // F
+    offset = ((col % F).astype(F32) + 0.5) / F - 0.5
+    side = jnp.where(offset > 0, base + 1, base - 1)
+    side = jnp.where(side < 0, side + nz, jnp.where(side >= nz, side - nz, side))
+    weight = jnp.abs(offset)
+    matrix = jnp.where(cell == base, 1.0 - weight, 0.0) + jnp.where(cell == side, weight, 0.0)
+    wide = joined3(jnp.dot(split3(lines), matrix.astype(BF16), preferred_element_type=F32))
+    sub = lax.broadcasted_iota(jnp.int32, (STRIP, cols), 0)
+    for plane in range(3):
+        for r in range(rows // STRIP):
+            row = r * STRIP + sub
+            off = ((row % F).astype(F32) + 0.5) / F - 0.5
+            wt = jnp.abs(off)
+            block = r * STRIP // F
+            near = block + 1
+            far = near + (1 if (r * STRIP) % F >= F // 2 else -1)
+            a = wide[plane * 4 + near : plane * 4 + near + 1]
+            c = wide[plane * 4 + far : plane * 4 + far + 1]
+            interp[plane, r * STRIP : (r + 1) * STRIP, :] = (1.0 - wt) * a + wt * c
+
+
 def sweep_kernel(
-    k_hbm, w_hbm, f_hbm, w_pl0, w_pl1, w_row0, w_row1, f_pl0, f_pl1, f_row0, f_row1,
-    w, f, k, cy, cz, g_ref, g_pl, g_row, sems,
+    k_hbm, w_hbm, f_hbm, got, w_pl0, w_pl1, w_row0, w_row1, f_pl0, f_pl1, f_row0, f_row1,
+    w, f, k, cy, cz, g_ref, g_pl, g_row, interp, coef, b_ref, u_ref, sems,
 ):
     planes, rows, cols = w.shape
     sl = strips(rows)
@@ -295,6 +379,7 @@
     for x in range(planes):
         for i in range(3):
             copy(i, x).start()
+    coarse_start(got, coef, b_ref, u_ref)
     arrive(0)
 
     def plane(x, carry):
@@ -331,6 +416,9 @@
             g_ref[x, a, :] = (2.0 - DAMPING) * u0 + w[x, a, :] * total
             if r + 1 < len(sl):
                 k0, u0, ku, uu = k1, u1, ku1, uu1
+        for _ in range(CSWEEPS // (2 * planes)):
+            coarse_sweep(0, 1, coef, b_ref, u_ref)
+            coarse_sweep(1, 0, coef, b_ref, u_ref)
         for place, y in ((low, 0), (high, rows - 1)):
             g_row[place, pl.ds(x, 1), :] = g_ref[x, y : y + 1, :]
         return carry
@@ -338,6 +426,7 @@
     lax.fori_loop(0, planes, plane, 0)
     for side, x in enumerate(edge_spots("gx", planes)):
         g_pl[side] = g_ref[x]
+    coarse_finish(u_ref, interp)
 
 
 def mid_kernel(
@@ -461,96 +550,6 @@
         c.wait()
 
 
-def coarse_kernel(got, interp, coef, b_ref, u_ref, *, nx, ny, rows):
-    nz = got.shape[1]
-    per = 2 * 2
-
-    def field(start):
-        return [
-            jnp.stack([got[pl.ds(p * ny * per + start + t, ny, stride=per), :] for p in range(nx)], 0)
-            for t in range(2)
-        ]
-
-    resid, cond = field(0), field(2)
-
-    def beside(a, t):
-        mine = a[t]
-        nxt = jnp.concatenate([mine[1:], mine[:1]], 0)
-        prv = jnp.concatenate([mine[-1:], mine[:-1]], 0)
-        up = a[1] if t == 0 else pltpu.roll(a[0], ny - 1, 1)
-        down = a[0] if t == 1 else pltpu.roll(a[1], 1, 1)
-        return nxt, prv, up, down, pltpu.roll(mine, 1, 2), pltpu.roll(mine, nz - 1, 2)
-
-    for t in range(2):
-        cs = [(0.5 * COARSE_FACTOR) * (cond[t] + other) for other in beside(cond, t)]
-        diag = REACTION
-        for c in cs:
-            diag = diag + c
-        inv = DAMPING / diag
-        for i, c in enumerate(cs):
-            coef[i, t] = inv * c
-        b_ref[t] = inv * resid[t]
-        u_ref[0, t] = b_ref[t]
-
-    def sweep(src, dst):
-        for p in range(nx):
-            pn, pp = (p + 1) % nx, (p - 1) % nx
-            u = [u_ref[src, t, p] for t in range(2)]
-            for t in range(2):
-                up = u[1] if t == 0 else pltpu.roll(u[0], ny - 1, 0)
-                down = u[0] if t == 1 else pltpu.roll(u[1], 1, 0)
-                a = b_ref[t, p] + (1.0 - DAMPING) * u[t]
-                a = a + coef[0, t, p] * u_ref[src, t, pn]
-                a = a + coef[1, t, p] * u_ref[src, t, pp]
-                c = coef[2, t, p] * up + coef[3, t, p] * down
-                c = c + coef[4, t, p] * pltpu.roll(u[t], 1, 1)
-                c = c + coef[5, t, p] * pltpu.roll(u[t], nz - 1, 1)
-                u_ref[dst, t, p] = a + c
-
-    def pair(i, carry):
-        sweep(0, 1)
-        sweep(1, 0)
-        return carry
-
-    steps = CSWEEPS - 1
-    lax.fori_loop(0, steps // 2, pair, 0)
-    last = 0
-    if steps % 2:
-        sweep(0, 1)
-        last = 1
-
-    gx, gy = lax.axis_index("gx"), lax.axis_index("gy")
-    lines = []
-    for d in (-1, 0, 1):
-        p = lax.rem(gx + d + nx, nx)
-        prev_s, next_s = lax.rem(gy + ny - 1, ny), lax.rem(gy + 1, ny)
-        for t, s in ((1, prev_s), (0, gy), (1, gy), (0, next_s)):
-            lines.append(u_ref[last, t, p, pl.ds(s, 1), :])
-    lines = jnp.concatenate(lines + lines[:4], 0)
-    cols = nz * F
-    cell = lax.broadcasted_iota(jnp.int32, (nz, cols), 0)
-    col = lax.broadcasted_iota(jnp.int32, (nz, cols), 1)
-    base = col // F
-    offset = ((col % F).astype(F32) + 0.5) / F - 0.5
-    side = jnp.where(offset > 0, base + 1, base - 1)
-    side = jnp.where(side < 0, side + nz, jnp.where(side >= nz, side - nz, side))
-    weight = jnp.abs(offset)
-    matrix = jnp.where(cell == base, 1.0 - weight, 0.0) + jnp.where(cell == side, weight, 0.0)
-    wide = joined3(jnp.dot(split3(lines), matrix.astype(BF16), preferred_element_type=F32))
-    sub = lax.broadcasted_iota(jnp.int32, (STRIP, cols), 0)
-    for plane in range(3):
-        for r in range(rows // STRIP):
-            row = r * STRIP + sub
-            off = ((row % F).astype(F32) + 0.5) / F - 0.5
-            wt = jnp.abs(off)
-            block = r * STRIP // F
-            near = block + 1
-            far = near + (1 if (r * STRIP) % F >= F // 2 else -1)
-            a = wide[plane * 4 + near : plane * 4 + near + 1]
-            c = wide[plane * 4 + far : plane * 4 + far + 1]
-            interp[plane, r * STRIP : (r + 1) * STRIP, :] = (1.0 - wt) * a + wt * c
-
-
 def swap(axis, first, second):
     count = lax.axis_size(axis)
     pairs = [(i, i ^ 1) for i in range(count)]
@@ -572,7 +571,7 @@
         in_specs=[HBM] * 2,
         out_specs=(VM,) * 2,
         scratch_shapes=[dma((2, 2))],
-        compiler_params=params(58),
+        compiler_params=params(50),
         cost_estimate=cost(0, n // 4),
         name="planes",
     )(v, k)
@@ -583,7 +582,7 @@
         in_specs=[HBM] * 2,
         out_specs=(VM,) * 2,
         scratch_shapes=[dma((2, 2))],
-        compiler_params=params(58),
+        compiler_params=params(50),
         cost_estimate=cost(0, n // 4),
         name="rows",
     )(v, k)
@@ -602,6 +601,7 @@
     )(v, s, k)
 
     devices = nx * ny
+    cells = (nx, ny, cols // F)
     out = pl.pallas_call(
         edge_kernel,
         out_shape=(edge, edge, line, line) * 2 + (edges, lines, sds(devices * 4, cols // F)),
@@ -620,16 +620,18 @@
 
     got, w, f, k = lax.optimization_barrier((got, w, f, k))
 
-    w, f, k, cy, cz, g, g_pl, g_row = pl.pallas_call(
+    w, f, k, cy, cz, g, g_pl, g_row, interp = pl.pallas_call(
         sweep_kernel,
-        out_shape=(full,) * 6 + (edges, lines),
-        in_specs=[HBM] * 3 + [VM] * 8,
-        out_specs=(VM,) * 8,
-        scratch_shapes=[dma((3, planes))],
-        compiler_params=params(26),
+        out_shape=(full,) * 6 + (edges, lines, sds(3, rows, cols)),
+        in_specs=[HBM] * 3 + [VM] * 9,
+        out_specs=(VM,) * 9,
+        scratch_shapes=[
+            vm((4, 2) + cells, F32), vm((2,) + cells, F32), vm((2, 2) + cells, F32), dma((3, planes)),
+        ],
+        compiler_params=params(24),
         cost_estimate=cost(40 * n, 12 * n),
         name="sweep",
-    )(k, w, f, *w_edges, *f_edges)
+    )(k, w, f, got, *w_edges, *f_edges)
 
     g_edges = pl.pallas_call(
         mid_kernel,
@@ -645,23 +647,6 @@
     gya, gyb = swap("gy", g_edges[2], g_edges[3])
     gxa, gxb = swap("gx", g_edges[0], g_edges[1])
 
-    cells = (nx, ny, cols // F)
-    interp = pl.pallas_call(
-        functools.partial(coarse_kernel, nx=nx, ny=ny, rows=rows),
-        out_shape=sds(3, rows, cols),
-        in_specs=[VM],
-        out_specs=VM,
-        scratch_shapes=[
-            vm((6, 2) + cells, F32),
-            vm((2,) + cells, F32),
-            vm((2, 2) + cells, F32),
-        ],
-        compiler_params=params(8),
-        cost_estimate=cost(20 * n, n),
-        name="coarse",
-    )(got)
-
-    b_side = sds(planes - 2, STRIP, cols)
     out, body = pl.pallas_call(
         last_kernel,
         out_shape=(full, full),

time: 74.8 us -> 75.9 us (1.015)
  waiting for transfers between devices: 4.42 us -> 7.16 us
  Pallas kernels: 38.3 us -> 36.3 us
    ppermute x6, waiting for transfers between devices: 3.12 us -> 4.75 us  [swap(): lax.ppermute(second, axis, others)]
    ppermute x6, waiting for transfers between devices: 0.02 us -> 1.13 us  [swap(): lax.ppermute(first, axis, pairs)]
    pallas_call x1, Pallas kernels: 2.23 us -> 1.22 us  [per_device(): pl.pallas_call(planes_kernel, out_shape=(edges, edges), in_specs=[HBM] *...]
    pallas_call x1, Pallas kernels: 2.01 us -> 1.21 us  [per_device(): pl.pallas_call(rows_kernel, out_shape=(lines, lines), in_specs=[HBM] * 2,...]
    pallas_call x2 -> x1, Pallas kernels: 12.5 us -> 12.3 us  [per_device(): pl.pallas_call(sweep_kernel, out_shape=(full,) * 6 + (edges, lines, sds(3...]
  transfers between devices with their start and end apart: 13 -> 13, of which waited for: 2 -> 4; matrix products, arithmetic and copies ran while one was open for 0% -> 0% of each run, Pallas kernels for 43% -> 41%
where the time goes in v8:
time: 75.9 us; the launch traced here: 75.7 us
  Pallas kernels  36.3 us (48%)
  starting transfers between devices  32.1 us (42%)
  waiting for transfers between devices  7.16 us (9%)
    ppermute x6, starting transfers between devices, swap(): lax.ppermute(second, axis, others)  17.1 us
    pallas_call x1, Pallas kernels, per_device(): pl.pallas_call(sweep_kernel, out_shape=(full,) * 6 + (edges, lines, sds(3...  12.3 us
    pallas_call x1, Pallas kernels, per_device(): pl.pallas_call(inner_kernel, out_shape=(full, full, edges, edges, lines,...  12 us
    ppermute x6, starting transfers between devices, swap(): lax.ppermute(first, axis, pairs)  8.2 us
    all_to_all x1, starting transfers between devices, per_device(): got = lax.all_to_all(payload, ('gx', 'gy'), 0, 0, tiled=True)  6.79 us
    pallas_call x1, Pallas kernels, per_device(): pl.pallas_call(last_kernel, out_shape=(full, full), in_specs=[VM] * 11, o...  5.96 us
    ppermute x6, waiting for transfers between devices, swap(): lax.ppermute(second, axis, others)  4.75 us
    pallas_call x1, Pallas kernels, per_device(): pl.pallas_call(edge_kernel, out_shape=(edge, edge, line, line) * 2 + (edg...  1.87 us
  transfers between devices with their start and end apart: 13, of which 4 were waited for; matrix products, arithmetic and copies ran while one was open for 0% of the time, Pallas kernels for 41%

profile of v8, /device:TPU:0, one launch (start us, length us, event | category | flops | bytes accessed | tf_op | source)
XLA Modules:
  0.0 75.7 jit_solution(5419470635215637554)
XLA Ops:
  0.0 1.2 %planes.1 = (f32[2,32,2048]{2,1,0:T(8,128)S(1)}, f32[2,32,2048]{2,1,0:T(8,128)S(1)}) custom-call(f32[16,32,2048]{2,1,0:T(8,128)} %v.3, f32[16,32,2048]{2,1,0:T(8,128)} %k_hbm.2), custom_call_target="tpu_custom_call" | custom-call | bytes 262144 | tf_op jit(solution)/shard_map/planes/pallas_call | solution.py:568
  1.2 0.1 collective-permute-start
  1.3 4.0 %collective-permute-start.1 = (f32[2,32,2048]{2,1,0:T(8,128)S(1)}, f32[2,32,2048]{2,1,0:T(8,128)S(1)}, u32[]{:S(2)}, u32[]{:S(2)}) collective-permute-start(f32[2,32,2048]{2,1,0:T(8,128)S(1)} %get-tuple-element.51.pl_b), channel_id=1, source_target_pairs={{0,120},{8,16},{16,8},{24,32},{32,24},{40,48},{48,40},{56,64},{64,... | collective-permute-start | bytes 1572872 | tf_op jit(solution)/shard_map/ppermute | solution.py:557
  5.3 1.2 %rows.1 = (f32[2,16,2048]{2,1,0:T(8,128)S(1)}, f32[2,16,2048]{2,1,0:T(8,128)S(1)}) custom-call(f32[16,32,2048]{2,1,0:T(8,128)} %v.3, f32[16,32,2048]{2,1,0:T(8,128)} %k_hbm.2), custom_call_target="tpu_custom_call" | custom-call | bytes 262144 | tf_op jit(solution)/shard_map/rows/pallas_call | solution.py:579
  6.5 3.0 %collective-permute-start.2 = (f32[2,16,2048]{2,1,0:T(8,128)S(1)}, f32[2,16,2048]{2,1,0:T(8,128)S(1)}, u32[]{:S(2)}, u32[]{:S(2)}) collective-permute-start(f32[2,16,2048]{2,1,0:T(8,128)S(1)} %get-tuple-element.52.rw_a), channel_id=1, source_target_pairs={{0,1},{1,0},{2,3},{3,2},{4,5},{5,4},{6,7},{7,6},{8,9},{9,8},{10,11... | collective-permute-start | bytes 786440 | tf_op jit(solution)/shard_map/ppermute | solution.py:557
  9.5 4.1 %collective-permute-start.3 = (f32[2,16,2048]{2,1,0:T(8,128)S(1)}, f32[2,16,2048]{2,1,0:T(8,128)S(1)}, u32[]{:S(2)}, u32[]{:S(2)}) collective-permute-start(f32[2,16,2048]{2,1,0:T(8,128)S(1)} %get-tuple-element.53.rw_b), channel_id=1, source_target_pairs={{0,7},{1,2},{2,1},{3,4},{4,3},{5,6},{6,5},{7,0},{8,15},{9,10},{10,... | collective-permute-start | bytes 786440 | tf_op jit(solution)/shard_map/ppermute | solution.py:557
  13.6 12.0 %inner.1 = (f32[16,32,2048]{2,1,0:T(8,128)}, f32[16,32,2048]{2,1,0:T(8,128)}, f32[2,32,2048]{2,1,0:T(8,128)S(1)}, f32[2,32,2048]{2,1,0:T(8,128)S(1)}, f32[2,16,2...) custom-call(f32[16,32,2048]{2,1,0:T(8,128)} %v.3, f32[16,32,2048]{2,1,0:T(8,128)} %s_hbm.1, ...), custom_call_target="tpu_custom_call" | custom-call | flops 52428800 | bytes 20971520 | tf_op jit(solution)/shard_map/inner/pallas_call | solution.py:591
  25.6 0.0 collective-permute-done.2.ya
  25.6 3.2 %collective-permute-done.3.yb = f32[2,16,2048]{2,1,0:T(8,128)S(1)} collective-permute-done((f32[2,16,2048]{2,1,0:T(8,128)S(1)}, f32[2,16,2048]{2,1,0:T(8,128)S(1)}, u32[]{:S(2)}, u32[]{:S(2)}) %collective-permute-start.3) | collective-permute-done | bytes 262176 | tf_op jit(solution)/shard_map/ppermute | solution.py:557
  28.8 0.0 collective-permute-done.xa
  28.8 0.0 collective-permute-done.1.xb
  28.8 1.9 %edge.1 = (f32[32,2048]{1,0:T(8,128)S(1)}, f32[32,2048]{1,0:T(8,128)S(1)}, f32[16,2048]{1,0:T(8,128)S(1)}, f32[16,2048]{1,0:T(8,128)S(1)}, f32[32,2048]{1,0:T(8,...) custom-call(f32[2,32,2048]{2,1,0:T(8,128)S(1)} %get-tuple-element.46, ...), custom_call_target="tpu_custom_call" | custom-call | flops 1310720 | bytes 1048576 | tf_op jit(solution)/shard_map/edge/pallas_call | solution.py:605
  30.7 6.8 %all-to-all-start = ((f32[128,4,128]{2,1,0:T(4,128)}), f32[128,4,128]{2,1,0:T(4,128)S(1)}, u32[]{:S(2)}, u32[]{:S(2)}) async-start(f32[128,4,128]{2,1,0:T(4,128)} %bitcast), calls=%async_computation | async-start | bytes 524288 | tf_op jit(solution)/shard_map/all_to_all | solution.py:619
  37.5 0.1 collective-permute-start.4
  37.6 3.2 %collective-permute-start.5 = (f32[32,2048]{1,0:T(8,128)S(1)}, f32[32,2048]{1,0:T(8,128)S(1)}, u32[]{:S(2)}, u32[]{:S(2)}) collective-permute-start(f32[32,2048]{1,0:T(8,128)S(1)} %get-tuple-element.67.f_pl1), channel_id=1, source_target_pairs={{0,120},{8,16},{16,8},{24,32},{32,24},{40,48},{48,40},{56,64},{64,... | collective-permute-start | bytes 786440 | tf_op jit(solution)/shard_map/ppermute | solution.py:557
  40.8 2.8 %collective-permute-start.6 = (f32[16,2048]{1,0:T(8,128)S(1)}, f32[16,2048]{1,0:T(8,128)S(1)}, u32[]{:S(2)}, u32[]{:S(2)}) collective-permute-start(f32[16,2048]{1,0:T(8,128)S(1)} %get-tuple-element.68.f_row0), channel_id=1, source_target_pairs={{0,1},{1,0},{2,3},{3,2},{4,5},{5,4},{6,7},{7,6},{8,9},{9,8},{10,11... | collective-permute-start | bytes 393224 | tf_op jit(solution)/shard_map/ppermute | solution.py:557
  43.5 3.6 %collective-permute-start.7 = (f32[16,2048]{1,0:T(8,128)S(1)}, f32[16,2048]{1,0:T(8,128)S(1)}, u32[]{:S(2)}, u32[]{:S(2)}) collective-permute-start(f32[16,2048]{1,0:T(8,128)S(1)} %get-tuple-element.69.f_row1), channel_id=1, source_target_pairs={{0,7},{1,2},{2,1},{3,4},{4,3},{5,6},{6,5},{7,0},{8,15},{9,10},{10,... | collective-permute-start | bytes 393224 | tf_op jit(solution)/shard_map/ppermute | solution.py:557
  47.2 1.3 %all-to-all-done = f32[128,4,128]{2,1,0:T(4,128)S(1)} async-done(((f32[128,4,128]{2,1,0:T(4,128)}), f32[128,4,128]{2,1,0:T(4,128)S(1)}, u32[]{:S(2)}, u32[]{:S(2)}) %all-to-all-start) | async-done | bytes 262176 | tf_op jit(solution)/shard_map/all_to_all | solution.py:619
  48.5 12.3 %sweep.1 = (f32[16,32,2048]{2,1,0:T(8,128)S(1)}, f32[16,32,2048]{2,1,0:T(8,128)S(1)}, f32[16,32,2048]{2,1,0:T(8,128)S(1)}, f32[16,32,2048]{2,1,0:T(8,128)S(1)}, ...) custom-call(f32[16,32,2048]{2,1,0:T(8,128)} %k_hbm.2, ...), custom_call_target="tpu_custom_call" | custom-call | flops 41943040 | bytes 12582912 | tf_op jit(solution)/shard_map/sweep/pallas_call | solution.py:623
  60.7 0.0 collective-permute-done.6.ya
  60.7 0.0 collective-permute-done.7.yb
  60.8 0.0 collective-permute-done.4.xa
  60.8 0.2 mid.1
  61.0 0.1 collective-permute-start.8
  61.1 1.0 %collective-permute-start.9 = (f32[32,2048]{1,0:T(8,128)S(1)}, f32[32,2048]{1,0:T(8,128)S(1)}, u32[]{:S(2)}, u32[]{:S(2)}) collective-permute-start(f32[32,2048]{1,0:T(8,128)S(1)} %get-tuple-element.82.g_pl1), channel_id=1, source_target_pairs={{0,120},{8,16},{16,8},{24,32},{32,24},{40,48},{48,40},{56,64},{64,... | collective-permute-start | bytes 786440 | tf_op jit(solution)/shard_map/ppermute | solution.py:557
  62.1 2.2 %collective-permute-start.10 = (f32[16,2048]{1,0:T(8,128)S(1)}, f32[16,2048]{1,0:T(8,128)S(1)}, u32[]{:S(2)}, u32[]{:S(2)}) collective-permute-start(f32[16,2048]{1,0:T(8,128)S(1)} %get-tuple-element.83.g_row0), channel_id=1, source_target_pairs={{0,1},{1,0},{2,3},{3,2},{4,5},{5,4},{6,7},{7,6},{8,9},{9,8},{10,11... | collective-permute-start | bytes 393224 | tf_op jit(solution)/shard_map/ppermute | solution.py:557
  64.3 1.2 %collective-permute-start.11 = (f32[16,2048]{1,0:T(8,128)S(1)}, f32[16,2048]{1,0:T(8,128)S(1)}, u32[]{:S(2)}, u32[]{:S(2)}) collective-permute-start(f32[16,2048]{1,0:T(8,128)S(1)} %get-tuple-element.84.g_row1), channel_id=1, source_target_pairs={{0,7},{1,2},{2,1},{3,4},{4,3},{5,6},{6,5},{7,0},{8,15},{9,10},{10,... | collective-permute-start | bytes 393224 | tf_op jit(solution)/shard_map/ppermute | solution.py:557
  65.5 6.0 %last.1 = (f32[16,32,2048]{2,1,0:T(8,128)}, f32[16,32,2048]{2,1,0:T(8,128)S(1)}) custom-call(f32[16,32,2048]{2,1,0:T(8,128)S(1)} %get-tuple-element.70.w, f32[16,32,2048]{2,1,0:T(8,128)S(1)} %get-tuple-element.71.f, f32[16,32,2048]{2,1,0:T(8,128)S(1)} %get-tuple-element.72.k, f32[16,32,2048]{2,1,0:T(8,128)S(1)} %get-tuple-element.73.cy, ...), custom_call_target="tpu_custom_call" | custom-call | flops 41943040 | bytes 20971520 | tf_op jit(solution)/shard_map/last/pallas_call | solution.py:650
  71.5 1.1 %collective-permute-done.10.ya = f32[16,2048]{1,0:T(8,128)S(1)} collective-permute-done((f32[16,2048]{1,0:T(8,128)S(1)}, f32[16,2048]{1,0:T(8,128)S(1)}, u32[]{:S(2)}, u32[]{:S(2)}) %collective-permute-start.10) | collective-permute-done | bytes 131104 | tf_op jit(solution)/shard_map/ppermute | solution.py:557
  72.6 1.5 %collective-permute-done.11.yb = f32[16,2048]{1,0:T(8,128)S(1)} collective-permute-done((f32[16,2048]{1,0:T(8,128)S(1)}, f32[16,2048]{1,0:T(8,128)S(1)}, u32[]{:S(2)}, u32[]{:S(2)}) %collective-permute-start.11) | collective-permute-done | bytes 131104 | tf_op jit(solution)/shard_map/ppermute | solution.py:557
  74.1 0.0 collective-permute-done.9.xb
  74.1 1.6 %finish.1 = f32[16,32,2048]{2,1,0:T(8,128)} custom-call(f32[16,32,2048]{2,1,0:T(8,128)} %get-tuple-element.85.src, f32[16,32,2048]{2,1,0:T(8,128)S(1)} %get-tuple-element.86.body, f32[2,32,2048]{2,1,0:T(8,128)S(1)} %get-tuple-element.79.wc_pl, f32[2,16,2048]{2,1,0:T(8,128)S(1)} %get-tuple-element.80.wc_row, ...), custom_call_target="tpu_custom_call", output_to_operand_aliasing={{}: (0, {})} | custom-call | flops 262144 | bytes 3145728 | tf_op jit(solution)/shard_map/finish/pallas_call | solution.py:662
  (2 shorter events, 0.0 us)
Async XLA Ops:
  1.2 27.6 %collective-permute-start = (f32[2,32,2048]{2,1,0:T(8,128)S(1)}, f32[2,32,2048]{2,1,0:T(8,128)S(1)}, u32[]{:S(2)}, u32[]{:S(2)}) collective-permute-start(f32[2,32,2048]{2,1,0:T(8,128)S(1)} %get-tuple-element.50.pl_a), channel_id=1, source_target_pairs={{0,8},{8,0},{16,24},{24,16},{32,40},{40,32},{48,56},{56,48},{64,72... | collective-permute-start | bytes 1572872 | tf_op jit(solution)/shard_map/ppermute | solution.py:557
  1.3 27.5 %collective-permute-start.1 = (f32[2,32,2048]{2,1,0:T(8,128)S(1)}, f32[2,32,2048]{2,1,0:T(8,128)S(1)}, u32[]{:S(2)}, u32[]{:S(2)}) collective-permute-start(f32[2,32,2048]{2,1,0:T(8,128)S(1)} %get-tuple-element.51.pl_b), channel_id=1, source_target_pairs={{0,120},{8,16},{16,8},{24,32},{32,24},{40,48},{48,40},{56,64},{64,... | collective-permute-start | bytes 1572872 | tf_op jit(solution)/shard_map/ppermute | solution.py:557
  6.5 19.1 %collective-permute-start.2 = (f32[2,16,2048]{2,1,0:T(8,128)S(1)}, f32[2,16,2048]{2,1,0:T(8,128)S(1)}, u32[]{:S(2)}, u32[]{:S(2)}) collective-permute-start(f32[2,16,2048]{2,1,0:T(8,128)S(1)} %get-tuple-element.52.rw_a), channel_id=1, source_target_pairs={{0,1},{1,0},{2,3},{3,2},{4,5},{5,4},{6,7},{7,6},{8,9},{9,8},{10,11... | collective-permute-start | bytes 786440 | tf_op jit(solution)/shard_map/ppermute | solution.py:557
  9.5 19.3 %collective-permute-start.3 = (f32[2,16,2048]{2,1,0:T(8,128)S(1)}, f32[2,16,2048]{2,1,0:T(8,128)S(1)}, u32[]{:S(2)}, u32[]{:S(2)}) collective-permute-start(f32[2,16,2048]{2,1,0:T(8,128)S(1)} %get-tuple-element.53.rw_b), channel_id=1, source_target_pairs={{0,7},{1,2},{2,1},{3,4},{4,3},{5,6},{6,5},{7,0},{8,15},{9,10},{10,... | collective-permute-start | bytes 786440 | tf_op jit(solution)/shard_map/ppermute | solution.py:557
  30.7 17.8 %all-to-all-start = ((f32[128,4,128]{2,1,0:T(4,128)}), f32[128,4,128]{2,1,0:T(4,128)S(1)}, u32[]{:S(2)}, u32[]{:S(2)}) async-start(f32[128,4,128]{2,1,0:T(4,128)} %bitcast), calls=%async_computation | async-start | bytes 524288 | tf_op jit(solution)/shard_map/all_to_all | solution.py:619
  37.5 23.3 %collective-permute-start.4 = (f32[32,2048]{1,0:T(8,128)S(1)}, f32[32,2048]{1,0:T(8,128)S(1)}, u32[]{:S(2)}, u32[]{:S(2)}) collective-permute-start(f32[32,2048]{1,0:T(8,128)S(1)} %get-tuple-element.66.f_pl0), channel_id=1, source_target_pairs={{0,8},{8,0},{16,24},{24,16},{32,40},{40,32},{48,56},{56,48},{64,72... | collective-permute-start | bytes 786440 | tf_op jit(solution)/shard_map/ppermute | solution.py:557
  37.6 23.2 %collective-permute-start.5 = (f32[32,2048]{1,0:T(8,128)S(1)}, f32[32,2048]{1,0:T(8,128)S(1)}, u32[]{:S(2)}, u32[]{:S(2)}) collective-permute-start(f32[32,2048]{1,0:T(8,128)S(1)} %get-tuple-element.67.f_pl1), channel_id=1, source_target_pairs={{0,120},{8,16},{16,8},{24,32},{32,24},{40,48},{48,40},{56,64},{64,... | collective-permute-start | bytes 786440 | tf_op jit(solution)/shard_map/ppermute | solution.py:557
  40.8 20.0 %collective-permute-start.6 = (f32[16,2048]{1,0:T(8,128)S(1)}, f32[16,2048]{1,0:T(8,128)S(1)}, u32[]{:S(2)}, u32[]{:S(2)}) collective-permute-start(f32[16,2048]{1,0:T(8,128)S(1)} %get-tuple-element.68.f_row0), channel_id=1, source_target_pairs={{0,1},{1,0},{2,3},{3,2},{4,5},{5,4},{6,7},{7,6},{8,9},{9,8},{10,11... | collective-permute-start | bytes 393224 | tf_op jit(solution)/shard_map/ppermute | solution.py:557
  43.5 17.2 %collective-permute-start.7 = (f32[16,2048]{1,0:T(8,128)S(1)}, f32[16,2048]{1,0:T(8,128)S(1)}, u32[]{:S(2)}, u32[]{:S(2)}) collective-permute-start(f32[16,2048]{1,0:T(8,128)S(1)} %get-tuple-element.69.f_row1), channel_id=1, source_target_pairs={{0,7},{1,2},{2,1},{3,4},{4,3},{5,6},{6,5},{7,0},{8,15},{9,10},{10,... | collective-permute-start | bytes 393224 | tf_op jit(solution)/shard_map/ppermute | solution.py:557
  61.0 13.1 %collective-permute-start.8 = (f32[32,2048]{1,0:T(8,128)S(1)}, f32[32,2048]{1,0:T(8,128)S(1)}, u32[]{:S(2)}, u32[]{:S(2)}) collective-permute-start(f32[32,2048]{1,0:T(8,128)S(1)} %get-tuple-element.81.g_pl0), channel_id=1, source_target_pairs={{0,8},{8,0},{16,24},{24,16},{32,40},{40,32},{48,56},{56,48},{64,72... | collective-permute-start | bytes 786440 | tf_op jit(solution)/shard_map/ppermute | solution.py:557
  61.1 13.0 %collective-permute-start.9 = (f32[32,2048]{1,0:T(8,128)S(1)}, f32[32,2048]{1,0:T(8,128)S(1)}, u32[]{:S(2)}, u32[]{:S(2)}) collective-permute-start(f32[32,2048]{1,0:T(8,128)S(1)} %get-tuple-element.82.g_pl1), channel_id=1, source_target_pairs={{0,120},{8,16},{16,8},{24,32},{32,24},{40,48},{48,40},{56,64},{64,... | collective-permute-start | bytes 786440 | tf_op jit(solution)/shard_map/ppermute | solution.py:557
  62.1 10.5 %collective-permute-start.10 = (f32[16,2048]{1,0:T(8,128)S(1)}, f32[16,2048]{1,0:T(8,128)S(1)}, u32[]{:S(2)}, u32[]{:S(2)}) collective-permute-start(f32[16,2048]{1,0:T(8,128)S(1)} %get-tuple-element.83.g_row0), channel_id=1, source_target_pairs={{0,1},{1,0},{2,3},{3,2},{4,5},{5,4},{6,7},{7,6},{8,9},{9,8},{10,11... | collective-permute-start | bytes 393224 | tf_op jit(solution)/shard_map/ppermute | solution.py:557
  64.3 9.8 %collective-permute-start.11 = (f32[16,2048]{1,0:T(8,128)S(1)}, f32[16,2048]{1,0:T(8,128)S(1)}, u32[]{:S(2)}, u32[]{:S(2)}) collective-permute-start(f32[16,2048]{1,0:T(8,128)S(1)} %get-tuple-element.84.g_row1), channel_id=1, source_target_pairs={{0,7},{1,2},{2,1},{3,4},{4,3},{5,6},{6,5},{7,0},{8,15},{9,10},{10,... | collective-permute-start | bytes 393224 | tf_op jit(solution)/shard_map/ppermute | solution.py:557

commit v9 on v7

--- a/solution.py
+++ b/solution.py
@@ -391,9 +391,7 @@
     planes, rows, cols = w.shape
 
     def copy(x):
-        return pltpu.make_async_copy(
-            body.at[x, STRIP : rows - STRIP, :], out.at[x, STRIP : rows - STRIP, :], sems.at[x]
-        )
+        return pltpu.make_async_copy(body.at[x], out.at[x], sems.at[x])
 
     def arrive(x):
         g[x] = g_in[x]
@@ -425,38 +423,29 @@
         copy(x).wait()
 
 
-def finish_kernel(
-    src, body, wc_pl, wc_row, xa, xb, ya, yb, out, s_pl, s_lo, s_hi, q_row, sems
-):
+def finish_kernel(src, body, wc_pl, wc_row, xa, xb, ya, yb, out, s_pl, s_row, q_row, pl_sems, row_sems):
     del src
     planes, rows, cols = out.shape
     xs, ys = edge_spots("gx", planes), edge_spots("gy", rows)
-    low, high = low_high("gy")
-    spots = (
-        (s_lo, out.at[1 : planes - 1, 0:STRIP, :]),
-        (s_hi, out.at[1 : planes - 1, rows - STRIP : rows, :]),
-        (s_pl.at[0], out.at[xs[0]]),
-        (s_pl.at[1], out.at[xs[1]]),
-    )
-    copies = [pltpu.make_async_copy(a, b, sems.at[i]) for i, (a, b) in enumerate(spots)]
-    sub = lax.broadcasted_iota(jnp.int32, (STRIP, cols), 0)
     q_row[0] = wc_row[0] * ya[...]
     q_row[1] = wc_row[1] * yb[...]
-    for x in range(1, planes - 1):
-        q = q_row[low, x : x + 1, :]
-        s_lo[x - 1] = body[x, :STRIP, :] + jnp.where(sub == 0, q, 0.0)
-    copies[0].start()
-    for x in range(1, planes - 1):
-        q = q_row[high, x : x + 1, :]
-        s_hi[x - 1] = body[x, rows - STRIP :, :] + jnp.where(sub == STRIP - 1, q, 0.0)
-    copies[1].start()
+    copies = []
+    for i, (place, y) in enumerate(zip(low_high("gy"), (0, rows - 1))):
+        mine = jnp.concatenate([body[x, y : y + 1, :] for x in range(planes)], 0)
+        s_row[i] = mine + q_row[place]
+        for x in range(1, planes - 1):
+            copies.append(
+                pltpu.make_async_copy(s_row.at[i, x], out.at[x, y, :], row_sems.at[i, x])
+            )
+            copies[-1].start()
     for side, other in ((0, xa), (1, xb)):
         x = xs[side]
         s_pl[side] = body[x] + wc_pl[side] * other[...]
         for b, y in enumerate(ys):
             py = pl.ds(y, 1)
             s_pl[side, py, :] = s_pl[side, py, :] + q_row[b, pl.ds(x, 1), :]
-        copies[2 + side].start()
+        copies.append(pltpu.make_async_copy(s_pl.at[side], out.at[x], pl_sems.at[side]))
+        copies[-1].start()
     for c in copies:
         c.wait()
 
@@ -685,14 +674,14 @@
         name="last",
     )(w, f, k, cy, cz, g, interp, *g_edges)
 
-    b_side = (planes - 2, STRIP, cols)
     return pl.pallas_call(
         finish_kernel,
         out_shape=full,
         in_specs=[HBM] + [VM] * 7,
         out_specs=HBM,
         scratch_shapes=[
-            vm(edges.shape, F32), vm(b_side, F32), vm(b_side, F32), vm(lines.shape, F32), dma((4,)),
+            vm(edges.shape, F32), vm(lines.shape, F32), vm(lines.shape, F32),
+            dma((2,)), dma((2, planes)),
         ],
         input_output_aliases={0: 0},
         compiler_params=params(6),

time: 73.5 us -> 73.4 us (level)
  no operation moved by 1% of the time
where the time goes in v9:
time: 73.4 us; the launch traced here: 73.2 us
  Pallas kernels  36.4 us (50%)
  starting transfers between devices  32.1 us (44%)
  waiting for transfers between devices  4.55 us (6%)
    ppermute x6, starting transfers between devices, swap(): lax.ppermute(second, axis, others)  17.1 us
    pallas_call x1, Pallas kernels, per_device(): pl.pallas_call(inner_kernel, out_shape=(full, full, edges, edges, lines,...  12 us
    pallas_call x1, Pallas kernels, per_device(): pl.pallas_call(sweep_kernel, out_shape=(full,) * 6 + (edges, lines), in_s...  8.4 us
    ppermute x6, starting transfers between devices, swap(): lax.ppermute(first, axis, pairs)  8.2 us
    all_to_all x1, starting transfers between devices, per_device(): got = lax.all_to_all(payload, ('gx', 'gy'), 0, 0, tiled=True)  6.79 us
    pallas_call x1, Pallas kernels, per_device(): pl.pallas_call(last_kernel, out_shape=(full, full), in_specs=[VM] * 11, o...  6.01 us
    pallas_call x1, Pallas kernels, per_device(): pl.pallas_call(functools.partial(coarse_kernel, nx=nx, ny=ny, rows=rows),...  4.09 us
    ppermute x6, waiting for transfers between devices, swap(): lax.ppermute(second, axis, others)  3.26 us
  transfers between devices with their start and end apart: 13, of which 2 were waited for; matrix products, arithmetic and copies ran while one was open for 0% of the time, Pallas kernels for 43%

profile of v9, /device:TPU:0, one launch (start us, length us, event | category | flops | bytes accessed | tf_op | source)
XLA Modules:
  0.0 73.2 jit_solution(12292296036205021028)
XLA Ops:
  0.0 1.2 %planes.1 = (f32[2,32,2048]{2,1,0:T(8,128)S(1)}, f32[2,32,2048]{2,1,0:T(8,128)S(1)}) custom-call(f32[16,32,2048]{2,1,0:T(8,128)} %v.3, f32[16,32,2048]{2,1,0:T(8,128)} %k_hbm.2), custom_call_target="tpu_custom_call" | custom-call | bytes 262144 | tf_op jit(solution)/shard_map/planes/pallas_call | solution.py:570
  1.2 0.1 collective-permute-start
  1.3 4.0 %collective-permute-start.1 = (f32[2,32,2048]{2,1,0:T(8,128)S(1)}, f32[2,32,2048]{2,1,0:T(8,128)S(1)}, u32[]{:S(2)}, u32[]{:S(2)}) collective-permute-start(f32[2,32,2048]{2,1,0:T(8,128)S(1)} %get-tuple-element.50.pl_b), channel_id=1, source_target_pairs={{0,120},{8,16},{16,8},{24,32},{32,24},{40,48},{48,40},{56,64},{64,... | collective-permute-start | bytes 1572872 | tf_op jit(solution)/shard_map/ppermute | solution.py:559
  5.3 1.2 %rows.1 = (f32[2,16,2048]{2,1,0:T(8,128)S(1)}, f32[2,16,2048]{2,1,0:T(8,128)S(1)}) custom-call(f32[16,32,2048]{2,1,0:T(8,128)} %v.3, f32[16,32,2048]{2,1,0:T(8,128)} %k_hbm.2), custom_call_target="tpu_custom_call" | custom-call | bytes 262144 | tf_op jit(solution)/shard_map/rows/pallas_call | solution.py:581
  6.5 3.0 %collective-permute-start.2 = (f32[2,16,2048]{2,1,0:T(8,128)S(1)}, f32[2,16,2048]{2,1,0:T(8,128)S(1)}, u32[]{:S(2)}, u32[]{:S(2)}) collective-permute-start(f32[2,16,2048]{2,1,0:T(8,128)S(1)} %get-tuple-element.51.rw_a), channel_id=1, source_target_pairs={{0,1},{1,0},{2,3},{3,2},{4,5},{5,4},{6,7},{7,6},{8,9},{9,8},{10,11... | collective-permute-start | bytes 786440 | tf_op jit(solution)/shard_map/ppermute | solution.py:559
  9.5 4.1 %collective-permute-start.3 = (f32[2,16,2048]{2,1,0:T(8,128)S(1)}, f32[2,16,2048]{2,1,0:T(8,128)S(1)}, u32[]{:S(2)}, u32[]{:S(2)}) collective-permute-start(f32[2,16,2048]{2,1,0:T(8,128)S(1)} %get-tuple-element.52.rw_b), channel_id=1, source_target_pairs={{0,7},{1,2},{2,1},{3,4},{4,3},{5,6},{6,5},{7,0},{8,15},{9,10},{10,... | collective-permute-start | bytes 786440 | tf_op jit(solution)/shard_map/ppermute | solution.py:559
  13.6 12.0 %inner.1 = (f32[16,32,2048]{2,1,0:T(8,128)}, f32[16,32,2048]{2,1,0:T(8,128)}, f32[2,32,2048]{2,1,0:T(8,128)S(1)}, f32[2,32,2048]{2,1,0:T(8,128)S(1)}, f32[2,16,2...) custom-call(f32[16,32,2048]{2,1,0:T(8,128)} %v.3, f32[16,32,2048]{2,1,0:T(8,128)} %s_hbm.1, ...), custom_call_target="tpu_custom_call" | custom-call | flops 52428800 | bytes 20971520 | tf_op jit(solution)/shard_map/inner/pallas_call | solution.py:593
  25.6 0.0 collective-permute-done.2.ya
  25.6 3.2 %collective-permute-done.3.yb = f32[2,16,2048]{2,1,0:T(8,128)S(1)} collective-permute-done((f32[2,16,2048]{2,1,0:T(8,128)S(1)}, f32[2,16,2048]{2,1,0:T(8,128)S(1)}, u32[]{:S(2)}, u32[]{:S(2)}) %collective-permute-start.3) | collective-permute-done | bytes 262176 | tf_op jit(solution)/shard_map/ppermute | solution.py:559
  28.8 0.0 collective-permute-done.xa
  28.8 0.0 collective-permute-done.1.xb
  28.8 1.9 %edge.1 = (f32[32,2048]{1,0:T(8,128)S(1)}, f32[32,2048]{1,0:T(8,128)S(1)}, f32[16,2048]{1,0:T(8,128)S(1)}, f32[16,2048]{1,0:T(8,128)S(1)}, f32[32,2048]{1,0:T(8,...) custom-call(f32[2,32,2048]{2,1,0:T(8,128)S(1)} %get-tuple-element.45, ...), custom_call_target="tpu_custom_call" | custom-call | flops 1310720 | bytes 1048576 | tf_op jit(solution)/shard_map/edge/pallas_call | solution.py:606
  30.7 6.8 %all-to-all-start = ((f32[128,4,128]{2,1,0:T(4,128)}), f32[128,4,128]{2,1,0:T(4,128)S(1)}, u32[]{:S(2)}, u32[]{:S(2)}) async-start(f32[128,4,128]{2,1,0:T(4,128)} %bitcast), calls=%async_computation | async-start | bytes 524288 | tf_op jit(solution)/shard_map/all_to_all | solution.py:620
  37.5 0.1 collective-permute-start.4
  37.6 3.2 %collective-permute-start.5 = (f32[32,2048]{1,0:T(8,128)S(1)}, f32[32,2048]{1,0:T(8,128)S(1)}, u32[]{:S(2)}, u32[]{:S(2)}) collective-permute-start(f32[32,2048]{1,0:T(8,128)S(1)} %get-tuple-element.65.f_pl1), channel_id=1, source_target_pairs={{0,120},{8,16},{16,8},{24,32},{32,24},{40,48},{48,40},{56,64},{64,... | collective-permute-start | bytes 786440 | tf_op jit(solution)/shard_map/ppermute | solution.py:559
  40.8 2.8 %collective-permute-start.6 = (f32[16,2048]{1,0:T(8,128)S(1)}, f32[16,2048]{1,0:T(8,128)S(1)}, u32[]{:S(2)}, u32[]{:S(2)}) collective-permute-start(f32[16,2048]{1,0:T(8,128)S(1)} %get-tuple-element.66.f_row0), channel_id=1, source_target_pairs={{0,1},{1,0},{2,3},{3,2},{4,5},{5,4},{6,7},{7,6},{8,9},{9,8},{10,11... | collective-permute-start | bytes 393224 | tf_op jit(solution)/shard_map/ppermute | solution.py:559
  43.5 3.6 %collective-permute-start.7 = (f32[16,2048]{1,0:T(8,128)S(1)}, f32[16,2048]{1,0:T(8,128)S(1)}, u32[]{:S(2)}, u32[]{:S(2)}) collective-permute-start(f32[16,2048]{1,0:T(8,128)S(1)} %get-tuple-element.67.f_row1), channel_id=1, source_target_pairs={{0,7},{1,2},{2,1},{3,4},{4,3},{5,6},{6,5},{7,0},{8,15},{9,10},{10,... | collective-permute-start | bytes 393224 | tf_op jit(solution)/shard_map/ppermute | solution.py:559
  47.2 1.3 %all-to-all-done = f32[128,4,128]{2,1,0:T(4,128)S(1)} async-done(((f32[128,4,128]{2,1,0:T(4,128)}), f32[128,4,128]{2,1,0:T(4,128)S(1)}, u32[]{:S(2)}, u32[]{:S(2)}) %all-to-all-start) | async-done | bytes 262176 | tf_op jit(solution)/shard_map/all_to_all | solution.py:620
  48.5 8.4 %sweep.1 = (f32[16,32,2048]{2,1,0:T(8,128)S(1)}, f32[16,32,2048]{2,1,0:T(8,128)S(1)}, f32[16,32,2048]{2,1,0:T(8,128)S(1)}, f32[16,32,2048]{2,1,0:T(8,128)S(1)}, ...) custom-call(f32[16,32,2048]{2,1,0:T(8,128)} %k_hbm.2, ...), custom_call_target="tpu_custom_call" | custom-call | flops 41943040 | bytes 12582912 | tf_op jit(solution)/shard_map/sweep/pallas_call | solution.py:624
  56.9 0.0 collective-permute-done.6.ya
  56.9 0.0 collective-permute-done.7.yb
  56.9 0.2 mid.1
  57.1 0.1 collective-permute-start.8
  57.2 1.0 %collective-permute-start.9 = (f32[32,2048]{1,0:T(8,128)S(1)}, f32[32,2048]{1,0:T(8,128)S(1)}, u32[]{:S(2)}, u32[]{:S(2)}) collective-permute-start(f32[32,2048]{1,0:T(8,128)S(1)} %get-tuple-element.80.g_pl1), channel_id=1, source_target_pairs={{0,120},{8,16},{16,8},{24,32},{32,24},{40,48},{48,40},{56,64},{64,... | collective-permute-start | bytes 786440 | tf_op jit(solution)/shard_map/ppermute | solution.py:559
  58.2 2.2 %collective-permute-start.10 = (f32[16,2048]{1,0:T(8,128)S(1)}, f32[16,2048]{1,0:T(8,128)S(1)}, u32[]{:S(2)}, u32[]{:S(2)}) collective-permute-start(f32[16,2048]{1,0:T(8,128)S(1)} %get-tuple-element.81.g_row0), channel_id=1, source_target_pairs={{0,1},{1,0},{2,3},{3,2},{4,5},{5,4},{6,7},{7,6},{8,9},{9,8},{10,11... | collective-permute-start | bytes 393224 | tf_op jit(solution)/shard_map/ppermute | solution.py:559
  60.4 1.2 %collective-permute-start.11 = (f32[16,2048]{1,0:T(8,128)S(1)}, f32[16,2048]{1,0:T(8,128)S(1)}, u32[]{:S(2)}, u32[]{:S(2)}) collective-permute-start(f32[16,2048]{1,0:T(8,128)S(1)} %get-tuple-element.82.g_row1), channel_id=1, source_target_pairs={{0,7},{1,2},{2,1},{3,4},{4,3},{5,6},{6,5},{7,0},{8,15},{9,10},{10,... | collective-permute-start | bytes 393224 | tf_op jit(solution)/shard_map/ppermute | solution.py:559
  61.6 4.1 %coarse.1.interp = f32[3,32,2048]{2,1,0:T(8,128)S(1)} custom-call(f32[512,128]{1,0:T(8,128)S(1)} %bitcast.2), custom_call_target="tpu_custom_call" | custom-call | flops 20971520 | bytes 1048576 | tf_op jit(solution)/shard_map/coarse/pallas_call | solution.py:650
  65.7 6.0 %last.1 = (f32[16,32,2048]{2,1,0:T(8,128)}, f32[16,32,2048]{2,1,0:T(8,128)S(1)}) custom-call(f32[16,32,2048]{2,1,0:T(8,128)S(1)} %get-tuple-element.68.w, f32[16,32,2048]{2,1,0:T(8,128)S(1)} %get-tuple-element.69.f, f32[16,32,2048]{2,1,0:T(8,128)S(1)} %get-tuple-element.70.k, f32[16,32,2048]{2,1,0:T(8,128)S(1)} %get-tuple-element.71.cy, ...), custom_call_target="tpu_custom_call" | custom-call | flops 41943040 | bytes 20971520 | tf_op jit(solution)/shard_map/last/pallas_call | solution.py:666
  71.7 0.0 collective-permute-done.10.ya
  71.8 0.0 collective-permute-done.11.yb
  71.8 0.0 collective-permute-done.9.xb
  71.8 1.4 %finish.1 = f32[16,32,2048]{2,1,0:T(8,128)} custom-call(f32[16,32,2048]{2,1,0:T(8,128)} %get-tuple-element.83.src, f32[16,32,2048]{2,1,0:T(8,128)S(1)} %get-tuple-element.84.body, f32[2,32,2048]{2,1,0:T(8,128)S(1)} %get-tuple-element.77.wc_pl, f32[2,16,2048]{2,1,0:T(8,128)S(1)} %get-tuple-element.78.wc_row, ...), custom_call_target="tpu_custom_call", output_to_operand_aliasing={{}: (0, {})} | custom-call | flops 262144 | bytes 3145728 | tf_op jit(solution)/shard_map/finish/pallas_call | solution.py:677
  (3 shorter events, 0.0 us)
Async XLA Ops:
  1.2 27.6 %collective-permute-start = (f32[2,32,2048]{2,1,0:T(8,128)S(1)}, f32[2,32,2048]{2,1,0:T(8,128)S(1)}, u32[]{:S(2)}, u32[]{:S(2)}) collective-permute-start(f32[2,32,2048]{2,1,0:T(8,128)S(1)} %get-tuple-element.49.pl_a), channel_id=1, source_target_pairs={{0,8},{8,0},{16,24},{24,16},{32,40},{40,32},{48,56},{56,48},{64,72... | collective-permute-start | bytes 1572872 | tf_op jit(solution)/shard_map/ppermute | solution.py:559
  1.3 27.5 %collective-permute-start.1 = (f32[2,32,2048]{2,1,0:T(8,128)S(1)}, f32[2,32,2048]{2,1,0:T(8,128)S(1)}, u32[]{:S(2)}, u32[]{:S(2)}) collective-permute-start(f32[2,32,2048]{2,1,0:T(8,128)S(1)} %get-tuple-element.50.pl_b), channel_id=1, source_target_pairs={{0,120},{8,16},{16,8},{24,32},{32,24},{40,48},{48,40},{56,64},{64,... | collective-permute-start | bytes 1572872 | tf_op jit(solution)/shard_map/ppermute | solution.py:559
  6.5 19.1 %collective-permute-start.2 = (f32[2,16,2048]{2,1,0:T(8,128)S(1)}, f32[2,16,2048]{2,1,0:T(8,128)S(1)}, u32[]{:S(2)}, u32[]{:S(2)}) collective-permute-start(f32[2,16,2048]{2,1,0:T(8,128)S(1)} %get-tuple-element.51.rw_a), channel_id=1, source_target_pairs={{0,1},{1,0},{2,3},{3,2},{4,5},{5,4},{6,7},{7,6},{8,9},{9,8},{10,11... | collective-permute-start | bytes 786440 | tf_op jit(solution)/shard_map/ppermute | solution.py:559
  9.5 19.3 %collective-permute-start.3 = (f32[2,16,2048]{2,1,0:T(8,128)S(1)}, f32[2,16,2048]{2,1,0:T(8,128)S(1)}, u32[]{:S(2)}, u32[]{:S(2)}) collective-permute-start(f32[2,16,2048]{2,1,0:T(8,128)S(1)} %get-tuple-element.52.rw_b), channel_id=1, source_target_pairs={{0,7},{1,2},{2,1},{3,4},{4,3},{5,6},{6,5},{7,0},{8,15},{9,10},{10,... | collective-permute-start | bytes 786440 | tf_op jit(solution)/shard_map/ppermute | solution.py:559
  30.7 17.8 %all-to-all-start = ((f32[128,4,128]{2,1,0:T(4,128)}), f32[128,4,128]{2,1,0:T(4,128)S(1)}, u32[]{:S(2)}, u32[]{:S(2)}) async-start(f32[128,4,128]{2,1,0:T(4,128)} %bitcast), calls=%async_computation | async-start | bytes 524288 | tf_op jit(solution)/shard_map/all_to_all | solution.py:620
  37.5 19.4 %collective-permute-start.4 = (f32[32,2048]{1,0:T(8,128)S(1)}, f32[32,2048]{1,0:T(8,128)S(1)}, u32[]{:S(2)}, u32[]{:S(2)}) collective-permute-start(f32[32,2048]{1,0:T(8,128)S(1)} %get-tuple-element.64.f_pl0), channel_id=1, source_target_pairs={{0,8},{8,0},{16,24},{24,16},{32,40},{40,32},{48,56},{56,48},{64,72... | collective-permute-start | bytes 786440 | tf_op jit(solution)/shard_map/ppermute | solution.py:559
  37.6 19.3 %collective-permute-start.5 = (f32[32,2048]{1,0:T(8,128)S(1)}, f32[32,2048]{1,0:T(8,128)S(1)}, u32[]{:S(2)}, u32[]{:S(2)}) collective-permute-start(f32[32,2048]{1,0:T(8,128)S(1)} %get-tuple-element.65.f_pl1), channel_id=1, source_target_pairs={{0,120},{8,16},{16,8},{24,32},{32,24},{40,48},{48,40},{56,64},{64,... | collective-permute-start | bytes 786440 | tf_op jit(solution)/shard_map/ppermute | solution.py:559
  40.8 16.1 %collective-permute-start.6 = (f32[16,2048]{1,0:T(8,128)S(1)}, f32[16,2048]{1,0:T(8,128)S(1)}, u32[]{:S(2)}, u32[]{:S(2)}) collective-permute-start(f32[16,2048]{1,0:T(8,128)S(1)} %get-tuple-element.66.f_row0), channel_id=1, source_target_pairs={{0,1},{1,0},{2,3},{3,2},{4,5},{5,4},{6,7},{7,6},{8,9},{9,8},{10,11... | collective-permute-start | bytes 393224 | tf_op jit(solution)/shard_map/ppermute | solution.py:559
  43.5 13.3 %collective-permute-start.7 = (f32[16,2048]{1,0:T(8,128)S(1)}, f32[16,2048]{1,0:T(8,128)S(1)}, u32[]{:S(2)}, u32[]{:S(2)}) collective-permute-start(f32[16,2048]{1,0:T(8,128)S(1)} %get-tuple-element.67.f_row1), channel_id=1, source_target_pairs={{0,7},{1,2},{2,1},{3,4},{4,3},{5,6},{6,5},{7,0},{8,15},{9,10},{10,... | collective-permute-start | bytes 393224 | tf_op jit(solution)/shard_map/ppermute | solution.py:559
  57.1 14.6 %collective-permute-start.8 = (f32[32,2048]{1,0:T(8,128)S(1)}, f32[32,2048]{1,0:T(8,128)S(1)}, u32[]{:S(2)}, u32[]{:S(2)}) collective-permute-start(f32[32,2048]{1,0:T(8,128)S(1)} %get-tuple-element.79.g_pl0), channel_id=1, source_target_pairs={{0,8},{8,0},{16,24},{24,16},{32,40},{40,32},{48,56},{56,48},{64,72... | collective-permute-start | bytes 786440 | tf_op jit(solution)/shard_map/ppermute | solution.py:559
  57.2 14.6 %collective-permute-start.9 = (f32[32,2048]{1,0:T(8,128)S(1)}, f32[32,2048]{1,0:T(8,128)S(1)}, u32[]{:S(2)}, u32[]{:S(2)}) collective-permute-start(f32[32,2048]{1,0:T(8,128)S(1)} %get-tuple-element.80.g_pl1), channel_id=1, source_target_pairs={{0,120},{8,16},{16,8},{24,32},{32,24},{40,48},{48,40},{56,64},{64,... | collective-permute-start | bytes 786440 | tf_op jit(solution)/shard_map/ppermute | solution.py:559
  58.2 13.5 %collective-permute-start.10 = (f32[16,2048]{1,0:T(8,128)S(1)}, f32[16,2048]{1,0:T(8,128)S(1)}, u32[]{:S(2)}, u32[]{:S(2)}) collective-permute-start(f32[16,2048]{1,0:T(8,128)S(1)} %get-tuple-element.81.g_row0), channel_id=1, source_target_pairs={{0,1},{1,0},{2,3},{3,2},{4,5},{5,4},{6,7},{7,6},{8,9},{9,8},{10,11... | collective-permute-start | bytes 393224 | tf_op jit(solution)/shard_map/ppermute | solution.py:559
  60.4 11.3 %collective-permute-start.11 = (f32[16,2048]{1,0:T(8,128)S(1)}, f32[16,2048]{1,0:T(8,128)S(1)}, u32[]{:S(2)}, u32[]{:S(2)}) collective-permute-start(f32[16,2048]{1,0:T(8,128)S(1)} %get-tuple-element.82.g_row1), channel_id=1, source_target_pairs={{0,7},{1,2},{2,1},{3,4},{4,3},{5,6},{6,5},{7,0},{8,15},{9,10},{10,... | collective-permute-start | bytes 393224 | tf_op jit(solution)/shard_map/ppermute | solution.py:559

commit v10 on v9

--- a/solution.py
+++ b/solution.py
@@ -272,6 +272,10 @@
             ref[x] = plane[...]
 
 
+def moved(r, d):
+    return slice(r * STRIP + d, (r + 1) * STRIP + d)
+
+
 def sweep_kernel(
     k_hbm, w_hbm, f_hbm, w_pl0, w_pl1, w_row0, w_row1, f_pl0, f_pl1, f_row0, f_row1,
     w, f, k, cy, cz, g_ref, g_pl, g_row, sems,
@@ -306,31 +310,28 @@
         h_next = jnp.where(x < planes - 1, 0.5, 0.0).astype(F32)
         h_prev = jnp.where(x > 0, 0.5, 0.0).astype(F32)
         xp = jnp.maximum(x - 1, 0)
-        dn = 0.0
-        k0, u0 = k[x, sl[0], :], f[x, sl[0], :]
-        ku, uu = upward(k0), upward(u0)
+        n = len(sl)
         for r, a in enumerate(sl):
+            k0, u0 = k[x, a, :], f[x, a, :]
             c_z = 0.5 * (k0 + left(k0))
             total = c_z * left(u0) + right(c_z * u0)
-            if r + 1 < len(sl):
-                k1, u1 = k[x, sl[r + 1], :], f[x, sl[r + 1], :]
-                ku1, uu1 = upward(k1), upward(u1)
-                c_y = 0.5 * (k0 + jnp.where(sub1, ku1, ku))
-                above = jnp.where(sub1, uu1, uu)
+            above, below = moved(r, 1), moved(r, -1)
+            if r + 1 < n:
+                c_y = 0.5 * (k0 + k[x, above, :])
+                total = total + c_y * f[x, above, :]
             else:
-                c_y = jnp.where(sub1, 0.0, 0.5 * (k0 + ku))
-                above = uu
-            nd = downward(c_y * u0)
-            total = total + (c_y * above + jnp.where(sub0, dn, nd))
-            dn = nd
+                c_y = jnp.where(sub1, 0.0, 0.5 * (k0 + upward(k0)))
+                total = total + c_y * upward(u0)
+            if r > 0:
+                total = total + 0.5 * (k0 + k[x, below, :]) * f[x, below, :]
+            else:
+                total = total + jnp.where(sub0, 0.0, downward(c_y * u0))
             c_x = h_next * (k0 + k[xn, a, :])
             c_p = h_prev * (k0 + k[xp, a, :])
             total = total + (c_x * f[xn, a, :] + c_p * f[xp, a, :])
             cy[x, a, :] = c_y
             cz[x, a, :] = c_z
             g_ref[x, a, :] = (2.0 - DAMPING) * u0 + w[x, a, :] * total
-            if r + 1 < len(sl):
-                k0, u0, ku, uu = k1, u1, ku1, uu1
         for place, y in ((low, 0), (high, rows - 1)):
             g_row[place, pl.ds(x, 1), :] = g_ref[x, y : y + 1, :]
         return carry
@@ -364,11 +365,8 @@
     ru = [left(u[x, a, tl[0]]) for a in sl]
     pm = [right(cz[x, a, tl[-1]] * u[x, a, tl[-1]]) for a in sl]
     for j, t in enumerate(tl):
-        us = [u[x, a, t] for a in sl]
-        uu = [upward(a) for a in us]
-        dn = 0.0
         for r, a in enumerate(sl):
-            u0, c_y, c_z = us[r], cy[x, a, t], cz[x, a, t]
+            u0, c_y, c_z = u[x, a, t], cy[x, a, t], cz[x, a, t]
             nu = left(u[x, a, tl[(j + 1) % len(tl)]])
             c_x = h_next * (k[x, a, t] + k[xn, a, t])
             c_p = h_prev * (k[x, a, t] + k[xp, a, t])
@@ -377,10 +375,14 @@
             mu = right(c_z * u0)
             total = total + jnp.where(lane == 0, pm[r], mu)
             ru[r], pm[r] = nu, mu
-            above = jnp.where(sub == STRIP - 1, uu[r + 1], uu[r]) if r + 1 < len(sl) else uu[r]
-            nd = downward(c_y * u0)
-            total = total + (c_y * above + jnp.where(sub == 0, dn, nd))
-            dn = nd
+            if r + 1 < len(sl):
+                total = total + c_y * u[x, moved(r, 1), t]
+            else:
+                total = total + c_y * upward(u0)
+            if r > 0:
+                total = total + cy[x, moved(r, -1), t] * u[x, moved(r, -1), t]
+            else:
+                total = total + jnp.where(sub == 0, 0.0, downward(c_y * u0))
             yield a, t, u0, total
 
 

time: 73.4 us -> 73.4 us (level)
  no operation moved by 1% of the time
where the time goes in v10:
time: 73.4 us; the launch traced here: 73.3 us
  Pallas kernels  36.4 us (50%)
  starting transfers between devices  32.1 us (44%)
  waiting for transfers between devices  4.55 us (6%)
    ppermute x6, starting transfers between devices, swap(): lax.ppermute(second, axis, others)  17.1 us
    pallas_call x1, Pallas kernels, per_device(): pl.pallas_call(inner_kernel, out_shape=(full, full, edges, edges, lines,...  12 us
    pallas_call x1, Pallas kernels, per_device(): pl.pallas_call(sweep_kernel, out_shape=(full,) * 6 + (edges, lines), in_s...  8.48 us
    ppermute x6, starting transfers between devices, swap(): lax.ppermute(first, axis, pairs)  8.2 us
    all_to_all x1, starting transfers between devices, per_device(): got = lax.all_to_all(payload, ('gx', 'gy'), 0, 0, tiled=True)  6.79 us
    pallas_call x1, Pallas kernels, per_device(): pl.pallas_call(last_kernel, out_shape=(full, full), in_specs=[VM] * 11, o...  6 us
    pallas_call x1, Pallas kernels, per_device(): pl.pallas_call(functools.partial(coarse_kernel, nx=nx, ny=ny, rows=rows),...  4.09 us
    ppermute x6, waiting for transfers between devices, swap(): lax.ppermute(second, axis, others)  3.26 us
  transfers between devices with their start and end apart: 13, of which 2 were waited for; matrix products, arithmetic and copies ran while one was open for 0% of the time, Pallas kernels for 43%

profile of v10, /device:TPU:0, one launch (start us, length us, event | category | flops | bytes accessed | tf_op | source)
XLA Modules:
  0.0 73.3 jit_solution(2366774887010371443)
XLA Ops:
  0.0 1.2 %planes.1 = (f32[2,32,2048]{2,1,0:T(8,128)S(1)}, f32[2,32,2048]{2,1,0:T(8,128)S(1)}) custom-call(f32[16,32,2048]{2,1,0:T(8,128)} %v.3, f32[16,32,2048]{2,1,0:T(8,128)} %k_hbm.2), custom_call_target="tpu_custom_call" | custom-call | bytes 262144 | tf_op jit(solution)/shard_map/planes/pallas_call | solution.py:572
  1.2 0.1 collective-permute-start
  1.3 4.0 %collective-permute-start.1 = (f32[2,32,2048]{2,1,0:T(8,128)S(1)}, f32[2,32,2048]{2,1,0:T(8,128)S(1)}, u32[]{:S(2)}, u32[]{:S(2)}) collective-permute-start(f32[2,32,2048]{2,1,0:T(8,128)S(1)} %get-tuple-element.50.pl_b), channel_id=1, source_target_pairs={{0,120},{8,16},{16,8},{24,32},{32,24},{40,48},{48,40},{56,64},{64,... | collective-permute-start | bytes 1572872 | tf_op jit(solution)/shard_map/ppermute | solution.py:561
  5.3 1.2 %rows.1 = (f32[2,16,2048]{2,1,0:T(8,128)S(1)}, f32[2,16,2048]{2,1,0:T(8,128)S(1)}) custom-call(f32[16,32,2048]{2,1,0:T(8,128)} %v.3, f32[16,32,2048]{2,1,0:T(8,128)} %k_hbm.2), custom_call_target="tpu_custom_call" | custom-call | bytes 262144 | tf_op jit(solution)/shard_map/rows/pallas_call | solution.py:583
  6.5 3.0 %collective-permute-start.2 = (f32[2,16,2048]{2,1,0:T(8,128)S(1)}, f32[2,16,2048]{2,1,0:T(8,128)S(1)}, u32[]{:S(2)}, u32[]{:S(2)}) collective-permute-start(f32[2,16,2048]{2,1,0:T(8,128)S(1)} %get-tuple-element.51.rw_a), channel_id=1, source_target_pairs={{0,1},{1,0},{2,3},{3,2},{4,5},{5,4},{6,7},{7,6},{8,9},{9,8},{10,11... | collective-permute-start | bytes 786440 | tf_op jit(solution)/shard_map/ppermute | solution.py:561
  9.5 4.1 %collective-permute-start.3 = (f32[2,16,2048]{2,1,0:T(8,128)S(1)}, f32[2,16,2048]{2,1,0:T(8,128)S(1)}, u32[]{:S(2)}, u32[]{:S(2)}) collective-permute-start(f32[2,16,2048]{2,1,0:T(8,128)S(1)} %get-tuple-element.52.rw_b), channel_id=1, source_target_pairs={{0,7},{1,2},{2,1},{3,4},{4,3},{5,6},{6,5},{7,0},{8,15},{9,10},{10,... | collective-permute-start | bytes 786440 | tf_op jit(solution)/shard_map/ppermute | solution.py:561
  13.6 12.0 %inner.1 = (f32[16,32,2048]{2,1,0:T(8,128)}, f32[16,32,2048]{2,1,0:T(8,128)}, f32[2,32,2048]{2,1,0:T(8,128)S(1)}, f32[2,32,2048]{2,1,0:T(8,128)S(1)}, f32[2,16,2...) custom-call(f32[16,32,2048]{2,1,0:T(8,128)} %v.3, f32[16,32,2048]{2,1,0:T(8,128)} %s_hbm.1, ...), custom_call_target="tpu_custom_call" | custom-call | flops 52428800 | bytes 20971520 | tf_op jit(solution)/shard_map/inner/pallas_call | solution.py:595
  25.6 0.0 collective-permute-done.2.ya
  25.6 3.2 %collective-permute-done.3.yb = f32[2,16,2048]{2,1,0:T(8,128)S(1)} collective-permute-done((f32[2,16,2048]{2,1,0:T(8,128)S(1)}, f32[2,16,2048]{2,1,0:T(8,128)S(1)}, u32[]{:S(2)}, u32[]{:S(2)}) %collective-permute-start.3) | collective-permute-done | bytes 262176 | tf_op jit(solution)/shard_map/ppermute | solution.py:561
  28.8 0.0 collective-permute-done.xa
  28.8 1.9 %edge.1 = (f32[32,2048]{1,0:T(8,128)S(1)}, f32[32,2048]{1,0:T(8,128)S(1)}, f32[16,2048]{1,0:T(8,128)S(1)}, f32[16,2048]{1,0:T(8,128)S(1)}, f32[32,2048]{1,0:T(8,...) custom-call(f32[2,32,2048]{2,1,0:T(8,128)S(1)} %get-tuple-element.45, ...), custom_call_target="tpu_custom_call" | custom-call | flops 1310720 | bytes 1048576 | tf_op jit(solution)/shard_map/edge/pallas_call | solution.py:608
  30.7 6.8 %all-to-all-start = ((f32[128,4,128]{2,1,0:T(4,128)}), f32[128,4,128]{2,1,0:T(4,128)S(1)}, u32[]{:S(2)}, u32[]{:S(2)}) async-start(f32[128,4,128]{2,1,0:T(4,128)} %bitcast), calls=%async_computation | async-start | bytes 524288 | tf_op jit(solution)/shard_map/all_to_all | solution.py:622
  37.5 0.1 collective-permute-start.4
  37.6 3.2 %collective-permute-start.5 = (f32[32,2048]{1,0:T(8,128)S(1)}, f32[32,2048]{1,0:T(8,128)S(1)}, u32[]{:S(2)}, u32[]{:S(2)}) collective-permute-start(f32[32,2048]{1,0:T(8,128)S(1)} %get-tuple-element.65.f_pl1), channel_id=1, source_target_pairs={{0,120},{8,16},{16,8},{24,32},{32,24},{40,48},{48,40},{56,64},{64,... | collective-permute-start | bytes 786440 | tf_op jit(solution)/shard_map/ppermute | solution.py:561
  40.8 2.8 %collective-permute-start.6 = (f32[16,2048]{1,0:T(8,128)S(1)}, f32[16,2048]{1,0:T(8,128)S(1)}, u32[]{:S(2)}, u32[]{:S(2)}) collective-permute-start(f32[16,2048]{1,0:T(8,128)S(1)} %get-tuple-element.66.f_row0), channel_id=1, source_target_pairs={{0,1},{1,0},{2,3},{3,2},{4,5},{5,4},{6,7},{7,6},{8,9},{9,8},{10,11... | collective-permute-start | bytes 393224 | tf_op jit(solution)/shard_map/ppermute | solution.py:561
  43.5 3.6 %collective-permute-start.7 = (f32[16,2048]{1,0:T(8,128)S(1)}, f32[16,2048]{1,0:T(8,128)S(1)}, u32[]{:S(2)}, u32[]{:S(2)}) collective-permute-start(f32[16,2048]{1,0:T(8,128)S(1)} %get-tuple-element.67.f_row1), channel_id=1, source_target_pairs={{0,7},{1,2},{2,1},{3,4},{4,3},{5,6},{6,5},{7,0},{8,15},{9,10},{10,... | collective-permute-start | bytes 393224 | tf_op jit(solution)/shard_map/ppermute | solution.py:561
  47.2 1.3 %all-to-all-done = f32[128,4,128]{2,1,0:T(4,128)S(1)} async-done(((f32[128,4,128]{2,1,0:T(4,128)}), f32[128,4,128]{2,1,0:T(4,128)S(1)}, u32[]{:S(2)}, u32[]{:S(2)}) %all-to-all-start) | async-done | bytes 262176 | tf_op jit(solution)/shard_map/all_to_all | solution.py:622
  48.5 8.5 %sweep.1 = (f32[16,32,2048]{2,1,0:T(8,128)S(1)}, f32[16,32,2048]{2,1,0:T(8,128)S(1)}, f32[16,32,2048]{2,1,0:T(8,128)S(1)}, f32[16,32,2048]{2,1,0:T(8,128)S(1)}, ...) custom-call(f32[16,32,2048]{2,1,0:T(8,128)} %k_hbm.2, ...), custom_call_target="tpu_custom_call" | custom-call | flops 41943040 | bytes 12582912 | tf_op jit(solution)/shard_map/sweep/pallas_call | solution.py:626
  56.9 0.0 collective-permute-done.6.ya
  57.0 0.0 collective-permute-done.4.xa
  57.0 0.0 collective-permute-done.5.xb
  57.0 0.2 mid.1
  57.2 0.1 collective-permute-start.8
  57.3 1.0 %collective-permute-start.9 = (f32[32,2048]{1,0:T(8,128)S(1)}, f32[32,2048]{1,0:T(8,128)S(1)}, u32[]{:S(2)}, u32[]{:S(2)}) collective-permute-start(f32[32,2048]{1,0:T(8,128)S(1)} %get-tuple-element.80.g_pl1), channel_id=1, source_target_pairs={{0,120},{8,16},{16,8},{24,32},{32,24},{40,48},{48,40},{56,64},{64,... | collective-permute-start | bytes 786440 | tf_op jit(solution)/shard_map/ppermute | solution.py:561
  58.3 2.2 %collective-permute-start.10 = (f32[16,2048]{1,0:T(8,128)S(1)}, f32[16,2048]{1,0:T(8,128)S(1)}, u32[]{:S(2)}, u32[]{:S(2)}) collective-permute-start(f32[16,2048]{1,0:T(8,128)S(1)} %get-tuple-element.81.g_row0), channel_id=1, source_target_pairs={{0,1},{1,0},{2,3},{3,2},{4,5},{5,4},{6,7},{7,6},{8,9},{9,8},{10,11... | collective-permute-start | bytes 393224 | tf_op jit(solution)/shard_map/ppermute | solution.py:561
  60.5 1.2 %collective-permute-start.11 = (f32[16,2048]{1,0:T(8,128)S(1)}, f32[16,2048]{1,0:T(8,128)S(1)}, u32[]{:S(2)}, u32[]{:S(2)}) collective-permute-start(f32[16,2048]{1,0:T(8,128)S(1)} %get-tuple-element.82.g_row1), channel_id=1, source_target_pairs={{0,7},{1,2},{2,1},{3,4},{4,3},{5,6},{6,5},{7,0},{8,15},{9,10},{10,... | collective-permute-start | bytes 393224 | tf_op jit(solution)/shard_map/ppermute | solution.py:561
  61.7 4.1 %coarse.1.interp = f32[3,32,2048]{2,1,0:T(8,128)S(1)} custom-call(f32[512,128]{1,0:T(8,128)S(1)} %bitcast.2), custom_call_target="tpu_custom_call" | custom-call | flops 20971520 | bytes 1048576 | tf_op jit(solution)/shard_map/coarse/pallas_call | solution.py:652
  65.8 6.0 %last.1 = (f32[16,32,2048]{2,1,0:T(8,128)}, f32[16,32,2048]{2,1,0:T(8,128)S(1)}) custom-call(f32[16,32,2048]{2,1,0:T(8,128)S(1)} %get-tuple-element.68.w, f32[16,32,2048]{2,1,0:T(8,128)S(1)} %get-tuple-element.69.f, f32[16,32,2048]{2,1,0:T(8,128)S(1)} %get-tuple-element.70.k, f32[16,32,2048]{2,1,0:T(8,128)S(1)} %get-tuple-element.71.cy, ...), custom_call_target="tpu_custom_call" | custom-call | flops 41943040 | bytes 20971520 | tf_op jit(solution)/shard_map/last/pallas_call | solution.py:668
  71.8 0.0 collective-permute-done.10.ya
  71.8 0.0 collective-permute-done.11.yb
  71.8 0.0 collective-permute-done.9.xb
  71.8 1.4 %finish.1 = f32[16,32,2048]{2,1,0:T(8,128)} custom-call(f32[16,32,2048]{2,1,0:T(8,128)} %get-tuple-element.83.src, f32[16,32,2048]{2,1,0:T(8,128)S(1)} %get-tuple-element.84.body, f32[2,32,2048]{2,1,0:T(8,128)S(1)} %get-tuple-element.77.wc_pl, f32[2,16,2048]{2,1,0:T(8,128)S(1)} %get-tuple-element.78.wc_row, ...), custom_call_target="tpu_custom_call", output_to_operand_aliasing={{}: (0, {})} | custom-call | flops 262144 | bytes 3145728 | tf_op jit(solution)/shard_map/finish/pallas_call | solution.py:679
  (3 shorter events, 0.0 us)
Async XLA Ops:
  1.2 27.6 %collective-permute-start = (f32[2,32,2048]{2,1,0:T(8,128)S(1)}, f32[2,32,2048]{2,1,0:T(8,128)S(1)}, u32[]{:S(2)}, u32[]{:S(2)}) collective-permute-start(f32[2,32,2048]{2,1,0:T(8,128)S(1)} %get-tuple-element.49.pl_a), channel_id=1, source_target_pairs={{0,8},{8,0},{16,24},{24,16},{32,40},{40,32},{48,56},{56,48},{64,72... | collective-permute-start | bytes 1572872 | tf_op jit(solution)/shard_map/ppermute | solution.py:561
  1.3 27.5 %collective-permute-start.1 = (f32[2,32,2048]{2,1,0:T(8,128)S(1)}, f32[2,32,2048]{2,1,0:T(8,128)S(1)}, u32[]{:S(2)}, u32[]{:S(2)}) collective-permute-start(f32[2,32,2048]{2,1,0:T(8,128)S(1)} %get-tuple-element.50.pl_b), channel_id=1, source_target_pairs={{0,120},{8,16},{16,8},{24,32},{32,24},{40,48},{48,40},{56,64},{64,... | collective-permute-start | bytes 1572872 | tf_op jit(solution)/shard_map/ppermute | solution.py:561
  6.5 19.1 %collective-permute-start.2 = (f32[2,16,2048]{2,1,0:T(8,128)S(1)}, f32[2,16,2048]{2,1,0:T(8,128)S(1)}, u32[]{:S(2)}, u32[]{:S(2)}) collective-permute-start(f32[2,16,2048]{2,1,0:T(8,128)S(1)} %get-tuple-element.51.rw_a), channel_id=1, source_target_pairs={{0,1},{1,0},{2,3},{3,2},{4,5},{5,4},{6,7},{7,6},{8,9},{9,8},{10,11... | collective-permute-start | bytes 786440 | tf_op jit(solution)/shard_map/ppermute | solution.py:561
  9.5 19.3 %collective-permute-start.3 = (f32[2,16,2048]{2,1,0:T(8,128)S(1)}, f32[2,16,2048]{2,1,0:T(8,128)S(1)}, u32[]{:S(2)}, u32[]{:S(2)}) collective-permute-start(f32[2,16,2048]{2,1,0:T(8,128)S(1)} %get-tuple-element.52.rw_b), channel_id=1, source_target_pairs={{0,7},{1,2},{2,1},{3,4},{4,3},{5,6},{6,5},{7,0},{8,15},{9,10},{10,... | collective-permute-start | bytes 786440 | tf_op jit(solution)/shard_map/ppermute | solution.py:561
  30.7 17.8 %all-to-all-start = ((f32[128,4,128]{2,1,0:T(4,128)}), f32[128,4,128]{2,1,0:T(4,128)S(1)}, u32[]{:S(2)}, u32[]{:S(2)}) async-start(f32[128,4,128]{2,1,0:T(4,128)} %bitcast), calls=%async_computation | async-start | bytes 524288 | tf_op jit(solution)/shard_map/all_to_all | solution.py:622
  37.5 19.5 %collective-permute-start.4 = (f32[32,2048]{1,0:T(8,128)S(1)}, f32[32,2048]{1,0:T(8,128)S(1)}, u32[]{:S(2)}, u32[]{:S(2)}) collective-permute-start(f32[32,2048]{1,0:T(8,128)S(1)} %get-tuple-element.64.f_pl0), channel_id=1, source_target_pairs={{0,8},{8,0},{16,24},{24,16},{32,40},{40,32},{48,56},{56,48},{64,72... | collective-permute-start | bytes 786440 | tf_op jit(solution)/shard_map/ppermute | solution.py:561
  37.6 19.4 %collective-permute-start.5 = (f32[32,2048]{1,0:T(8,128)S(1)}, f32[32,2048]{1,0:T(8,128)S(1)}, u32[]{:S(2)}, u32[]{:S(2)}) collective-permute-start(f32[32,2048]{1,0:T(8,128)S(1)} %get-tuple-element.65.f_pl1), channel_id=1, source_target_pairs={{0,120},{8,16},{16,8},{24,32},{32,24},{40,48},{48,40},{56,64},{64,... | collective-permute-start | bytes 786440 | tf_op jit(solution)/shard_map/ppermute | solution.py:561
  40.8 16.2 %collective-permute-start.6 = (f32[16,2048]{1,0:T(8,128)S(1)}, f32[16,2048]{1,0:T(8,128)S(1)}, u32[]{:S(2)}, u32[]{:S(2)}) collective-permute-start(f32[16,2048]{1,0:T(8,128)S(1)} %get-tuple-element.66.f_row0), channel_id=1, source_target_pairs={{0,1},{1,0},{2,3},{3,2},{4,5},{5,4},{6,7},{7,6},{8,9},{9,8},{10,11... | collective-permute-start | bytes 393224 | tf_op jit(solution)/shard_map/ppermute | solution.py:561
  43.5 13.4 %collective-permute-start.7 = (f32[16,2048]{1,0:T(8,128)S(1)}, f32[16,2048]{1,0:T(8,128)S(1)}, u32[]{:S(2)}, u32[]{:S(2)}) collective-permute-start(f32[16,2048]{1,0:T(8,128)S(1)} %get-tuple-element.67.f_row1), channel_id=1, source_target_pairs={{0,7},{1,2},{2,1},{3,4},{4,3},{5,6},{6,5},{7,0},{8,15},{9,10},{10,... | collective-permute-start | bytes 393224 | tf_op jit(solution)/shard_map/ppermute | solution.py:561
  57.2 14.6 %collective-permute-start.8 = (f32[32,2048]{1,0:T(8,128)S(1)}, f32[32,2048]{1,0:T(8,128)S(1)}, u32[]{:S(2)}, u32[]{:S(2)}) collective-permute-start(f32[32,2048]{1,0:T(8,128)S(1)} %get-tuple-element.79.g_pl0), channel_id=1, source_target_pairs={{0,8},{8,0},{16,24},{24,16},{32,40},{40,32},{48,56},{56,48},{64,72... | collective-permute-start | bytes 786440 | tf_op jit(solution)/shard_map/ppermute | solution.py:561
  57.3 14.5 %collective-permute-start.9 = (f32[32,2048]{1,0:T(8,128)S(1)}, f32[32,2048]{1,0:T(8,128)S(1)}, u32[]{:S(2)}, u32[]{:S(2)}) collective-permute-start(f32[32,2048]{1,0:T(8,128)S(1)} %get-tuple-element.80.g_pl1), channel_id=1, source_target_pairs={{0,120},{8,16},{16,8},{24,32},{32,24},{40,48},{48,40},{56,64},{64,... | collective-permute-start | bytes 786440 | tf_op jit(solution)/shard_map/ppermute | solution.py:561
  58.3 13.5 %collective-permute-start.10 = (f32[16,2048]{1,0:T(8,128)S(1)}, f32[16,2048]{1,0:T(8,128)S(1)}, u32[]{:S(2)}, u32[]{:S(2)}) collective-permute-start(f32[16,2048]{1,0:T(8,128)S(1)} %get-tuple-element.81.g_row0), channel_id=1, source_target_pairs={{0,1},{1,0},{2,3},{3,2},{4,5},{5,4},{6,7},{7,6},{8,9},{9,8},{10,11... | collective-permute-start | bytes 393224 | tf_op jit(solution)/shard_map/ppermute | solution.py:561
  60.5 11.3 %collective-permute-start.11 = (f32[16,2048]{1,0:T(8,128)S(1)}, f32[16,2048]{1,0:T(8,128)S(1)}, u32[]{:S(2)}, u32[]{:S(2)}) collective-permute-start(f32[16,2048]{1,0:T(8,128)S(1)} %get-tuple-element.82.g_row1), channel_id=1, source_target_pairs={{0,7},{1,2},{2,1},{3,4},{4,3},{5,6},{6,5},{7,0},{8,15},{9,10},{10,... | collective-permute-start | bytes 393224 | tf_op jit(solution)/shard_map/ppermute | solution.py:561
